TPU v7x, 128 devices: a whole 4x4x4 slice. The times are simulated.
128 devices in a mesh: com: 32 (over x, y, core), arc: 4 (over z).
Axes of the slice: x: 4, y: 4, z: 4, core: 2. Of those that a mesh axis runs over, the one named last changes fastest.
Arguments:
- flow_start: float32 [1024, 65536], P('com', 'arc'), may hold values from 0 to 1
- price_start: float32 [1024, 16384], P('com'), may hold values from -3 to 3
- cost: float32 [1024, 65536], P('com', 'arc'), may hold values from -6 to 6
- demand: float32 [1024, 16384], P('com'), may hold values from -6 to 6
- head_block: int32 [512], P('arc'), may hold values from 0 to 127
- tail_block: int32 [512], P('arc'), may hold values from 0 to 127
- head_local: int32 [65536], P('arc'), may hold values from 0 to 127
- tail_local: int32 [65536], P('arc'), may hold values from 0 to 127
- cap_class: int32 [65536], P('arc'), may hold values from 0 to 7
- cap_levels: float32 [8], replicated, may hold values from 102 to 512
Outputs:
- flow: float32 [1024, 65536], P('com', 'arc')
- price: float32 [1024, 16384], P('com')
Inputs may be any that keep to these rules, and one draw needn't show every extreme that they name: `head_block`: node block indices. `tail_block`: node block indices. `head_local`: positions within a node block. `tail_local`: positions within a node block.
All inputs are finite; a program needn't handle non-finite values.
Results may differ from a plain program's by a relative error of at most 0.00016.
Values sent between devices are 32-bit elements; how exact they have to be, the bound alone decides.
No kernel may reach another device: no remote copies, remote signals or barrier semaphores. Data moves between devices by JAX's collectives and lax.ppermute only.
A program may use at most 128 MiB of HBM per device.

v0:
```python
import jax
import jax.numpy as jnp
from jax import lax
from jax.sharding import PartitionSpec as P

NODES = 16384
BLOCK = 128
CLASSES = 8
ITERS = 4
NEWTON = 3


step_primal = 0.25
step_dual = 0.1
soft_width = 0.05
highest = lax.Precision.HIGHEST


def column_sums(values, theta):
    excess = jnp.maximum(values - theta, 0.0)
    return (jnp.sum(excess, axis=0), jnp.sum(jnp.minimum(excess / soft_width, 1.0), axis=0))


def theta_step(theta, total, active, capacity):
    return theta + jnp.maximum(total - capacity, 0.0) / jnp.maximum(active, 1.0)


def on_device(
    flow_start,
    price_start,
    cost,
    demand,
    head_block,
    tail_block,
    head_local,
    tail_local,
    cap_class,
    cap_levels,
):
    com_rows, arc_cols = flow_start.shape
    blocks = arc_cols // BLOCK
    node_blocks = NODES // BLOCK
    lanes = jnp.arange(BLOCK, dtype=jnp.int32)
    head_table = (head_local.reshape(blocks, BLOCK)[:, :, None] == lanes).astype(jnp.float32)
    tail_table = (tail_local.reshape(blocks, BLOCK)[:, :, None] == lanes).astype(jnp.float32)
    block_ids = jnp.arange(node_blocks, dtype=jnp.int32)
    head_owner = (head_block[:, None] == block_ids).astype(jnp.float32)
    tail_owner = (tail_block[:, None] == block_ids).astype(jnp.float32)
    class_ids = jnp.arange(CLASSES, dtype=jnp.int32)
    capacity = jnp.sum(
        jnp.where(cap_class[:, None] == class_ids, cap_levels[None, :], 0.0), axis=1
    ).reshape(blocks, BLOCK)
    flow = flow_start.reshape(com_rows, blocks, BLOCK)
    unit_cost = cost.reshape(com_rows, blocks, BLOCK)
    price = price_start
    for step in range(ITERS):
        grid = price.reshape(com_rows, node_blocks, BLOCK)
        at_head = jnp.einsum("jn,knl->jkl", head_owner, grid, precision=highest)
        at_head = jnp.einsum("jkl,jal->kja", at_head, head_table, precision=highest)
        at_tail = jnp.einsum("jn,knl->jkl", tail_owner, grid, precision=highest)
        at_tail = jnp.einsum("jkl,jal->kja", at_tail, tail_table, precision=highest)
        trial = flow - step_primal * (unit_cost - (at_head - at_tail))
        values = lax.all_to_all(trial, "com", split_axis=1, concat_axis=0, tiled=True)
        limits = lax.all_to_all(capacity[None], "com", split_axis=1, concat_axis=0, tiled=True)
        theta = jnp.zeros(values.shape[1:], jnp.float32)
        for inner in range(NEWTON):
            total, active = column_sums(values, theta)
            theta = theta_step(theta, total, active, limits[0])
        fresh = lax.all_to_all(
            jnp.maximum(values - theta, 0.0), "com", split_axis=0, concat_axis=1, tiled=True
        )
        flows = 2.0 * fresh - flow
        inward = jnp.einsum("kja,jal->jkl", flows, head_table, precision=highest)
        inward = jnp.einsum("jn,jkl->knl", head_owner, inward, precision=highest)
        outward = jnp.einsum("kja,jal->jkl", flows, tail_table, precision=highest)
        outward = jnp.einsum("jn,jkl->knl", tail_owner, outward, precision=highest)
        balance = (inward - outward).reshape(com_rows, NODES)
        summed = lax.psum(balance, "arc")
        price = price + step_dual * (demand - summed)
        flow = fresh
    return (flow.reshape(com_rows, arc_cols), price)


def solution(mesh):
    return jax.shard_map(
        on_device,
        mesh=mesh,
        in_specs=(
            P("com", "arc"),
            P("com", None),
            P("com", "arc"),
            P("com", None),
            P("arc"),
            P("arc"),
            P("arc"),
            P("arc"),
            P("arc"),
            P(),
        ),
        out_specs=(P("com", "arc"), P("com", None)),
        check_vma=False,
    )
```

profile of v0, /device:TPU:6, one launch (start us, length us, event | category | flops | bytes accessed | tf_op | source)
XLA Modules:
  0.0 768.5 jit_solution(1024255487486587289)
XLA Ops:
  11.9 9.8 %fusion.7 = f32[128,128,32]{1,2,0:T(8,128)S(1)} fusion(s32[128,128]{1,0:T(8,128)S(1)} %bitcast.325, f32[128,32,128]{2,0,1:T(8,128)S(1)} %fusion.132), kind=kOutput, calls=%fused_computation.8 | convolution fusion | flops 807403520 | bytes 4259840 | tf_op jit(solution)/shard_map/jkl,jal->kja/dot_general | solution.py:61
  21.8 9.1 %fusion.33 = f32[32,128,128]{2,0,1:T(8,128)} fusion(f32[128,128,32]{1,2,0:T(8,128)S(1)} %fusion.7, f32[128,32,128]{2,0,1:T(8,128)S(1)} %fusion.119, s32[128,128]{1,0:T(8,128)S(1)} %bitcast.317, f32[32,16384]{1,0:T(8,128)S(1)} %copy-done, f32[32,16384]{1,0:T(8,128)S(1)} %copy-done.9), kind=kOutput, calls=%fused_computation.43 | convolution fusion | flops 809500672 | bytes 10551296 | tf_op jit(solution)/shard_map/jkl,jal->kja/dot_general | solution.py:59
  30.8 7.8 %all-to-all-start = ((f32[32,128,128]{2,0,1:T(8,128)}), f32[32,128,128]{2,0,1:T(8,128)}, u32[]{:S(2)}, u32[]{:S(2)}) async-start(f32[32,128,128]{2,0,1:T(8,128)} %fusion.33), calls=%async_computation | async-start | bytes 4194304 | tf_op jit(solution)/shard_map/all_to_all | solution.py:63
  39.6 25.4 %all-to-all-done = f32[32,128,128]{2,0,1:T(8,128)} async-done(((f32[32,128,128]{2,0,1:T(8,128)}), f32[32,128,128]{2,0,1:T(8,128)}, u32[]{:S(2)}, u32[]{:S(2)}) %all-to-all-start) | async-done | bytes 2097184 | tf_op jit(solution)/shard_map/all_to_all | solution.py:63
  65.0 6.5 all-to-all-start.1
  82.8 33.6 %all_to_all.168 = f32[1024,4,128]{2,1,0:T(4,128)S(1)} all-to-all(f32[1024,4,128]{2,1,0:T(4,128)S(1)} %copy.114), channel_id=1, replica_groups=mesh['com'=32,'arc'=4] {'com'}, dimensions={0} | all-to-all | bytes 4194304 | tf_op jit(solution)/shard_map/all_to_all | solution.py:69
  119.4 7.4 fusion.6
  126.9 7.5 fusion.14
  148.3 59.0 %all-reduce.5.cloned.1.call-done = f32[32,16384]{1,0:T(8,128)} async-done(((f32[32,16384]{1,0:T(8,128)}), f32[32,16384]{1,0:T(8,128)}) %all-reduce.5.cloned.1.call-update) | async-done | bytes 2097168 | tf_op jit(solution)/shard_map/psum | solution.py:78
  213.4 9.8 %fusion.5 = f32[128,128,32]{1,2,0:T(8,128)S(1)} fusion(s32[128,128]{1,0:T(8,128)S(1)} %bitcast.327, f32[128,32,128]{2,0,1:T(8,128)S(1)} %fusion.129), kind=kOutput, calls=%fused_computation.6 | convolution fusion | flops 807403520 | bytes 4259840 | tf_op jit(solution)/shard_map/jkl,jal->kja/dot_general | solution.py:61
  223.3 10.2 %fusion.35 = f32[32,128,128]{2,0,1:T(8,128)S(1)} fusion(f32[32,32,4,128]{3,0,2,1:T(8,128)S(1)} %copy-done.6, f32[128,128,32]{1,2,0:T(8,128)S(1)} %fusion.5, f32[128,32,128]{2,0,1:T(8,128)S(1)} %fusion.116, s32[128,128]{1,0:T(8,128)S(1)} %bitcast.319, f32[32,16384]{1,0:T(8,128)S(1)} %copy-done), kind=kOutput, calls=%fused_computation.45 | convolution fusion | flops 809500672 | bytes 10551296 | tf_op jit(solution)/shard_map/jkl,jal->kja/dot_general | solution.py:59
  233.5 33.8 %all_to_all.169 = f32[32,128,128]{2,0,1:T(8,128)S(1)} all-to-all(f32[32,128,128]{2,0,1:T(8,128)S(1)} %fusion.35), channel_id=1, replica_groups=mesh['com'=32,'arc'=4] {'com'}, dimensions={1} | all-to-all | bytes 4194304 | tf_op jit(solution)/shard_map/all_to_all | solution.py:63
  270.2 32.5 %all_to_all.170 = f32[1024,4,128]{2,1,0:T(4,128)S(1)} all-to-all(f32[1024,4,128]{2,1,0:T(4,128)S(1)} %copy.125), channel_id=1, replica_groups=mesh['com'=32,'arc'=4] {'com'}, dimensions={0} | all-to-all | bytes 4194304 | tf_op jit(solution)/shard_map/all_to_all | solution.py:69
  304.4 7.4 fusion.4
  311.8 7.5 fusion.12
  333.2 56.6 %all-reduce.7.cloned.1.call-done = f32[32,16384]{1,0:T(8,128)} async-done(((f32[32,16384]{1,0:T(8,128)}), f32[32,16384]{1,0:T(8,128)}) %all-reduce.7.cloned.1.call-update) | async-done | bytes 2097168 | tf_op jit(solution)/shard_map/psum | solution.py:78
  397.6 9.8 %fusion.3 = f32[128,128,32]{1,2,0:T(8,128)S(1)} fusion(s32[128,128]{1,0:T(8,128)S(1)} %bitcast.329, f32[128,32,128]{2,0,1:T(8,128)S(1)} %fusion.126), kind=kOutput, calls=%fused_computation.4 | convolution fusion | flops 807403520 | bytes 4259840 | tf_op jit(solution)/shard_map/jkl,jal->kja/dot_general | solution.py:61
  407.4 10.2 %fusion.37 = f32[32,128,128]{2,0,1:T(8,128)S(1)} fusion(f32[32,32,4,128]{3,0,2,1:T(8,128)S(1)} %copy-done.4, f32[128,128,32]{1,2,0:T(8,128)S(1)} %fusion.3, f32[128,32,128]{2,0,1:T(8,128)S(1)} %fusion.113, s32[128,128]{1,0:T(8,128)S(1)} %bitcast.321, f32[32,16384]{1,0:T(8,128)S(1)} %copy-done), kind=kOutput, calls=%fused_computation.47 | convolution fusion | flops 809500672 | bytes 10551296 | tf_op jit(solution)/shard_map/jkl,jal->kja/dot_general | solution.py:59
  417.6 33.8 %all_to_all.171 = f32[32,128,128]{2,0,1:T(8,128)S(1)} all-to-all(f32[32,128,128]{2,0,1:T(8,128)S(1)} %fusion.37), channel_id=1, replica_groups=mesh['com'=32,'arc'=4] {'com'}, dimensions={1} | all-to-all | bytes 4194304 | tf_op jit(solution)/shard_map/all_to_all | solution.py:63
  454.4 32.2 %all_to_all.172 = f32[1024,4,128]{2,1,0:T(4,128)S(1)} all-to-all(f32[1024,4,128]{2,1,0:T(4,128)S(1)} %copy.135), channel_id=1, replica_groups=mesh['com'=32,'arc'=4] {'com'}, dimensions={0} | all-to-all | bytes 4194304 | tf_op jit(solution)/shard_map/all_to_all | solution.py:69
  488.3 7.4 fusion.2
  495.7 7.5 fusion.10
  517.1 56.5 %all-reduce.9.cloned.1.call-done = f32[32,16384]{1,0:T(8,128)} async-done(((f32[32,16384]{1,0:T(8,128)}), f32[32,16384]{1,0:T(8,128)}) %all-reduce.9.cloned.1.call-update) | async-done | bytes 2097168 | tf_op jit(solution)/shard_map/psum | solution.py:78
  579.7 9.8 %fusion.1 = f32[128,128,32]{1,2,0:T(8,128)S(1)} fusion(s32[128,128]{1,0:T(8,128)S(1)} %bitcast.331, f32[128,32,128]{2,0,1:T(8,128)S(1)} %fusion.123), kind=kOutput, calls=%fused_computation.2 | convolution fusion | flops 807403520 | bytes 4259840 | tf_op jit(solution)/shard_map/jkl,jal->kja/dot_general | solution.py:61
  589.5 10.2 %fusion.39 = f32[32,128,128]{2,0,1:T(8,128)S(1)} fusion(f32[32,32,4,128]{3,0,2,1:T(8,128)S(1)} %copy-done.2, f32[128,128,32]{1,2,0:T(8,128)S(1)} %fusion.1, f32[128,32,128]{2,0,1:T(8,128)S(1)} %fusion.110, s32[128,128]{1,0:T(8,128)S(1)} %bitcast.323, f32[32,16384]{1,0:T(8,128)S(1)} %copy-done), kind=kOutput, calls=%fused_computation.49 | convolution fusion | flops 809500672 | bytes 10551296 | tf_op jit(solution)/shard_map/jkl,jal->kja/dot_general | solution.py:59
  599.8 33.8 %all_to_all.173 = f32[32,128,128]{2,0,1:T(8,128)S(1)} all-to-all(f32[32,128,128]{2,0,1:T(8,128)S(1)} %fusion.39), channel_id=1, replica_groups=mesh['com'=32,'arc'=4] {'com'}, dimensions={1} | all-to-all | bytes 4194304 | tf_op jit(solution)/shard_map/all_to_all | solution.py:63
  636.5 32.3 %all_to_all.174 = f32[1024,4,128]{2,1,0:T(4,128)S(1)} all-to-all(f32[1024,4,128]{2,1,0:T(4,128)S(1)} %copy.145), channel_id=1, replica_groups=mesh['com'=32,'arc'=4] {'com'}, dimensions={0} | all-to-all | bytes 4194304 | tf_op jit(solution)/shard_map/all_to_all | solution.py:69
  670.7 7.5 fusion
  678.2 7.5 fusion.8
  699.4 4.3 copy.147
  706.9 49.3 %all-reduce.11.cloned.1.call-done = f32[32,16384]{1,0:T(8,128)} async-done(((f32[32,16384]{1,0:T(8,128)}), f32[32,16384]{1,0:T(8,128)}) %all-reduce.11.cloned.1.call-update) | async-done | bytes 2097168 | tf_op jit(solution)/shard_map/psum | solution.py:78
  756.2 5.2 multiply_add_fusion
  (127 shorter events, 112.4 us)
Async XLA Ops:
  7.2 14.6 %copy-start = (f32[32,16384]{1,0:T(8,128)S(1)}, f32[32,16384]{1,0:T(8,128)}, u32[]{:S(2)}) copy-start(f32[32,16384]{1,0:T(8,128)} %param.12) | copy-start | bytes 6291460
  7.2 2.1 copy-start.15
  9.3 1.3 copy-start.16
  10.6 1.3 copy-start.13
  11.9 9.9 %copy-start.9 = (f32[32,16384]{1,0:T(8,128)S(1)}, f32[32,16384]{1,0:T(8,128)}, u32[]{:S(2)}) copy-start(f32[32,16384]{1,0:T(8,128)} %param.10) | copy-start | bytes 6291460
  11.9 9.9 %copy-start.12 = (s32[16384]{0:T(1024)S(1)}, s32[16384]{0:T(1024)}, u32[]{:S(2)}) copy-start(s32[16384]{0:T(1024)} %param.16) | copy-start | bytes 196612
  30.8 7.8 %copy-start.14 = (s32[16384]{0:T(1024)S(1)}, s32[16384]{0:T(1024)}, u32[]{:S(2)}) copy-start(s32[16384]{0:T(1024)} %param.18) | copy-start | bytes 196612
  30.8 7.8 %copy-start.17 = (f32[8]{0:T(128)S(1)}, f32[8]{0:T(128)}, u32[]{:S(2)}) copy-start(f32[8]{0:T(128)} %param.19) | copy-start | bytes 100
  30.8 34.2 %all-to-all-start = ((f32[32,128,128]{2,0,1:T(8,128)}), f32[32,128,128]{2,0,1:T(8,128)}, u32[]{:S(2)}, u32[]{:S(2)}) async-start(f32[32,128,128]{2,0,1:T(8,128)} %fusion.33), calls=%async_computation | async-start | bytes 4194304 | tf_op jit(solution)/shard_map/all_to_all | solution.py:63
  65.0 12.0 %all-to-all-start.1 = ((f32[1,128,128]{2,0,1:T(1,128)}), f32[1,128,128]{2,0,1:T(1,128)S(1)}, u32[]{:S(2)}, u32[]{:S(2)}) async-start(f32[1,128,128]{2,0,1:T(1,128)} %bitcast.8), calls=%async_computation.1 | async-start | bytes 131072 | tf_op jit(solution)/shard_map/all_to_all | solution.py:64
  71.5 135.9 %all-reduce.5.cloned.1.call-start = ((), (), s32[]{:S(2)}) async-start(), calls=%async_computation.9 | async-start | bytes 4194304 | tf_op jit(solution)/shard_map/psum | solution.py:78
  77.1 4.2 copy-start.11
  116.5 1.6 copy-start.10
  118.1 1.3 copy-start.5
  148.0 241.7 %all-reduce.7.cloned.1.call-start = ((), (), s32[]{:S(2)}) async-start(), calls=%async_computation.10 | async-start | bytes 4194304 | tf_op jit(solution)/shard_map/psum | solution.py:78
  213.4 9.9 %copy-start.6 = (f32[32,32,4,128]{3,0,2,1:T(8,128)S(1)}, f32[32,32,4,128]{3,0,2,1:T(8,128)}, u32[]{:S(2)}) copy-start(f32[32,32,4,128]{3,0,2,1:T(8,128)} %copy-done.5) | copy-start | bytes 6291460
  303.1 1.3 copy-start.3
  332.9 240.7 %all-reduce.9.cloned.1.call-start = ((), (), s32[]{:S(2)}) async-start(), calls=%async_computation.11 | async-start | bytes 4194304 | tf_op jit(solution)/shard_map/psum | solution.py:78
  393.7 1.4 copy-start.7
  397.5 9.9 %copy-start.4 = (f32[32,32,4,128]{3,0,2,1:T(8,128)S(1)}, f32[32,32,4,128]{3,0,2,1:T(8,128)}, u32[]{:S(2)}) copy-start(f32[32,32,4,128]{3,0,2,1:T(8,128)} %copy-done.3) | copy-start | bytes 6291460
  486.9 1.3 copy-start.1
  516.8 239.4 %all-reduce.11.cloned.1.call-start = ((), (), s32[]{:S(2)}) async-start(), calls=%async_computation.12 | async-start | bytes 4194304 | tf_op jit(solution)/shard_map/psum | solution.py:78
  579.7 9.9 %copy-start.2 = (f32[32,32,4,128]{3,0,2,1:T(8,128)S(1)}, f32[32,32,4,128]{3,0,2,1:T(8,128)}, u32[]{:S(2)}) copy-start(f32[32,32,4,128]{3,0,2,1:T(8,128)} %copy-done.1) | copy-start | bytes 6291460
  668.9 1.3 copy-start.8
Sparse Core Ops, SparseCore 0:
  148.2 59.1 all-reduce.4
  333.1 56.6 all-reduce.6
  516.9 56.6 all-reduce.8
  699.5 56.6 all-reduce.10
where the time goes:
time: 777 us; the launch traced here: 768 us
  waiting for transfers between devices  247 us (32%)
  blocking collectives  232 us (30%)
  matrix products  175 us (23%)
  local copies, waits for them, and re-layouts  55.5 us (7%)
  other arithmetic  28.6 us (4%)
  starting transfers between devices  15.1 us (2%)
  between operations  15 us (2%)
    psum x4, waiting for transfers between devices, on_device(): summed = lax.psum(balance, 'arc')  221 us
    all_to_all x4, blocking collectives, on_device(): lax.all_to_all(jnp.maximum(values - theta, 0.0), 'com', split_axis=0, con...  130 us
    all_to_all x3, blocking collectives, on_device(): lax.all_to_all(trial, 'com', split_axis=1, concat_axis=0, tiled=True)  101 us
    dot_general x4, matrix products, on_device(): at_head = jnp.einsum('jkl,jal->kja', at_head, head_table, precision=highest)  39.7 us
    dot_general x4, matrix products, on_device(): at_tail = jnp.einsum('jkl,jal->kja', at_tail, tail_table, precision=highest)  39.3 us
    dot_general x4, matrix products, on_device(): inward = jnp.einsum('kja,jal->jkl', flows, head_table, precision=highest)  29.9 us
    dot_general x4, matrix products, on_device(): outward = jnp.einsum('kja,jal->jkl', flows, tail_table, precision=highest)  29.7 us
    unnamed x44, local copies, waits for them, and re-layouts  25.7 us
  transfers between devices with their start and end apart: 6, of which 6 were waited for; matrix products, arithmetic and copies ran while one was open for 2% of the time, Pallas kernels for 0%

commit v1 on v0

v1 whole, which is shorter than its diff:
```python
import functools

import jax
import jax.numpy as jnp
from jax import lax
from jax.experimental import pallas as pl
from jax.experimental.pallas import tpu as pltpu
from jax.sharding import PartitionSpec as P

NODES = 16384
BLOCK = 128
ITERS = 4
NEWTON = 3

step_primal = 0.25
step_dual = 0.1
soft_width = 0.05

SHARDS = 4
OWNERS = 32
OWN = 512
QUADS = OWN // BLOCK
UNROLL = 2
LIMIT = 48 << 20

f32 = jnp.float32
bf16 = jnp.bfloat16
vmem = pl.BlockSpec(memory_space=pltpu.VMEM)
smem = pl.BlockSpec(memory_space=pltpu.SMEM)
params = pltpu.CompilerParams(vmem_limit_bytes=LIMIT)


def node_slice(block):
    return pl.ds(pl.multiple_of(block * BLOCK, BLOCK), BLOCK)


def arc_slice(start, piece):
    return pl.ds(pl.multiple_of(start + piece * BLOCK, BLOCK), BLOCK)


def gather_kernel(head_block, tail_block, head_local, tail_local, price, flow, cost, trial):
    for shard in range(SHARDS):

        def step(o, carry):
            for u in range(UNROLL):
                owner = o * UNROLL + u
                start = owner * OWN
                for q in range(QUADS):
                    j = (shard * OWNERS + owner) * QUADS + q
                    head = jnp.broadcast_to(head_local[pl.ds(j, 1), :], (8, BLOCK))
                    tail = jnp.broadcast_to(tail_local[pl.ds(j, 1), :], (8, BLOCK))
                    at_head = jnp.take_along_axis(price[:, node_slice(head_block[j])], head, axis=1)
                    at_tail = jnp.take_along_axis(price[:, node_slice(tail_block[j])], tail, axis=1)
                    where = arc_slice(start, q)
                    trial[shard * OWNERS + owner, :, q * BLOCK : (q + 1) * BLOCK] = flow[
                        shard, :, where
                    ] - step_primal * (cost[shard, :, where] - (at_head - at_tail))
            return carry

        lax.fori_loop(0, OWNERS // UNROLL, step, 0)


def project_kernel(levels, classes, values, theta_out):
    cls = classes[...]
    capacity = jnp.zeros((QUADS, BLOCK), f32)
    for k in range(8):
        capacity = jnp.where(cls == k, levels[k], capacity)
    caps = [capacity[q : q + 1] for q in range(QUADS)]
    thetas = [jnp.zeros((1, BLOCK), f32) for q in range(QUADS)]
    groups = values.shape[0]
    for inner in range(NEWTON):
        wide = [jnp.broadcast_to(t, (8, BLOCK)) for t in thetas]

        def step(o, carry):
            out = list(carry)
            for u in range(8):
                for q in range(QUADS):
                    excess = jnp.maximum(values[o * 8 + u, :, q * BLOCK : (q + 1) * BLOCK] - wide[q], 0.0)
                    out[2 * q] = out[2 * q] + excess
                    out[2 * q + 1] = out[2 * q + 1] + jnp.minimum(excess * (1.0 / soft_width), 1.0)
            return tuple(out)

        sums = lax.fori_loop(0, groups // 8, step, tuple(jnp.zeros((8, BLOCK), f32) for _ in range(2 * QUADS)))
        for q in range(QUADS):
            total = jnp.sum(sums[2 * q], axis=0, keepdims=True)
            active = jnp.sum(sums[2 * q + 1], axis=0, keepdims=True)
            thetas[q] = thetas[q] + jnp.maximum(total - caps[q], 0.0) / jnp.maximum(active, 1.0)
    tile = jnp.concatenate(thetas, axis=0)

    def store(i, carry):
        theta_out[i] = tile
        return carry

    lax.fori_loop(0, theta_out.shape[0], store, 0, unroll=8)


def scatter_kernel(
    head_block, tail_block, head_local, tail_local, trial, theta, flow, price, demand, fresh_out, price_out, balance
):
    balance[...] = jnp.zeros_like(balance)
    lanes = lax.broadcasted_iota(jnp.int32, (BLOCK, BLOCK), 0).astype(jnp.int16)
    one = jnp.ones((), bf16)
    zero = jnp.zeros((), bf16)

    def table(local):
        return jnp.where(lanes == jnp.broadcast_to(local.astype(jnp.int16), (BLOCK, BLOCK)), one, zero)

    for shard in range(SHARDS):

        def step(o, carry):
            found = []
            for u in range(UNROLL):
                owner = o * UNROLL + u
                start = owner * OWN
                for q in range(QUADS):
                    j = (shard * OWNERS + owner) * QUADS + q
                    where = arc_slice(start, q)
                    limit = theta[shard * OWNERS + owner, q : q + 1, :]
                    fresh = jnp.maximum(
                        trial[shard * OWNERS + owner, :, q * BLOCK : (q + 1) * BLOCK] - limit, 0.0
                    )
                    fresh_out[shard, :, where] = fresh
                    extra = 2.0 * fresh - flow[shard, :, where]
                    high = extra.astype(bf16)
                    low = (extra - high.astype(f32)).astype(bf16)
                    both = jnp.concatenate([high, low], axis=0)
                    tables = jnp.concatenate(
                        [table(head_local[pl.ds(j, 1), :]), table(tail_local[pl.ds(j, 1), :])], axis=0
                    )
                    sums = lax.dot_general(both, tables, (((1,), (1,)), ((), ())), preferred_element_type=f32)
                    found.append((j, sums[:8] + sums[8:]))
            for j, sums in found:
                balance[:, node_slice(head_block[j])] += sums[:, :BLOCK]
                balance[:, node_slice(tail_block[j])] -= sums[:, BLOCK:]
            return carry

        lax.fori_loop(0, OWNERS // UNROLL, step, 0)
    price_out[...] = price[...] + step_dual * (demand[...] - balance[...])


def gather(tables, price, flow, cost):
    return pl.pallas_call(
        gather_kernel,
        in_specs=[smem, smem] + [vmem] * 5,
        out_specs=vmem,
        out_shape=jax.ShapeDtypeStruct((SHARDS * OWNERS, 8, OWN), f32),
        compiler_params=params,
        name="arc_trial",
    )(*tables, price, flow, cost)


def project(levels, classes, values, receivers):
    return pl.pallas_call(
        project_kernel,
        in_specs=[smem, vmem, vmem],
        out_specs=vmem,
        out_shape=jax.ShapeDtypeStruct((receivers, QUADS, BLOCK), f32),
        compiler_params=params,
        name="project",
    )(levels, classes, values)


def scatter(tables, trial, theta, flow, price, demand):
    return pl.pallas_call(
        scatter_kernel,
        in_specs=[smem, smem] + [vmem] * 7,
        out_specs=[vmem, vmem],
        out_shape=[
            jax.ShapeDtypeStruct((SHARDS, 8, OWNERS * OWN), f32),
            jax.ShapeDtypeStruct((8, NODES), f32),
        ],
        scratch_shapes=[pltpu.VMEM((8, NODES), f32)],
        compiler_params=params,
        name="balance",
    )(*tables, trial, theta, flow, price, demand)


def on_device(
    flow_start,
    price_start,
    cost,
    demand,
    head_block,
    tail_block,
    head_local,
    tail_local,
    cap_class,
    cap_levels,
):
    com_rows, arc_cols = flow_start.shape
    part = lax.axis_index("arc")
    place = lax.axis_index("com")
    blocks = arc_cols // BLOCK

    packed = jnp.concatenate(
        [
            head_local.reshape(blocks, BLOCK),
            tail_local.reshape(blocks, BLOCK),
            head_block.reshape(1, BLOCK),
            tail_block.reshape(1, BLOCK),
            jnp.zeros((6, BLOCK), jnp.int32),
        ],
        axis=0,
    )
    every = lax.all_gather(packed, "arc", axis=0)
    tables = (
        every[:, 2 * blocks].reshape(SHARDS * blocks),
        every[:, 2 * blocks + 1].reshape(SHARDS * blocks),
        every[:, :blocks].reshape(SHARDS * blocks, BLOCK),
        every[:, blocks : 2 * blocks].reshape(SHARDS * blocks, BLOCK),
    )
    classes = lax.dynamic_slice(cap_class.reshape(blocks, BLOCK), (place * QUADS, 0), (QUADS, BLOCK))

    def spread(values):
        return lax.all_to_all(values.reshape(SHARDS, 8, arc_cols), "arc", split_axis=0, concat_axis=0, tiled=True)

    flow = spread(flow_start)
    unit_cost = spread(cost)
    price = lax.dynamic_slice(price_start, (part * 8, 0), (8, NODES))
    wanted = lax.dynamic_slice(demand, (part * 8, 0), (8, NODES))
    both = ("arc", "com")
    for step in range(ITERS):
        trial = gather(tables, price, flow, unit_cost)
        values = lax.all_to_all(trial, both, split_axis=0, concat_axis=0, tiled=True)
        theta = project(cap_levels, classes, values, SHARDS * OWNERS)
        theta = lax.all_to_all(theta, both, split_axis=0, concat_axis=0, tiled=True)
        flow, price = scatter(tables, trial, theta, flow, price, wanted)
    out = spread(flow).reshape(com_rows, arc_cols)
    return out, lax.all_gather(price, "arc", axis=0, tiled=True)


def solution(mesh):
    return jax.shard_map(
        on_device,
        mesh=mesh,
        in_specs=(
            P("com", "arc"),
            P("com", None),
            P("com", "arc"),
            P("com", None),
            P("arc"),
            P("arc"),
            P("arc"),
            P("arc"),
            P("arc"),
            P(),
        ),
        out_specs=(P("com", "arc"), P("com", None)),
        check_vma=False,
    )
```

time: 777 us -> 470 us (0.60)
  waiting for transfers between devices: 247 us -> 59.7 us
  matrix products: 175 us -> 0 us
  Pallas kernels: 0 us -> 126 us
  local copies, waits for them, and re-layouts: 55.5 us -> 10.9 us
  other arithmetic: 28.6 us -> 0 us
  starting transfers between devices: 15.1 us -> 23.5 us
    psum x4 -> x0, waiting for transfers between devices: 221 us -> none  [on_device(): summed = lax.psum(balance, 'arc')]
    dot_general x32 -> x0, matrix products: 175 us -> none  [the longest x4 39.7 us: on_device(): at_head = jnp.einsum('jkl,jal->kja', at_head, head_table, precision=highest)]
    pallas_call x0 -> x12, Pallas kernels: none -> 126 us  [the longest x4 76.9 us: scatter(): pl.pallas_call(scatter_kernel, in_specs=[smem, smem] + [vmem] * 7, out_sp...]
    all_gather x0 -> x1, blocking collectives: none -> 35.3 us  [on_device(): every = lax.all_gather(packed, 'arc', axis=0)]
    all_to_all x7, blocking collectives: 232 us -> 197 us  [the longest x3 105 us: on_device(): lax.all_to_all(trial, both, split_axis=0, concat_axis=0, tiled=True)]
    all_to_all x2 -> x4, waiting for transfers between devices: 25.9 us -> 59.7 us  [the longest x1 28.3 us: on_device(): lax.all_to_all(trial, both, split_axis=0, concat_axis=0, tiled=True)]
    unnamed x44 -> x38, local copies, waits for them, and re-layouts: 25.7 us -> 9.05 us
    sub x4 -> x0, local copies, waits for them, and re-layouts: 11.7 us -> none  [on_device(): balance = (inward - outward).reshape(com_rows, NODES)]
  transfers between devices with their start and end apart: 6 -> 5, of which waited for: 6 -> 3; matrix products, arithmetic and copies ran while one was open for 2% -> 0% of each run, Pallas kernels for 0% -> 0%
where the time goes in v1:
time: 470 us; the launch traced here: 466 us
  blocking collectives  232 us (49%)
  Pallas kernels  126 us (27%)
  waiting for transfers between devices  59.7 us (13%)
  starting transfers between devices  23.5 us (5%)
  between operations  14.3 us (3%)
  local copies, waits for them, and re-layouts  10.9 us (2%)
    all_to_all x3, blocking collectives, on_device(): lax.all_to_all(trial, both, split_axis=0, concat_axis=0, tiled=True)  105 us
    pallas_call x4, Pallas kernels, scatter(): pl.pallas_call(scatter_kernel, in_specs=[smem, smem] + [vmem] * 7, out_sp...  76.9 us
    all_to_all x1, blocking collectives, spread(): lax.all_to_all(values.reshape(SHARDS, 8, arc_cols), 'arc', split_axis=0,...  48 us
    all_to_all x3, blocking collectives, on_device(): theta = lax.all_to_all(theta, both, split_axis=0, concat_axis=0, tiled=True)  44 us
    pallas_call x4, Pallas kernels, gather(): pl.pallas_call(gather_kernel, in_specs=[smem, smem] + [vmem] * 5, out_spe...  39.1 us
    all_gather x1, blocking collectives, on_device(): every = lax.all_gather(packed, 'arc', axis=0)  35.3 us
    all_to_all x1, waiting for transfers between devices, on_device(): lax.all_to_all(trial, both, split_axis=0, concat_axis=0, tiled=True)  28.3 us
    all_to_all x2, waiting for transfers between devices, spread(): lax.all_to_all(values.reshape(SHARDS, 8, arc_cols), 'arc', split_axis=0,...  22.7 us
  transfers between devices with their start and end apart: 5, of which 3 were waited for; matrix products, arithmetic and copies ran while one was open for 0% of the time, Pallas kernels for 0%

profile of v1, /device:TPU:6, one launch (start us, length us, event | category | flops | bytes accessed | tf_op | source)
XLA Modules:
  0.0 466.4 jit_solution(5164250028353092259)
XLA Ops:
  7.2 5.5 %all-to-all-start = ((f32[4,8,16384]{2,1,0:T(8,128)}), f32[4,8,16384]{2,1,0:T(8,128)}, u32[]{:S(2)}, u32[]{:S(2)}) async-start(f32[4,8,16384]{2,1,0:T(8,128)} %bitcast.48), calls=%async_computation | async-start | bytes 4194304 | tf_op jit(solution)/shard_map/all_to_all | solution.py:215
  12.7 35.3 %all-gather = s32[1056,128]{1,0:T(8,128)S(1)} all-gather(s32[264,128]{1,0:T(8,128)S(1)} %concatenate.3), channel_id=2, replica_groups=mesh['com'=32,'arc'=4] {'arc'}, dimensions={0}, use_global_device_ids=true | all-gather | bytes 675840 | tf_op jit(solution)/shard_map/all_gather | solution.py:205
  48.1 4.5 all-to-all-start.1
  52.6 22.7 %all-to-all-done.1.cost = f32[4,8,16384]{2,1,0:T(8,128)} async-done(((f32[4,8,16384]{2,1,0:T(8,128)}), f32[4,8,16384]{2,1,0:T(8,128)}, u32[]{:S(2)}, u32[]{:S(2)}) %all-to-all-start.1) | async-done | bytes 2097184 | tf_op jit(solution)/shard_map/all_to_all | solution.py:215
  75.3 9.7 %arc_trial.4.trial = f32[128,8,512]{2,1,0:T(8,128)S(1)} custom-call(s32[512]{0:T(512)S(1)} %bitcast.37, s32[512]{0:T(512)S(1)} %bitcast.29, s32[512,128]{1,0:T(8,128)S(1)} %bitcast.21, s32[512,128]{1,0:T(8,128)S(1)} %bitcast.13, f32[8,16384]{1,0:T(8,128)S(1)} %constant_dynamic-slice_fusion.2.price, f32[4,8,16384]{2,1,0:T(8,128)} %all-to-all-done.flow, ...), custom_call_target="tpu_custom_call" | custom-call | tf_op jit(solution)/shard_map/arc_trial/pallas_call | solution.py:142
  85.0 1.3 copy-done.1
  86.4 8.1 %all-to-all-start.2 = ((f32[128,8,512]{2,1,0:T(8,128)}), f32[128,8,512]{2,1,0:T(8,128)}, u32[]{:S(2)}, u32[]{:S(2)}) async-start(f32[128,8,512]{2,1,0:T(8,128)} %copy-done.1), calls=%async_computation.2 | async-start | bytes 4194304 | tf_op jit(solution)/shard_map/all_to_all | solution.py:224
  95.1 28.3 %all-to-all-done.2.values = f32[128,8,512]{2,1,0:T(8,128)} async-done(((f32[128,8,512]{2,1,0:T(8,128)}), f32[128,8,512]{2,1,0:T(8,128)}, u32[]{:S(2)}, u32[]{:S(2)}) %all-to-all-start.2) | async-done | bytes 2097184 | tf_op jit(solution)/shard_map/all_to_all | solution.py:224
  123.4 3.8 project.4
  127.3 5.5 %all-to-all-start.3 = ((f32[128,4,128]{2,1,0:T(4,128)}), f32[128,4,128]{2,1,0:T(4,128)S(1)}, u32[]{:S(2)}, u32[]{:S(2)}) async-start(f32[128,4,128]{2,1,0:T(4,128)} %project.4), calls=%async_computation.3 | async-start | bytes 524288 | tf_op jit(solution)/shard_map/all_to_all | solution.py:226
  132.8 1.1 constant_dynamic-slice_fusion.demand
  133.9 8.7 %all-to-all-done.3.theta = f32[128,4,128]{2,1,0:T(4,128)S(1)} async-done(((f32[128,4,128]{2,1,0:T(4,128)}), f32[128,4,128]{2,1,0:T(4,128)S(1)}, u32[]{:S(2)}, u32[]{:S(2)}) %all-to-all-start.3) | async-done | bytes 262176 | tf_op jit(solution)/shard_map/all_to_all | solution.py:226
  143.6 19.2 %balance.4 = (f32[4,8,16384]{2,1,0:T(8,128)S(1)}, f32[8,16384]{1,0:T(8,128)S(1)}) custom-call(s32[512]{0:T(512)S(1)} %bitcast.38, s32[512]{0:T(512)S(1)} %bitcast.30, s32[512,128]{1,0:T(8,128)S(1)} %bitcast.22, s32[512,128]{1,0:T(8,128)S(1)} %bitcast.14, f32[128,8,512]{2,1,0:T(8,128)} %copy-done.1, f32[128,4,128]{2,1,0:T(4,128)S(1)} %all-to-all-done.3.theta, ...), custom_call_target="tpu_custom_call" | custom-call | tf_op jit(solution)/shard_map/balance/pallas_call | solution.py:164
  162.9 9.8 %arc_trial.5.trial = f32[128,8,512]{2,1,0:T(8,128)S(1)} custom-call(s32[512]{0:T(512)S(1)} %bitcast.39, s32[512]{0:T(512)S(1)} %bitcast.31, s32[512,128]{1,0:T(8,128)S(1)} %bitcast.23, s32[512,128]{1,0:T(8,128)S(1)} %bitcast.15, f32[8,16384]{1,0:T(8,128)S(1)} %get-tuple-element.10.price, f32[4,8,16384]{2,1,0:T(8,128)S(1)} %get-tuple-element.11.flow, ...), custom_call_target="tpu_custom_call" | custom-call | tf_op jit(solution)/shard_map/arc_trial/pallas_call | solution.py:142
  172.7 34.9 %all_to_all.55.values = f32[128,8,512]{2,1,0:T(8,128)S(1)} all-to-all(f32[128,8,512]{2,1,0:T(8,128)S(1)} %arc_trial.5.trial), channel_id=1, replica_groups=mesh['com'=32,'arc'=4] {'arc','com'}, dimensions={0} | all-to-all | bytes 4194304 | tf_op jit(solution)/shard_map/all_to_all | solution.py:224
  207.6 2.1 project.5
  209.7 14.7 %all_to_all.56.theta = f32[128,4,128]{2,1,0:T(4,128)S(1)} all-to-all(f32[128,4,128]{2,1,0:T(4,128)S(1)} %project.5), channel_id=1, replica_groups=mesh['com'=32,'arc'=4] {'arc','com'}, dimensions={0} | all-to-all | bytes 524288 | tf_op jit(solution)/shard_map/all_to_all | solution.py:226
  224.3 19.2 %balance.5 = (f32[4,8,16384]{2,1,0:T(8,128)S(1)}, f32[8,16384]{1,0:T(8,128)S(1)}) custom-call(s32[512]{0:T(512)S(1)} %bitcast.40, s32[512]{0:T(512)S(1)} %bitcast.32, s32[512,128]{1,0:T(8,128)S(1)} %bitcast.24, s32[512,128]{1,0:T(8,128)S(1)} %bitcast.16, f32[128,8,512]{2,1,0:T(8,128)} %copy-done.3, f32[128,4,128]{2,1,0:T(4,128)S(1)} %all_to_all.56.theta, ...), custom_call_target="tpu_custom_call" | custom-call | tf_op jit(solution)/shard_map/balance/pallas_call | solution.py:164
  243.6 9.8 %arc_trial.6.trial = f32[128,8,512]{2,1,0:T(8,128)S(1)} custom-call(s32[512]{0:T(512)S(1)} %bitcast.41, s32[512]{0:T(512)S(1)} %bitcast.33, s32[512,128]{1,0:T(8,128)S(1)} %bitcast.25, s32[512,128]{1,0:T(8,128)S(1)} %bitcast.17, f32[8,16384]{1,0:T(8,128)S(1)} %get-tuple-element.12.price, f32[4,8,16384]{2,1,0:T(8,128)S(1)} %get-tuple-element.13.flow, ...), custom_call_target="tpu_custom_call" | custom-call | tf_op jit(solution)/shard_map/arc_trial/pallas_call | solution.py:142
  253.4 34.9 %all_to_all.57.values = f32[128,8,512]{2,1,0:T(8,128)S(1)} all-to-all(f32[128,8,512]{2,1,0:T(8,128)S(1)} %arc_trial.6.trial), channel_id=1, replica_groups=mesh['com'=32,'arc'=4] {'arc','com'}, dimensions={0} | all-to-all | bytes 4194304 | tf_op jit(solution)/shard_map/all_to_all | solution.py:224
  288.3 2.1 project.6
  290.3 14.7 %all_to_all.58.theta = f32[128,4,128]{2,1,0:T(4,128)S(1)} all-to-all(f32[128,4,128]{2,1,0:T(4,128)S(1)} %project.6), channel_id=1, replica_groups=mesh['com'=32,'arc'=4] {'arc','com'}, dimensions={0} | all-to-all | bytes 524288 | tf_op jit(solution)/shard_map/all_to_all | solution.py:226
  305.0 19.2 %balance.6 = (f32[4,8,16384]{2,1,0:T(8,128)S(1)}, f32[8,16384]{1,0:T(8,128)S(1)}) custom-call(s32[512]{0:T(512)S(1)} %bitcast.42, s32[512]{0:T(512)S(1)} %bitcast.34, s32[512,128]{1,0:T(8,128)S(1)} %bitcast.26, s32[512,128]{1,0:T(8,128)S(1)} %bitcast.18, f32[128,8,512]{2,1,0:T(8,128)} %copy-done.4, f32[128,4,128]{2,1,0:T(4,128)S(1)} %all_to_all.58.theta, ...), custom_call_target="tpu_custom_call" | custom-call | tf_op jit(solution)/shard_map/balance/pallas_call | solution.py:164
  324.3 9.8 %arc_trial.7.trial = f32[128,8,512]{2,1,0:T(8,128)S(1)} custom-call(s32[512]{0:T(512)S(1)} %bitcast.43, s32[512]{0:T(512)S(1)} %bitcast.35, s32[512,128]{1,0:T(8,128)S(1)} %bitcast.27, s32[512,128]{1,0:T(8,128)S(1)} %bitcast.19, f32[8,16384]{1,0:T(8,128)S(1)} %get-tuple-element.14.price, f32[4,8,16384]{2,1,0:T(8,128)S(1)} %get-tuple-element.15.flow, ...), custom_call_target="tpu_custom_call" | custom-call | tf_op jit(solution)/shard_map/arc_trial/pallas_call | solution.py:142
  334.1 34.9 %all_to_all.59.values = f32[128,8,512]{2,1,0:T(8,128)S(1)} all-to-all(f32[128,8,512]{2,1,0:T(8,128)S(1)} %arc_trial.7.trial), channel_id=1, replica_groups=mesh['com'=32,'arc'=4] {'arc','com'}, dimensions={0} | all-to-all | bytes 4194304 | tf_op jit(solution)/shard_map/all_to_all | solution.py:224
  369.0 2.1 project.7
  371.0 14.7 %all_to_all.60.theta = f32[128,4,128]{2,1,0:T(4,128)S(1)} all-to-all(f32[128,4,128]{2,1,0:T(4,128)S(1)} %project.7), channel_id=1, replica_groups=mesh['com'=32,'arc'=4] {'arc','com'}, dimensions={0} | all-to-all | bytes 524288 | tf_op jit(solution)/shard_map/all_to_all | solution.py:226
  385.7 19.2 %balance.7 = (f32[4,8,16384]{2,1,0:T(8,128)S(1)}, f32[8,16384]{1,0:T(8,128)S(1)}) custom-call(s32[512]{0:T(512)S(1)} %bitcast.44, s32[512]{0:T(512)S(1)} %bitcast.36, s32[512,128]{1,0:T(8,128)S(1)} %bitcast.28, s32[512,128]{1,0:T(8,128)S(1)} %bitcast.20, f32[128,8,512]{2,1,0:T(8,128)} %copy-done.2, f32[128,4,128]{2,1,0:T(4,128)S(1)} %all_to_all.60.theta, ...), custom_call_target="tpu_custom_call" | custom-call | tf_op jit(solution)/shard_map/balance/pallas_call | solution.py:164
  404.9 1.3 copy-done.10
  407.1 48.0 %all_to_all.61 = f32[4,8,16384]{2,1,0:T(8,128)} all-to-all(f32[4,8,16384]{2,1,0:T(8,128)} %copy-done.10), channel_id=1, replica_groups=mesh['com'=32,'arc'=4] {'arc'}, dimensions={0} | all-to-all | bytes 4194304 | tf_op jit(solution)/shard_map/all_to_all | solution.py:215
  455.1 3.2 copy.14
  458.3 1.3 copy.15
  (44 shorter events, 2.8 us)
Async XLA Ops:
  7.2 45.4 %copy-start = (f32[32,16384]{1,0:T(8,128)S(1)}, f32[32,16384]{1,0:T(8,128)}, u32[]{:S(2)}) copy-start(f32[32,16384]{1,0:T(8,128)} %param.11) | copy-start | bytes 6291460
  7.2 5.5 %copy-start.14 = (s32[16384]{0:T(1024)S(1)}, s32[16384]{0:T(1024)}, u32[]{:S(2)}) copy-start(s32[16384]{0:T(1024)} %param.16) | copy-start | bytes 196612
  7.2 5.5 %copy-start.15 = (s32[16384]{0:T(1024)S(1)}, s32[16384]{0:T(1024)}, u32[]{:S(2)}) copy-start(s32[16384]{0:T(1024)} %param.17) | copy-start | bytes 196612
  7.2 5.5 %copy-start.16 = (s32[128]{0:T(128)S(1)}, s32[128]{0:T(128)}, u32[]{:S(2)}) copy-start(s32[128]{0:T(128)} %param.14) | copy-start | bytes 1540
  7.2 5.5 %copy-start.17 = (s32[128]{0:T(128)S(1)}, s32[128]{0:T(128)}, u32[]{:S(2)}) copy-start(s32[128]{0:T(128)} %param.15) | copy-start | bytes 1540
  7.2 40.8 %all-to-all-start = ((f32[4,8,16384]{2,1,0:T(8,128)}), f32[4,8,16384]{2,1,0:T(8,128)}, u32[]{:S(2)}, u32[]{:S(2)}) async-start(f32[4,8,16384]{2,1,0:T(8,128)} %bitcast.48), calls=%async_computation | async-start | bytes 4194304 | tf_op jit(solution)/shard_map/all_to_all | solution.py:215
  48.1 27.3 %all-to-all-start.1 = ((f32[4,8,16384]{2,1,0:T(8,128)}), f32[4,8,16384]{2,1,0:T(8,128)}, u32[]{:S(2)}, u32[]{:S(2)}) async-start(f32[4,8,16384]{2,1,0:T(8,128)} %bitcast.49), calls=%async_computation.1 | async-start | bytes 4194304 | tf_op jit(solution)/shard_map/all_to_all | solution.py:215
  52.6 32.4 %copy-start.8 = (f32[8,16384]{1,0:T(8,128)}, f32[8,16384]{1,0:T(8,128)S(1)}, u32[]{:S(2)}) copy-start(f32[8,16384]{1,0:T(8,128)S(1)} %constant_dynamic-slice_fusion.2.price) | copy-start | bytes 1572868
  85.0 1.3 copy-start.1
  86.4 37.1 %copy-start.12 = (f32[8]{0:T(128)S(1)}, f32[8]{0:T(128)}, u32[]{:S(2)}) copy-start(f32[8]{0:T(128)} %levels.7) | copy-start | bytes 100
  86.4 37.1 %all-to-all-start.2 = ((f32[128,8,512]{2,1,0:T(8,128)}), f32[128,8,512]{2,1,0:T(8,128)}, u32[]{:S(2)}, u32[]{:S(2)}) async-start(f32[128,8,512]{2,1,0:T(8,128)} %copy-done.1), calls=%async_computation.2 | async-start | bytes 4194304 | tf_op jit(solution)/shard_map/all_to_all | solution.py:224
  127.3 15.3 %all-to-all-start.3 = ((f32[128,4,128]{2,1,0:T(4,128)}), f32[128,4,128]{2,1,0:T(4,128)S(1)}, u32[]{:S(2)}, u32[]{:S(2)}) async-start(f32[128,4,128]{2,1,0:T(4,128)} %project.4), calls=%async_computation.3 | async-start | bytes 524288 | tf_op jit(solution)/shard_map/all_to_all | solution.py:226
  132.8 322.3 %all-gather.3.cloned.1.call-start = ((), (), s32[]{:S(2)}) async-start(), calls=%async_computation.11 | async-start | bytes 2621440 | tf_op jit(solution)/shard_map/all_gather | solution.py:229
  142.6 1.0 copy-start.9
  162.9 9.8 %copy-start.6 = (f32[4,8,16384]{2,1,0:T(8,128)}, f32[4,8,16384]{2,1,0:T(8,128)S(1)}, u32[]{:S(2)}) copy-start(f32[4,8,16384]{2,1,0:T(8,128)S(1)} %get-tuple-element.11.flow) | copy-start | bytes 6291460
  172.7 34.9 %copy-start.3 = (f32[128,8,512]{2,1,0:T(8,128)}, f32[128,8,512]{2,1,0:T(8,128)S(1)}, u32[]{:S(2)}) copy-start(f32[128,8,512]{2,1,0:T(8,128)S(1)} %arc_trial.5.trial) | copy-start | bytes 6291460
  243.6 9.8 %copy-start.7 = (f32[4,8,16384]{2,1,0:T(8,128)}, f32[4,8,16384]{2,1,0:T(8,128)S(1)}, u32[]{:S(2)}) copy-start(f32[4,8,16384]{2,1,0:T(8,128)S(1)} %get-tuple-element.13.flow) | copy-start | bytes 6291460
  253.4 34.9 %copy-start.4 = (f32[128,8,512]{2,1,0:T(8,128)}, f32[128,8,512]{2,1,0:T(8,128)S(1)}, u32[]{:S(2)}) copy-start(f32[128,8,512]{2,1,0:T(8,128)S(1)} %arc_trial.6.trial) | copy-start | bytes 6291460
  324.2 9.8 %copy-start.5 = (f32[4,8,16384]{2,1,0:T(8,128)}, f32[4,8,16384]{2,1,0:T(8,128)S(1)}, u32[]{:S(2)}) copy-start(f32[4,8,16384]{2,1,0:T(8,128)S(1)} %get-tuple-element.15.flow) | copy-start | bytes 6291460
  334.1 34.9 %copy-start.2 = (f32[128,8,512]{2,1,0:T(8,128)}, f32[128,8,512]{2,1,0:T(8,128)S(1)}, u32[]{:S(2)}) copy-start(f32[128,8,512]{2,1,0:T(8,128)S(1)} %arc_trial.7.trial) | copy-start | bytes 6291460
  404.9 1.3 copy-start.10
  406.3 0.8 copy-start.11
  455.1 3.2 copy-start.13
Sparse Core Ops, SparseCore 0:
  407.2 47.4 all-gather.2

commit v2 on v1

v2 whole, which is shorter than its diff:
```python
import functools

import jax
import jax.numpy as jnp
from jax import lax
from jax.experimental import pallas as pl
from jax.experimental.pallas import tpu as pltpu
from jax.sharding import PartitionSpec as P

NODES = 16384
BLOCK = 128
ITERS = 4
NEWTON = 3

step_primal = 0.25
step_dual = 0.1
soft_width = 0.05

SHARDS = 4
OWNERS = 32
OWN = 512
QUADS = OWN // BLOCK
CHUNK = 4096
UNROLL = 8
LIMIT = 48 << 20

f32 = jnp.float32
bf16 = jnp.bfloat16
vmem = pl.BlockSpec(memory_space=pltpu.VMEM)
smem = pl.BlockSpec(memory_space=pltpu.SMEM)
params = pltpu.CompilerParams(vmem_limit_bytes=LIMIT)


def node_slice(block):
    return pl.ds(pl.multiple_of(block * BLOCK, BLOCK), BLOCK)


def arc_slice(start, piece):
    return pl.ds(pl.multiple_of(start + piece * BLOCK, BLOCK), BLOCK)


def own_trial_kernel(head_block, tail_block, head_local, tail_local, price, flow, cost, trial):
    first = pl.program_id(1) * (CHUNK // BLOCK)
    for i in range(CHUNK // BLOCK):
        j = first + i
        head = jnp.broadcast_to(head_local[pl.ds(j, 1), :], (8, BLOCK))
        tail = jnp.broadcast_to(tail_local[pl.ds(j, 1), :], (8, BLOCK))
        at_head = jnp.take_along_axis(price[:, node_slice(head_block[j])], head, axis=1)
        at_tail = jnp.take_along_axis(price[:, node_slice(tail_block[j])], tail, axis=1)
        q = i % QUADS
        where = slice(i * BLOCK, (i + 1) * BLOCK)
        trial[i // QUADS, :, q * BLOCK : (q + 1) * BLOCK] = flow[:, where] - step_primal * (
            cost[:, where] - (at_head - at_tail)
        )


def gather_kernel(part, blocks, *refs):
    locals_, price, flow, cost, trial = refs[:4], refs[4], refs[5:9], refs[9:13], refs[13]
    for k in range(SHARDS):
        shard = (part[0] - k) & (SHARDS - 1)

        def step(o, carry):
            for u in range(UNROLL):
                owner = o * UNROLL + u
                start = owner * OWN
                for q in range(QUADS):
                    j = owner * QUADS + q
                    head = jnp.broadcast_to(locals_[k][pl.ds(j, 1), :], (8, BLOCK))
                    tail = jnp.broadcast_to(locals_[k][pl.ds(BLOCK + j, 1), :], (8, BLOCK))
                    at_head = jnp.take_along_axis(price[:, node_slice(blocks[2 * k, j])], head, axis=1)
                    at_tail = jnp.take_along_axis(price[:, node_slice(blocks[2 * k + 1, j])], tail, axis=1)
                    where = arc_slice(start, q)
                    trial[owner * SHARDS + shard, :, q * BLOCK : (q + 1) * BLOCK] = flow[k][
                        :, where
                    ] - step_primal * (cost[k][:, where] - (at_head - at_tail))
            return carry

        lax.fori_loop(0, OWNERS // UNROLL, step, 0)


def project_kernel(levels, classes, values, theta_out, *fresh_out):
    cls = classes[...]
    capacity = jnp.zeros((QUADS, BLOCK), f32)
    for k in range(8):
        capacity = jnp.where(cls == k, levels[k], capacity)
    caps = [capacity[q : q + 1] for q in range(QUADS)]
    thetas = [jnp.zeros((1, BLOCK), f32) for q in range(QUADS)]
    groups = values.shape[0]
    for inner in range(NEWTON):
        wide = [jnp.broadcast_to(t, (8, BLOCK)) for t in thetas]

        def step(o, carry):
            out = list(carry)
            for u in range(8):
                for q in range(QUADS):
                    excess = jnp.maximum(values[o * 8 + u, :, q * BLOCK : (q + 1) * BLOCK] - wide[q], 0.0)
                    out[2 * q] = out[2 * q] + excess
                    out[2 * q + 1] = out[2 * q + 1] + jnp.minimum(excess * (1.0 / soft_width), 1.0)
            return tuple(out)

        sums = lax.fori_loop(0, groups // 8, step, tuple(jnp.zeros((8, BLOCK), f32) for _ in range(2 * QUADS)))
        for q in range(QUADS):
            total = jnp.sum(sums[2 * q], axis=0, keepdims=True)
            active = jnp.sum(sums[2 * q + 1], axis=0, keepdims=True)
            thetas[q] = thetas[q] + jnp.maximum(total - caps[q], 0.0) / jnp.maximum(active, 1.0)
    tile = jnp.concatenate(thetas, axis=0)

    def store(i, carry):
        theta_out[i] = tile
        return carry

    lax.fori_loop(0, theta_out.shape[0], store, 0, unroll=8)
    if fresh_out:
        wide = [jnp.broadcast_to(t, (8, BLOCK)) for t in thetas]

        def keep(o, carry):
            for u in range(8):
                for q in range(QUADS):
                    where = slice(q * BLOCK, (q + 1) * BLOCK)
                    fresh_out[0][o * 8 + u, :, where] = jnp.maximum(values[o * 8 + u, :, where] - wide[q], 0.0)
            return carry

        lax.fori_loop(0, groups // 8, keep, 0)


def scatter_kernel(part, blocks, *refs, last):
    locals_, trial, theta, flow, price, demand = refs[:4], refs[4], refs[5], refs[6:10], refs[10], refs[11]
    fresh_out, price_out, balance = refs[12:-2], refs[-2], refs[-1]
    balance[...] = jnp.zeros_like(balance)
    lanes = lax.broadcasted_iota(jnp.int32, (BLOCK, BLOCK), 0).astype(jnp.int16)
    one = jnp.ones((), bf16)
    zero = jnp.zeros((), bf16)

    def table(local):
        return jnp.where(lanes == jnp.broadcast_to(local.astype(jnp.int16), (BLOCK, BLOCK)), one, zero)

    for k in range(SHARDS):
        shard = (part[0] - k) & (SHARDS - 1)

        def step(o, carry):
            found = []
            for u in range(UNROLL):
                owner = o * UNROLL + u
                start = owner * OWN
                for q in range(QUADS):
                    j = owner * QUADS + q
                    where = arc_slice(start, q)
                    limit = theta[owner * SHARDS + shard, q : q + 1, :]
                    fresh = jnp.maximum(
                        trial[owner * SHARDS + shard, :, q * BLOCK : (q + 1) * BLOCK] - limit, 0.0
                    )
                    if not last:
                        fresh_out[k][:, where] = fresh
                    extra = 2.0 * fresh - flow[k][:, where]
                    high = extra.astype(bf16)
                    low = (extra - high.astype(f32)).astype(bf16)
                    both = jnp.concatenate([high, low], axis=0)
                    tables = jnp.concatenate(
                        [table(locals_[k][pl.ds(j, 1), :]), table(locals_[k][pl.ds(BLOCK + j, 1), :])], axis=0
                    )
                    sums = lax.dot_general(both, tables, (((1,), (1,)), ((), ())), preferred_element_type=f32)
                    found.append((j, sums[:8] + sums[8:]))
            for j, sums in found:
                balance[:, node_slice(blocks[2 * k, j])] += sums[:, :BLOCK]
                balance[:, node_slice(blocks[2 * k + 1, j])] -= sums[:, BLOCK:]
            return carry

        lax.fori_loop(0, OWNERS // UNROLL, step, 0)
    price_out[...] = price[...] + step_dual * (demand[...] - balance[...])


def own_trial(head_block, tail_block, head_local, tail_local, price, flow, cost):
    whole = pl.BlockSpec((BLOCK, BLOCK), lambda r, c: (0, 0))
    return pl.pallas_call(
        own_trial_kernel,
        grid=(SHARDS, OWNERS * OWN // CHUNK),
        in_specs=[
            smem,
            smem,
            whole,
            whole,
            pl.BlockSpec((8, NODES), lambda r, c: (r, 0)),
            pl.BlockSpec((8, CHUNK), lambda r, c: (r, c)),
            pl.BlockSpec((8, CHUNK), lambda r, c: (r, c)),
        ],
        out_specs=pl.BlockSpec((CHUNK // OWN, 8, OWN), lambda r, c: (c, r, 0)),
        out_shape=jax.ShapeDtypeStruct((OWNERS, SHARDS * 8, OWN), f32),
        compiler_params=params,
        name="own_trial",
    )(head_block, tail_block, head_local, tail_local, price, flow, cost)


def gather(part, blocks, locals_, price, flow, cost):
    return pl.pallas_call(
        gather_kernel,
        in_specs=[smem, smem] + [vmem] * 13,
        out_specs=vmem,
        out_shape=jax.ShapeDtypeStruct((OWNERS * SHARDS, 8, OWN), f32),
        compiler_params=params,
        name="trial",
    )(part, blocks, *locals_, price, *flow, *cost)


def project(levels, classes, values, last):
    shape = [jax.ShapeDtypeStruct((SHARDS * OWNERS, QUADS, BLOCK), f32)]
    if last:
        shape.append(jax.ShapeDtypeStruct(values.shape, f32))
    return pl.pallas_call(
        project_kernel,
        in_specs=[smem, vmem, vmem],
        out_specs=[vmem] * len(shape),
        out_shape=shape,
        compiler_params=params,
        name="project",
    )(levels, classes, values)


def scatter(part, blocks, locals_, trial, theta, flow, price, demand, last):
    shape = [] if last else [jax.ShapeDtypeStruct((8, OWNERS * OWN), f32)] * SHARDS
    shape = shape + [jax.ShapeDtypeStruct((8, NODES), f32)]
    out = pl.pallas_call(
        functools.partial(scatter_kernel, last=last),
        in_specs=[smem, smem] + [vmem] * 12,
        out_specs=[vmem] * len(shape),
        out_shape=shape,
        scratch_shapes=[pltpu.VMEM((8, NODES), f32)],
        compiler_params=params,
        name="balance",
    )(part, blocks, *locals_, trial, theta, *flow, price, demand)
    return list(out[:-1]), out[-1]


def on_device(
    flow_start,
    price_start,
    cost,
    demand,
    head_block,
    tail_block,
    head_local,
    tail_local,
    cap_class,
    cap_levels,
):
    com_rows, arc_cols = flow_start.shape
    part = lax.axis_index("arc")
    place = lax.axis_index("com")
    blocks = arc_cols // BLOCK
    head_rows = head_local.reshape(blocks, BLOCK)
    tail_rows = tail_local.reshape(blocks, BLOCK)
    everyone = ("com", "arc")

    def exchange(values, axes):
        return lax.all_to_all(values, axes, split_axis=0, concat_axis=0, tiled=True)

    def around(values, k):
        return lax.ppermute(values, "arc", [(i, (i + k) % SHARDS) for i in range(SHARDS)])

    def rows_of(values, k):
        return lax.dynamic_slice(values, (((part + k) & (SHARDS - 1)) * 8, 0), (8, values.shape[1]))

    def slots(values):
        return [rows_of(values, 0)] + [around(rows_of(values, k), k) for k in range(1, SHARDS)]

    first = own_trial(head_block, tail_block, head_rows, tail_rows, price_start, flow_start, cost)
    values = exchange(first, "com").reshape(OWNERS * SHARDS, 8, OWN)

    packed = jnp.concatenate(
        [
            head_rows,
            tail_rows,
            head_block.reshape(1, BLOCK),
            tail_block.reshape(1, BLOCK),
            jnp.zeros((6, BLOCK), jnp.int32),
        ],
        axis=0,
    )
    locals_ = [packed] + [around(packed, k) for k in range(1, SHARDS)]
    block_ids = jnp.concatenate([x[2 * blocks : 2 * blocks + 2] for x in locals_], axis=0)
    flow = slots(flow_start)
    unit_cost = slots(cost)
    price = rows_of(price_start, 0)
    wanted = rows_of(demand, 0)
    classes = lax.dynamic_slice(cap_class.reshape(blocks, BLOCK), (place * QUADS, 0), (QUADS, BLOCK))
    own = part.astype(jnp.int32).reshape(1)

    for step in range(ITERS):
        last = step == ITERS - 1
        trial = gather(own, block_ids, locals_, price, flow, unit_cost)
        if step > 0:
            values = exchange(trial, everyone)
        theta, *kept = project(cap_levels, classes, values, last)
        theta = exchange(theta, everyone)
        flow, price = scatter(own, block_ids, locals_, trial, theta, flow, price, wanted, last)
    back = exchange(kept[0].reshape(OWNERS, com_rows, OWN), "com")
    out = back.transpose(1, 0, 2).reshape(com_rows, arc_cols)
    return out, lax.all_gather(price, "arc", axis=0, tiled=True)


def solution(mesh):
    return jax.shard_map(
        on_device,
        mesh=mesh,
        in_specs=(
            P("com", "arc"),
            P("com", None),
            P("com", "arc"),
            P("com", None),
            P("arc"),
            P("arc"),
            P("arc"),
            P("arc"),
            P("arc"),
            P(),
        ),
        out_specs=(P("com", "arc"), P("com", None)),
        check_vma=False,
    )
```

time: 470 us -> 407 us (0.87)
  blocking collectives: 232 us -> 181 us
  Pallas kernels: 126 us -> 100 us
  local copies, waits for them, and re-layouts: 10.9 us -> 26.9 us
  waiting for transfers between devices: 59.7 us -> 48.9 us
  starting transfers between devices: 23.5 us -> 30.6 us
    all_to_all x4 -> x2, waiting for transfers between devices: 59.7 us -> 15.2 us  [exchange(): return lax.all_to_all(values, axes, split_axis=0, concat_axis=0, tiled=True)]
    all_gather x1 -> x0, blocking collectives: 35.3 us -> none  [on_device(): every = lax.all_gather(packed, 'arc', axis=0)]
    ppermute x0 -> x9, waiting for transfers between devices: none -> 33.7 us  [around(): lax.ppermute(values, 'arc', [(i, (i + k) % SHARDS) for i in range(SHARDS)])]
    pallas_call x12 -> x13, Pallas kernels: 126 us -> 100 us  [the longest x4 53 us: scatter(): pl.pallas_call(functools.partial(scatter_kernel, last=last), in_specs=[sm...]
    ppermute x0 -> x9, starting transfers between devices: none -> 15.9 us  [around(): lax.ppermute(values, 'arc', [(i, (i + k) % SHARDS) for i in range(SHARDS)])]
    all_to_all x7, blocking collectives: 197 us -> 181 us  [exchange(): return lax.all_to_all(values, axes, split_axis=0, concat_axis=0, tiled=True)]
    all_to_all x4 -> x2, starting transfers between devices: 23.5 us -> 14.6 us  [exchange(): return lax.all_to_all(values, axes, split_axis=0, concat_axis=0, tiled=True)]
    unnamed x38 -> x37, local copies, waits for them, and re-layouts: 9.05 us -> 15.1 us
  transfers between devices with their start and end apart: 5 -> 12, of which waited for: 3 -> 4; matrix products, arithmetic and copies ran while one was open for 0% -> 2% of each run, Pallas kernels for 0% -> 5%
where the time goes in v2:
time: 407 us; the launch traced here: 403 us
  blocking collectives  181 us (44%)
  Pallas kernels  100 us (25%)
  waiting for transfers between devices  48.9 us (12%)
  starting transfers between devices  30.6 us (8%)
  local copies, waits for them, and re-layouts  26.9 us (7%)
  between operations  14.2 us (3%)
    all_to_all x7, blocking collectives, exchange(): return lax.all_to_all(values, axes, split_axis=0, concat_axis=0, tiled=True)  181 us
    pallas_call x4, Pallas kernels, scatter(): pl.pallas_call(functools.partial(scatter_kernel, last=last), in_specs=[sm...  53 us
    ppermute x9, waiting for transfers between devices, around(): lax.ppermute(values, 'arc', [(i, (i + k) % SHARDS) for i in range(SHARDS)])  33.7 us
    pallas_call x4, Pallas kernels, gather(): pl.pallas_call(gather_kernel, in_specs=[smem, smem] + [vmem] * 13, out_sp...  27.5 us
    ppermute x9, starting transfers between devices, around(): lax.ppermute(values, 'arc', [(i, (i + k) % SHARDS) for i in range(SHARDS)])  15.9 us
    all_to_all x2, waiting for transfers between devices, exchange(): return lax.all_to_all(values, axes, split_axis=0, concat_axis=0, tiled=True)  15.2 us
    unnamed x37, local copies, waits for them, and re-layouts  15.1 us
    all_to_all x2, starting transfers between devices, exchange(): return lax.all_to_all(values, axes, split_axis=0, concat_axis=0, tiled=True)  14.6 us
  transfers between devices with their start and end apart: 12, of which 4 were waited for; matrix products, arithmetic and copies ran while one was open for 2% of the time, Pallas kernels for 5%

profile of v2, /device:TPU:6, one launch (start us, length us, event | category | flops | bytes accessed | tf_op | source)
XLA Modules:
  0.0 402.6 jit_solution(14550399589369055466)
XLA Ops:
  7.2 2.5 concatenate.8.refs_0_
  9.7 4.0 %collective-permute-start.2 = (s32[264,128]{1,0:T(8,128)S(1)}, s32[264,128]{1,0:T(8,128)S(1)}, u32[]{:S(2)}, u32[]{:S(2)}) collective-permute-start(s32[264,128]{1,0:T(8,128)S(1)} %concatenate.8.refs_0_), channel_id=1, source_target_pairs={{0,3},{1,0},{2,1},{3,2},{4,7},{5,4},{6,5},{7,6},{8,11},{9,8},{10,9... | collective-permute-start | bytes 405512 | tf_op jit(solution)/shard_map/ppermute | solution.py:257
  19.6 10.5 %own_trial.1 = f32[32,32,512]{2,1,0:T(8,128)S(1)} custom-call(s32[128]{0:T(128)S(1)} %copy-done.13, s32[128]{0:T(128)S(1)} %copy-done.15, s32[128,128]{1,0:T(8,128)S(1)} %bitcast.13, s32[128,128]{1,0:T(8,128)S(1)} %bitcast.15, f32[32,16384]{1,0:T(8,128)S(1)} %copy-done.7, f32[32,16384]{1,0:T(8,128)} %flow.1, f32[32,16384]{1,0:T(8,128)} %cost.1), custom_call_target="tpu_custom_call" | custom-call | tf_op jit(solution)/shard_map/own_trial/pallas_call | solution.py:174
  31.4 7.7 %all-to-all-start = ((f32[32,32,512]{2,1,0:T(8,128)}), f32[32,32,512]{2,1,0:T(8,128)}, u32[]{:S(2)}, u32[]{:S(2)}) async-start(f32[32,32,512]{2,1,0:T(8,128)} %copy-done.2), calls=%async_computation | async-start | bytes 4194304 | tf_op jit(solution)/shard_map/all_to_all | solution.py:254
  39.1 3.1 constant_dynamic-slice_fusion.5
  42.1 2.0 collective-permute-start.5
  44.1 2.3 collective-permute-start.4
  50.2 15.2 %all-to-all-done = f32[32,32,512]{2,1,0:T(8,128)} async-done(((f32[32,32,512]{2,1,0:T(8,128)}), f32[32,32,512]{2,1,0:T(8,128)}, u32[]{:S(2)}, u32[]{:S(2)}) %all-to-all-start) | async-done | bytes 2097184 | tf_op jit(solution)/shard_map/all_to_all | solution.py:254
  65.4 3.1 project.4
  69.2 6.9 %all-to-all-start.1 = ((f32[128,4,128]{2,1,0:T(4,128)}), f32[128,4,128]{2,1,0:T(4,128)S(1)}, u32[]{:S(2)}, u32[]{:S(2)}) async-start(f32[128,4,128]{2,1,0:T(4,128)} %copy-done.9), calls=%async_computation.1 | async-start | bytes 524288 | tf_op jit(solution)/shard_map/all_to_all | solution.py:254
  83.5 11.5 %collective-permute-done.3.refs_6_.refs_7_ = f32[8,16384]{1,0:T(8,128)} collective-permute-done((f32[8,16384]{1,0:T(8,128)}, f32[8,16384]{1,0:T(8,128)}, u32[]{:S(2)}, u32[]{:S(2)}) %collective-permute-start.3) | collective-permute-done | bytes 524320 | tf_op jit(solution)/shard_map/ppermute | solution.py:257
  95.0 11.9 %collective-permute-done.7.refs_11_ = f32[8,16384]{1,0:T(8,128)} collective-permute-done((f32[8,16384]{1,0:T(8,128)}, f32[8,16384]{1,0:T(8,128)}, u32[]{:S(2)}, u32[]{:S(2)}) %collective-permute-start.7) | collective-permute-done | bytes 524320 | tf_op jit(solution)/shard_map/ppermute | solution.py:257
  106.9 10.3 %collective-permute-done.6.refs_10_ = f32[8,16384]{1,0:T(8,128)} collective-permute-done((f32[8,16384]{1,0:T(8,128)}, f32[8,16384]{1,0:T(8,128)}, u32[]{:S(2)}, u32[]{:S(2)}) %collective-permute-start.6) | collective-permute-done | bytes 524320 | tf_op jit(solution)/shard_map/ppermute | solution.py:257
  119.3 7.2 %trial.4.refs_4_ = f32[128,8,512]{2,1,0:T(8,128)} custom-call(s32[1]{0:T(128)} %bitcast.1.part, s32[8,128]{1,0:T(8,128)S(1)} %concatenate.9.blocks, s32[264,128]{1,0:T(8,128)S(1)} %concatenate.8.refs_0_, s32[264,128]{1,0:T(8,128)S(1)} %collective-permute-done.refs_1_, s32[264,128]{1,0:T(8,128)S(1)} %collective-permute-done.1.refs_2_, ...), custom_call_target="tpu_custom_call" | custom-call | tf_op jit(solution)/shard_map/trial/pallas_call | solution.py:194
  128.6 13.4 %balance.4 = (f32[8,16384]{1,0:T(8,128)S(1)}, f32[8,16384]{1,0:T(8,128)S(1)}, f32[8,16384]{1,0:T(8,128)S(1)}, f32[8,16384]{1,0:T(8,128)S(1)}, f32[8,16384]{1,0:T(8,128)S(1)}) custom-call(s32[1]{0:T(128)} %bitcast.1.part, s32[8,128]{1,0:T(8,128)S(1)} %concatenate.9.blocks, s32[264,128]{1,0:T(8,128)S(1)} %concatenate.8.refs_0_, ...), custom_call_target="tpu_custom_call" | custom-call | tf_op jit(solution)/shard_map/balance/pallas_call | solution.py:221
  142.0 6.8 %trial.5.refs_4_ = f32[128,8,512]{2,1,0:T(8,128)} custom-call(s32[1]{0:T(128)} %bitcast.1.part, s32[8,128]{1,0:T(8,128)S(1)} %concatenate.9.blocks, s32[264,128]{1,0:T(8,128)S(1)} %concatenate.8.refs_0_, s32[264,128]{1,0:T(8,128)S(1)} %collective-permute-done.refs_1_, s32[264,128]{1,0:T(8,128)S(1)} %collective-permute-done.1.refs_2_, ...), custom_call_target="tpu_custom_call" | custom-call | tf_op jit(solution)/shard_map/trial/pallas_call | solution.py:194
  148.8 35.6 %all_to_all.45.values = f32[128,8,512]{2,1,0:T(8,128)S(1)} all-to-all(f32[128,8,512]{2,1,0:T(8,128)} %trial.5.refs_4_), channel_id=1, replica_groups=mesh['com'=32,'arc'=4] {'com','arc'}, dimensions={0} | all-to-all | bytes 4194304 | tf_op jit(solution)/shard_map/all_to_all | solution.py:254
  184.4 2.1 project.5
  186.4 14.4 %all_to_all.46.refs_5_ = f32[128,4,128]{2,1,0:T(4,128)S(1)} all-to-all(f32[128,4,128]{2,1,0:T(4,128)S(1)} %project.5), channel_id=1, replica_groups=mesh['com'=32,'arc'=4] {'com','arc'}, dimensions={0} | all-to-all | bytes 524288 | tf_op jit(solution)/shard_map/all_to_all | solution.py:254
  200.9 13.0 %balance.5 = (f32[8,16384]{1,0:T(8,128)S(1)}, f32[8,16384]{1,0:T(8,128)S(1)}, f32[8,16384]{1,0:T(8,128)S(1)}, f32[8,16384]{1,0:T(8,128)S(1)}, f32[8,16384]{1,0:T(8,128)S(1)}) custom-call(s32[1]{0:T(128)} %bitcast.1.part, s32[8,128]{1,0:T(8,128)S(1)} %concatenate.9.blocks, s32[264,128]{1,0:T(8,128)S(1)} %concatenate.8.refs_0_, ...), custom_call_target="tpu_custom_call" | custom-call | tf_op jit(solution)/shard_map/balance/pallas_call | solution.py:221
  213.8 6.8 %trial.6.refs_4_ = f32[128,8,512]{2,1,0:T(8,128)} custom-call(s32[1]{0:T(128)} %bitcast.1.part, s32[8,128]{1,0:T(8,128)S(1)} %concatenate.9.blocks, s32[264,128]{1,0:T(8,128)S(1)} %concatenate.8.refs_0_, s32[264,128]{1,0:T(8,128)S(1)} %collective-permute-done.refs_1_, s32[264,128]{1,0:T(8,128)S(1)} %collective-permute-done.1.refs_2_, ...), custom_call_target="tpu_custom_call" | custom-call | tf_op jit(solution)/shard_map/trial/pallas_call | solution.py:194
  220.6 35.1 %all_to_all.47.values = f32[128,8,512]{2,1,0:T(8,128)S(1)} all-to-all(f32[128,8,512]{2,1,0:T(8,128)} %trial.6.refs_4_), channel_id=1, replica_groups=mesh['com'=32,'arc'=4] {'com','arc'}, dimensions={0} | all-to-all | bytes 4194304 | tf_op jit(solution)/shard_map/all_to_all | solution.py:254
  255.7 2.1 project.6
  257.7 14.4 %all_to_all.48.refs_5_ = f32[128,4,128]{2,1,0:T(4,128)S(1)} all-to-all(f32[128,4,128]{2,1,0:T(4,128)S(1)} %project.6), channel_id=1, replica_groups=mesh['com'=32,'arc'=4] {'com','arc'}, dimensions={0} | all-to-all | bytes 524288 | tf_op jit(solution)/shard_map/all_to_all | solution.py:254
  272.2 13.0 %balance.6 = (f32[8,16384]{1,0:T(8,128)S(1)}, f32[8,16384]{1,0:T(8,128)S(1)}, f32[8,16384]{1,0:T(8,128)S(1)}, f32[8,16384]{1,0:T(8,128)S(1)}, f32[8,16384]{1,0:T(8,128)S(1)}) custom-call(s32[1]{0:T(128)} %bitcast.1.part, s32[8,128]{1,0:T(8,128)S(1)} %concatenate.9.blocks, s32[264,128]{1,0:T(8,128)S(1)} %concatenate.8.refs_0_, ...), custom_call_target="tpu_custom_call" | custom-call | tf_op jit(solution)/shard_map/balance/pallas_call | solution.py:221
  285.1 6.8 %trial.7.refs_4_ = f32[128,8,512]{2,1,0:T(8,128)} custom-call(s32[1]{0:T(128)} %bitcast.1.part, s32[8,128]{1,0:T(8,128)S(1)} %concatenate.9.blocks, s32[264,128]{1,0:T(8,128)S(1)} %concatenate.8.refs_0_, s32[264,128]{1,0:T(8,128)S(1)} %collective-permute-done.refs_1_, s32[264,128]{1,0:T(8,128)S(1)} %collective-permute-done.1.refs_2_, ...), custom_call_target="tpu_custom_call" | custom-call | tf_op jit(solution)/shard_map/trial/pallas_call | solution.py:194
  291.9 35.1 %all_to_all.49.values = f32[128,8,512]{2,1,0:T(8,128)S(1)} all-to-all(f32[128,8,512]{2,1,0:T(8,128)} %trial.7.refs_4_), channel_id=1, replica_groups=mesh['com'=32,'arc'=4] {'com','arc'}, dimensions={0} | all-to-all | bytes 4194304 | tf_op jit(solution)/shard_map/all_to_all | solution.py:254
  327.0 2.3 project.7
  330.6 14.4 %all_to_all.50.refs_5_ = f32[128,4,128]{2,1,0:T(4,128)S(1)} all-to-all(f32[128,4,128]{2,1,0:T(4,128)S(1)} %get-tuple-element.35), channel_id=1, replica_groups=mesh['com'=32,'arc'=4] {'com','arc'}, dimensions={0} | all-to-all | bytes 524288 | tf_op jit(solution)/shard_map/all_to_all | solution.py:254
  345.0 13.7 %balance.7 = f32[8,16384]{1,0:T(8,128)} custom-call(s32[1]{0:T(128)} %bitcast.1.part, s32[8,128]{1,0:T(8,128)S(1)} %concatenate.9.blocks, s32[264,128]{1,0:T(8,128)S(1)} %concatenate.8.refs_0_, s32[264,128]{1,0:T(8,128)S(1)} %collective-permute-done.refs_1_, s32[264,128]{1,0:T(8,128)S(1)} %collective-permute-done.1.refs_2_, ...), custom_call_target="tpu_custom_call" | custom-call | tf_op jit(solution)/shard_map/balance/pallas_call | solution.py:221
  358.7 32.4 %all_to_all.51 = f32[32,32,512]{2,1,0:T(8,128)S(1)} all-to-all(f32[32,32,512]{2,1,0:T(8,128)} %bitcast.11), channel_id=1, replica_groups=mesh['com'=32,'arc'=4] {'com'}, dimensions={0} | all-to-all | bytes 4194304 | tf_op jit(solution)/shard_map/all_to_all | solution.py:254
  392.7 3.0 copy.15
  (62 shorter events, 25.9 us)
Async XLA Ops:
  7.2 75.4 %copy-start = (f32[32,16384]{1,0:T(8,128)S(1)}, f32[32,16384]{1,0:T(8,128)}, u32[]{:S(2)}) copy-start(f32[32,16384]{1,0:T(8,128)} %param.13) | copy-start | bytes 6291460
  9.7 66.5 %collective-permute-start.2 = (s32[264,128]{1,0:T(8,128)S(1)}, s32[264,128]{1,0:T(8,128)S(1)}, u32[]{:S(2)}, u32[]{:S(2)}) collective-permute-start(s32[264,128]{1,0:T(8,128)S(1)} %concatenate.8.refs_0_), channel_id=1, source_target_pairs={{0,3},{1,0},{2,1},{3,2},{4,7},{5,4},{6,5},{7,6},{8,11},{9,8},{10,9... | collective-permute-start | bytes 405512 | tf_op jit(solution)/shard_map/ppermute | solution.py:257
  13.8 64.2 %collective-permute-start.1 = (s32[264,128]{1,0:T(8,128)S(1)}, s32[264,128]{1,0:T(8,128)S(1)}, u32[]{:S(2)}, u32[]{:S(2)}) collective-permute-start(s32[264,128]{1,0:T(8,128)S(1)} %concatenate.8.refs_0_), channel_id=1, source_target_pairs={{0,2},{1,3},{2,0},{3,1},{4,6},{5,7},{6,4},{7,5},{8,10},{9,11},{10,... | collective-permute-start | bytes 405512 | tf_op jit(solution)/shard_map/ppermute | solution.py:257
  13.8 66.0 %collective-permute-start = (s32[264,128]{1,0:T(8,128)S(1)}, s32[264,128]{1,0:T(8,128)S(1)}, u32[]{:S(2)}, u32[]{:S(2)}) collective-permute-start(s32[264,128]{1,0:T(8,128)S(1)} %concatenate.8.refs_0_), channel_id=1, source_target_pairs={{0,1},{1,2},{2,3},{3,0},{4,5},{5,6},{6,7},{7,4},{8,9},{9,10},{10,1... | collective-permute-start | bytes 405512 | tf_op jit(solution)/shard_map/ppermute | solution.py:257
  15.0 1.6 copy-start.7
  16.6 0.8 copy-start.10
  17.4 0.8 copy-start.11
  18.3 0.7 copy-start.13
  18.9 0.7 copy-start.15
  30.1 1.3 copy-start.2
  31.4 34.1 %all-to-all-start = ((f32[32,32,512]{2,1,0:T(8,128)}), f32[32,32,512]{2,1,0:T(8,128)}, u32[]{:S(2)}, u32[]{:S(2)}) async-start(f32[32,32,512]{2,1,0:T(8,128)} %copy-done.2), calls=%async_computation | async-start | bytes 4194304 | tf_op jit(solution)/shard_map/all_to_all | solution.py:254
  39.1 7.4 %copy-start.17 = (f32[32,16384]{1,0:T(8,128)S(1)}, f32[32,16384]{1,0:T(8,128)}, u32[]{:S(2)}) copy-start(f32[32,16384]{1,0:T(8,128)} %cost.1) | copy-start | bytes 6291460
  42.1 39.6 %collective-permute-start.5 = (f32[8,16384]{1,0:T(8,128)}, f32[8,16384]{1,0:T(8,128)}, u32[]{:S(2)}, u32[]{:S(2)}) collective-permute-start(f32[8,16384]{1,0:T(8,128)} %get-tuple-element.40), channel_id=1, source_target_pairs={{0,3},{1,0},{2,1},{3,2},{4,7},{5,4},{6,5},{7,6},{8,11},{9,8},{10,9... | collective-permute-start | bytes 1572872 | tf_op jit(solution)/shard_map/ppermute | solution.py:257
  44.1 21.3 %copy-start.12 = (f32[8]{0:T(128)S(1)}, f32[8]{0:T(128)}, u32[]{:S(2)}) copy-start(f32[8]{0:T(128)} %levels.7) | copy-start | bytes 100
  44.1 39.3 %collective-permute-start.4 = (f32[8,16384]{1,0:T(8,128)}, f32[8,16384]{1,0:T(8,128)}, u32[]{:S(2)}, u32[]{:S(2)}) collective-permute-start(f32[8,16384]{1,0:T(8,128)} %get-tuple-element.41), channel_id=1, source_target_pairs={{0,2},{1,3},{2,0},{3,1},{4,6},{5,7},{6,4},{7,5},{8,10},{9,11},{10,... | collective-permute-start | bytes 1572872 | tf_op jit(solution)/shard_map/ppermute | solution.py:257
  49.5 33.9 %copy-start.14 = (s32[128]{0:T(128)S(1)}, s32[128]{0:T(128)}, u32[]{:S(2)}) copy-start(s32[128]{0:T(128)} %head_block.1) | copy-start | bytes 1540
  49.5 33.9 %copy-start.16 = (s32[128]{0:T(128)S(1)}, s32[128]{0:T(128)}, u32[]{:S(2)}) copy-start(s32[128]{0:T(128)} %tail_block.1) | copy-start | bytes 1540
  68.6 0.7 copy-start.9
  69.2 57.2 %all-to-all-start.1 = ((f32[128,4,128]{2,1,0:T(4,128)}), f32[128,4,128]{2,1,0:T(4,128)S(1)}, u32[]{:S(2)}, u32[]{:S(2)}) async-start(f32[128,4,128]{2,1,0:T(4,128)} %copy-done.9), calls=%async_computation.1 | async-start | bytes 524288 | tf_op jit(solution)/shard_map/all_to_all | solution.py:254
  76.2 316.5 %all-gather.2.cloned.1.call-start = ((), (), s32[]{:S(2)}) async-start(), calls=%async_computation.9 | async-start | bytes 2621440 | tf_op jit(solution)/shard_map/all_gather | solution.py:297
  76.2 18.8 %collective-permute-start.3 = (f32[8,16384]{1,0:T(8,128)}, f32[8,16384]{1,0:T(8,128)}, u32[]{:S(2)}, u32[]{:S(2)}) collective-permute-start(f32[8,16384]{1,0:T(8,128)} %get-tuple-element.42), channel_id=1, source_target_pairs={{0,1},{1,2},{2,3},{3,0},{4,5},{5,6},{6,7},{7,4},{8,9},{9,10},{10,1... | collective-permute-start | bytes 1572872 | tf_op jit(solution)/shard_map/ppermute | solution.py:257
  77.9 17.1 %collective-permute-start.8 = (f32[8,16384]{1,0:T(8,128)}, f32[8,16384]{1,0:T(8,128)}, u32[]{:S(2)}, u32[]{:S(2)}) collective-permute-start(f32[8,16384]{1,0:T(8,128)} %get-tuple-element.36), channel_id=1, source_target_pairs={{0,3},{1,0},{2,1},{3,2},{4,7},{5,4},{6,5},{7,6},{8,11},{9,8},{10,9... | collective-permute-start | bytes 1572872 | tf_op jit(solution)/shard_map/ppermute | solution.py:257
  79.8 27.1 %collective-permute-start.7 = (f32[8,16384]{1,0:T(8,128)}, f32[8,16384]{1,0:T(8,128)}, u32[]{:S(2)}, u32[]{:S(2)}) collective-permute-start(f32[8,16384]{1,0:T(8,128)} %get-tuple-element.37), channel_id=1, source_target_pairs={{0,2},{1,3},{2,0},{3,1},{4,6},{5,7},{6,4},{7,5},{8,10},{9,11},{10,... | collective-permute-start | bytes 1572872 | tf_op jit(solution)/shard_map/ppermute | solution.py:257
  81.7 35.5 %collective-permute-start.6 = (f32[8,16384]{1,0:T(8,128)}, f32[8,16384]{1,0:T(8,128)}, u32[]{:S(2)}, u32[]{:S(2)}) collective-permute-start(f32[8,16384]{1,0:T(8,128)} %get-tuple-element.38), channel_id=1, source_target_pairs={{0,1},{1,2},{2,3},{3,0},{4,5},{5,6},{6,7},{7,4},{8,9},{9,10},{10,1... | collective-permute-start | bytes 1572872 | tf_op jit(solution)/shard_map/ppermute | solution.py:257
  117.2 1.0 copy-start.3
  118.3 1.0 copy-start.5
  126.5 1.0 copy-start.4
  127.5 1.0 copy-start.6
  327.0 18.0 %copy-start.1 = (f32[8,16384]{1,0:T(8,128)S(1)}, f32[8,16384]{1,0:T(8,128)}, u32[]{:S(2)}) copy-start(f32[8,16384]{1,0:T(8,128)} %constant_dynamic-slice_fusion.refs_11_) | copy-start | bytes 1572868
  329.2 1.3 copy-start.8
Sparse Core Ops, SparseCore 0:
  358.8 28.7 all-gather.1

commit v3 on v2

--- a/solution.py
+++ b/solution.py
@@ -20,15 +20,18 @@
 OWNERS = 32
 OWN = 512
 QUADS = OWN // BLOCK
-CHUNK = 4096
+CHUNK = 8192
 UNROLL = 8
-LIMIT = 48 << 20
+COVER = 40_000_000
 
 f32 = jnp.float32
 bf16 = jnp.bfloat16
 vmem = pl.BlockSpec(memory_space=pltpu.VMEM)
 smem = pl.BlockSpec(memory_space=pltpu.SMEM)
-params = pltpu.CompilerParams(vmem_limit_bytes=LIMIT)
+
+
+def params(mib):
+    return pltpu.CompilerParams(vmem_limit_bytes=mib << 20)
 
 
 def node_slice(block):
@@ -41,21 +44,30 @@
 
 def own_trial_kernel(head_block, tail_block, head_local, tail_local, price, flow, cost, trial):
     first = pl.program_id(1) * (CHUNK // BLOCK)
-    for i in range(CHUNK // BLOCK):
-        j = first + i
-        head = jnp.broadcast_to(head_local[pl.ds(j, 1), :], (8, BLOCK))
-        tail = jnp.broadcast_to(tail_local[pl.ds(j, 1), :], (8, BLOCK))
-        at_head = jnp.take_along_axis(price[:, node_slice(head_block[j])], head, axis=1)
-        at_tail = jnp.take_along_axis(price[:, node_slice(tail_block[j])], tail, axis=1)
-        q = i % QUADS
-        where = slice(i * BLOCK, (i + 1) * BLOCK)
-        trial[i // QUADS, :, q * BLOCK : (q + 1) * BLOCK] = flow[:, where] - step_primal * (
-            cost[:, where] - (at_head - at_tail)
-        )
+
+    def step(o, carry):
+        for i in range(UNROLL * QUADS):
+            owner = o * UNROLL + i // QUADS
+            q = i % QUADS
+            j = first + owner * QUADS + q
+            head = jnp.broadcast_to(head_local[pl.ds(j, 1), :], (8, BLOCK))
+            tail = jnp.broadcast_to(tail_local[pl.ds(j, 1), :], (8, BLOCK))
+            at_head = jnp.take_along_axis(price[:, node_slice(head_block[j])], head, axis=1)
+            at_tail = jnp.take_along_axis(price[:, node_slice(tail_block[j])], tail, axis=1)
+            where = arc_slice(owner * OWN, q)
+            trial[owner, :, q * BLOCK : (q + 1) * BLOCK] = flow[:, where] - step_primal * (
+                cost[:, where] - (at_head - at_tail)
+            )
+        return carry
+
+    lax.fori_loop(0, CHUNK // OWN // UNROLL, step, 0)
 
 
 def gather_kernel(part, blocks, *refs):
-    locals_, price, flow, cost, trial = refs[:4], refs[4], refs[5:9], refs[9:13], refs[13]
+    fill_trial(part, blocks, refs[:4], refs[4], refs[5:9], refs[9:13], refs[13])
+
+
+def fill_trial(part, blocks, locals_, price, flow, cost, trial):
     for k in range(SHARDS):
         shard = (part[0] - k) & (SHARDS - 1)
 
@@ -123,9 +135,14 @@
         lax.fori_loop(0, groups // 8, keep, 0)
 
 
-def scatter_kernel(part, blocks, *refs, last):
+def step_kernel(part, blocks, *refs, last):
     locals_, trial, theta, flow, price, demand = refs[:4], refs[4], refs[5], refs[6:10], refs[10], refs[11]
-    fresh_out, price_out, balance = refs[12:-2], refs[-2], refs[-1]
+    balance = refs[-1]
+    if last:
+        (price_out,) = refs[12:-1]
+        fresh_out = cost = following = None
+    else:
+        cost, following, price_out, fresh_out = refs[12:16], refs[16], refs[17], refs[18:22]
     balance[...] = jnp.zeros_like(balance)
     lanes = lax.broadcasted_iota(jnp.int32, (BLOCK, BLOCK), 0).astype(jnp.int16)
     one = jnp.ones((), bf16)
@@ -167,6 +184,8 @@
 
         lax.fori_loop(0, OWNERS // UNROLL, step, 0)
     price_out[...] = price[...] + step_dual * (demand[...] - balance[...])
+    if not last:
+        fill_trial(part, blocks, locals_, price_out, fresh_out, cost, following)
 
 
 def own_trial(head_block, tail_block, head_local, tail_local, price, flow, cost):
@@ -185,9 +204,15 @@
         ],
         out_specs=pl.BlockSpec((CHUNK // OWN, 8, OWN), lambda r, c: (c, r, 0)),
         out_shape=jax.ShapeDtypeStruct((OWNERS, SHARDS * 8, OWN), f32),
-        compiler_params=params,
+        compiler_params=params(8),
         name="own_trial",
-    )(head_block, tail_block, head_local, tail_local, price, flow, cost)
+    )(
+        head_block,
+        tail_block,
+        head_local,
+        tail_local,
+        *in_hbm([price, flow, cost]),
+    )
 
 
 def gather(part, blocks, locals_, price, flow, cost):
@@ -196,7 +221,7 @@
         in_specs=[smem, smem] + [vmem] * 13,
         out_specs=vmem,
         out_shape=jax.ShapeDtypeStruct((OWNERS * SHARDS, 8, OWN), f32),
-        compiler_params=params,
+        compiler_params=params(12),
         name="trial",
     )(part, blocks, *locals_, price, *flow, *cost)
 
@@ -210,24 +235,58 @@
         in_specs=[smem, vmem, vmem],
         out_specs=[vmem] * len(shape),
         out_shape=shape,
-        compiler_params=params,
+        compiler_params=params(8),
         name="project",
     )(levels, classes, values)
 
 
-def scatter(part, blocks, locals_, trial, theta, flow, price, demand, last):
-    shape = [] if last else [jax.ShapeDtypeStruct((8, OWNERS * OWN), f32)] * SHARDS
-    shape = shape + [jax.ShapeDtypeStruct((8, NODES), f32)]
+def in_hbm(values):
+    return [pltpu.with_memory_space_constraint(x, pltpu.HBM) for x in values]
+
+
+def advance(part, blocks, locals_, trial, theta, flow, price, demand, cost, first, last):
+    if first or last:
+        trial, price, demand, *flow = in_hbm([trial, price, demand, *flow])
+    shape = [jax.ShapeDtypeStruct((8, NODES), f32)]
+    if not last:
+        shape = [jax.ShapeDtypeStruct(trial.shape, f32)] + shape
+        shape = shape + [jax.ShapeDtypeStruct((8, OWNERS * OWN), f32)] * SHARDS
     out = pl.pallas_call(
-        functools.partial(scatter_kernel, last=last),
-        in_specs=[smem, smem] + [vmem] * 12,
+        functools.partial(step_kernel, last=last),
+        in_specs=[smem, smem] + [vmem] * (12 if last else 16),
         out_specs=[vmem] * len(shape),
         out_shape=shape,
         scratch_shapes=[pltpu.VMEM((8, NODES), f32)],
-        compiler_params=params,
-        name="balance",
-    )(part, blocks, *locals_, trial, theta, *flow, price, demand)
-    return list(out[:-1]), out[-1]
+        compiler_params=params(14),
+        cost_estimate=pl.CostEstimate(flops=2 * 16 * 256 * OWNERS * OWN * SHARDS, transcendentals=0, bytes_accessed=COVER),
+        name="step",
+    )(part, blocks, *locals_, trial, theta, *flow, price, demand, *([] if last else cost))
+    return (None, out[0], None) if last else (out[0], out[1], out[2:])
+
+
+def assemble_kernel(part, *refs):
+    near, left, right, far_left, far_right, out = refs
+    half = NODES // 2
+
+    def rows(k):
+        return pl.ds(pl.multiple_of(((part[0] - k) & (SHARDS - 1)) * 8, 8), 8)
+
+    out[rows(0), :] = near[...]
+    out[rows(1), :] = left[...]
+    out[rows(3), :] = right[...]
+    out[rows(2), :half] = far_left[...]
+    out[rows(2), half:] = far_right[...]
+
+
+def assemble(part, *pieces):
+    return pl.pallas_call(
+        assemble_kernel,
+        in_specs=[smem] + [vmem] * 5,
+        out_specs=vmem,
+        out_shape=jax.ShapeDtypeStruct((SHARDS * 8, NODES), f32),
+        compiler_params=params(8),
+        name="assemble",
+    )(part, *pieces)
 
 
 def on_device(
@@ -263,8 +322,13 @@
         return [rows_of(values, 0)] + [around(rows_of(values, k), k) for k in range(1, SHARDS)]
 
     first = own_trial(head_block, tail_block, head_rows, tail_rows, price_start, flow_start, cost)
+    first, flow_start, cost, price_start, head_rows, tail_rows, head_block, tail_block = lax.optimization_barrier(
+        (first, flow_start, cost, price_start, head_rows, tail_rows, head_block, tail_block)
+    )
     values = exchange(first, "com").reshape(OWNERS * SHARDS, 8, OWN)
 
+    flow = slots(flow_start)
+    unit_cost = slots(cost)
     packed = jnp.concatenate(
         [
             head_rows,
@@ -276,25 +340,28 @@
         axis=0,
     )
     locals_ = [packed] + [around(packed, k) for k in range(1, SHARDS)]
+    values, flow, locals_, unit_cost[1] = lax.optimization_barrier((values, flow, locals_, unit_cost[1]))
     block_ids = jnp.concatenate([x[2 * blocks : 2 * blocks + 2] for x in locals_], axis=0)
-    flow = slots(flow_start)
-    unit_cost = slots(cost)
     price = rows_of(price_start, 0)
     wanted = rows_of(demand, 0)
     classes = lax.dynamic_slice(cap_class.reshape(blocks, BLOCK), (place * QUADS, 0), (QUADS, BLOCK))
     own = part.astype(jnp.int32).reshape(1)
 
+    trial = gather(own, block_ids, locals_, price, flow, unit_cost)
     for step in range(ITERS):
         last = step == ITERS - 1
-        trial = gather(own, block_ids, locals_, price, flow, unit_cost)
         if step > 0:
             values = exchange(trial, everyone)
         theta, *kept = project(cap_levels, classes, values, last)
         theta = exchange(theta, everyone)
-        flow, price = scatter(own, block_ids, locals_, trial, theta, flow, price, wanted, last)
+        trial, price, flow = advance(own, block_ids, locals_, trial, theta, flow, price, wanted, unit_cost, step == 0, last)
     back = exchange(kept[0].reshape(OWNERS, com_rows, OWN), "com")
     out = back.transpose(1, 0, 2).reshape(com_rows, arc_cols)
-    return out, lax.all_gather(price, "arc", axis=0, tiled=True)
+    left = around(price, 1)
+    right = around(price, 3)
+    half = NODES // 2
+    full = assemble(own, price, left, right, around(left[:, :half], 1), around(right[:, half:], 3))
+    return out, full
 
 
 def solution(mesh):

time: 407 us -> 357 us (0.88)
  blocking collectives: 181 us -> 152 us
  between operations: 14.2 us -> 0.92 us
  starting transfers between devices: 30.6 us -> 43.3 us
  Pallas kernels: 100 us -> 89.7 us
  local copies, waits for them, and re-layouts: 26.9 us -> 21.9 us
    all_to_all x7 -> x6, blocking collectives: 181 us -> 152 us  [exchange(): return lax.all_to_all(values, axes, split_axis=0, concat_axis=0, tiled=True)]
    pallas_call x4 -> x1, Pallas kernels: 27.5 us -> 5.78 us  [gather(): pl.pallas_call(gather_kernel, in_specs=[smem, smem] + [vmem] * 13, out_sp...]
    all_to_all x2 -> x3, waiting for transfers between devices: 15.2 us -> 0.01 us  [exchange(): return lax.all_to_all(values, axes, split_axis=0, concat_axis=0, tiled=True)]
    ppermute x9 -> x13, waiting for transfers between devices: 33.7 us -> 48.5 us  [around(): lax.ppermute(values, 'arc', [(i, (i + k) % SHARDS) for i in range(SHARDS)])]
    pallas_call x4 -> x5, Pallas kernels: 53 us -> 66.8 us  [the longest x4 65.3 us: advance(): pl.pallas_call(functools.partial(step_kernel, last=last), in_specs=[smem,...]
    all_to_all x2 -> x3, starting transfers between devices: 14.6 us -> 23.3 us  [exchange(): return lax.all_to_all(values, axes, split_axis=0, concat_axis=0, tiled=True)]
    ppermute x9 -> x13, starting transfers between devices: 15.9 us -> 20 us  [around(): lax.ppermute(values, 'arc', [(i, (i + k) % SHARDS) for i in range(SHARDS)])]
    unnamed x37 -> x52, local copies, waits for them, and re-layouts: 15.1 us -> 11.1 us
  transfers between devices with their start and end apart: 12 -> 16, of which waited for: 4 -> 6; matrix products, arithmetic and copies ran while one was open for 2% -> 2% of each run, Pallas kernels for 5% -> 7%
where the time goes in v3:
time: 357 us; the launch traced here: 356 us
  blocking collectives  152 us (43%)
  Pallas kernels  89.7 us (25%)
  waiting for transfers between devices  48.5 us (14%)
  starting transfers between devices  43.3 us (12%)
  local copies, waits for them, and re-layouts  21.9 us (6%)
    all_to_all x6, blocking collectives, exchange(): return lax.all_to_all(values, axes, split_axis=0, concat_axis=0, tiled=True)  152 us
    pallas_call x4, Pallas kernels, advance(): pl.pallas_call(functools.partial(step_kernel, last=last), in_specs=[smem,...  65.3 us
    ppermute x13, waiting for transfers between devices, around(): lax.ppermute(values, 'arc', [(i, (i + k) % SHARDS) for i in range(SHARDS)])  48.5 us
    all_to_all x3, starting transfers between devices, exchange(): return lax.all_to_all(values, axes, split_axis=0, concat_axis=0, tiled=True)  23.3 us
    ppermute x13, starting transfers between devices, around(): lax.ppermute(values, 'arc', [(i, (i + k) % SHARDS) for i in range(SHARDS)])  20 us
    unnamed x52, local copies, waits for them, and re-layouts  11.1 us
    pallas_call x4, Pallas kernels, project(): pl.pallas_call(project_kernel, in_specs=[smem, vmem, vmem], out_specs=[vm...  9.5 us
    pallas_call x1, Pallas kernels, own_trial(): pl.pallas_call(own_trial_kernel, grid=(SHARDS, OWNERS * OWN // CHUNK), in...  7.66 us
  transfers between devices with their start and end apart: 16, of which 6 were waited for; matrix products, arithmetic and copies ran while one was open for 2% of the time, Pallas kernels for 7%

profile of v3, /device:TPU:6, one launch (start us, length us, event | category | flops | bytes accessed | tf_op | source)
XLA Modules:
  0.0 356.1 jit_solution(9698359362963494259)
XLA Ops:
  3.8 7.7 %own_trial.1 = f32[32,32,512]{2,1,0:T(8,128)S(1)} custom-call(s32[128]{0:T(128)S(1)} %copy-done.22, s32[128]{0:T(128)S(1)} %copy-done.24, s32[128,128]{1,0:T(8,128)S(1)} %bitcast.12, s32[128,128]{1,0:T(8,128)S(1)} %bitcast.14, f32[32,16384]{1,0:T(8,128)} %price.1, f32[32,16384]{1,0:T(8,128)} %flow.1, f32[32,16384]{1,0:T(8,128)} %cost.1), custom_call_target="tpu_custom_call" | custom-call | tf_op jit(solution)/shard_map/own_trial/pallas_call | solution.py:193
  12.8 4.1 %collective-permute-start.5 = (s32[264,128]{1,0:T(8,128)S(1)}, s32[264,128]{1,0:T(8,128)S(1)}, u32[]{:S(2)}, u32[]{:S(2)}) collective-permute-start(s32[264,128]{1,0:T(8,128)S(1)} %concatenate.6.refs_0_), channel_id=1, source_target_pairs={{0,3},{1,0},{2,1},{3,2},{4,7},{5,4},{6,5},{7,6},{8,11},{9,8},{10,9... | collective-permute-start | bytes 405512 | tf_op jit(solution)/shard_map/ppermute | solution.py:316
  18.2 7.7 %all-to-all-start = ((f32[32,32,512]{2,1,0:T(8,128)}), f32[32,32,512]{2,1,0:T(8,128)}, u32[]{:S(2)}, u32[]{:S(2)}) async-start(f32[32,32,512]{2,1,0:T(8,128)} %copy-done.2), calls=%async_computation | async-start | bytes 4194304 | tf_op jit(solution)/shard_map/all_to_all | solution.py:313
  25.9 3.0 constant_dynamic-slice_fusion.6
  28.9 2.0 collective-permute-start.2
  30.9 2.3 collective-permute-start.1
  37.2 2.2 collective-permute-start.8
  39.4 15.1 %collective-permute-done.2.refs_8_.refs_9_ = f32[8,16384]{1,0:T(8,128)} collective-permute-done((f32[8,16384]{1,0:T(8,128)}, f32[8,16384]{1,0:T(8,128)}, u32[]{:S(2)}, u32[]{:S(2)}) %collective-permute-start.2) | collective-permute-done | bytes 524320 | tf_op jit(solution)/shard_map/ppermute | solution.py:316
  54.5 2.4 collective-permute-start.7
  57.7 12.1 %collective-permute-done.6.refs_10_.refs_13_ = f32[8,16384]{1,0:T(8,128)S(1)} collective-permute-done((f32[8,16384]{1,0:T(8,128)}, f32[8,16384]{1,0:T(8,128)S(1)}, u32[]{:S(2)}, u32[]{:S(2)}) %collective-permute-start.6) | collective-permute-done | bytes 524320 | tf_op jit(solution)/shard_map/ppermute | solution.py:316
  70.5 3.1 project.4
  74.3 9.0 %all-to-all-start.1 = ((f32[128,4,128]{2,1,0:T(4,128)}), f32[128,4,128]{2,1,0:T(4,128)}, u32[]{:S(2)}, u32[]{:S(2)}) async-start(f32[128,4,128]{2,1,0:T(4,128)} %copy-done.8), calls=%async_computation.1 | async-start | bytes 524288 | tf_op jit(solution)/shard_map/all_to_all | solution.py:313
  86.2 5.8 %trial.1.refs_4_ = f32[128,8,512]{2,1,0:T(8,128)S(1)} custom-call(s32[1]{0:T(128)} %bitcast.1.part, s32[8,128]{1,0:T(8,128)S(1)} %pad_add_fusion.blocks, s32[264,128]{1,0:T(8,128)S(1)} %concatenate.6.refs_0_, s32[264,128]{1,0:T(8,128)} %collective-permute-done.3.refs_1_, s32[264,128]{1,0:T(8,128)S(1)} %collective-permute-done.4.refs_2_, ...), custom_call_target="tpu_custom_call" | custom-call | tf_op jit(solution)/shard_map/trial/pallas_call | solution.py:219
  94.1 18.2 %step.4 = (f32[128,8,512]{2,1,0:T(8,128)S(1)}, f32[8,16384]{1,0:T(8,128)S(1)}, f32[8,16384]{1,0:T(8,128)S(1)}, f32[8,16384]{1,0:T(8,128)S(1)}, f32[8,16384]{1,0:T(8,128)S(1)}, /*index=5*/f32[8,16384]{1,0:T(8,128)S(1)}) custom-call(s32[1]{0:T(128)} %bitcast.1.part, s32[8,128]{1,0:T(8,128)S(1)} %pad_add_fusion.blocks, s32[264,128]{1,0:T(8,128)S(1)} %concatenate.6.refs_0_, ...), custom_call_target="tpu_custom_call" | custom-call | flops 536870912 | bytes 40000000 | tf_op jit(solution)/shard_map/step/pallas_call | solution.py:254
  112.4 38.8 %all_to_all.45.values = f32[128,8,512]{2,1,0:T(8,128)S(1)} all-to-all(f32[128,8,512]{2,1,0:T(8,128)S(1)} %get-tuple-element.58.refs_4_), channel_id=1, replica_groups=mesh['com'=32,'arc'=4] {'com','arc'}, dimensions={0} | all-to-all | bytes 4194304 | tf_op jit(solution)/shard_map/all_to_all | solution.py:313
  151.1 2.1 project.5
  153.2 14.4 %all_to_all.46.refs_5_ = f32[128,4,128]{2,1,0:T(4,128)S(1)} all-to-all(f32[128,4,128]{2,1,0:T(4,128)S(1)} %project.5), channel_id=1, replica_groups=mesh['com'=32,'arc'=4] {'com','arc'}, dimensions={0} | all-to-all | bytes 524288 | tf_op jit(solution)/shard_map/all_to_all | solution.py:313
  167.6 16.6 %step.5 = (f32[128,8,512]{2,1,0:T(8,128)S(1)}, f32[8,16384]{1,0:T(8,128)S(1)}, f32[8,16384]{1,0:T(8,128)S(1)}, f32[8,16384]{1,0:T(8,128)S(1)}, f32[8,16384]{1,0:T(8,128)S(1)}, /*index=5*/f32[8,16384]{1,0:T(8,128)S(1)}) custom-call(s32[1]{0:T(128)} %bitcast.1.part, s32[8,128]{1,0:T(8,128)S(1)} %pad_add_fusion.blocks, s32[264,128]{1,0:T(8,128)S(1)} %concatenate.6.refs_0_, ...), custom_call_target="tpu_custom_call" | custom-call | flops 536870912 | bytes 40000000 | tf_op jit(solution)/shard_map/step/pallas_call | solution.py:254
  184.3 34.9 %all_to_all.47.values = f32[128,8,512]{2,1,0:T(8,128)S(1)} all-to-all(f32[128,8,512]{2,1,0:T(8,128)S(1)} %get-tuple-element.64.refs_4_), channel_id=1, replica_groups=mesh['com'=32,'arc'=4] {'com','arc'}, dimensions={0} | all-to-all | bytes 4194304 | tf_op jit(solution)/shard_map/all_to_all | solution.py:313
  219.1 2.1 project.6
  221.2 14.4 %all_to_all.48.refs_5_ = f32[128,4,128]{2,1,0:T(4,128)S(1)} all-to-all(f32[128,4,128]{2,1,0:T(4,128)S(1)} %project.6), channel_id=1, replica_groups=mesh['com'=32,'arc'=4] {'com','arc'}, dimensions={0} | all-to-all | bytes 524288 | tf_op jit(solution)/shard_map/all_to_all | solution.py:313
  235.6 16.6 %step.6 = (f32[128,8,512]{2,1,0:T(8,128)S(1)}, f32[8,16384]{1,0:T(8,128)S(1)}, f32[8,16384]{1,0:T(8,128)S(1)}, f32[8,16384]{1,0:T(8,128)S(1)}, f32[8,16384]{1,0:T(8,128)S(1)}, /*index=5*/f32[8,16384]{1,0:T(8,128)S(1)}) custom-call(s32[1]{0:T(128)} %bitcast.1.part, s32[8,128]{1,0:T(8,128)S(1)} %pad_add_fusion.blocks, s32[264,128]{1,0:T(8,128)S(1)} %concatenate.6.refs_0_, ...), custom_call_target="tpu_custom_call" | custom-call | flops 536870912 | bytes 40000000 | tf_op jit(solution)/shard_map/step/pallas_call | solution.py:254
  253.1 34.9 %all_to_all.49.values = f32[128,8,512]{2,1,0:T(8,128)S(1)} all-to-all(f32[128,8,512]{2,1,0:T(8,128)S(1)} %get-tuple-element.70.refs_4_), channel_id=1, replica_groups=mesh['com'=32,'arc'=4] {'com','arc'}, dimensions={0} | all-to-all | bytes 4194304 | tf_op jit(solution)/shard_map/all_to_all | solution.py:313
  288.0 2.3 project.7
  291.6 14.4 %all_to_all.50.refs_5_ = f32[128,4,128]{2,1,0:T(4,128)S(1)} all-to-all(f32[128,4,128]{2,1,0:T(4,128)S(1)} %get-tuple-element.72), channel_id=1, replica_groups=mesh['com'=32,'arc'=4] {'com','arc'}, dimensions={0} | all-to-all | bytes 524288 | tf_op jit(solution)/shard_map/all_to_all | solution.py:313
  306.0 6.6 %all-to-all-start.7 = ((f32[32,32,512]{2,1,0:T(8,128)}), f32[32,32,512]{2,1,0:T(8,128)}, u32[]{:S(2)}, u32[]{:S(2)}) async-start(f32[32,32,512]{2,1,0:T(8,128)} %bitcast.11), calls=%async_computation.7 | async-start | bytes 4194304 | tf_op jit(solution)/shard_map/all_to_all | solution.py:313
  312.6 13.8 %step.7.refs_0_ = f32[8,16384]{1,0:T(8,128)S(1)} custom-call(s32[1]{0:T(128)} %bitcast.1.part, s32[8,128]{1,0:T(8,128)S(1)} %pad_add_fusion.blocks, s32[264,128]{1,0:T(8,128)S(1)} %concatenate.6.refs_0_, s32[264,128]{1,0:T(8,128)} %collective-permute-done.3.refs_1_, s32[264,128]{1,0:T(8,128)S(1)} %collective-permute-done.4.refs_2_, ...), custom_call_target="tpu_custom_call" | custom-call | flops 536870912 | bytes 40000000 | tf_op jit(solution)/shard_map/step/pallas_call | solution.py:254
  328.6 12.0 %collective-permute-done.10.refs_2_ = f32[8,16384]{1,0:T(8,128)S(1)} collective-permute-done((f32[8,16384]{1,0:T(8,128)S(1)}, f32[8,16384]{1,0:T(8,128)S(1)}, u32[]{:S(2)}, u32[]{:S(2)}) %collective-permute-start.10) | collective-permute-done | bytes 524320 | tf_op jit(solution)/shard_map/ppermute | solution.py:316
  340.5 2.4 collective-permute-start.12
  343.1 5.1 %collective-permute-done.12.refs_4_ = f32[8,8192]{1,0:T(8,128)S(1)} collective-permute-done((f32[8,8192]{1,0:T(8,128)S(1)}, f32[8,8192]{1,0:T(8,128)S(1)}, u32[]{:S(2)}, u32[]{:S(2)}) %collective-permute-start.12) | collective-permute-done | bytes 262176 | tf_op jit(solution)/shard_map/ppermute | solution.py:316
  348.1 3.4 collective-permute-done.11.refs_3_
  353.0 3.1 copy.13
  (84 shorter events, 22.7 us)
Async XLA Ops:
  0.6 35.0 %copy-start = (f32[32,16384]{1,0:T(8,128)S(1)}, f32[32,16384]{1,0:T(8,128)}, u32[]{:S(2)}) copy-start(f32[32,16384]{1,0:T(8,128)} %param.13) | copy-start | bytes 6291460
  3.8 9.0 %copy-start.15 = (s32[16384]{0:T(1024)S(1)}, s32[16384]{0:T(1024)}, u32[]{:S(2)}) copy-start(s32[16384]{0:T(1024)} %param.16) | copy-start | bytes 196612
  3.8 9.0 %copy-start.17 = (s32[16384]{0:T(1024)S(1)}, s32[16384]{0:T(1024)}, u32[]{:S(2)}) copy-start(s32[16384]{0:T(1024)} %param.17) | copy-start | bytes 196612
  3.8 9.0 %copy-start.23 = (s32[128]{0:T(128)S(1)}, s32[128]{0:T(128)}, u32[]{:S(2)}) copy-start(s32[128]{0:T(128)} %head_block.1) | copy-start | bytes 1540
  11.5 1.3 copy-start.2
  12.8 21.7 %collective-permute-start.5 = (s32[264,128]{1,0:T(8,128)S(1)}, s32[264,128]{1,0:T(8,128)S(1)}, u32[]{:S(2)}, u32[]{:S(2)}) collective-permute-start(s32[264,128]{1,0:T(8,128)S(1)} %concatenate.6.refs_0_), channel_id=1, source_target_pairs={{0,3},{1,0},{2,1},{3,2},{4,7},{5,4},{6,5},{7,6},{8,11},{9,8},{10,9... | collective-permute-start | bytes 405512 | tf_op jit(solution)/shard_map/ppermute | solution.py:316
  16.9 17.6 %collective-permute-start.4 = (s32[264,128]{1,0:T(8,128)S(1)}, s32[264,128]{1,0:T(8,128)S(1)}, u32[]{:S(2)}, u32[]{:S(2)}) collective-permute-start(s32[264,128]{1,0:T(8,128)S(1)} %concatenate.6.refs_0_), channel_id=1, source_target_pairs={{0,2},{1,3},{2,0},{3,1},{4,6},{5,7},{6,4},{7,5},{8,10},{9,11},{10,... | collective-permute-start | bytes 405512 | tf_op jit(solution)/shard_map/ppermute | solution.py:316
  16.9 20.3 %collective-permute-start.3 = (s32[264,128]{1,0:T(8,128)S(1)}, s32[264,128]{1,0:T(8,128)}, u32[]{:S(2)}, u32[]{:S(2)}) collective-permute-start(s32[264,128]{1,0:T(8,128)S(1)} %concatenate.6.refs_0_), channel_id=1, source_target_pairs={{0,1},{1,2},{2,3},{3,0},{4,5},{5,6},{6,7},{7,4},{8,9},{9,10},{10,1... | collective-permute-start | bytes 405512 | tf_op jit(solution)/shard_map/ppermute | solution.py:316
  18.2 51.6 %all-to-all-start = ((f32[32,32,512]{2,1,0:T(8,128)}), f32[32,32,512]{2,1,0:T(8,128)}, u32[]{:S(2)}, u32[]{:S(2)}) async-start(f32[32,32,512]{2,1,0:T(8,128)} %copy-done.2), calls=%async_computation | async-start | bytes 4194304 | tf_op jit(solution)/shard_map/all_to_all | solution.py:313
  25.9 7.3 %copy-start.25 = (f32[32,16384]{1,0:T(8,128)S(1)}, f32[32,16384]{1,0:T(8,128)}, u32[]{:S(2)}) copy-start(f32[32,16384]{1,0:T(8,128)} %cost.1) | copy-start | bytes 6291460
  28.9 25.6 %collective-permute-start.2 = (f32[8,16384]{1,0:T(8,128)}, f32[8,16384]{1,0:T(8,128)}, u32[]{:S(2)}, u32[]{:S(2)}) collective-permute-start(f32[8,16384]{1,0:T(8,128)} %get-tuple-element.82), channel_id=1, source_target_pairs={{0,3},{1,0},{2,1},{3,2},{4,7},{5,4},{6,5},{7,6},{8,11},{9,8},{10,9... | collective-permute-start | bytes 1572872 | tf_op jit(solution)/shard_map/ppermute | solution.py:316
  30.9 26.0 %collective-permute-start.1 = (f32[8,16384]{1,0:T(8,128)}, f32[8,16384]{1,0:T(8,128)}, u32[]{:S(2)}, u32[]{:S(2)}) collective-permute-start(f32[8,16384]{1,0:T(8,128)} %get-tuple-element.83), channel_id=1, source_target_pairs={{0,2},{1,3},{2,0},{3,1},{4,6},{5,7},{6,4},{7,5},{8,10},{9,11},{10,... | collective-permute-start | bytes 1572872 | tf_op jit(solution)/shard_map/ppermute | solution.py:316
  34.5 23.3 %collective-permute-start = (f32[8,16384]{1,0:T(8,128)}, f32[8,16384]{1,0:T(8,128)}, u32[]{:S(2)}, u32[]{:S(2)}) collective-permute-start(f32[8,16384]{1,0:T(8,128)} %get-tuple-element.84), channel_id=1, source_target_pairs={{0,1},{1,2},{2,3},{3,0},{4,5},{5,6},{6,7},{7,4},{8,9},{9,10},{10,1... | collective-permute-start | bytes 1572872 | tf_op jit(solution)/shard_map/ppermute | solution.py:316
  34.5 35.3 %collective-permute-start.6 = (f32[8,16384]{1,0:T(8,128)}, f32[8,16384]{1,0:T(8,128)S(1)}, u32[]{:S(2)}, u32[]{:S(2)}) collective-permute-start(f32[8,16384]{1,0:T(8,128)} %get-tuple-element.81), channel_id=1, source_target_pairs={{0,1},{1,2},{2,3},{3,0},{4,5},{5,6},{6,7},{7,4},{8,9},{9,10},{10,1... | collective-permute-start | bytes 1572872 | tf_op jit(solution)/shard_map/ppermute | solution.py:316
  37.2 47.9 %copy-start.18 = (s32[4,128]{1,0:T(4,128)}, s32[4,128]{1,0:T(4,128)S(1)}, u32[]{:S(2)}) copy-start(s32[4,128]{1,0:T(4,128)S(1)} %constant_dynamic-slice_fusion.10.classes) | copy-start | bytes 6148
  37.2 47.9 %collective-permute-start.8 = (f32[8,16384]{1,0:T(8,128)}, f32[8,16384]{1,0:T(8,128)}, u32[]{:S(2)}, u32[]{:S(2)}) collective-permute-start(f32[8,16384]{1,0:T(8,128)} %get-tuple-element.78), channel_id=1, source_target_pairs={{0,3},{1,0},{2,1},{3,2},{4,7},{5,4},{6,5},{7,6},{8,11},{9,8},{10,9... | collective-permute-start | bytes 1572872 | tf_op jit(solution)/shard_map/ppermute | solution.py:316
  54.5 30.6 %collective-permute-start.7 = (f32[8,16384]{1,0:T(8,128)}, f32[8,16384]{1,0:T(8,128)}, u32[]{:S(2)}, u32[]{:S(2)}) collective-permute-start(f32[8,16384]{1,0:T(8,128)} %get-tuple-element.79), channel_id=1, source_target_pairs={{0,2},{1,3},{2,0},{3,1},{4,6},{5,7},{6,4},{7,5},{8,10},{9,11},{10,... | collective-permute-start | bytes 1572872 | tf_op jit(solution)/shard_map/ppermute | solution.py:316
  74.3 19.7 %all-to-all-start.1 = ((f32[128,4,128]{2,1,0:T(4,128)}), f32[128,4,128]{2,1,0:T(4,128)}, u32[]{:S(2)}, u32[]{:S(2)}) async-start(f32[128,4,128]{2,1,0:T(4,128)} %copy-done.8), calls=%async_computation.1 | async-start | bytes 524288 | tf_op jit(solution)/shard_map/all_to_all | solution.py:313
  92.0 1.3 copy-start.4
  112.3 38.8 %copy-start.19 = (s32[4,128]{1,0:T(4,128)S(1)}, s32[4,128]{1,0:T(4,128)}, u32[]{:S(2)}) copy-start(s32[4,128]{1,0:T(4,128)} %copy-done.18) | copy-start | bytes 6148
  112.3 38.8 %copy-start.21 = (f32[8]{0:T(128)S(1)}, f32[8]{0:T(128)}, u32[]{:S(2)}) copy-start(f32[8]{0:T(128)} %levels.7) | copy-start | bytes 100
  151.1 16.5 %copy-start.1 = (f32[8,16384]{1,0:T(8,128)S(1)}, f32[8,16384]{1,0:T(8,128)}, u32[]{:S(2)}) copy-start(f32[8,16384]{1,0:T(8,128)} %constant_dynamic-slice_fusion.refs_11_) | copy-start | bytes 1572868
  253.1 34.9 %copy-start.3 = (f32[128,8,512]{2,1,0:T(8,128)}, f32[128,8,512]{2,1,0:T(8,128)S(1)}, u32[]{:S(2)}) copy-start(f32[128,8,512]{2,1,0:T(8,128)S(1)} %get-tuple-element.70.refs_4_) | copy-start | bytes 6291460
  253.1 34.9 %copy-start.9 = (f32[8,16384]{1,0:T(8,128)}, f32[8,16384]{1,0:T(8,128)S(1)}, u32[]{:S(2)}) copy-start(f32[8,16384]{1,0:T(8,128)S(1)} %get-tuple-element.77.refs_10_) | copy-start | bytes 1572868
  253.1 34.9 %copy-start.10 = (f32[8,16384]{1,0:T(8,128)}, f32[8,16384]{1,0:T(8,128)S(1)}, u32[]{:S(2)}) copy-start(f32[8,16384]{1,0:T(8,128)S(1)} %get-tuple-element.73.refs_6_) | copy-start | bytes 1572868
  253.1 34.9 %copy-start.11 = (f32[8,16384]{1,0:T(8,128)}, f32[8,16384]{1,0:T(8,128)S(1)}, u32[]{:S(2)}) copy-start(f32[8,16384]{1,0:T(8,128)S(1)} %get-tuple-element.74.refs_7_) | copy-start | bytes 1572868
  253.1 34.9 %copy-start.12 = (f32[8,16384]{1,0:T(8,128)}, f32[8,16384]{1,0:T(8,128)S(1)}, u32[]{:S(2)}) copy-start(f32[8,16384]{1,0:T(8,128)S(1)} %get-tuple-element.75.refs_8_) | copy-start | bytes 1572868
  306.0 47.0 %all-to-all-start.7 = ((f32[32,32,512]{2,1,0:T(8,128)}), f32[32,32,512]{2,1,0:T(8,128)}, u32[]{:S(2)}, u32[]{:S(2)}) async-start(f32[32,32,512]{2,1,0:T(8,128)} %bitcast.11), calls=%async_computation.7 | async-start | bytes 4194304 | tf_op jit(solution)/shard_map/all_to_all | solution.py:313
  326.5 14.0 %collective-permute-start.10 = (f32[8,16384]{1,0:T(8,128)S(1)}, f32[8,16384]{1,0:T(8,128)S(1)}, u32[]{:S(2)}, u32[]{:S(2)}) collective-permute-start(f32[8,16384]{1,0:T(8,128)S(1)} %step.7.refs_0_), channel_id=1, source_target_pairs={{0,3},{1,0},{2,1},{3,2},{4,7},{5,4},{6,5},{7,6},{8,11},{9,8},{10,9... | collective-permute-start | bytes 1572872 | tf_op jit(solution)/shard_map/ppermute | solution.py:316
  327.7 15.3 %collective-permute-start.9 = (f32[8,16384]{1,0:T(8,128)S(1)}, f32[8,16384]{1,0:T(8,128)S(1)}, u32[]{:S(2)}, u32[]{:S(2)}) collective-permute-start(f32[8,16384]{1,0:T(8,128)S(1)} %step.7.refs_0_), channel_id=1, source_target_pairs={{0,1},{1,2},{2,3},{3,0},{4,5},{5,6},{6,7},{7,4},{8,9},{9,10},{10,1... | collective-permute-start | bytes 1572872 | tf_op jit(solution)/shard_map/ppermute | solution.py:316
  340.5 7.6 %collective-permute-start.12 = (f32[8,8192]{1,0:T(8,128)S(1)}, f32[8,8192]{1,0:T(8,128)S(1)}, u32[]{:S(2)}, u32[]{:S(2)}) collective-permute-start(f32[8,8192]{1,0:T(8,128)S(1)} %slice.25), channel_id=1, source_target_pairs={{0,3},{1,0},{2,1},{3,2},{4,7},{5,4},{6,5},{7,6},{8,11},{9,8},{10,9... | collective-permute-start | bytes 786440 | tf_op jit(solution)/shard_map/ppermute | solution.py:316
  343.0 8.5 %collective-permute-start.11 = (f32[8,8192]{1,0:T(8,128)S(1)}, f32[8,8192]{1,0:T(8,128)S(1)}, u32[]{:S(2)}, u32[]{:S(2)}) collective-permute-start(f32[8,8192]{1,0:T(8,128)S(1)} %slice.24), channel_id=1, source_target_pairs={{0,1},{1,2},{2,3},{3,0},{4,5},{5,6},{6,7},{7,4},{8,9},{9,10},{10,1... | collective-permute-start | bytes 786440 | tf_op jit(solution)/shard_map/ppermute | solution.py:316
  (10 other events, 8.5 us)

commit v4 on v3

--- a/solution.py
+++ b/solution.py
@@ -64,7 +64,7 @@
 
 
 def gather_kernel(part, blocks, *refs):
-    fill_trial(part, blocks, refs[:4], refs[4], refs[5:9], refs[9:13], refs[13])
+    fill_trial(part, blocks, refs[:4], refs[4], refs[5:9], refs[5:9], refs[9])
 
 
 def fill_trial(part, blocks, locals_, price, flow, cost, trial):
@@ -83,8 +83,8 @@
                     at_tail = jnp.take_along_axis(price[:, node_slice(blocks[2 * k + 1, j])], tail, axis=1)
                     where = arc_slice(start, q)
                     trial[owner * SHARDS + shard, :, q * BLOCK : (q + 1) * BLOCK] = flow[k][
-                        :, where
-                    ] - step_primal * (cost[k][:, where] - (at_head - at_tail))
+                        :8, where
+                    ] - step_primal * (cost[k][8:, where] - (at_head - at_tail))
             return carry
 
         lax.fori_loop(0, OWNERS // UNROLL, step, 0)
@@ -135,14 +135,15 @@
         lax.fori_loop(0, groups // 8, keep, 0)
 
 
-def step_kernel(part, blocks, *refs, last):
-    locals_, trial, theta, flow, price, demand = refs[:4], refs[4], refs[5], refs[6:10], refs[10], refs[11]
+def step_kernel(part, blocks, *refs, first, last):
+    locals_, trial, theta, price, demand, flow = refs[:4], refs[4], refs[5], refs[6], refs[7], refs[8:12]
     balance = refs[-1]
     if last:
-        (price_out,) = refs[12:-1]
+        price_out = refs[12]
         fresh_out = cost = following = None
     else:
-        cost, following, price_out, fresh_out = refs[12:16], refs[16], refs[17], refs[18:22]
+        cost, rest = (flow, refs[12:]) if first else (refs[12:16], refs[16:])
+        following, price_out, fresh_out = rest[0], rest[1], rest[2:6]
     balance[...] = jnp.zeros_like(balance)
     lanes = lax.broadcasted_iota(jnp.int32, (BLOCK, BLOCK), 0).astype(jnp.int16)
     one = jnp.ones((), bf16)
@@ -168,7 +169,7 @@
                     )
                     if not last:
                         fresh_out[k][:, where] = fresh
-                    extra = 2.0 * fresh - flow[k][:, where]
+                    extra = 2.0 * fresh - flow[k][:8, where]
                     high = extra.astype(bf16)
                     low = (extra - high.astype(f32)).astype(bf16)
                     both = jnp.concatenate([high, low], axis=0)
@@ -186,6 +187,31 @@
     price_out[...] = price[...] + step_dual * (demand[...] - balance[...])
     if not last:
         fill_trial(part, blocks, locals_, price_out, fresh_out, cost, following)
+
+
+def pack_kernel(part, *refs):
+    for k in range(SHARDS):
+        refs[2 * SHARDS + k][:8] = refs[k][...]
+        refs[2 * SHARDS + k][8:] = refs[SHARDS + k][...]
+
+
+def pack(part, flow, cost):
+    def rows(k):
+        return pl.BlockSpec((8, CHUNK), lambda c, part: ((part[0] + k) & (SHARDS - 1), c))
+
+    width = OWNERS * OWN
+    return pl.pallas_call(
+        pack_kernel,
+        grid_spec=pltpu.PrefetchScalarGridSpec(
+            num_scalar_prefetch=1,
+            grid=(width // CHUNK,),
+            in_specs=[rows(k) for k in range(SHARDS)] * 2,
+            out_specs=[pl.BlockSpec((16, CHUNK), lambda c, part: (0, c))] * SHARDS,
+        ),
+        out_shape=[jax.ShapeDtypeStruct((16, width), f32)] * SHARDS,
+        compiler_params=params(12),
+        name="pack",
+    )(part, *in_hbm([flow] * SHARDS + [cost] * SHARDS))
 
 
 def own_trial(head_block, tail_block, head_local, tail_local, price, flow, cost):
@@ -206,24 +232,18 @@
         out_shape=jax.ShapeDtypeStruct((OWNERS, SHARDS * 8, OWN), f32),
         compiler_params=params(8),
         name="own_trial",
-    )(
-        head_block,
-        tail_block,
-        head_local,
-        tail_local,
-        *in_hbm([price, flow, cost]),
-    )
-
-
-def gather(part, blocks, locals_, price, flow, cost):
+    )(*in_hbm([head_block, tail_block, head_local, tail_local, price, flow, cost]))
+
+
+def gather(part, blocks, locals_, price, flow_cost):
     return pl.pallas_call(
         gather_kernel,
-        in_specs=[smem, smem] + [vmem] * 13,
+        in_specs=[smem, smem] + [vmem] * 9,
         out_specs=vmem,
         out_shape=jax.ShapeDtypeStruct((OWNERS * SHARDS, 8, OWN), f32),
         compiler_params=params(12),
         name="trial",
-    )(part, blocks, *locals_, price, *flow, *cost)
+    )(part, blocks, *locals_, price, *flow_cost)
 
 
 def project(levels, classes, values, last):
@@ -244,23 +264,24 @@
     return [pltpu.with_memory_space_constraint(x, pltpu.HBM) for x in values]
 
 
-def advance(part, blocks, locals_, trial, theta, flow, price, demand, cost, first, last):
+def advance(part, blocks, locals_, trial, theta, flow, price, demand, flow_cost, first, last):
     if first or last:
         trial, price, demand, *flow = in_hbm([trial, price, demand, *flow])
+    operands = [trial, theta, price, demand] + list(flow) + ([] if first or last else list(flow_cost))
     shape = [jax.ShapeDtypeStruct((8, NODES), f32)]
     if not last:
         shape = [jax.ShapeDtypeStruct(trial.shape, f32)] + shape
         shape = shape + [jax.ShapeDtypeStruct((8, OWNERS * OWN), f32)] * SHARDS
     out = pl.pallas_call(
-        functools.partial(step_kernel, last=last),
-        in_specs=[smem, smem] + [vmem] * (12 if last else 16),
+        functools.partial(step_kernel, first=first, last=last),
+        in_specs=[smem, smem] + [vmem] * (SHARDS + len(operands)),
         out_specs=[vmem] * len(shape),
         out_shape=shape,
         scratch_shapes=[pltpu.VMEM((8, NODES), f32)],
         compiler_params=params(14),
         cost_estimate=pl.CostEstimate(flops=2 * 16 * 256 * OWNERS * OWN * SHARDS, transcendentals=0, bytes_accessed=COVER),
         name="step",
-    )(part, blocks, *locals_, trial, theta, *flow, price, demand, *([] if last else cost))
+    )(part, blocks, *locals_, *operands)
     return (None, out[0], None) if last else (out[0], out[1], out[2:])
 
 
@@ -318,17 +339,14 @@
     def rows_of(values, k):
         return lax.dynamic_slice(values, (((part + k) & (SHARDS - 1)) * 8, 0), (8, values.shape[1]))
 
-    def slots(values):
-        return [rows_of(values, 0)] + [around(rows_of(values, k), k) for k in range(1, SHARDS)]
-
+    own = part.astype(jnp.int32).reshape(1)
+    pairs = pack(own, flow_start, cost)
+    pairs, flow_start, cost, price_start = lax.optimization_barrier((pairs, flow_start, cost, price_start))
+    flow_cost = [pairs[0]] + [around(pairs[k], k) for k in (1, 3, 2)]
+    flow_cost = [flow_cost[0], flow_cost[1], flow_cost[3], flow_cost[2]]
     first = own_trial(head_block, tail_block, head_rows, tail_rows, price_start, flow_start, cost)
-    first, flow_start, cost, price_start, head_rows, tail_rows, head_block, tail_block = lax.optimization_barrier(
-        (first, flow_start, cost, price_start, head_rows, tail_rows, head_block, tail_block)
-    )
     values = exchange(first, "com").reshape(OWNERS * SHARDS, 8, OWN)
 
-    flow = slots(flow_start)
-    unit_cost = slots(cost)
     packed = jnp.concatenate(
         [
             head_rows,
@@ -339,29 +357,32 @@
         ],
         axis=0,
     )
+    flow_cost[1], packed = lax.optimization_barrier((flow_cost[1], packed))
     locals_ = [packed] + [around(packed, k) for k in range(1, SHARDS)]
-    values, flow, locals_, unit_cost[1] = lax.optimization_barrier((values, flow, locals_, unit_cost[1]))
+    values, locals_, flow_cost[1] = lax.optimization_barrier((values, locals_, flow_cost[1]))
     block_ids = jnp.concatenate([x[2 * blocks : 2 * blocks + 2] for x in locals_], axis=0)
     price = rows_of(price_start, 0)
     wanted = rows_of(demand, 0)
     classes = lax.dynamic_slice(cap_class.reshape(blocks, BLOCK), (place * QUADS, 0), (QUADS, BLOCK))
-    own = part.astype(jnp.int32).reshape(1)
-
-    trial = gather(own, block_ids, locals_, price, flow, unit_cost)
+
+    trial = gather(own, block_ids, locals_, price, flow_cost)
+    flow = flow_cost
     for step in range(ITERS):
         last = step == ITERS - 1
         if step > 0:
             values = exchange(trial, everyone)
         theta, *kept = project(cap_levels, classes, values, last)
         theta = exchange(theta, everyone)
-        trial, price, flow = advance(own, block_ids, locals_, trial, theta, flow, price, wanted, unit_cost, step == 0, last)
+        trial, price, flow = advance(own, block_ids, locals_, trial, theta, flow, price, wanted, flow_cost, step == 0, last)
     back = exchange(kept[0].reshape(OWNERS, com_rows, OWN), "com")
     out = back.transpose(1, 0, 2).reshape(com_rows, arc_cols)
     left = around(price, 1)
     right = around(price, 3)
     half = NODES // 2
-    full = assemble(own, price, left, right, around(left[:, :half], 1), around(right[:, half:], 3))
-    return out, full
+    far_left = around(left[:, :half], 1)
+    far_right = around(right[:, half:], 3)
+    out, price = lax.optimization_barrier((out, price))
+    return out, assemble(own, price, left, right, far_left, far_right)
 
 
 def solution(mesh):

time: 357 us -> 369 us (1.034)
  starting transfers between devices: 43.3 us -> 64.1 us
  waiting for transfers between devices: 48.5 us -> 35.4 us
  Pallas kernels: 89.7 us -> 95.7 us
    ppermute x13 -> x10, starting transfers between devices: 20 us -> 38.2 us  [around(): lax.ppermute(values, 'arc', [(i, (i + k) % SHARDS) for i in range(SHARDS)])]
    ppermute x13 -> x10, waiting for transfers between devices: 48.5 us -> 35.4 us  [around(): lax.ppermute(values, 'arc', [(i, (i + k) % SHARDS) for i in range(SHARDS)])]
    pallas_call x5 -> x6, Pallas kernels: 71.1 us -> 76.2 us  [the longest x4 67 us: advance(): pl.pallas_call(functools.partial(step_kernel, first=first, last=last), in...]
    unnamed x52 -> x58, local copies, waits for them, and re-layouts: 11.1 us -> 11.7 us
  transfers between devices with their start and end apart: 16 -> 13, of which waited for: 6 -> 5; matrix products, arithmetic and copies ran while one was open for 2% -> 2% of each run, Pallas kernels for 7% -> 8%
where the time goes in v4:
time: 369 us; the launch traced here: 368 us
  blocking collectives  152 us (41%)
  Pallas kernels  95.7 us (26%)
  starting transfers between devices  64.1 us (17%)
  waiting for transfers between devices  35.4 us (10%)
  local copies, waits for them, and re-layouts  20.4 us (6%)
    all_to_all x6, blocking collectives, exchange(): return lax.all_to_all(values, axes, split_axis=0, concat_axis=0, tiled=True)  152 us
    pallas_call x4, Pallas kernels, advance(): pl.pallas_call(functools.partial(step_kernel, first=first, last=last), in...  67 us
    ppermute x10, starting transfers between devices, around(): lax.ppermute(values, 'arc', [(i, (i + k) % SHARDS) for i in range(SHARDS)])  38.2 us
    ppermute x10, waiting for transfers between devices, around(): lax.ppermute(values, 'arc', [(i, (i + k) % SHARDS) for i in range(SHARDS)])  35.4 us
    all_to_all x3, starting transfers between devices, exchange(): return lax.all_to_all(values, axes, split_axis=0, concat_axis=0, tiled=True)  25.8 us
    unnamed x58, local copies, waits for them, and re-layouts  11.7 us
    pallas_call x4, Pallas kernels, project(): pl.pallas_call(project_kernel, in_specs=[smem, vmem, vmem], out_specs=[vm...  9.5 us
    pallas_call x1, Pallas kernels, own_trial(): pl.pallas_call(own_trial_kernel, grid=(SHARDS, OWNERS * OWN // CHUNK), in...  7.67 us
  transfers between devices with their start and end apart: 13, of which 5 were waited for; matrix products, arithmetic and copies ran while one was open for 2% of the time, Pallas kernels for 8%

profile of v4, /device:TPU:6, one launch (start us, length us, event | category | flops | bytes accessed | tf_op | source)
XLA Modules:
  0.0 368.3 jit_solution(3222951098881336929)
XLA Ops:
  0.6 3.3 pack.1
  5.9 1.9 collective-permute-start
  7.9 7.7 %own_trial.1 = f32[32,32,512]{2,1,0:T(8,128)S(1)} custom-call(s32[128]{0:T(128)} %head_block.1, s32[128]{0:T(128)} %tail_block.1, s32[128,128]{1,0:T(8,128)} %bitcast.13, s32[128,128]{1,0:T(8,128)} %bitcast.15, f32[32,16384]{1,0:T(8,128)} %price, f32[32,16384]{1,0:T(8,128)} %flow, f32[32,16384]{1,0:T(8,128)} %cost), custom_call_target="tpu_custom_call" | custom-call | tf_op jit(solution)/shard_map/own_trial/pallas_call | solution.py:219
  16.9 7.8 %all-to-all-start = ((f32[32,32,512]{2,1,0:T(8,128)}), f32[32,32,512]{2,1,0:T(8,128)}, u32[]{:S(2)}, u32[]{:S(2)}) async-start(f32[32,32,512]{2,1,0:T(8,128)} %copy-done.4), calls=%async_computation | async-start | bytes 4194304 | tf_op jit(solution)/shard_map/all_to_all | solution.py:334
  24.7 3.7 collective-permute-start.4
  29.4 4.0 %collective-permute-done.refs_6_.refs_9_.refs_13_ = f32[16,16384]{1,0:T(8,128)} collective-permute-done((f32[16,16384]{1,0:T(8,128)}, f32[16,16384]{1,0:T(8,128)}, u32[]{:S(2)}, u32[]{:S(2)}) %collective-permute-start) | collective-permute-done | bytes 1048608 | tf_op jit(solution)/shard_map/ppermute | solution.py:337
  33.5 2.9 collective-permute-start.3
  36.3 22.9 %collective-permute-start.2 = (s32[264,128]{1,0:T(8,128)S(1)}, s32[264,128]{1,0:T(8,128)S(1)}, u32[]{:S(2)}, u32[]{:S(2)}) collective-permute-start(s32[264,128]{1,0:T(8,128)S(1)} %concatenate.6.refs_0_), channel_id=1, source_target_pairs={{0,2},{1,3},{2,0},{3,1},{4,6},{5,7},{6,4},{7,5},{8,10},{9,11},{10,... | collective-permute-start | bytes 405512 | tf_op jit(solution)/shard_map/ppermute | solution.py:337
  60.7 1.9 constant_dynamic-slice_fusion.1.refs_4_.refs_6_
  63.2 14.5 %collective-permute-done.3.refs_3_ = s32[264,128]{1,0:T(8,128)S(1)} collective-permute-done((s32[264,128]{1,0:T(8,128)S(1)}, s32[264,128]{1,0:T(8,128)S(1)}, u32[]{:S(2)}, u32[]{:S(2)}) %collective-permute-start.3) | collective-permute-done | bytes 135200 | tf_op jit(solution)/shard_map/ppermute | solution.py:337
  78.4 3.1 project.4
  82.2 11.4 %all-to-all-start.1 = ((f32[128,4,128]{2,1,0:T(4,128)}), f32[128,4,128]{2,1,0:T(4,128)}, u32[]{:S(2)}, u32[]{:S(2)}) async-start(f32[128,4,128]{2,1,0:T(4,128)} %copy-done.11), calls=%async_computation.1 | async-start | bytes 524288 | tf_op jit(solution)/shard_map/all_to_all | solution.py:334
  96.3 5.9 %trial.1.refs_4_ = f32[128,8,512]{2,1,0:T(8,128)S(1)} custom-call(s32[1]{0:T(128)} %bitcast.1.part, s32[8,128]{1,0:T(8,128)S(1)} %pad_add_fusion.blocks, s32[264,128]{1,0:T(8,128)S(1)} %concatenate.6.refs_0_, s32[264,128]{1,0:T(8,128)} %collective-permute-done.1.refs_1_, s32[264,128]{1,0:T(8,128)S(1)} %collective-permute-done.2.refs_2_, ...), custom_call_target="tpu_custom_call" | custom-call | tf_op jit(solution)/shard_map/trial/pallas_call | solution.py:239
  103.6 18.6 %step.4 = (f32[128,8,512]{2,1,0:T(8,128)S(1)}, f32[8,16384]{1,0:T(8,128)S(1)}, f32[8,16384]{1,0:T(8,128)S(1)}, f32[8,16384]{1,0:T(8,128)S(1)}, f32[8,16384]{1,0:T(8,128)S(1)}, /*index=5*/f32[8,16384]{1,0:T(8,128)S(1)}) custom-call(s32[1]{0:T(128)} %bitcast.1.part, s32[8,128]{1,0:T(8,128)S(1)} %pad_add_fusion.blocks, s32[264,128]{1,0:T(8,128)S(1)} %concatenate.6.refs_0_, ...), custom_call_target="tpu_custom_call" | custom-call | flops 536870912 | bytes 40000000 | tf_op jit(solution)/shard_map/step/pallas_call | solution.py:275
  122.2 38.7 %all_to_all.45.values = f32[128,8,512]{2,1,0:T(8,128)S(1)} all-to-all(f32[128,8,512]{2,1,0:T(8,128)S(1)} %get-tuple-element.62.refs_4_), channel_id=1, replica_groups=mesh['com'=32,'arc'=4] {'com','arc'}, dimensions={0} | all-to-all | bytes 4194304 | tf_op jit(solution)/shard_map/all_to_all | solution.py:334
  161.0 2.1 project.5
  163.0 14.4 %all_to_all.46.refs_5_ = f32[128,4,128]{2,1,0:T(4,128)S(1)} all-to-all(f32[128,4,128]{2,1,0:T(4,128)S(1)} %project.5), channel_id=1, replica_groups=mesh['com'=32,'arc'=4] {'com','arc'}, dimensions={0} | all-to-all | bytes 524288 | tf_op jit(solution)/shard_map/all_to_all | solution.py:334
  177.5 17.3 %step.5 = (f32[128,8,512]{2,1,0:T(8,128)S(1)}, f32[8,16384]{1,0:T(8,128)S(1)}, f32[8,16384]{1,0:T(8,128)S(1)}, f32[8,16384]{1,0:T(8,128)S(1)}, f32[8,16384]{1,0:T(8,128)S(1)}, /*index=5*/f32[8,16384]{1,0:T(8,128)S(1)}) custom-call(s32[1]{0:T(128)} %bitcast.1.part, s32[8,128]{1,0:T(8,128)S(1)} %pad_add_fusion.blocks, s32[264,128]{1,0:T(8,128)S(1)} %concatenate.6.refs_0_, ...), custom_call_target="tpu_custom_call" | custom-call | flops 536870912 | bytes 40000000 | tf_op jit(solution)/shard_map/step/pallas_call | solution.py:275
  194.7 34.9 %all_to_all.47.values = f32[128,8,512]{2,1,0:T(8,128)S(1)} all-to-all(f32[128,8,512]{2,1,0:T(8,128)S(1)} %get-tuple-element.68.refs_4_), channel_id=1, replica_groups=mesh['com'=32,'arc'=4] {'com','arc'}, dimensions={0} | all-to-all | bytes 4194304 | tf_op jit(solution)/shard_map/all_to_all | solution.py:334
  229.6 2.1 project.6
  231.7 14.4 %all_to_all.48.refs_5_ = f32[128,4,128]{2,1,0:T(4,128)S(1)} all-to-all(f32[128,4,128]{2,1,0:T(4,128)S(1)} %project.6), channel_id=1, replica_groups=mesh['com'=32,'arc'=4] {'com','arc'}, dimensions={0} | all-to-all | bytes 524288 | tf_op jit(solution)/shard_map/all_to_all | solution.py:334
  246.1 17.3 %step.6 = (f32[128,8,512]{2,1,0:T(8,128)S(1)}, f32[8,16384]{1,0:T(8,128)S(1)}, f32[8,16384]{1,0:T(8,128)S(1)}, f32[8,16384]{1,0:T(8,128)S(1)}, f32[8,16384]{1,0:T(8,128)S(1)}, /*index=5*/f32[8,16384]{1,0:T(8,128)S(1)}) custom-call(s32[1]{0:T(128)} %bitcast.1.part, s32[8,128]{1,0:T(8,128)S(1)} %pad_add_fusion.blocks, s32[264,128]{1,0:T(8,128)S(1)} %concatenate.6.refs_0_, ...), custom_call_target="tpu_custom_call" | custom-call | flops 536870912 | bytes 40000000 | tf_op jit(solution)/shard_map/step/pallas_call | solution.py:275
  264.2 34.9 %all_to_all.49.values = f32[128,8,512]{2,1,0:T(8,128)S(1)} all-to-all(f32[128,8,512]{2,1,0:T(8,128)S(1)} %get-tuple-element.74.refs_4_), channel_id=1, replica_groups=mesh['com'=32,'arc'=4] {'com','arc'}, dimensions={0} | all-to-all | bytes 4194304 | tf_op jit(solution)/shard_map/all_to_all | solution.py:334
  299.1 2.3 project.7
  302.7 14.4 %all_to_all.50.refs_5_ = f32[128,4,128]{2,1,0:T(4,128)S(1)} all-to-all(f32[128,4,128]{2,1,0:T(4,128)S(1)} %get-tuple-element.76), channel_id=1, replica_groups=mesh['com'=32,'arc'=4] {'com','arc'}, dimensions={0} | all-to-all | bytes 524288 | tf_op jit(solution)/shard_map/all_to_all | solution.py:334
  317.1 6.6 %all-to-all-start.7 = ((f32[32,32,512]{2,1,0:T(8,128)}), f32[32,32,512]{2,1,0:T(8,128)}, u32[]{:S(2)}, u32[]{:S(2)}) async-start(f32[32,32,512]{2,1,0:T(8,128)} %bitcast.11), calls=%async_computation.7 | async-start | bytes 4194304 | tf_op jit(solution)/shard_map/all_to_all | solution.py:334
  323.7 13.8 %step.7.refs_0_ = f32[8,16384]{1,0:T(8,128)S(1)} custom-call(s32[1]{0:T(128)} %bitcast.1.part, s32[8,128]{1,0:T(8,128)S(1)} %pad_add_fusion.blocks, s32[264,128]{1,0:T(8,128)S(1)} %concatenate.6.refs_0_, s32[264,128]{1,0:T(8,128)} %collective-permute-done.1.refs_1_, s32[264,128]{1,0:T(8,128)S(1)} %collective-permute-done.2.refs_2_, ...), custom_call_target="tpu_custom_call" | custom-call | flops 536870912 | bytes 40000000 | tf_op jit(solution)/shard_map/step/pallas_call | solution.py:275
  339.7 12.0 %collective-permute-done.7.refs_2_ = f32[8,16384]{1,0:T(8,128)S(1)} collective-permute-done((f32[8,16384]{1,0:T(8,128)S(1)}, f32[8,16384]{1,0:T(8,128)S(1)}, u32[]{:S(2)}, u32[]{:S(2)}) %collective-permute-start.7) | collective-permute-done | bytes 524320 | tf_op jit(solution)/shard_map/ppermute | solution.py:337
  352.3 2.4 collective-permute-start.9
  356.2 3.2 copy.13
  360.8 4.2 %collective-permute-done.8.refs_3_ = f32[8,8192]{1,0:T(8,128)} collective-permute-done((f32[8,8192]{1,0:T(8,128)}, f32[8,8192]{1,0:T(8,128)}, u32[]{:S(2)}, u32[]{:S(2)}) %collective-permute-start.8) | collective-permute-done | bytes 262176 | tf_op jit(solution)/shard_map/ppermute | solution.py:337
  365.9 2.4 assemble.1
  (83 shorter events, 20.6 us)
Async XLA Ops:
  0.6 93.1 %copy-start = (f32[32,16384]{1,0:T(8,128)S(1)}, f32[32,16384]{1,0:T(8,128)}, u32[]{:S(2)}) copy-start(f32[32,16384]{1,0:T(8,128)} %param.13) | copy-start | bytes 6291460
  5.9 89.4 %copy-start.1 = (f32[16,16384]{1,0:T(8,128)}, f32[16,16384]{1,0:T(8,128)S(1)}, u32[]{:S(2)}) copy-start(f32[16,16384]{1,0:T(8,128)S(1)} %get-tuple-element.57.refs_5_.refs_8_.refs_12_) | copy-start | bytes 3145732
  5.9 27.5 %collective-permute-start = (f32[16,16384]{1,0:T(8,128)}, f32[16,16384]{1,0:T(8,128)}, u32[]{:S(2)}, u32[]{:S(2)}) collective-permute-start(f32[16,16384]{1,0:T(8,128)} %get-tuple-element.50), channel_id=1, source_target_pairs={{0,1},{1,2},{2,3},{3,0},{4,5},{5,6},{6,7},{7,4},{8,9},{9,10},{10,1... | collective-permute-start | bytes 3145736 | tf_op jit(solution)/shard_map/ppermute | solution.py:337
  15.5 1.3 copy-start.4
  16.9 12.5 %copy-start.25 = (s32[16384]{0:T(1024)S(1)}, s32[16384]{0:T(1024)}, u32[]{:S(2)}) copy-start(s32[16384]{0:T(1024)} %param.16) | copy-start | bytes 196612
  16.9 12.5 %copy-start.26 = (s32[16384]{0:T(1024)S(1)}, s32[16384]{0:T(1024)}, u32[]{:S(2)}) copy-start(s32[16384]{0:T(1024)} %param.17) | copy-start | bytes 196612
  16.9 12.5 %copy-start.27 = (s32[128]{0:T(128)S(1)}, s32[128]{0:T(128)}, u32[]{:S(2)}) copy-start(s32[128]{0:T(128)} %head_block.1) | copy-start | bytes 1540
  16.9 12.5 %copy-start.28 = (s32[128]{0:T(128)S(1)}, s32[128]{0:T(128)}, u32[]{:S(2)}) copy-start(s32[128]{0:T(128)} %tail_block.1) | copy-start | bytes 1540
  16.9 60.9 %all-to-all-start = ((f32[32,32,512]{2,1,0:T(8,128)}), f32[32,32,512]{2,1,0:T(8,128)}, u32[]{:S(2)}, u32[]{:S(2)}) async-start(f32[32,32,512]{2,1,0:T(8,128)} %copy-done.4), calls=%async_computation | async-start | bytes 4194304 | tf_op jit(solution)/shard_map/all_to_all | solution.py:334
  24.7 70.6 %collective-permute-start.4 = (f32[16,16384]{1,0:T(8,128)}, f32[16,16384]{1,0:T(8,128)}, u32[]{:S(2)}, u32[]{:S(2)}) collective-permute-start(f32[16,16384]{1,0:T(8,128)} %copy-done.24), channel_id=1, source_target_pairs={{0,2},{1,3},{2,0},{3,1},{4,6},{5,7},{6,4},{7,5},{8,10},{9,11},{10,... | collective-permute-start | bytes 3145736 | tf_op jit(solution)/shard_map/ppermute | solution.py:337
  28.3 66.9 %collective-permute-start.5 = (f32[16,16384]{1,0:T(8,128)}, f32[16,16384]{1,0:T(8,128)}, u32[]{:S(2)}, u32[]{:S(2)}) collective-permute-start(f32[16,16384]{1,0:T(8,128)} %copy-done.23), channel_id=1, source_target_pairs={{0,3},{1,0},{2,1},{3,2},{4,7},{5,4},{6,5},{7,6},{8,11},{9,8},{10,9... | collective-permute-start | bytes 3145736 | tf_op jit(solution)/shard_map/ppermute | solution.py:337
  33.5 44.3 %collective-permute-start.3 = (s32[264,128]{1,0:T(8,128)S(1)}, s32[264,128]{1,0:T(8,128)S(1)}, u32[]{:S(2)}, u32[]{:S(2)}) collective-permute-start(s32[264,128]{1,0:T(8,128)S(1)} %concatenate.6.refs_0_), channel_id=1, source_target_pairs={{0,3},{1,0},{2,1},{3,2},{4,7},{5,4},{6,5},{7,6},{8,11},{9,8},{10,9... | collective-permute-start | bytes 405512 | tf_op jit(solution)/shard_map/ppermute | solution.py:337
  36.3 41.4 %collective-permute-start.2 = (s32[264,128]{1,0:T(8,128)S(1)}, s32[264,128]{1,0:T(8,128)S(1)}, u32[]{:S(2)}, u32[]{:S(2)}) collective-permute-start(s32[264,128]{1,0:T(8,128)S(1)} %concatenate.6.refs_0_), channel_id=1, source_target_pairs={{0,2},{1,3},{2,0},{3,1},{4,6},{5,7},{6,4},{7,5},{8,10},{9,11},{10,... | collective-permute-start | bytes 405512 | tf_op jit(solution)/shard_map/ppermute | solution.py:337
  59.2 18.5 %collective-permute-start.1 = (s32[264,128]{1,0:T(8,128)S(1)}, s32[264,128]{1,0:T(8,128)}, u32[]{:S(2)}, u32[]{:S(2)}) collective-permute-start(s32[264,128]{1,0:T(8,128)S(1)} %concatenate.6.refs_0_), channel_id=1, source_target_pairs={{0,1},{1,2},{2,3},{3,0},{4,5},{5,6},{6,7},{7,4},{8,9},{9,10},{10,1... | collective-permute-start | bytes 405512 | tf_op jit(solution)/shard_map/ppermute | solution.py:337
  63.2 32.0 %copy-start.19 = (s32[4,128]{1,0:T(4,128)}, s32[4,128]{1,0:T(4,128)S(1)}, u32[]{:S(2)}) copy-start(s32[4,128]{1,0:T(4,128)S(1)} %constant_dynamic-slice_fusion.2.classes) | copy-start | bytes 6148
  82.2 21.4 %all-to-all-start.1 = ((f32[128,4,128]{2,1,0:T(4,128)}), f32[128,4,128]{2,1,0:T(4,128)}, u32[]{:S(2)}, u32[]{:S(2)}) async-start(f32[128,4,128]{2,1,0:T(4,128)} %copy-done.11), calls=%async_computation.1 | async-start | bytes 524288 | tf_op jit(solution)/shard_map/all_to_all | solution.py:334
  102.3 1.3 copy-start.6
  122.2 38.8 %copy-start.20 = (s32[4,128]{1,0:T(4,128)S(1)}, s32[4,128]{1,0:T(4,128)}, u32[]{:S(2)}) copy-start(s32[4,128]{1,0:T(4,128)} %copy-done.19) | copy-start | bytes 6148
  122.2 38.8 %copy-start.22 = (f32[8]{0:T(128)S(1)}, f32[8]{0:T(128)}, u32[]{:S(2)}) copy-start(f32[8]{0:T(128)} %levels.7) | copy-start | bytes 100
  161.0 16.5 %copy-start.2 = (f32[16,16384]{1,0:T(8,128)S(1)}, f32[16,16384]{1,0:T(8,128)}, u32[]{:S(2)}) copy-start(f32[16,16384]{1,0:T(8,128)} %copy-done.1) | copy-start | bytes 3145732
  161.0 16.5 %copy-start.3 = (f32[8,16384]{1,0:T(8,128)S(1)}, f32[8,16384]{1,0:T(8,128)}, u32[]{:S(2)}) copy-start(f32[8,16384]{1,0:T(8,128)} %constant_dynamic-slice_fusion.refs_7_) | copy-start | bytes 1572868
  264.2 34.9 %copy-start.5 = (f32[128,8,512]{2,1,0:T(8,128)}, f32[128,8,512]{2,1,0:T(8,128)S(1)}, u32[]{:S(2)}) copy-start(f32[128,8,512]{2,1,0:T(8,128)S(1)} %get-tuple-element.74.refs_4_) | copy-start | bytes 6291460
  264.2 34.9 %copy-start.12 = (f32[8,16384]{1,0:T(8,128)}, f32[8,16384]{1,0:T(8,128)S(1)}, u32[]{:S(2)}) copy-start(f32[8,16384]{1,0:T(8,128)S(1)} %get-tuple-element.77.refs_6_) | copy-start | bytes 1572868
  264.2 34.9 %copy-start.13 = (f32[8,16384]{1,0:T(8,128)}, f32[8,16384]{1,0:T(8,128)S(1)}, u32[]{:S(2)}) copy-start(f32[8,16384]{1,0:T(8,128)S(1)} %get-tuple-element.78.refs_8_) | copy-start | bytes 1572868
  264.2 34.9 %copy-start.14 = (f32[8,16384]{1,0:T(8,128)}, f32[8,16384]{1,0:T(8,128)S(1)}, u32[]{:S(2)}) copy-start(f32[8,16384]{1,0:T(8,128)S(1)} %get-tuple-element.79.refs_9_) | copy-start | bytes 1572868
  264.2 34.9 %copy-start.15 = (f32[8,16384]{1,0:T(8,128)}, f32[8,16384]{1,0:T(8,128)S(1)}, u32[]{:S(2)}) copy-start(f32[8,16384]{1,0:T(8,128)S(1)} %get-tuple-element.80.refs_10_) | copy-start | bytes 1572868
  317.1 39.1 %all-to-all-start.7 = ((f32[32,32,512]{2,1,0:T(8,128)}), f32[32,32,512]{2,1,0:T(8,128)}, u32[]{:S(2)}, u32[]{:S(2)}) async-start(f32[32,32,512]{2,1,0:T(8,128)} %bitcast.11), calls=%async_computation.7 | async-start | bytes 4194304 | tf_op jit(solution)/shard_map/all_to_all | solution.py:334
  337.6 14.0 %collective-permute-start.7 = (f32[8,16384]{1,0:T(8,128)S(1)}, f32[8,16384]{1,0:T(8,128)S(1)}, u32[]{:S(2)}, u32[]{:S(2)}) collective-permute-start(f32[8,16384]{1,0:T(8,128)S(1)} %step.7.refs_0_), channel_id=1, source_target_pairs={{0,3},{1,0},{2,1},{3,2},{4,7},{5,4},{6,5},{7,6},{8,11},{9,8},{10,9... | collective-permute-start | bytes 1572872 | tf_op jit(solution)/shard_map/ppermute | solution.py:337
  338.8 15.9 %collective-permute-start.6 = (f32[8,16384]{1,0:T(8,128)S(1)}, f32[8,16384]{1,0:T(8,128)S(1)}, u32[]{:S(2)}, u32[]{:S(2)}) collective-permute-start(f32[8,16384]{1,0:T(8,128)S(1)} %step.7.refs_0_), channel_id=1, source_target_pairs={{0,1},{1,2},{2,3},{3,0},{4,5},{5,6},{6,7},{7,4},{8,9},{9,10},{10,1... | collective-permute-start | bytes 1572872 | tf_op jit(solution)/shard_map/ppermute | solution.py:337
  352.3 7.7 %collective-permute-start.9 = (f32[8,8192]{1,0:T(8,128)}, f32[8,8192]{1,0:T(8,128)S(1)}, u32[]{:S(2)}, u32[]{:S(2)}) collective-permute-start(f32[8,8192]{1,0:T(8,128)} %slice.25), channel_id=1, source_target_pairs={{0,3},{1,0},{2,1},{3,2},{4,7},{5,4},{6,5},{7,6},{8,11},{9,8},{10,9... | collective-permute-start | bytes 786440 | tf_op jit(solution)/shard_map/ppermute | solution.py:337
  356.2 8.8 %collective-permute-start.8 = (f32[8,8192]{1,0:T(8,128)}, f32[8,8192]{1,0:T(8,128)}, u32[]{:S(2)}, u32[]{:S(2)}) collective-permute-start(f32[8,8192]{1,0:T(8,128)} %slice.24), channel_id=1, source_target_pairs={{0,1},{1,2},{2,3},{3,0},{4,5},{5,6},{6,7},{7,4},{8,9},{9,10},{10,1... | collective-permute-start | bytes 786440 | tf_op jit(solution)/shard_map/ppermute | solution.py:337
  356.2 8.8 %copy-start.10 = (f32[8,16384]{1,0:T(8,128)S(1)}, f32[8,16384]{1,0:T(8,128)}, u32[]{:S(2)}) copy-start(f32[8,16384]{1,0:T(8,128)} %copy-done.9) | copy-start | bytes 1572868
  (10 other events, 9.0 us)

commit v5 on v4

--- a/solution.py
+++ b/solution.py
@@ -36,6 +36,11 @@
 
 def node_slice(block):
     return pl.ds(pl.multiple_of(block * BLOCK, BLOCK), BLOCK)
+
+
+def rows_at(view, where):
+    ref, start = view
+    return ref[start : start + 8, where]
 
 
 def arc_slice(start, piece):
@@ -64,7 +69,15 @@
 
 
 def gather_kernel(part, blocks, *refs):
-    fill_trial(part, blocks, refs[:4], refs[4], refs[5:9], refs[5:9], refs[9])
+    fill_trial(part, blocks, refs[:4], refs[4], flow_views(refs[5:10]), cost_views(refs[5:10]), refs[10])
+
+
+def flow_views(pairs):
+    return [(pairs[0], 0), (pairs[1], 0), (pairs[2], 0), (pairs[4], 0)]
+
+
+def cost_views(pairs):
+    return [(pairs[0], 8), (pairs[1], 8), (pairs[3], 0), (pairs[4], 8)]
 
 
 def fill_trial(part, blocks, locals_, price, flow, cost, trial):
@@ -82,9 +95,9 @@
                     at_head = jnp.take_along_axis(price[:, node_slice(blocks[2 * k, j])], head, axis=1)
                     at_tail = jnp.take_along_axis(price[:, node_slice(blocks[2 * k + 1, j])], tail, axis=1)
                     where = arc_slice(start, q)
-                    trial[owner * SHARDS + shard, :, q * BLOCK : (q + 1) * BLOCK] = flow[k][
-                        :8, where
-                    ] - step_primal * (cost[k][8:, where] - (at_head - at_tail))
+                    trial[owner * SHARDS + shard, :, q * BLOCK : (q + 1) * BLOCK] = rows_at(
+                        flow[k], where
+                    ) - step_primal * (rows_at(cost[k], where) - (at_head - at_tail))
             return carry
 
         lax.fori_loop(0, OWNERS // UNROLL, step, 0)
@@ -136,13 +149,17 @@
 
 
 def step_kernel(part, blocks, *refs, first, last):
-    locals_, trial, theta, price, demand, flow = refs[:4], refs[4], refs[5], refs[6], refs[7], refs[8:12]
-    balance = refs[-1]
+    locals_, trial, theta, price, demand = refs[:4], refs[4], refs[5], refs[6], refs[7]
+    balance, rest = refs[-1], refs[8:-1]
+    if first:
+        flow, cost, rest = flow_views(rest[:5]), cost_views(rest[:5]), rest[5:]
+    else:
+        flow, rest = [(ref, 0) for ref in rest[:SHARDS]], rest[SHARDS:]
+        if not last:
+            cost, rest = cost_views(rest[:5]), rest[5:]
     if last:
-        price_out = refs[12]
-        fresh_out = cost = following = None
+        price_out = rest[0]
     else:
-        cost, rest = (flow, refs[12:]) if first else (refs[12:16], refs[16:])
         following, price_out, fresh_out = rest[0], rest[1], rest[2:6]
     balance[...] = jnp.zeros_like(balance)
     lanes = lax.broadcasted_iota(jnp.int32, (BLOCK, BLOCK), 0).astype(jnp.int16)
@@ -169,7 +186,7 @@
                     )
                     if not last:
                         fresh_out[k][:, where] = fresh
-                    extra = 2.0 * fresh - flow[k][:8, where]
+                    extra = 2.0 * fresh - rows_at(flow[k], where)
                     high = extra.astype(bf16)
                     low = (extra - high.astype(f32)).astype(bf16)
                     both = jnp.concatenate([high, low], axis=0)
@@ -186,32 +203,49 @@
         lax.fori_loop(0, OWNERS // UNROLL, step, 0)
     price_out[...] = price[...] + step_dual * (demand[...] - balance[...])
     if not last:
-        fill_trial(part, blocks, locals_, price_out, fresh_out, cost, following)
+        fill_trial(part, blocks, locals_, price_out, [(ref, 0) for ref in fresh_out], cost, following)
 
 
 def pack_kernel(part, *refs):
-    for k in range(SHARDS):
-        refs[2 * SHARDS + k][:8] = refs[k][...]
-        refs[2 * SHARDS + k][8:] = refs[SHARDS + k][...]
-
-
-def pack(part, flow, cost):
+    flow, cost, ids = refs[:SHARDS], refs[SHARDS : 2 * SHARDS], refs[2 * SHARDS : 2 * SHARDS + 4]
+    own, near, far_flow, far_cost, back, packed = refs[2 * SHARDS + 4 :]
+    for k, out in ((0, own), (1, near), (3, back)):
+        out[:8] = flow[k][...]
+        out[8:] = cost[k][...]
+    far_flow[...] = flow[2][...]
+    far_cost[...] = cost[2][...]
+    packed[:BLOCK] = ids[0][...]
+    packed[BLOCK : 2 * BLOCK] = ids[1][...]
+    packed[2 * BLOCK : 2 * BLOCK + 1] = ids[2][...]
+    packed[2 * BLOCK + 1 : 2 * BLOCK + 2] = ids[3][...]
+    packed[2 * BLOCK + 2 :] = jnp.zeros((6, BLOCK), jnp.int32)
+
+
+def pack(part, flow, cost, ids):
     def rows(k):
         return pl.BlockSpec((8, CHUNK), lambda c, part: ((part[0] + k) & (SHARDS - 1), c))
 
+    def whole(x):
+        return pl.BlockSpec(x.shape, lambda c, part: (0, 0))
+
+    def out(count):
+        return pl.BlockSpec((count, CHUNK), lambda c, part: (0, c))
+
     width = OWNERS * OWN
+    counts = [16, 16, 8, 8, 16]
+    packed = jax.ShapeDtypeStruct((2 * BLOCK + 8, BLOCK), jnp.int32)
     return pl.pallas_call(
         pack_kernel,
         grid_spec=pltpu.PrefetchScalarGridSpec(
             num_scalar_prefetch=1,
             grid=(width // CHUNK,),
-            in_specs=[rows(k) for k in range(SHARDS)] * 2,
-            out_specs=[pl.BlockSpec((16, CHUNK), lambda c, part: (0, c))] * SHARDS,
+            in_specs=[rows(k) for k in range(SHARDS)] * 2 + [whole(x) for x in ids],
+            out_specs=[out(count) for count in counts] + [whole(packed)],
         ),
-        out_shape=[jax.ShapeDtypeStruct((16, width), f32)] * SHARDS,
+        out_shape=[jax.ShapeDtypeStruct((count, width), f32) for count in counts] + [packed],
         compiler_params=params(12),
         name="pack",
-    )(part, *in_hbm([flow] * SHARDS + [cost] * SHARDS))
+    )(part, *in_hbm([flow] * SHARDS + [cost] * SHARDS + ids))
 
 
 def own_trial(head_block, tail_block, head_local, tail_local, price, flow, cost):
@@ -238,7 +272,7 @@
 def gather(part, blocks, locals_, price, flow_cost):
     return pl.pallas_call(
         gather_kernel,
-        in_specs=[smem, smem] + [vmem] * 9,
+        in_specs=[smem, smem] + [vmem] * 10,
         out_specs=vmem,
         out_shape=jax.ShapeDtypeStruct((OWNERS * SHARDS, 8, OWN), f32),
         compiler_params=params(12),
@@ -285,24 +319,23 @@
     return (None, out[0], None) if last else (out[0], out[1], out[2:])
 
 
-def assemble_kernel(part, *refs):
-    near, left, right, far_left, far_right, out = refs
+def assemble_kernel(part, near, *refs):
+    halves, out = refs[:-1], refs[-1]
     half = NODES // 2
 
     def rows(k):
         return pl.ds(pl.multiple_of(((part[0] - k) & (SHARDS - 1)) * 8, 8), 8)
 
     out[rows(0), :] = near[...]
-    out[rows(1), :] = left[...]
-    out[rows(3), :] = right[...]
-    out[rows(2), :half] = far_left[...]
-    out[rows(2), half:] = far_right[...]
+    for i, k in enumerate((1, 3, 2)):
+        out[rows(k), :half] = halves[2 * i][...]
+        out[rows(k), half:] = halves[2 * i + 1][...]
 
 
 def assemble(part, *pieces):
     return pl.pallas_call(
         assemble_kernel,
-        in_specs=[smem] + [vmem] * 5,
+        in_specs=[smem] + [vmem] * len(pieces),
         out_specs=vmem,
         out_shape=jax.ShapeDtypeStruct((SHARDS * 8, NODES), f32),
         compiler_params=params(8),
@@ -340,26 +373,22 @@
         return lax.dynamic_slice(values, (((part + k) & (SHARDS - 1)) * 8, 0), (8, values.shape[1]))
 
     own = part.astype(jnp.int32).reshape(1)
-    pairs = pack(own, flow_start, cost)
-    pairs, flow_start, cost, price_start = lax.optimization_barrier((pairs, flow_start, cost, price_start))
-    flow_cost = [pairs[0]] + [around(pairs[k], k) for k in (1, 3, 2)]
-    flow_cost = [flow_cost[0], flow_cost[1], flow_cost[3], flow_cost[2]]
+    ids = [head_rows, tail_rows, head_block.reshape(1, BLOCK), tail_block.reshape(1, BLOCK)]
+    pieces = pack(own, flow_start, cost, ids)
+    pieces, flow_start, cost, price_start = lax.optimization_barrier((pieces, flow_start, cost, price_start))
+    here, near, far_flow, far_cost, behind, packed = pieces
+    far_flow = around(far_flow, 1)
+    far_cost = around(far_cost, 3)
+    near = around(near, 1)
+    behind = around(behind, 3)
     first = own_trial(head_block, tail_block, head_rows, tail_rows, price_start, flow_start, cost)
     values = exchange(first, "com").reshape(OWNERS * SHARDS, 8, OWN)
-
-    packed = jnp.concatenate(
-        [
-            head_rows,
-            tail_rows,
-            head_block.reshape(1, BLOCK),
-            tail_block.reshape(1, BLOCK),
-            jnp.zeros((6, BLOCK), jnp.int32),
-        ],
-        axis=0,
-    )
-    flow_cost[1], packed = lax.optimization_barrier((flow_cost[1], packed))
+    far_flow, far_cost, packed = lax.optimization_barrier((far_flow, far_cost, packed))
+    far_flow = around(far_flow, 1)
+    far_cost = around(far_cost, 3)
     locals_ = [packed] + [around(packed, k) for k in range(1, SHARDS)]
-    values, locals_, flow_cost[1] = lax.optimization_barrier((values, locals_, flow_cost[1]))
+    flow_cost = [here, near, far_flow, far_cost, behind]
+    values, near = lax.optimization_barrier((values, near))
     block_ids = jnp.concatenate([x[2 * blocks : 2 * blocks + 2] for x in locals_], axis=0)
     price = rows_of(price_start, 0)
     wanted = rows_of(demand, 0)
@@ -376,13 +405,13 @@
         trial, price, flow = advance(own, block_ids, locals_, trial, theta, flow, price, wanted, flow_cost, step == 0, last)
     back = exchange(kept[0].reshape(OWNERS, com_rows, OWN), "com")
     out = back.transpose(1, 0, 2).reshape(com_rows, arc_cols)
-    left = around(price, 1)
-    right = around(price, 3)
     half = NODES // 2
-    far_left = around(left[:, :half], 1)
-    far_right = around(right[:, half:], 3)
+    west, east = price[:, :half], price[:, half:]
+    left_west, right_east = around(west, 1), around(east, 3)
+    left_east, right_west = around(east, 1), around(west, 3)
+    far_west, far_east = around(left_west, 1), around(right_east, 3)
     out, price = lax.optimization_barrier((out, price))
-    return out, assemble(own, price, left, right, far_left, far_right)
+    return out, assemble(own, price, left_west, left_east, right_west, right_east, far_west, far_east)
 
 
 def solution(mesh):

time: 369 us -> 356 us (0.965)
  starting transfers between devices: 64.1 us -> 44.7 us
  waiting for transfers between devices: 35.4 us -> 45 us
    ppermute x10 -> x15, starting transfers between devices: 38.2 us -> 20.5 us  [around(): lax.ppermute(values, 'arc', [(i, (i + k) % SHARDS) for i in range(SHARDS)])]
    ppermute x10 -> x15, waiting for transfers between devices: 35.4 us -> 45 us  [around(): lax.ppermute(values, 'arc', [(i, (i + k) % SHARDS) for i in range(SHARDS)])]
    unnamed x58 -> x46, local copies, waits for them, and re-layouts: 11.7 us -> 9.95 us
  transfers between devices with their start and end apart: 13 -> 18, of which waited for: 5 -> 6; matrix products, arithmetic and copies ran while one was open for 2% -> 2% of each run, Pallas kernels for 8% -> 9%
where the time goes in v5:
time: 356 us; the launch traced here: 355 us
  blocking collectives  151 us (42%)
  Pallas kernels  95.6 us (27%)
  waiting for transfers between devices  45 us (13%)
  starting transfers between devices  44.7 us (13%)
  local copies, waits for them, and re-layouts  18 us (5%)
    all_to_all x6, blocking collectives, exchange(): return lax.all_to_all(values, axes, split_axis=0, concat_axis=0, tiled=True)  151 us
    pallas_call x4, Pallas kernels, advance(): pl.pallas_call(functools.partial(step_kernel, first=first, last=last), in...  66.6 us
    ppermute x15, waiting for transfers between devices, around(): lax.ppermute(values, 'arc', [(i, (i + k) % SHARDS) for i in range(SHARDS)])  45 us
    all_to_all x3, starting transfers between devices, exchange(): return lax.all_to_all(values, axes, split_axis=0, concat_axis=0, tiled=True)  24.2 us
    ppermute x15, starting transfers between devices, around(): lax.ppermute(values, 'arc', [(i, (i + k) % SHARDS) for i in range(SHARDS)])  20.5 us
    unnamed x46, local copies, waits for them, and re-layouts  9.95 us
    pallas_call x4, Pallas kernels, project(): pl.pallas_call(project_kernel, in_specs=[smem, vmem, vmem], out_specs=[vm...  9.5 us
    pallas_call x1, Pallas kernels, own_trial(): pl.pallas_call(own_trial_kernel, grid=(SHARDS, OWNERS * OWN // CHUNK), in...  7.68 us
  transfers between devices with their start and end apart: 18, of which 6 were waited for; matrix products, arithmetic and copies ran while one was open for 2% of the time, Pallas kernels for 9%

profile of v5, /device:TPU:6, one launch (start us, length us, event | category | flops | bytes accessed | tf_op | source)
XLA Modules:
  0.0 355.0 jit_solution(6623379224794776739)
XLA Ops:
  0.6 3.4 pack.1
  7.9 2.1 collective-permute-start.1
  10.1 7.7 %own_trial.1 = f32[32,32,512]{2,1,0:T(8,128)S(1)} custom-call(s32[128]{0:T(128)} %head_block.1, s32[128]{0:T(128)} %tail_block.1, s32[128,128]{1,0:T(8,128)} %bitcast.14, s32[128,128]{1,0:T(8,128)} %bitcast.16, f32[32,16384]{1,0:T(8,128)} %price, f32[32,16384]{1,0:T(8,128)} %flow, f32[32,16384]{1,0:T(8,128)} %cost), custom_call_target="tpu_custom_call" | custom-call | tf_op jit(solution)/shard_map/own_trial/pallas_call | solution.py:253
  19.1 7.7 %all-to-all-start = ((f32[32,32,512]{2,1,0:T(8,128)}), f32[32,32,512]{2,1,0:T(8,128)}, u32[]{:S(2)}, u32[]{:S(2)}) async-start(f32[32,32,512]{2,1,0:T(8,128)} %copy-done.4), calls=%async_computation | async-start | bytes 4194304 | tf_op jit(solution)/shard_map/all_to_all | solution.py:367
  26.8 3.2 collective-permute-start.8
  34.7 22.2 %collective-permute-done.5.refs_6_.refs_9_.refs_13_ = f32[16,16384]{1,0:T(8,128)} collective-permute-done((f32[16,16384]{1,0:T(8,128)}, f32[16,16384]{1,0:T(8,128)}, u32[]{:S(2)}, u32[]{:S(2)}) %collective-permute-start.5) | collective-permute-done | bytes 1048608 | tf_op jit(solution)/shard_map/ppermute | solution.py:370
  57.6 3.1 project.4
  61.4 9.9 %all-to-all-start.1 = ((f32[128,4,128]{2,1,0:T(4,128)}), f32[128,4,128]{2,1,0:T(4,128)}, u32[]{:S(2)}, u32[]{:S(2)}) async-start(f32[128,4,128]{2,1,0:T(4,128)} %copy-done.11), calls=%async_computation.1 | async-start | bytes 524288 | tf_op jit(solution)/shard_map/all_to_all | solution.py:367
  71.4 3.5 collective-permute-start.7
  76.4 11.5 %collective-permute-done.7.refs_8_.refs_11_.refs_15_ = f32[8,16384]{1,0:T(8,128)S(1)} collective-permute-done((f32[8,16384]{1,0:T(8,128)}, f32[8,16384]{1,0:T(8,128)S(1)}, u32[]{:S(2)}, u32[]{:S(2)}) %collective-permute-start.7) | collective-permute-done | bytes 524320 | tf_op jit(solution)/shard_map/ppermute | solution.py:370
  89.0 5.8 %trial.1.refs_4_ = f32[128,8,512]{2,1,0:T(8,128)S(1)} custom-call(s32[1]{0:T(128)} %bitcast.1.part, s32[8,128]{1,0:T(8,128)S(1)} %pad_add_fusion.blocks, s32[264,128]{1,0:T(8,128)S(1)} %get-tuple-element.52.refs_0_, s32[264,128]{1,0:T(8,128)} %collective-permute-done.2.refs_1_, s32[264,128]{1,0:T(8,128)S(1)} %collective-permute-done.3.refs_2_, ...), custom_call_target="tpu_custom_call" | custom-call | tf_op jit(solution)/shard_map/trial/pallas_call | solution.py:273
  96.9 18.6 %step.4 = (f32[128,8,512]{2,1,0:T(8,128)S(1)}, f32[8,16384]{1,0:T(8,128)S(1)}, f32[8,16384]{1,0:T(8,128)S(1)}, f32[8,16384]{1,0:T(8,128)S(1)}, f32[8,16384]{1,0:T(8,128)S(1)}, /*index=5*/f32[8,16384]{1,0:T(8,128)S(1)}) custom-call(s32[1]{0:T(128)} %bitcast.1.part, s32[8,128]{1,0:T(8,128)S(1)} %pad_add_fusion.blocks, ...), custom_call_target="tpu_custom_call" | custom-call | flops 536870912 | bytes 40000000 | tf_op jit(solution)/shard_map/step/pallas_call | solution.py:309
  115.5 37.8 %all_to_all.45.values = f32[128,8,512]{2,1,0:T(8,128)S(1)} all-to-all(f32[128,8,512]{2,1,0:T(8,128)S(1)} %get-tuple-element.62.refs_4_), channel_id=1, replica_groups=mesh['com'=32,'arc'=4] {'com','arc'}, dimensions={0} | all-to-all | bytes 4194304 | tf_op jit(solution)/shard_map/all_to_all | solution.py:367
  153.3 2.1 project.5
  155.3 14.4 %all_to_all.46.refs_5_ = f32[128,4,128]{2,1,0:T(4,128)S(1)} all-to-all(f32[128,4,128]{2,1,0:T(4,128)S(1)} %project.5), channel_id=1, replica_groups=mesh['com'=32,'arc'=4] {'com','arc'}, dimensions={0} | all-to-all | bytes 524288 | tf_op jit(solution)/shard_map/all_to_all | solution.py:367
  169.8 17.1 %step.5 = (f32[128,8,512]{2,1,0:T(8,128)S(1)}, f32[8,16384]{1,0:T(8,128)S(1)}, f32[8,16384]{1,0:T(8,128)S(1)}, f32[8,16384]{1,0:T(8,128)S(1)}, f32[8,16384]{1,0:T(8,128)S(1)}, /*index=5*/f32[8,16384]{1,0:T(8,128)S(1)}) custom-call(s32[1]{0:T(128)} %bitcast.1.part, s32[8,128]{1,0:T(8,128)S(1)} %pad_add_fusion.blocks, ...), custom_call_target="tpu_custom_call" | custom-call | flops 536870912 | bytes 40000000 | tf_op jit(solution)/shard_map/step/pallas_call | solution.py:309
  186.9 34.9 %all_to_all.47.values = f32[128,8,512]{2,1,0:T(8,128)S(1)} all-to-all(f32[128,8,512]{2,1,0:T(8,128)S(1)} %get-tuple-element.68.refs_4_), channel_id=1, replica_groups=mesh['com'=32,'arc'=4] {'com','arc'}, dimensions={0} | all-to-all | bytes 4194304 | tf_op jit(solution)/shard_map/all_to_all | solution.py:367
  223.8 14.4 %all_to_all.48.refs_5_ = f32[128,4,128]{2,1,0:T(4,128)S(1)} all-to-all(f32[128,4,128]{2,1,0:T(4,128)S(1)} %project.6), channel_id=1, replica_groups=mesh['com'=32,'arc'=4] {'com','arc'}, dimensions={0} | all-to-all | bytes 524288 | tf_op jit(solution)/shard_map/all_to_all | solution.py:367
  238.3 17.1 %step.6 = (f32[128,8,512]{2,1,0:T(8,128)S(1)}, f32[8,16384]{1,0:T(8,128)S(1)}, f32[8,16384]{1,0:T(8,128)S(1)}, f32[8,16384]{1,0:T(8,128)S(1)}, f32[8,16384]{1,0:T(8,128)S(1)}, /*index=5*/f32[8,16384]{1,0:T(8,128)S(1)}) custom-call(s32[1]{0:T(128)} %bitcast.1.part, s32[8,128]{1,0:T(8,128)S(1)} %pad_add_fusion.blocks, ...), custom_call_target="tpu_custom_call" | custom-call | flops 536870912 | bytes 40000000 | tf_op jit(solution)/shard_map/step/pallas_call | solution.py:309
  256.2 34.9 %all_to_all.49.values = f32[128,8,512]{2,1,0:T(8,128)S(1)} all-to-all(f32[128,8,512]{2,1,0:T(8,128)S(1)} %get-tuple-element.74.refs_4_), channel_id=1, replica_groups=mesh['com'=32,'arc'=4] {'com','arc'}, dimensions={0} | all-to-all | bytes 4194304 | tf_op jit(solution)/shard_map/all_to_all | solution.py:367
  291.1 2.3 project.7
  294.7 14.4 %all_to_all.50.refs_5_ = f32[128,4,128]{2,1,0:T(4,128)S(1)} all-to-all(f32[128,4,128]{2,1,0:T(4,128)S(1)} %get-tuple-element.76), channel_id=1, replica_groups=mesh['com'=32,'arc'=4] {'com','arc'}, dimensions={0} | all-to-all | bytes 524288 | tf_op jit(solution)/shard_map/all_to_all | solution.py:367
  309.1 6.6 %all-to-all-start.7 = ((f32[32,32,512]{2,1,0:T(8,128)}), f32[32,32,512]{2,1,0:T(8,128)}, u32[]{:S(2)}, u32[]{:S(2)}) async-start(f32[32,32,512]{2,1,0:T(8,128)} %bitcast.11), calls=%async_computation.7 | async-start | bytes 4194304 | tf_op jit(solution)/shard_map/all_to_all | solution.py:367
  315.7 13.8 %step.7.near = f32[8,16384]{1,0:T(8,128)S(1)} custom-call(s32[1]{0:T(128)} %bitcast.1.part, s32[8,128]{1,0:T(8,128)S(1)} %pad_add_fusion.blocks, s32[264,128]{1,0:T(8,128)S(1)} %get-tuple-element.52.refs_0_, s32[264,128]{1,0:T(8,128)} %collective-permute-done.2.refs_1_, s32[264,128]{1,0:T(8,128)S(1)} %collective-permute-done.3.refs_2_, ...), custom_call_target="tpu_custom_call" | custom-call | flops 536870912 | bytes 40000000 | tf_op jit(solution)/shard_map/step/pallas_call | solution.py:309
  333.3 2.4 collective-permute-start.11
  335.7 4.1 %collective-permute-done.12.refs_3_ = f32[8,8192]{1,0:T(8,128)S(1)} collective-permute-done((f32[8,8192]{1,0:T(8,128)}, f32[8,8192]{1,0:T(8,128)S(1)}, u32[]{:S(2)}, u32[]{:S(2)}) %collective-permute-start.12) | collective-permute-done | bytes 262176 | tf_op jit(solution)/shard_map/ppermute | solution.py:370
  339.8 2.4 collective-permute-start.14
  342.2 3.1 copy.13
  345.3 2.5 collective-permute-done.10.refs_1_
  347.8 2.5 collective-permute-done.14.refs_5_
  350.3 2.1 collective-permute-done.13.refs_4_
  352.4 2.6 assemble.1
  (78 shorter events, 24.0 us)
Async XLA Ops:
  0.6 74.2 %copy-start = (f32[32,16384]{1,0:T(8,128)S(1)}, f32[32,16384]{1,0:T(8,128)}, u32[]{:S(2)}) copy-start(f32[32,16384]{1,0:T(8,128)} %param.13) | copy-start | bytes 6291460
  6.0 81.9 %copy-start.1 = (f32[16,16384]{1,0:T(8,128)}, f32[16,16384]{1,0:T(8,128)S(1)}, u32[]{:S(2)}) copy-start(f32[16,16384]{1,0:T(8,128)S(1)} %get-tuple-element.54.refs_5_.refs_8_.refs_12_) | copy-start | bytes 3145732
  6.0 24.0 %collective-permute-start = (f32[8,16384]{1,0:T(8,128)}, f32[8,16384]{1,0:T(8,128)}, u32[]{:S(2)}, u32[]{:S(2)}) collective-permute-start(f32[8,16384]{1,0:T(8,128)} %get-tuple-element.49), channel_id=1, source_target_pairs={{0,1},{1,2},{2,3},{3,0},{4,5},{5,6},{6,7},{7,4},{8,9},{9,10},{10,1... | collective-permute-start | bytes 1572872 | tf_op jit(solution)/shard_map/ppermute | solution.py:370
  7.9 22.1 %collective-permute-start.1 = (f32[8,16384]{1,0:T(8,128)}, f32[8,16384]{1,0:T(8,128)}, u32[]{:S(2)}, u32[]{:S(2)}) collective-permute-start(f32[8,16384]{1,0:T(8,128)} %get-tuple-element.50), channel_id=1, source_target_pairs={{0,3},{1,0},{2,1},{3,2},{4,7},{5,4},{6,5},{7,6},{8,11},{9,8},{10,9... | collective-permute-start | bytes 1572872 | tf_op jit(solution)/shard_map/ppermute | solution.py:370
  19.1 37.9 %all-to-all-start = ((f32[32,32,512]{2,1,0:T(8,128)}), f32[32,32,512]{2,1,0:T(8,128)}, u32[]{:S(2)}, u32[]{:S(2)}) async-start(f32[32,32,512]{2,1,0:T(8,128)} %copy-done.4), calls=%async_computation | async-start | bytes 4194304 | tf_op jit(solution)/shard_map/all_to_all | solution.py:367
  26.7 30.2 %collective-permute-start.5 = (f32[16,16384]{1,0:T(8,128)}, f32[16,16384]{1,0:T(8,128)}, u32[]{:S(2)}, u32[]{:S(2)}) collective-permute-start(f32[16,16384]{1,0:T(8,128)} %copy-done.22), channel_id=1, source_target_pairs={{0,1},{1,2},{2,3},{3,0},{4,5},{5,6},{6,7},{7,4},{8,9},{9,10},{10,1... | collective-permute-start | bytes 3145736 | tf_op jit(solution)/shard_map/ppermute | solution.py:370
  26.8 61.1 %collective-permute-start.8 = (f32[16,16384]{1,0:T(8,128)}, f32[16,16384]{1,0:T(8,128)}, u32[]{:S(2)}, u32[]{:S(2)}) collective-permute-start(f32[16,16384]{1,0:T(8,128)} %copy-done.21), channel_id=1, source_target_pairs={{0,3},{1,0},{2,1},{3,2},{4,7},{5,4},{6,5},{7,6},{8,11},{9,8},{10,9... | collective-permute-start | bytes 3145736 | tf_op jit(solution)/shard_map/ppermute | solution.py:370
  30.0 41.3 %collective-permute-start.4 = (s32[264,128]{1,0:T(8,128)S(1)}, s32[264,128]{1,0:T(8,128)S(1)}, u32[]{:S(2)}, u32[]{:S(2)}) collective-permute-start(s32[264,128]{1,0:T(8,128)S(1)} %get-tuple-element.52.refs_0_), channel_id=1, source_target_pairs={{0,3},{1,0},{2,1},{3,2},{4,7},{5,4},{6,5},{7,6},{8,11},{9,8},{10,9... | collective-permute-start | bytes 405512 | tf_op jit(solution)/shard_map/ppermute | solution.py:370
  33.4 42.2 %copy-start.17 = (s32[4,128]{1,0:T(4,128)}, s32[4,128]{1,0:T(4,128)S(1)}, u32[]{:S(2)}) copy-start(s32[4,128]{1,0:T(4,128)S(1)} %constant_dynamic-slice_fusion.2.classes) | copy-start | bytes 6148
  33.4 42.2 %collective-permute-start.3 = (s32[264,128]{1,0:T(8,128)S(1)}, s32[264,128]{1,0:T(8,128)S(1)}, u32[]{:S(2)}, u32[]{:S(2)}) collective-permute-start(s32[264,128]{1,0:T(8,128)S(1)} %get-tuple-element.52.refs_0_), channel_id=1, source_target_pairs={{0,2},{1,3},{2,0},{3,1},{4,6},{5,7},{6,4},{7,5},{8,10},{9,11},{10,... | collective-permute-start | bytes 405512 | tf_op jit(solution)/shard_map/ppermute | solution.py:370
  33.6 42.1 %collective-permute-start.2 = (s32[264,128]{1,0:T(8,128)S(1)}, s32[264,128]{1,0:T(8,128)}, u32[]{:S(2)}, u32[]{:S(2)}) collective-permute-start(s32[264,128]{1,0:T(8,128)S(1)} %get-tuple-element.52.refs_0_), channel_id=1, source_target_pairs={{0,1},{1,2},{2,3},{3,0},{4,5},{5,6},{6,7},{7,4},{8,9},{9,10},{10,1... | collective-permute-start | bytes 405512 | tf_op jit(solution)/shard_map/ppermute | solution.py:370
  56.9 19.4 %collective-permute-start.6 = (f32[8,16384]{1,0:T(8,128)}, f32[8,16384]{1,0:T(8,128)}, u32[]{:S(2)}, u32[]{:S(2)}) collective-permute-start(f32[8,16384]{1,0:T(8,128)} %collective-permute-done), channel_id=1, source_target_pairs={{0,1},{1,2},{2,3},{3,0},{4,5},{5,6},{6,7},{7,4},{8,9},{9,10},{10,1... | collective-permute-start | bytes 1572872 | tf_op jit(solution)/shard_map/ppermute | solution.py:370
  61.4 35.4 %all-to-all-start.1 = ((f32[128,4,128]{2,1,0:T(4,128)}), f32[128,4,128]{2,1,0:T(4,128)}, u32[]{:S(2)}, u32[]{:S(2)}) async-start(f32[128,4,128]{2,1,0:T(4,128)} %copy-done.11), calls=%async_computation.1 | async-start | bytes 524288 | tf_op jit(solution)/shard_map/all_to_all | solution.py:367
  71.4 16.6 %collective-permute-start.7 = (f32[8,16384]{1,0:T(8,128)}, f32[8,16384]{1,0:T(8,128)S(1)}, u32[]{:S(2)}, u32[]{:S(2)}) collective-permute-start(f32[8,16384]{1,0:T(8,128)} %collective-permute-done.1), channel_id=1, source_target_pairs={{0,3},{1,0},{2,1},{3,2},{4,7},{5,4},{6,5},{7,6},{8,11},{9,8},{10,9... | collective-permute-start | bytes 1572872 | tf_op jit(solution)/shard_map/ppermute | solution.py:370
  94.8 1.3 copy-start.6
  115.5 37.8 %copy-start.18 = (s32[4,128]{1,0:T(4,128)S(1)}, s32[4,128]{1,0:T(4,128)}, u32[]{:S(2)}) copy-start(s32[4,128]{1,0:T(4,128)} %copy-done.17) | copy-start | bytes 6148
  115.5 37.8 %copy-start.20 = (f32[8]{0:T(128)S(1)}, f32[8]{0:T(128)}, u32[]{:S(2)}) copy-start(f32[8]{0:T(128)} %levels.7) | copy-start | bytes 100
  153.3 16.5 %copy-start.2 = (f32[16,16384]{1,0:T(8,128)S(1)}, f32[16,16384]{1,0:T(8,128)}, u32[]{:S(2)}) copy-start(f32[16,16384]{1,0:T(8,128)} %copy-done.1) | copy-start | bytes 3145732
  153.3 16.5 %copy-start.3 = (f32[8,16384]{1,0:T(8,128)S(1)}, f32[8,16384]{1,0:T(8,128)}, u32[]{:S(2)}) copy-start(f32[8,16384]{1,0:T(8,128)} %constant_dynamic-slice_fusion.refs_7_) | copy-start | bytes 1572868
  153.3 16.5 %copy-start.8 = (f32[8,16384]{1,0:T(8,128)S(1)}, f32[8,16384]{1,0:T(8,128)}, u32[]{:S(2)}) copy-start(f32[8,16384]{1,0:T(8,128)} %copy-done.7) | copy-start | bytes 1572868
  256.2 34.9 %copy-start.5 = (f32[128,8,512]{2,1,0:T(8,128)}, f32[128,8,512]{2,1,0:T(8,128)S(1)}, u32[]{:S(2)}) copy-start(f32[128,8,512]{2,1,0:T(8,128)S(1)} %get-tuple-element.74.refs_4_) | copy-start | bytes 6291460
  256.2 34.9 %copy-start.12 = (f32[8,16384]{1,0:T(8,128)}, f32[8,16384]{1,0:T(8,128)S(1)}, u32[]{:S(2)}) copy-start(f32[8,16384]{1,0:T(8,128)S(1)} %get-tuple-element.77.refs_6_) | copy-start | bytes 1572868
  256.2 34.9 %copy-start.13 = (f32[8,16384]{1,0:T(8,128)}, f32[8,16384]{1,0:T(8,128)S(1)}, u32[]{:S(2)}) copy-start(f32[8,16384]{1,0:T(8,128)S(1)} %get-tuple-element.78.refs_8_) | copy-start | bytes 1572868
  256.2 34.9 %copy-start.14 = (f32[8,16384]{1,0:T(8,128)}, f32[8,16384]{1,0:T(8,128)S(1)}, u32[]{:S(2)}) copy-start(f32[8,16384]{1,0:T(8,128)S(1)} %get-tuple-element.79.refs_9_) | copy-start | bytes 1572868
  256.2 34.9 %copy-start.15 = (f32[8,16384]{1,0:T(8,128)}, f32[8,16384]{1,0:T(8,128)S(1)}, u32[]{:S(2)}) copy-start(f32[8,16384]{1,0:T(8,128)S(1)} %get-tuple-element.80.refs_10_) | copy-start | bytes 1572868
  309.1 33.1 %all-to-all-start.7 = ((f32[32,32,512]{2,1,0:T(8,128)}), f32[32,32,512]{2,1,0:T(8,128)}, u32[]{:S(2)}, u32[]{:S(2)}) async-start(f32[32,32,512]{2,1,0:T(8,128)} %bitcast.11), calls=%async_computation.7 | async-start | bytes 4194304 | tf_op jit(solution)/shard_map/all_to_all | solution.py:367
  330.4 9.4 %collective-permute-start.12 = (f32[8,8192]{1,0:T(8,128)}, f32[8,8192]{1,0:T(8,128)S(1)}, u32[]{:S(2)}, u32[]{:S(2)}) collective-permute-start(f32[8,8192]{1,0:T(8,128)} %get-tuple-element.84), channel_id=1, source_target_pairs={{0,3},{1,0},{2,1},{3,2},{4,7},{5,4},{6,5},{7,6},{8,11},{9,8},{10,9... | collective-permute-start | bytes 786440 | tf_op jit(solution)/shard_map/ppermute | solution.py:370
  331.6 10.6 %collective-permute-start.9 = (f32[8,8192]{1,0:T(8,128)}, f32[8,8192]{1,0:T(8,128)S(1)}, u32[]{:S(2)}, u32[]{:S(2)}) collective-permute-start(f32[8,8192]{1,0:T(8,128)} %get-tuple-element.85), channel_id=1, source_target_pairs={{0,1},{1,2},{2,3},{3,0},{4,5},{5,6},{6,7},{7,4},{8,9},{9,10},{10,1... | collective-permute-start | bytes 786440 | tf_op jit(solution)/shard_map/ppermute | solution.py:370
  332.4 15.4 %collective-permute-start.10 = (f32[8,8192]{1,0:T(8,128)}, f32[8,8192]{1,0:T(8,128)S(1)}, u32[]{:S(2)}, u32[]{:S(2)}) collective-permute-start(f32[8,8192]{1,0:T(8,128)} %get-tuple-element.84), channel_id=1, source_target_pairs={{0,1},{1,2},{2,3},{3,0},{4,5},{5,6},{6,7},{7,4},{8,9},{9,10},{10,1... | collective-permute-start | bytes 786440 | tf_op jit(solution)/shard_map/ppermute | solution.py:370
  333.3 14.5 %collective-permute-start.11 = (f32[8,8192]{1,0:T(8,128)}, f32[8,8192]{1,0:T(8,128)}, u32[]{:S(2)}, u32[]{:S(2)}) collective-permute-start(f32[8,8192]{1,0:T(8,128)} %get-tuple-element.85), channel_id=1, source_target_pairs={{0,3},{1,0},{2,1},{3,2},{4,7},{5,4},{6,5},{7,6},{8,11},{9,8},{10,9... | collective-permute-start | bytes 786440 | tf_op jit(solution)/shard_map/ppermute | solution.py:370
  339.8 10.6 %collective-permute-start.14 = (f32[8,8192]{1,0:T(8,128)S(1)}, f32[8,8192]{1,0:T(8,128)}, u32[]{:S(2)}, u32[]{:S(2)}) collective-permute-start(f32[8,8192]{1,0:T(8,128)S(1)} %collective-permute-done.12.refs_3_), channel_id=1, source_target_pairs={{0,3},{1,0},{2,1},{3,2},{4,7},{5,4},{6,5},{7,6},{8,11},{9,8},{10,9... | collective-permute-start | bytes 786440 | tf_op jit(solution)/shard_map/ppermute | solution.py:370
  342.2 10.2 %collective-permute-start.13 = (f32[8,8192]{1,0:T(8,128)S(1)}, f32[8,8192]{1,0:T(8,128)}, u32[]{:S(2)}, u32[]{:S(2)}) collective-permute-start(f32[8,8192]{1,0:T(8,128)S(1)} %collective-permute-done.9.refs_0_), channel_id=1, source_target_pairs={{0,1},{1,2},{2,3},{3,0},{4,5},{5,6},{6,7},{7,4},{8,9},{9,10},{10,1... | collective-permute-start | bytes 786440 | tf_op jit(solution)/shard_map/ppermute | solution.py:370
  (9 other events, 8.6 us)

commit v6 on v5

--- a/solution.py
+++ b/solution.py
@@ -158,7 +158,7 @@
         if not last:
             cost, rest = cost_views(rest[:5]), rest[5:]
     if last:
-        price_out = rest[0]
+        halves = rest
     else:
         following, price_out, fresh_out = rest[0], rest[1], rest[2:6]
     balance[...] = jnp.zeros_like(balance)
@@ -201,8 +201,13 @@
             return carry
 
         lax.fori_loop(0, OWNERS // UNROLL, step, 0)
-    price_out[...] = price[...] + step_dual * (demand[...] - balance[...])
-    if not last:
+    if last:
+        half = NODES // 2
+        for i in range(2):
+            where = slice(i * half, (i + 1) * half)
+            halves[i][...] = price[:, where] + step_dual * (demand[:, where] - balance[:, where])
+    else:
+        price_out[...] = price[...] + step_dual * (demand[...] - balance[...])
         fill_trial(part, blocks, locals_, price_out, [(ref, 0) for ref in fresh_out], cost, following)
 
 
@@ -243,7 +248,7 @@
             out_specs=[out(count) for count in counts] + [whole(packed)],
         ),
         out_shape=[jax.ShapeDtypeStruct((count, width), f32) for count in counts] + [packed],
-        compiler_params=params(12),
+        compiler_params=params(52),
         name="pack",
     )(part, *in_hbm([flow] * SHARDS + [cost] * SHARDS + ids))
 
@@ -264,7 +269,7 @@
         ],
         out_specs=pl.BlockSpec((CHUNK // OWN, 8, OWN), lambda r, c: (c, r, 0)),
         out_shape=jax.ShapeDtypeStruct((OWNERS, SHARDS * 8, OWN), f32),
-        compiler_params=params(8),
+        compiler_params=params(52),
         name="own_trial",
     )(*in_hbm([head_block, tail_block, head_local, tail_local, price, flow, cost]))
 
@@ -302,7 +307,7 @@
     if first or last:
         trial, price, demand, *flow = in_hbm([trial, price, demand, *flow])
     operands = [trial, theta, price, demand] + list(flow) + ([] if first or last else list(flow_cost))
-    shape = [jax.ShapeDtypeStruct((8, NODES), f32)]
+    shape = [jax.ShapeDtypeStruct((8, NODES // 2), f32)] * 2 if last else [jax.ShapeDtypeStruct((8, NODES), f32)]
     if not last:
         shape = [jax.ShapeDtypeStruct(trial.shape, f32)] + shape
         shape = shape + [jax.ShapeDtypeStruct((8, OWNERS * OWN), f32)] * SHARDS
@@ -316,18 +321,17 @@
         cost_estimate=pl.CostEstimate(flops=2 * 16 * 256 * OWNERS * OWN * SHARDS, transcendentals=0, bytes_accessed=COVER),
         name="step",
     )(part, blocks, *locals_, *operands)
-    return (None, out[0], None) if last else (out[0], out[1], out[2:])
-
-
-def assemble_kernel(part, near, *refs):
+    return (None, out, None) if last else (out[0], out[1], out[2:])
+
+
+def assemble_kernel(part, *refs):
     halves, out = refs[:-1], refs[-1]
     half = NODES // 2
 
     def rows(k):
         return pl.ds(pl.multiple_of(((part[0] - k) & (SHARDS - 1)) * 8, 8), 8)
 
-    out[rows(0), :] = near[...]
-    for i, k in enumerate((1, 3, 2)):
+    for i, k in enumerate((0, 1, 3, 2)):
         out[rows(k), :half] = halves[2 * i][...]
         out[rows(k), half:] = halves[2 * i + 1][...]
 
@@ -387,8 +391,8 @@
     far_flow = around(far_flow, 1)
     far_cost = around(far_cost, 3)
     locals_ = [packed] + [around(packed, k) for k in range(1, SHARDS)]
+    values, near, behind, far_flow, far_cost = lax.optimization_barrier((values, near, behind, far_flow, far_cost))
     flow_cost = [here, near, far_flow, far_cost, behind]
-    values, near = lax.optimization_barrier((values, near))
     block_ids = jnp.concatenate([x[2 * blocks : 2 * blocks + 2] for x in locals_], axis=0)
     price = rows_of(price_start, 0)
     wanted = rows_of(demand, 0)
@@ -405,13 +409,12 @@
         trial, price, flow = advance(own, block_ids, locals_, trial, theta, flow, price, wanted, flow_cost, step == 0, last)
     back = exchange(kept[0].reshape(OWNERS, com_rows, OWN), "com")
     out = back.transpose(1, 0, 2).reshape(com_rows, arc_cols)
-    half = NODES // 2
-    west, east = price[:, :half], price[:, half:]
+    west, east = price
     left_west, right_east = around(west, 1), around(east, 3)
     left_east, right_west = around(east, 1), around(west, 3)
     far_west, far_east = around(left_west, 1), around(right_east, 3)
-    out, price = lax.optimization_barrier((out, price))
-    return out, assemble(own, price, left_west, left_east, right_west, right_east, far_west, far_east)
+    out, west = lax.optimization_barrier((out, west))
+    return out, assemble(own, west, east, left_west, left_east, right_west, right_east, far_west, far_east)
 
 
 def solution(mesh):

time: 356 us -> 348 us (0.978)
  waiting for transfers between devices: 45 us -> 38 us
  local copies, waits for them, and re-layouts: 18 us -> 13.3 us
    ppermute x15, waiting for transfers between devices: 45 us -> 38 us  [around(): lax.ppermute(values, 'arc', [(i, (i + k) % SHARDS) for i in range(SHARDS)])]
    unnamed x46 -> x36, local copies, waits for them, and re-layouts: 9.95 us -> 5.93 us
  transfers between devices with their start and end apart: 18 -> 18, of which waited for: 6 -> 3; matrix products, arithmetic and copies ran while one was open for 2% -> 2% of each run, Pallas kernels for 9% -> 9%
where the time goes in v6:
time: 348 us; the launch traced here: 347 us
  blocking collectives  152 us (44%)
  Pallas kernels  97.2 us (28%)
  starting transfers between devices  45.8 us (13%)
  waiting for transfers between devices  38 us (11%)
  local copies, waits for them, and re-layouts  13.3 us (4%)
    all_to_all x6, blocking collectives, exchange(): return lax.all_to_all(values, axes, split_axis=0, concat_axis=0, tiled=True)  152 us
    pallas_call x4, Pallas kernels, advance(): pl.pallas_call(functools.partial(step_kernel, first=first, last=last), in...  66.9 us
    ppermute x15, waiting for transfers between devices, around(): lax.ppermute(values, 'arc', [(i, (i + k) % SHARDS) for i in range(SHARDS)])  38 us
    all_to_all x3, starting transfers between devices, exchange(): return lax.all_to_all(values, axes, split_axis=0, concat_axis=0, tiled=True)  24.9 us
    ppermute x15, starting transfers between devices, around(): lax.ppermute(values, 'arc', [(i, (i + k) % SHARDS) for i in range(SHARDS)])  20.9 us
    pallas_call x4, Pallas kernels, project(): pl.pallas_call(project_kernel, in_specs=[smem, vmem, vmem], out_specs=[vm...  9.5 us
    pallas_call x1, Pallas kernels, own_trial(): pl.pallas_call(own_trial_kernel, grid=(SHARDS, OWNERS * OWN // CHUNK), in...  8.51 us
  transfers between devices with their start and end apart: 18, of which 3 were waited for; matrix products, arithmetic and copies ran while one was open for 2% of the time, Pallas kernels for 9%

profile of v6, /device:TPU:6, one launch (start us, length us, event | category | flops | bytes accessed | tf_op | source)
XLA Modules:
  0.0 346.9 jit_solution(2949719417571175788)
XLA Ops:
  0.6 3.7 %pack.1 = (f32[16,16384]{1,0:T(8,128)}, f32[16,16384]{1,0:T(8,128)}, f32[8,16384]{1,0:T(8,128)S(1)}, f32[8,16384]{1,0:T(8,128)S(1)}, f32[16,16384]{1,0:T(8,128)}, /*index=5*/s32[264,128]{1,0:T(8,128)S(1)}) custom-call(s32[1]{0:T(128)} %bitcast.1.part, f32[32,16384]{1,0:T(8,128)} %flow, f32[32,16384]{1,0:T(8,128)} %flow, f32[32,16384]{1,0:T(8,128)} %flow, ...), custom_call_target="tpu_custom_call" | custom-call | tf_op jit(solution)/shard_map/pack/pallas_call | solution.py:242
  4.4 2.0 collective-permute-start
  6.3 2.2 collective-permute-start.1
  8.5 8.5 %own_trial.1 = f32[32,32,512]{2,1,0:T(8,128)} custom-call(s32[128]{0:T(128)} %head_block.1, s32[128]{0:T(128)} %tail_block.1, s32[128,128]{1,0:T(8,128)} %bitcast.14, s32[128,128]{1,0:T(8,128)} %bitcast.16, f32[32,16384]{1,0:T(8,128)} %price, f32[32,16384]{1,0:T(8,128)} %flow, f32[32,16384]{1,0:T(8,128)} %cost), custom_call_target="tpu_custom_call" | custom-call | tf_op jit(solution)/shard_map/own_trial/pallas_call | solution.py:258
  17.0 7.7 %all-to-all-start = ((f32[32,32,512]{2,1,0:T(8,128)}), f32[32,32,512]{2,1,0:T(8,128)}, u32[]{:S(2)}, u32[]{:S(2)}) async-start(f32[32,32,512]{2,1,0:T(8,128)} %own_trial.1), calls=%async_computation | async-start | bytes 4194304 | tf_op jit(solution)/shard_map/all_to_all | solution.py:371
  24.8 3.2 collective-permute-start.6
  28.0 3.2 collective-permute-start.8
  34.0 28.8 %collective-permute-done.7.refs_7_.refs_10_.refs_14_ = f32[8,16384]{1,0:T(8,128)} collective-permute-done((f32[8,16384]{1,0:T(8,128)}, f32[8,16384]{1,0:T(8,128)}, u32[]{:S(2)}, u32[]{:S(2)}) %collective-permute-start.7) | collective-permute-done | bytes 524320 | tf_op jit(solution)/shard_map/ppermute | solution.py:374
  65.0 3.1 project.4
  68.9 10.6 %all-to-all-start.1 = ((f32[128,4,128]{2,1,0:T(4,128)}), f32[128,4,128]{2,1,0:T(4,128)}, u32[]{:S(2)}, u32[]{:S(2)}) async-start(f32[128,4,128]{2,1,0:T(4,128)} %copy-done.8), calls=%async_computation.1 | async-start | bytes 524288 | tf_op jit(solution)/shard_map/all_to_all | solution.py:371
  82.1 5.9 %trial.1.refs_4_ = f32[128,8,512]{2,1,0:T(8,128)S(1)} custom-call(s32[1]{0:T(128)} %bitcast.1.part, s32[8,128]{1,0:T(8,128)S(1)} %pad_add_fusion.blocks, s32[264,128]{1,0:T(8,128)S(1)} %get-tuple-element.58.refs_0_, s32[264,128]{1,0:T(8,128)} %collective-permute-done.2.refs_1_, s32[264,128]{1,0:T(8,128)S(1)} %collective-permute-done.3.refs_2_, ...), custom_call_target="tpu_custom_call" | custom-call | tf_op jit(solution)/shard_map/trial/pallas_call | solution.py:278
  89.4 18.6 %step.4 = (f32[128,8,512]{2,1,0:T(8,128)S(1)}, f32[8,16384]{1,0:T(8,128)S(1)}, f32[8,16384]{1,0:T(8,128)S(1)}, f32[8,16384]{1,0:T(8,128)S(1)}, f32[8,16384]{1,0:T(8,128)S(1)}, /*index=5*/f32[8,16384]{1,0:T(8,128)S(1)}) custom-call(s32[1]{0:T(128)} %bitcast.1.part, s32[8,128]{1,0:T(8,128)S(1)} %pad_add_fusion.blocks, ...), custom_call_target="tpu_custom_call" | custom-call | flops 536870912 | bytes 40000000 | tf_op jit(solution)/shard_map/step/pallas_call | solution.py:314
  108.0 38.7 %all_to_all.45.values = f32[128,8,512]{2,1,0:T(8,128)S(1)} all-to-all(f32[128,8,512]{2,1,0:T(8,128)S(1)} %get-tuple-element.72.refs_4_), channel_id=1, replica_groups=mesh['com'=32,'arc'=4] {'com','arc'}, dimensions={0} | all-to-all | bytes 4194304 | tf_op jit(solution)/shard_map/all_to_all | solution.py:371
  146.7 2.1 project.5
  148.8 14.4 %all_to_all.46.refs_5_ = f32[128,4,128]{2,1,0:T(4,128)S(1)} all-to-all(f32[128,4,128]{2,1,0:T(4,128)S(1)} %project.5), channel_id=1, replica_groups=mesh['com'=32,'arc'=4] {'com','arc'}, dimensions={0} | all-to-all | bytes 524288 | tf_op jit(solution)/shard_map/all_to_all | solution.py:371
  163.2 17.3 %step.5 = (f32[128,8,512]{2,1,0:T(8,128)S(1)}, f32[8,16384]{1,0:T(8,128)S(1)}, f32[8,16384]{1,0:T(8,128)S(1)}, f32[8,16384]{1,0:T(8,128)S(1)}, f32[8,16384]{1,0:T(8,128)S(1)}, /*index=5*/f32[8,16384]{1,0:T(8,128)S(1)}) custom-call(s32[1]{0:T(128)} %bitcast.1.part, s32[8,128]{1,0:T(8,128)S(1)} %pad_add_fusion.blocks, ...), custom_call_target="tpu_custom_call" | custom-call | flops 536870912 | bytes 40000000 | tf_op jit(solution)/shard_map/step/pallas_call | solution.py:314
  180.5 34.9 %all_to_all.47.values = f32[128,8,512]{2,1,0:T(8,128)S(1)} all-to-all(f32[128,8,512]{2,1,0:T(8,128)S(1)} %get-tuple-element.78.refs_4_), channel_id=1, replica_groups=mesh['com'=32,'arc'=4] {'com','arc'}, dimensions={0} | all-to-all | bytes 4194304 | tf_op jit(solution)/shard_map/all_to_all | solution.py:371
  215.4 2.1 project.6
  217.4 14.4 %all_to_all.48.refs_5_ = f32[128,4,128]{2,1,0:T(4,128)S(1)} all-to-all(f32[128,4,128]{2,1,0:T(4,128)S(1)} %project.6), channel_id=1, replica_groups=mesh['com'=32,'arc'=4] {'com','arc'}, dimensions={0} | all-to-all | bytes 524288 | tf_op jit(solution)/shard_map/all_to_all | solution.py:371
  231.9 17.3 %step.6 = (f32[128,8,512]{2,1,0:T(8,128)S(1)}, f32[8,16384]{1,0:T(8,128)S(1)}, f32[8,16384]{1,0:T(8,128)S(1)}, f32[8,16384]{1,0:T(8,128)S(1)}, f32[8,16384]{1,0:T(8,128)S(1)}, /*index=5*/f32[8,16384]{1,0:T(8,128)S(1)}) custom-call(s32[1]{0:T(128)} %bitcast.1.part, s32[8,128]{1,0:T(8,128)S(1)} %pad_add_fusion.blocks, ...), custom_call_target="tpu_custom_call" | custom-call | flops 536870912 | bytes 40000000 | tf_op jit(solution)/shard_map/step/pallas_call | solution.py:314
  250.0 34.9 %all_to_all.49.values = f32[128,8,512]{2,1,0:T(8,128)S(1)} all-to-all(f32[128,8,512]{2,1,0:T(8,128)S(1)} %get-tuple-element.84.refs_4_), channel_id=1, replica_groups=mesh['com'=32,'arc'=4] {'com','arc'}, dimensions={0} | all-to-all | bytes 4194304 | tf_op jit(solution)/shard_map/all_to_all | solution.py:371
  284.9 2.3 project.7
  288.5 14.4 %all_to_all.50.refs_5_ = f32[128,4,128]{2,1,0:T(4,128)S(1)} all-to-all(f32[128,4,128]{2,1,0:T(4,128)S(1)} %get-tuple-element.86), channel_id=1, replica_groups=mesh['com'=32,'arc'=4] {'com','arc'}, dimensions={0} | all-to-all | bytes 524288 | tf_op jit(solution)/shard_map/all_to_all | solution.py:371
  302.9 6.6 %all-to-all-start.7 = ((f32[32,32,512]{2,1,0:T(8,128)}), f32[32,32,512]{2,1,0:T(8,128)}, u32[]{:S(2)}, u32[]{:S(2)}) async-start(f32[32,32,512]{2,1,0:T(8,128)} %bitcast.11), calls=%async_computation.7 | async-start | bytes 4194304 | tf_op jit(solution)/shard_map/all_to_all | solution.py:371
  309.5 13.8 %step.7 = (f32[8,8192]{1,0:T(8,128)S(1)}, f32[8,8192]{1,0:T(8,128)S(1)}) custom-call(s32[1]{0:T(128)} %bitcast.1.part, s32[8,128]{1,0:T(8,128)S(1)} %pad_add_fusion.blocks, s32[264,128]{1,0:T(8,128)S(1)} %get-tuple-element.58.refs_0_, s32[264,128]{1,0:T(8,128)} %collective-permute-done.2.refs_1_, s32[264,128]{1,0:T(8,128)S(1)} %collective-permute-done.3.refs_2_, ...), custom_call_target="tpu_custom_call" | custom-call | flops 536870912 | bytes 40000000 | tf_op jit(solution)/shard_map/step/pallas_call | solution.py:314
  324.3 2.4 collective-permute-start.12
  326.7 2.0 collective-permute-start.10
  328.7 5.1 %collective-permute-done.9.refs_2_ = f32[8,8192]{1,0:T(8,128)S(1)} collective-permute-done((f32[8,8192]{1,0:T(8,128)S(1)}, f32[8,8192]{1,0:T(8,128)S(1)}, u32[]{:S(2)}, u32[]{:S(2)}) %collective-permute-start.9) | collective-permute-done | bytes 262176 | tf_op jit(solution)/shard_map/ppermute | solution.py:374
  333.8 3.3 collective-permute-start.14
  337.1 3.1 copy.13
  340.2 4.1 %collective-permute-done.13.refs_6_ = f32[8,8192]{1,0:T(8,128)} collective-permute-done((f32[8,8192]{1,0:T(8,128)S(1)}, f32[8,8192]{1,0:T(8,128)}, u32[]{:S(2)}, u32[]{:S(2)}) %collective-permute-start.13) | collective-permute-done | bytes 262176 | tf_op jit(solution)/shard_map/ppermute | solution.py:374
  344.4 2.6 assemble.1
  (67 shorter events, 12.8 us)
Async XLA Ops:
  0.6 78.9 %copy-start = (f32[32,16384]{1,0:T(8,128)S(1)}, f32[32,16384]{1,0:T(8,128)}, u32[]{:S(2)}) copy-start(f32[32,16384]{1,0:T(8,128)} %param.13) | copy-start | bytes 6291460
  4.4 23.7 %collective-permute-start = (f32[8,16384]{1,0:T(8,128)S(1)}, f32[8,16384]{1,0:T(8,128)}, u32[]{:S(2)}, u32[]{:S(2)}) collective-permute-start(f32[8,16384]{1,0:T(8,128)S(1)} %get-tuple-element.55), channel_id=1, source_target_pairs={{0,1},{1,2},{2,3},{3,0},{4,5},{5,6},{6,7},{7,4},{8,9},{9,10},{10,1... | collective-permute-start | bytes 1572872 | tf_op jit(solution)/shard_map/ppermute | solution.py:374
  6.3 21.7 %collective-permute-start.1 = (f32[8,16384]{1,0:T(8,128)S(1)}, f32[8,16384]{1,0:T(8,128)}, u32[]{:S(2)}, u32[]{:S(2)}) collective-permute-start(f32[8,16384]{1,0:T(8,128)S(1)} %get-tuple-element.56), channel_id=1, source_target_pairs={{0,3},{1,0},{2,1},{3,2},{4,7},{5,4},{6,5},{7,6},{8,11},{9,8},{10,9... | collective-permute-start | bytes 1572872 | tf_op jit(solution)/shard_map/ppermute | solution.py:374
  17.0 47.3 %all-to-all-start = ((f32[32,32,512]{2,1,0:T(8,128)}), f32[32,32,512]{2,1,0:T(8,128)}, u32[]{:S(2)}, u32[]{:S(2)}) async-start(f32[32,32,512]{2,1,0:T(8,128)} %own_trial.1), calls=%async_computation | async-start | bytes 4194304 | tf_op jit(solution)/shard_map/all_to_all | solution.py:371
  24.7 39.6 %collective-permute-start.5 = (f32[16,16384]{1,0:T(8,128)}, f32[16,16384]{1,0:T(8,128)}, u32[]{:S(2)}, u32[]{:S(2)}) collective-permute-start(f32[16,16384]{1,0:T(8,128)} %get-tuple-element.63), channel_id=1, source_target_pairs={{0,1},{1,2},{2,3},{3,0},{4,5},{5,6},{6,7},{7,4},{8,9},{9,10},{10,1... | collective-permute-start | bytes 3145736 | tf_op jit(solution)/shard_map/ppermute | solution.py:374
  24.8 39.6 %collective-permute-start.6 = (f32[16,16384]{1,0:T(8,128)}, f32[16,16384]{1,0:T(8,128)}, u32[]{:S(2)}, u32[]{:S(2)}) collective-permute-start(f32[16,16384]{1,0:T(8,128)} %get-tuple-element.64), channel_id=1, source_target_pairs={{0,3},{1,0},{2,1},{3,2},{4,7},{5,4},{6,5},{7,6},{8,11},{9,8},{10,9... | collective-permute-start | bytes 3145736 | tf_op jit(solution)/shard_map/ppermute | solution.py:374
  28.0 34.7 %collective-permute-start.7 = (f32[8,16384]{1,0:T(8,128)}, f32[8,16384]{1,0:T(8,128)}, u32[]{:S(2)}, u32[]{:S(2)}) collective-permute-start(f32[8,16384]{1,0:T(8,128)} %collective-permute-done), channel_id=1, source_target_pairs={{0,1},{1,2},{2,3},{3,0},{4,5},{5,6},{6,7},{7,4},{8,9},{9,10},{10,1... | collective-permute-start | bytes 1572872 | tf_op jit(solution)/shard_map/ppermute | solution.py:374
  28.0 35.3 %collective-permute-start.8 = (f32[8,16384]{1,0:T(8,128)}, f32[8,16384]{1,0:T(8,128)}, u32[]{:S(2)}, u32[]{:S(2)}) collective-permute-start(f32[8,16384]{1,0:T(8,128)} %collective-permute-done.1), channel_id=1, source_target_pairs={{0,3},{1,0},{2,1},{3,2},{4,7},{5,4},{6,5},{7,6},{8,11},{9,8},{10,9... | collective-permute-start | bytes 1572872 | tf_op jit(solution)/shard_map/ppermute | solution.py:374
  33.2 47.9 %copy-start.1 = (f32[16,16384]{1,0:T(8,128)S(1)}, f32[16,16384]{1,0:T(8,128)}, u32[]{:S(2)}) copy-start(f32[16,16384]{1,0:T(8,128)} %get-tuple-element.60.refs_5_.refs_8_.refs_12_) | copy-start | bytes 3145732
  34.0 46.4 %copy-start.14 = (s32[4,128]{1,0:T(4,128)}, s32[4,128]{1,0:T(4,128)S(1)}, u32[]{:S(2)}) copy-start(s32[4,128]{1,0:T(4,128)S(1)} %constant_dynamic-slice_fusion.2.classes) | copy-start | bytes 6148
  34.0 46.4 %collective-permute-start.4 = (s32[264,128]{1,0:T(8,128)S(1)}, s32[264,128]{1,0:T(8,128)S(1)}, u32[]{:S(2)}, u32[]{:S(2)}) collective-permute-start(s32[264,128]{1,0:T(8,128)S(1)} %get-tuple-element.58.refs_0_), channel_id=1, source_target_pairs={{0,3},{1,0},{2,1},{3,2},{4,7},{5,4},{6,5},{7,6},{8,11},{9,8},{10,9... | collective-permute-start | bytes 405512 | tf_op jit(solution)/shard_map/ppermute | solution.py:374
  62.8 17.6 %collective-permute-start.3 = (s32[264,128]{1,0:T(8,128)S(1)}, s32[264,128]{1,0:T(8,128)S(1)}, u32[]{:S(2)}, u32[]{:S(2)}) collective-permute-start(s32[264,128]{1,0:T(8,128)S(1)} %get-tuple-element.58.refs_0_), channel_id=1, source_target_pairs={{0,2},{1,3},{2,0},{3,1},{4,6},{5,7},{6,4},{7,5},{8,10},{9,11},{10,... | collective-permute-start | bytes 405512 | tf_op jit(solution)/shard_map/ppermute | solution.py:374
  63.3 17.0 %collective-permute-start.2 = (s32[264,128]{1,0:T(8,128)S(1)}, s32[264,128]{1,0:T(8,128)}, u32[]{:S(2)}, u32[]{:S(2)}) collective-permute-start(s32[264,128]{1,0:T(8,128)S(1)} %get-tuple-element.58.refs_0_), channel_id=1, source_target_pairs={{0,1},{1,2},{2,3},{3,0},{4,5},{5,6},{6,7},{7,4},{8,9},{9,10},{10,1... | collective-permute-start | bytes 405512 | tf_op jit(solution)/shard_map/ppermute | solution.py:374
  68.9 20.5 %all-to-all-start.1 = ((f32[128,4,128]{2,1,0:T(4,128)}), f32[128,4,128]{2,1,0:T(4,128)}, u32[]{:S(2)}, u32[]{:S(2)}) async-start(f32[128,4,128]{2,1,0:T(4,128)} %copy-done.8), calls=%async_computation.1 | async-start | bytes 524288 | tf_op jit(solution)/shard_map/all_to_all | solution.py:371
  88.1 1.3 copy-start.4
  108.0 38.8 %copy-start.15 = (s32[4,128]{1,0:T(4,128)S(1)}, s32[4,128]{1,0:T(4,128)}, u32[]{:S(2)}) copy-start(s32[4,128]{1,0:T(4,128)} %copy-done.14) | copy-start | bytes 6148
  108.0 38.7 %copy-start.17 = (f32[8]{0:T(128)S(1)}, f32[8]{0:T(128)}, u32[]{:S(2)}) copy-start(f32[8]{0:T(128)} %levels.7) | copy-start | bytes 100
  146.7 16.5 %copy-start.2 = (f32[16,16384]{1,0:T(8,128)S(1)}, f32[16,16384]{1,0:T(8,128)}, u32[]{:S(2)}) copy-start(f32[16,16384]{1,0:T(8,128)} %get-tuple-element.60.refs_5_.refs_8_.refs_12_) | copy-start | bytes 3145732
  146.7 16.5 %copy-start.3 = (f32[8,16384]{1,0:T(8,128)S(1)}, f32[8,16384]{1,0:T(8,128)}, u32[]{:S(2)}) copy-start(f32[8,16384]{1,0:T(8,128)} %constant_dynamic-slice_fusion.refs_7_) | copy-start | bytes 1572868
  250.0 34.9 %copy-start.5 = (f32[128,8,512]{2,1,0:T(8,128)}, f32[128,8,512]{2,1,0:T(8,128)S(1)}, u32[]{:S(2)}) copy-start(f32[128,8,512]{2,1,0:T(8,128)S(1)} %get-tuple-element.84.refs_4_) | copy-start | bytes 6291460
  250.0 34.9 %copy-start.9 = (f32[8,16384]{1,0:T(8,128)}, f32[8,16384]{1,0:T(8,128)S(1)}, u32[]{:S(2)}) copy-start(f32[8,16384]{1,0:T(8,128)S(1)} %get-tuple-element.87.refs_6_) | copy-start | bytes 1572868
  250.0 34.9 %copy-start.10 = (f32[8,16384]{1,0:T(8,128)}, f32[8,16384]{1,0:T(8,128)S(1)}, u32[]{:S(2)}) copy-start(f32[8,16384]{1,0:T(8,128)S(1)} %get-tuple-element.88.refs_8_) | copy-start | bytes 1572868
  250.0 34.9 %copy-start.11 = (f32[8,16384]{1,0:T(8,128)}, f32[8,16384]{1,0:T(8,128)S(1)}, u32[]{:S(2)}) copy-start(f32[8,16384]{1,0:T(8,128)S(1)} %get-tuple-element.89.refs_9_) | copy-start | bytes 1572868
  250.0 34.9 %copy-start.12 = (f32[8,16384]{1,0:T(8,128)}, f32[8,16384]{1,0:T(8,128)S(1)}, u32[]{:S(2)}) copy-start(f32[8,16384]{1,0:T(8,128)S(1)} %get-tuple-element.90.refs_10_) | copy-start | bytes 1572868
  287.2 1.3 copy-start.7
  302.9 34.2 %all-to-all-start.7 = ((f32[32,32,512]{2,1,0:T(8,128)}), f32[32,32,512]{2,1,0:T(8,128)}, u32[]{:S(2)}, u32[]{:S(2)}) async-start(f32[32,32,512]{2,1,0:T(8,128)} %bitcast.11), calls=%async_computation.7 | async-start | bytes 4194304 | tf_op jit(solution)/shard_map/all_to_all | solution.py:371
  323.4 10.4 %collective-permute-start.9 = (f32[8,8192]{1,0:T(8,128)S(1)}, f32[8,8192]{1,0:T(8,128)S(1)}, u32[]{:S(2)}, u32[]{:S(2)}) collective-permute-start(f32[8,8192]{1,0:T(8,128)S(1)} %get-tuple-element.94.refs_0_), channel_id=1, source_target_pairs={{0,1},{1,2},{2,3},{3,0},{4,5},{5,6},{6,7},{7,4},{8,9},{9,10},{10,1... | collective-permute-start | bytes 786440 | tf_op jit(solution)/shard_map/ppermute | solution.py:374
  324.3 9.5 %collective-permute-start.12 = (f32[8,8192]{1,0:T(8,128)S(1)}, f32[8,8192]{1,0:T(8,128)S(1)}, u32[]{:S(2)}, u32[]{:S(2)}) collective-permute-start(f32[8,8192]{1,0:T(8,128)S(1)} %get-tuple-element.95.refs_1_), channel_id=1, source_target_pairs={{0,3},{1,0},{2,1},{3,2},{4,7},{5,4},{6,5},{7,6},{8,11},{9,8},{10,9... | collective-permute-start | bytes 786440 | tf_op jit(solution)/shard_map/ppermute | solution.py:374
  326.7 13.5 %collective-permute-start.11 = (f32[8,8192]{1,0:T(8,128)S(1)}, f32[8,8192]{1,0:T(8,128)S(1)}, u32[]{:S(2)}, u32[]{:S(2)}) collective-permute-start(f32[8,8192]{1,0:T(8,128)S(1)} %get-tuple-element.94.refs_0_), channel_id=1, source_target_pairs={{0,3},{1,0},{2,1},{3,2},{4,7},{5,4},{6,5},{7,6},{8,11},{9,8},{10,9... | collective-permute-start | bytes 786440 | tf_op jit(solution)/shard_map/ppermute | solution.py:374
  326.7 13.5 %collective-permute-start.10 = (f32[8,8192]{1,0:T(8,128)S(1)}, f32[8,8192]{1,0:T(8,128)}, u32[]{:S(2)}, u32[]{:S(2)}) collective-permute-start(f32[8,8192]{1,0:T(8,128)S(1)} %get-tuple-element.95.refs_1_), channel_id=1, source_target_pairs={{0,1},{1,2},{2,3},{3,0},{4,5},{5,6},{6,7},{7,4},{8,9},{9,10},{10,1... | collective-permute-start | bytes 786440 | tf_op jit(solution)/shard_map/ppermute | solution.py:374
  333.8 10.6 %collective-permute-start.13 = (f32[8,8192]{1,0:T(8,128)S(1)}, f32[8,8192]{1,0:T(8,128)}, u32[]{:S(2)}, u32[]{:S(2)}) collective-permute-start(f32[8,8192]{1,0:T(8,128)S(1)} %collective-permute-done.9.refs_2_), channel_id=1, source_target_pairs={{0,1},{1,2},{2,3},{3,0},{4,5},{5,6},{6,7},{7,4},{8,9},{9,10},{10,1... | collective-permute-start | bytes 786440 | tf_op jit(solution)/shard_map/ppermute | solution.py:374
  333.8 10.5 %collective-permute-start.14 = (f32[8,8192]{1,0:T(8,128)S(1)}, f32[8,8192]{1,0:T(8,128)}, u32[]{:S(2)}, u32[]{:S(2)}) collective-permute-start(f32[8,8192]{1,0:T(8,128)S(1)} %collective-permute-done.12.refs_5_), channel_id=1, source_target_pairs={{0,3},{1,0},{2,1},{3,2},{4,7},{5,4},{6,5},{7,6},{8,11},{9,8},{10,9... | collective-permute-start | bytes 786440 | tf_op jit(solution)/shard_map/ppermute | solution.py:374
  (4 other events, 3.3 us)

commit v7 on v6

--- a/solution.py
+++ b/solution.py
@@ -280,7 +280,7 @@
         in_specs=[smem, smem] + [vmem] * 10,
         out_specs=vmem,
         out_shape=jax.ShapeDtypeStruct((OWNERS * SHARDS, 8, OWN), f32),
-        compiler_params=params(12),
+        compiler_params=params(52),
         name="trial",
     )(part, blocks, *locals_, price, *flow_cost)
 
@@ -331,9 +331,10 @@
     def rows(k):
         return pl.ds(pl.multiple_of(((part[0] - k) & (SHARDS - 1)) * 8, 8), 8)
 
-    for i, k in enumerate((0, 1, 3, 2)):
+    for i, k in enumerate((0, 1, 3)):
         out[rows(k), :half] = halves[2 * i][...]
         out[rows(k), half:] = halves[2 * i + 1][...]
+    out[rows(2), :] = jnp.zeros((8, NODES), f32)
 
 
 def assemble(part, *pieces):
@@ -342,9 +343,38 @@
         in_specs=[smem] + [vmem] * len(pieces),
         out_specs=vmem,
         out_shape=jax.ShapeDtypeStruct((SHARDS * 8, NODES), f32),
-        compiler_params=params(8),
+        compiler_params=params(52),
         name="assemble",
     )(part, *pieces)
+
+
+def complete_kernel(part, west, east, whole, out):
+    del part, whole
+
+    @pl.when(pl.program_id(0) == 0)
+    def _():
+        out[...] = west[...]
+
+    @pl.when(pl.program_id(0) == 1)
+    def _():
+        out[...] = east[...]
+
+
+def complete(part, west, east, whole):
+    half = NODES // 2
+    return pl.pallas_call(
+        complete_kernel,
+        grid_spec=pltpu.PrefetchScalarGridSpec(
+            num_scalar_prefetch=1,
+            grid=(2,),
+            in_specs=[pl.BlockSpec((8, half), lambda i, part: (0, 0))] * 2 + [pl.BlockSpec(memory_space=pl.ANY)],
+            out_specs=pl.BlockSpec((8, half), lambda i, part: ((part[0] + 2) & (SHARDS - 1), i)),
+        ),
+        out_shape=jax.ShapeDtypeStruct(whole.shape, f32),
+        input_output_aliases={3: 0},
+        compiler_params=params(8),
+        name="complete",
+    )(part, west, east, whole)
 
 
 def on_device(
@@ -383,15 +413,15 @@
     here, near, far_flow, far_cost, behind, packed = pieces
     far_flow = around(far_flow, 1)
     far_cost = around(far_cost, 3)
+    first = own_trial(head_block, tail_block, head_rows, tail_rows, price_start, flow_start, cost)
+    values = exchange(first, "com").reshape(OWNERS * SHARDS, 8, OWN)
+    far_flow, far_cost, packed, near, behind = lax.optimization_barrier((far_flow, far_cost, packed, near, behind))
+    far_flow = around(far_flow, 1)
+    far_cost = around(far_cost, 3)
     near = around(near, 1)
     behind = around(behind, 3)
-    first = own_trial(head_block, tail_block, head_rows, tail_rows, price_start, flow_start, cost)
-    values = exchange(first, "com").reshape(OWNERS * SHARDS, 8, OWN)
-    far_flow, far_cost, packed = lax.optimization_barrier((far_flow, far_cost, packed))
-    far_flow = around(far_flow, 1)
-    far_cost = around(far_cost, 3)
     locals_ = [packed] + [around(packed, k) for k in range(1, SHARDS)]
-    values, near, behind, far_flow, far_cost = lax.optimization_barrier((values, near, behind, far_flow, far_cost))
+    values, far_flow, far_cost, locals_ = lax.optimization_barrier((values, far_flow, far_cost, locals_))
     flow_cost = [here, near, far_flow, far_cost, behind]
     block_ids = jnp.concatenate([x[2 * blocks : 2 * blocks + 2] for x in locals_], axis=0)
     price = rows_of(price_start, 0)
@@ -413,8 +443,9 @@
     left_west, right_east = around(west, 1), around(east, 3)
     left_east, right_west = around(east, 1), around(west, 3)
     far_west, far_east = around(left_west, 1), around(right_east, 3)
-    out, west = lax.optimization_barrier((out, west))
-    return out, assemble(own, west, east, left_west, left_east, right_west, right_east, far_west, far_east)
+    whole = assemble(own, west, east, left_west, left_east, right_west, right_east)
+    out, whole, far_west, far_east = lax.optimization_barrier((out, whole, far_west, far_east))
+    return out, complete(own, far_west, far_east, whole)
 
 
 def solution(mesh):

time: 348 us -> 336 us (0.966)
  waiting for transfers between devices: 38 us -> 29.9 us
    ppermute x15, waiting for transfers between devices: 38 us -> 26.7 us  [around(): lax.ppermute(values, 'arc', [(i, (i + k) % SHARDS) for i in range(SHARDS)])]
  transfers between devices with their start and end apart: 18 -> 18, of which waited for: 3 -> 7; matrix products, arithmetic and copies ran while one was open for 2% -> 2% of each run, Pallas kernels for 9% -> 10%
where the time goes in v7:
time: 336 us; the launch traced here: 335 us
  blocking collectives  149 us (44%)
  Pallas kernels  97.9 us (29%)
  starting transfers between devices  44.1 us (13%)
  waiting for transfers between devices  29.9 us (9%)
  local copies, waits for them, and re-layouts  12.7 us (4%)
    all_to_all x6, blocking collectives, exchange(): return lax.all_to_all(values, axes, split_axis=0, concat_axis=0, tiled=True)  149 us
    pallas_call x4, Pallas kernels, advance(): pl.pallas_call(functools.partial(step_kernel, first=first, last=last), in...  66.3 us
    ppermute x15, waiting for transfers between devices, around(): lax.ppermute(values, 'arc', [(i, (i + k) % SHARDS) for i in range(SHARDS)])  26.7 us
    ppermute x15, starting transfers between devices, around(): lax.ppermute(values, 'arc', [(i, (i + k) % SHARDS) for i in range(SHARDS)])  22.6 us
    all_to_all x3, starting transfers between devices, exchange(): return lax.all_to_all(values, axes, split_axis=0, concat_axis=0, tiled=True)  21.5 us
    pallas_call x4, Pallas kernels, project(): pl.pallas_call(project_kernel, in_specs=[smem, vmem, vmem], out_specs=[vm...  9.5 us
    pallas_call x1, Pallas kernels, own_trial(): pl.pallas_call(own_trial_kernel, grid=(SHARDS, OWNERS * OWN // CHUNK), in...  8.51 us
    pallas_call x1, Pallas kernels, gather(): pl.pallas_call(gather_kernel, in_specs=[smem, smem] + [vmem] * 10, out_sp...  7.6 us
  transfers between devices with their start and end apart: 18, of which 7 were waited for; matrix products, arithmetic and copies ran while one was open for 2% of the time, Pallas kernels for 10%

profile of v7, /device:TPU:6, one launch (start us, length us, event | category | flops | bytes accessed | tf_op | source)
XLA Modules:
  0.0 334.6 jit_solution(17380012817374311465)
XLA Ops:
  0.6 3.7 %pack.1 = (f32[16,16384]{1,0:T(8,128)}, f32[16,16384]{1,0:T(8,128)}, f32[8,16384]{1,0:T(8,128)S(1)}, f32[8,16384]{1,0:T(8,128)S(1)}, f32[16,16384]{1,0:T(8,128)}, /*index=5*/s32[264,128]{1,0:T(8,128)S(1)}) custom-call(s32[1]{0:T(128)} %bitcast.1.part, f32[32,16384]{1,0:T(8,128)} %flow, f32[32,16384]{1,0:T(8,128)} %flow, f32[32,16384]{1,0:T(8,128)} %flow, ...), custom_call_target="tpu_custom_call" | custom-call | tf_op jit(solution)/shard_map/pack/pallas_call | solution.py:242
  6.4 2.2 collective-permute-start.1
  8.6 8.5 %own_trial.1 = f32[32,32,512]{2,1,0:T(8,128)} custom-call(s32[128]{0:T(128)} %head_block.1, s32[128]{0:T(128)} %tail_block.1, s32[128,128]{1,0:T(8,128)} %bitcast.14, s32[128,128]{1,0:T(8,128)} %bitcast.16, f32[32,16384]{1,0:T(8,128)} %price, f32[32,16384]{1,0:T(8,128)} %flow, f32[32,16384]{1,0:T(8,128)} %cost), custom_call_target="tpu_custom_call" | custom-call | tf_op jit(solution)/shard_map/own_trial/pallas_call | solution.py:258
  17.1 7.7 %all-to-all-start = ((f32[32,32,512]{2,1,0:T(8,128)}), f32[32,32,512]{2,1,0:T(8,128)}, u32[]{:S(2)}, u32[]{:S(2)}) async-start(f32[32,32,512]{2,1,0:T(8,128)} %own_trial.1), calls=%async_computation | async-start | bytes 4194304 | tf_op jit(solution)/shard_map/all_to_all | solution.py:401
  24.8 2.0 collective-permute-start.6
  28.0 2.2 collective-permute-start.2
  34.9 2.2 collective-permute-start.8
  37.2 10.8 %collective-permute-done.2.refs_7_.refs_10_.refs_14_ = f32[8,16384]{1,0:T(8,128)} collective-permute-done((f32[8,16384]{1,0:T(8,128)}, f32[8,16384]{1,0:T(8,128)}, u32[]{:S(2)}, u32[]{:S(2)}) %collective-permute-start.2) | collective-permute-done | bytes 524320 | tf_op jit(solution)/shard_map/ppermute | solution.py:404
  48.0 3.1 all-to-all-done
  51.8 3.1 project.4
  55.6 7.3 %all-to-all-start.1 = ((f32[128,4,128]{2,1,0:T(4,128)}), f32[128,4,128]{2,1,0:T(4,128)}, u32[]{:S(2)}, u32[]{:S(2)}) async-start(f32[128,4,128]{2,1,0:T(4,128)} %copy-done.8), calls=%async_computation.1 | async-start | bytes 524288 | tf_op jit(solution)/shard_map/all_to_all | solution.py:401
  64.4 8.2 %collective-permute-done.7.refs_6_.refs_9_.refs_13_ = f32[16,16384]{1,0:T(8,128)S(1)} collective-permute-done((f32[16,16384]{1,0:T(8,128)}, f32[16,16384]{1,0:T(8,128)S(1)}, u32[]{:S(2)}, u32[]{:S(2)}) %collective-permute-start.7) | collective-permute-done | bytes 1048608 | tf_op jit(solution)/shard_map/ppermute | solution.py:404
  74.7 7.6 %trial.1.refs_4_ = f32[128,8,512]{2,1,0:T(8,128)} custom-call(s32[1]{0:T(128)} %bitcast.1.part, s32[8,128]{1,0:T(8,128)S(1)} %pad_add_fusion.blocks, s32[264,128]{1,0:T(8,128)S(1)} %get-tuple-element.72.refs_0_, s32[264,128]{1,0:T(8,128)} %collective-permute-done.4.refs_1_, s32[264,128]{1,0:T(8,128)S(1)} %collective-permute-done.5.refs_2_, ...), custom_call_target="tpu_custom_call" | custom-call | tf_op jit(solution)/shard_map/trial/pallas_call | solution.py:278
  82.3 18.6 %step.4 = (f32[128,8,512]{2,1,0:T(8,128)S(1)}, f32[8,16384]{1,0:T(8,128)S(1)}, f32[8,16384]{1,0:T(8,128)S(1)}, f32[8,16384]{1,0:T(8,128)S(1)}, f32[8,16384]{1,0:T(8,128)S(1)}, /*index=5*/f32[8,16384]{1,0:T(8,128)S(1)}) custom-call(s32[1]{0:T(128)} %bitcast.1.part, s32[8,128]{1,0:T(8,128)S(1)} %pad_add_fusion.blocks, ...), custom_call_target="tpu_custom_call" | custom-call | flops 536870912 | bytes 40000000 | tf_op jit(solution)/shard_map/step/pallas_call | solution.py:314
  100.9 36.1 %all_to_all.45.values = f32[128,8,512]{2,1,0:T(8,128)S(1)} all-to-all(f32[128,8,512]{2,1,0:T(8,128)S(1)} %get-tuple-element.82.refs_4_), channel_id=1, replica_groups=mesh['com'=32,'arc'=4] {'com','arc'}, dimensions={0} | all-to-all | bytes 4194304 | tf_op jit(solution)/shard_map/all_to_all | solution.py:401
  137.0 2.1 project.5
  139.1 14.4 %all_to_all.46.refs_5_ = f32[128,4,128]{2,1,0:T(4,128)S(1)} all-to-all(f32[128,4,128]{2,1,0:T(4,128)S(1)} %project.5), channel_id=1, replica_groups=mesh['com'=32,'arc'=4] {'com','arc'}, dimensions={0} | all-to-all | bytes 524288 | tf_op jit(solution)/shard_map/all_to_all | solution.py:401
  153.5 17.0 %step.5 = (f32[128,8,512]{2,1,0:T(8,128)S(1)}, f32[8,16384]{1,0:T(8,128)S(1)}, f32[8,16384]{1,0:T(8,128)S(1)}, f32[8,16384]{1,0:T(8,128)S(1)}, f32[8,16384]{1,0:T(8,128)S(1)}, /*index=5*/f32[8,16384]{1,0:T(8,128)S(1)}) custom-call(s32[1]{0:T(128)} %bitcast.1.part, s32[8,128]{1,0:T(8,128)S(1)} %pad_add_fusion.blocks, ...), custom_call_target="tpu_custom_call" | custom-call | flops 536870912 | bytes 40000000 | tf_op jit(solution)/shard_map/step/pallas_call | solution.py:314
  170.5 34.9 %all_to_all.47.values = f32[128,8,512]{2,1,0:T(8,128)S(1)} all-to-all(f32[128,8,512]{2,1,0:T(8,128)S(1)} %get-tuple-element.88.refs_4_), channel_id=1, replica_groups=mesh['com'=32,'arc'=4] {'com','arc'}, dimensions={0} | all-to-all | bytes 4194304 | tf_op jit(solution)/shard_map/all_to_all | solution.py:401
  205.3 2.1 project.6
  207.4 14.4 %all_to_all.48.refs_5_ = f32[128,4,128]{2,1,0:T(4,128)S(1)} all-to-all(f32[128,4,128]{2,1,0:T(4,128)S(1)} %project.6), channel_id=1, replica_groups=mesh['com'=32,'arc'=4] {'com','arc'}, dimensions={0} | all-to-all | bytes 524288 | tf_op jit(solution)/shard_map/all_to_all | solution.py:401
  221.8 16.9 %step.6 = (f32[128,8,512]{2,1,0:T(8,128)S(1)}, f32[8,16384]{1,0:T(8,128)S(1)}, f32[8,16384]{1,0:T(8,128)S(1)}, f32[8,16384]{1,0:T(8,128)S(1)}, f32[8,16384]{1,0:T(8,128)S(1)}, /*index=5*/f32[8,16384]{1,0:T(8,128)S(1)}) custom-call(s32[1]{0:T(128)} %bitcast.1.part, s32[8,128]{1,0:T(8,128)S(1)} %pad_add_fusion.blocks, ...), custom_call_target="tpu_custom_call" | custom-call | flops 536870912 | bytes 40000000 | tf_op jit(solution)/shard_map/step/pallas_call | solution.py:314
  239.6 34.9 %all_to_all.49.values = f32[128,8,512]{2,1,0:T(8,128)S(1)} all-to-all(f32[128,8,512]{2,1,0:T(8,128)S(1)} %get-tuple-element.94.refs_4_), channel_id=1, replica_groups=mesh['com'=32,'arc'=4] {'com','arc'}, dimensions={0} | all-to-all | bytes 4194304 | tf_op jit(solution)/shard_map/all_to_all | solution.py:401
  274.5 2.3 project.7
  278.1 14.4 %all_to_all.50.refs_5_ = f32[128,4,128]{2,1,0:T(4,128)S(1)} all-to-all(f32[128,4,128]{2,1,0:T(4,128)S(1)} %get-tuple-element.96), channel_id=1, replica_groups=mesh['com'=32,'arc'=4] {'com','arc'}, dimensions={0} | all-to-all | bytes 524288 | tf_op jit(solution)/shard_map/all_to_all | solution.py:401
  292.5 6.6 %all-to-all-start.7 = ((f32[32,32,512]{2,1,0:T(8,128)}), f32[32,32,512]{2,1,0:T(8,128)}, u32[]{:S(2)}, u32[]{:S(2)}) async-start(f32[32,32,512]{2,1,0:T(8,128)} %bitcast.11), calls=%async_computation.7 | async-start | bytes 4194304 | tf_op jit(solution)/shard_map/all_to_all | solution.py:401
  299.1 13.8 %step.7 = (f32[8,8192]{1,0:T(8,128)S(1)}, f32[8,8192]{1,0:T(8,128)S(1)}) custom-call(s32[1]{0:T(128)} %bitcast.1.part, s32[8,128]{1,0:T(8,128)S(1)} %pad_add_fusion.blocks, s32[264,128]{1,0:T(8,128)S(1)} %get-tuple-element.72.refs_0_, s32[264,128]{1,0:T(8,128)} %collective-permute-done.4.refs_1_, s32[264,128]{1,0:T(8,128)S(1)} %collective-permute-done.5.refs_2_, ...), custom_call_target="tpu_custom_call" | custom-call | flops 536870912 | bytes 40000000 | tf_op jit(solution)/shard_map/step/pallas_call | solution.py:314
  313.8 2.4 collective-permute-start.12
  318.3 5.1 %collective-permute-done.9.refs_2_ = f32[8,8192]{1,0:T(8,128)S(1)} collective-permute-done((f32[8,8192]{1,0:T(8,128)S(1)}, f32[8,8192]{1,0:T(8,128)S(1)}, u32[]{:S(2)}, u32[]{:S(2)}) %collective-permute-start.9) | collective-permute-done | bytes 262176 | tf_op jit(solution)/shard_map/ppermute | solution.py:404
  323.4 3.3 collective-permute-start.14
  326.6 2.0 collective-permute-done.11.refs_4_
  330.5 3.1 copy.14
  (68 shorter events, 20.8 us)
Async XLA Ops:
  0.6 62.3 %copy-start = (f32[32,16384]{1,0:T(8,128)S(1)}, f32[32,16384]{1,0:T(8,128)}, u32[]{:S(2)}) copy-start(f32[32,16384]{1,0:T(8,128)} %param.13) | copy-start | bytes 6291460
  4.4 20.4 %collective-permute-start = (f32[8,16384]{1,0:T(8,128)S(1)}, f32[8,16384]{1,0:T(8,128)}, u32[]{:S(2)}, u32[]{:S(2)}) collective-permute-start(f32[8,16384]{1,0:T(8,128)S(1)} %get-tuple-element.64), channel_id=1, source_target_pairs={{0,1},{1,2},{2,3},{3,0},{4,5},{5,6},{6,7},{7,4},{8,9},{9,10},{10,1... | collective-permute-start | bytes 1572872 | tf_op jit(solution)/shard_map/ppermute | solution.py:404
  6.4 18.4 %collective-permute-start.1 = (f32[8,16384]{1,0:T(8,128)S(1)}, f32[8,16384]{1,0:T(8,128)}, u32[]{:S(2)}, u32[]{:S(2)}) collective-permute-start(f32[8,16384]{1,0:T(8,128)S(1)} %get-tuple-element.65), channel_id=1, source_target_pairs={{0,3},{1,0},{2,1},{3,2},{4,7},{5,4},{6,5},{7,6},{8,11},{9,8},{10,9... | collective-permute-start | bytes 1572872 | tf_op jit(solution)/shard_map/ppermute | solution.py:404
  17.1 34.1 %all-to-all-start = ((f32[32,32,512]{2,1,0:T(8,128)}), f32[32,32,512]{2,1,0:T(8,128)}, u32[]{:S(2)}, u32[]{:S(2)}) async-start(f32[32,32,512]{2,1,0:T(8,128)} %own_trial.1), calls=%async_computation | async-start | bytes 4194304 | tf_op jit(solution)/shard_map/all_to_all | solution.py:401
  24.8 9.1 %collective-permute-start.6 = (s32[264,128]{1,0:T(8,128)S(1)}, s32[264,128]{1,0:T(8,128)S(1)}, u32[]{:S(2)}, u32[]{:S(2)}) collective-permute-start(s32[264,128]{1,0:T(8,128)S(1)} %get-tuple-element.72.refs_0_), channel_id=1, source_target_pairs={{0,3},{1,0},{2,1},{3,2},{4,7},{5,4},{6,5},{7,6},{8,11},{9,8},{10,9... | collective-permute-start | bytes 405512 | tf_op jit(solution)/shard_map/ppermute | solution.py:404
  26.8 8.1 %collective-permute-start.5 = (s32[264,128]{1,0:T(8,128)S(1)}, s32[264,128]{1,0:T(8,128)S(1)}, u32[]{:S(2)}, u32[]{:S(2)}) collective-permute-start(s32[264,128]{1,0:T(8,128)S(1)} %get-tuple-element.72.refs_0_), channel_id=1, source_target_pairs={{0,2},{1,3},{2,0},{3,1},{4,6},{5,7},{6,4},{7,5},{8,10},{9,11},{10,... | collective-permute-start | bytes 405512 | tf_op jit(solution)/shard_map/ppermute | solution.py:404
  26.8 10.4 %collective-permute-start.4 = (s32[264,128]{1,0:T(8,128)S(1)}, s32[264,128]{1,0:T(8,128)}, u32[]{:S(2)}, u32[]{:S(2)}) collective-permute-start(s32[264,128]{1,0:T(8,128)S(1)} %get-tuple-element.72.refs_0_), channel_id=1, source_target_pairs={{0,1},{1,2},{2,3},{3,0},{4,5},{5,6},{6,7},{7,4},{8,9},{9,10},{10,1... | collective-permute-start | bytes 405512 | tf_op jit(solution)/shard_map/ppermute | solution.py:404
  28.0 19.9 %collective-permute-start.2 = (f32[8,16384]{1,0:T(8,128)}, f32[8,16384]{1,0:T(8,128)}, u32[]{:S(2)}, u32[]{:S(2)}) collective-permute-start(f32[8,16384]{1,0:T(8,128)} %collective-permute-done), channel_id=1, source_target_pairs={{0,1},{1,2},{2,3},{3,0},{4,5},{5,6},{6,7},{7,4},{8,9},{9,10},{10,1... | collective-permute-start | bytes 1572872 | tf_op jit(solution)/shard_map/ppermute | solution.py:404
  30.3 17.7 %collective-permute-start.3 = (f32[8,16384]{1,0:T(8,128)}, f32[8,16384]{1,0:T(8,128)}, u32[]{:S(2)}, u32[]{:S(2)}) collective-permute-start(f32[8,16384]{1,0:T(8,128)} %collective-permute-done.1), channel_id=1, source_target_pairs={{0,3},{1,0},{2,1},{3,2},{4,7},{5,4},{6,5},{7,6},{8,11},{9,8},{10,9... | collective-permute-start | bytes 1572872 | tf_op jit(solution)/shard_map/ppermute | solution.py:404
  33.8 30.6 %copy-start.14 = (s32[4,128]{1,0:T(4,128)}, s32[4,128]{1,0:T(4,128)S(1)}, u32[]{:S(2)}) copy-start(s32[4,128]{1,0:T(4,128)S(1)} %constant_dynamic-slice_fusion.2.classes) | copy-start | bytes 6148
  33.8 38.8 %collective-permute-start.7 = (f32[16,16384]{1,0:T(8,128)}, f32[16,16384]{1,0:T(8,128)S(1)}, u32[]{:S(2)}, u32[]{:S(2)}) collective-permute-start(f32[16,16384]{1,0:T(8,128)} %get-tuple-element.77), channel_id=1, source_target_pairs={{0,1},{1,2},{2,3},{3,0},{4,5},{5,6},{6,7},{7,4},{8,9},{9,10},{10,1... | collective-permute-start | bytes 3145736 | tf_op jit(solution)/shard_map/ppermute | solution.py:404
  34.9 37.8 %collective-permute-start.8 = (f32[16,16384]{1,0:T(8,128)}, f32[16,16384]{1,0:T(8,128)}, u32[]{:S(2)}, u32[]{:S(2)}) collective-permute-start(f32[16,16384]{1,0:T(8,128)} %get-tuple-element.80), channel_id=1, source_target_pairs={{0,3},{1,0},{2,1},{3,2},{4,7},{5,4},{6,5},{7,6},{8,11},{9,8},{10,9... | collective-permute-start | bytes 3145736 | tf_op jit(solution)/shard_map/ppermute | solution.py:404
  55.6 26.7 %all-to-all-start.1 = ((f32[128,4,128]{2,1,0:T(4,128)}), f32[128,4,128]{2,1,0:T(4,128)}, u32[]{:S(2)}, u32[]{:S(2)}) async-start(f32[128,4,128]{2,1,0:T(4,128)} %copy-done.8), calls=%async_computation.1 | async-start | bytes 524288 | tf_op jit(solution)/shard_map/all_to_all | solution.py:401
  73.7 1.0 copy-start.6
  100.9 36.1 %copy-start.15 = (s32[4,128]{1,0:T(4,128)S(1)}, s32[4,128]{1,0:T(4,128)}, u32[]{:S(2)}) copy-start(s32[4,128]{1,0:T(4,128)} %copy-done.14) | copy-start | bytes 6148
  100.9 36.1 %copy-start.17 = (f32[8]{0:T(128)S(1)}, f32[8]{0:T(128)}, u32[]{:S(2)}) copy-start(f32[8]{0:T(128)} %levels.7) | copy-start | bytes 100
  137.0 16.5 %copy-start.1 = (f32[16,16384]{1,0:T(8,128)S(1)}, f32[16,16384]{1,0:T(8,128)}, u32[]{:S(2)}) copy-start(f32[16,16384]{1,0:T(8,128)} %get-tuple-element.76.refs_5_.refs_8_.refs_12_) | copy-start | bytes 3145732
  137.0 16.5 %copy-start.3 = (f32[16,16384]{1,0:T(8,128)S(1)}, f32[16,16384]{1,0:T(8,128)}, u32[]{:S(2)}) copy-start(f32[16,16384]{1,0:T(8,128)} %copy-done.2) | copy-start | bytes 3145732
  137.0 16.5 %copy-start.4 = (f32[8,16384]{1,0:T(8,128)S(1)}, f32[8,16384]{1,0:T(8,128)}, u32[]{:S(2)}) copy-start(f32[8,16384]{1,0:T(8,128)} %constant_dynamic-slice_fusion.refs_7_) | copy-start | bytes 1572868
  239.6 34.9 %copy-start.5 = (f32[128,8,512]{2,1,0:T(8,128)}, f32[128,8,512]{2,1,0:T(8,128)S(1)}, u32[]{:S(2)}) copy-start(f32[128,8,512]{2,1,0:T(8,128)S(1)} %get-tuple-element.94.refs_4_) | copy-start | bytes 6291460
  239.6 34.9 %copy-start.9 = (f32[8,16384]{1,0:T(8,128)}, f32[8,16384]{1,0:T(8,128)S(1)}, u32[]{:S(2)}) copy-start(f32[8,16384]{1,0:T(8,128)S(1)} %get-tuple-element.97.refs_6_) | copy-start | bytes 1572868
  239.6 34.9 %copy-start.10 = (f32[8,16384]{1,0:T(8,128)}, f32[8,16384]{1,0:T(8,128)S(1)}, u32[]{:S(2)}) copy-start(f32[8,16384]{1,0:T(8,128)S(1)} %get-tuple-element.98.refs_8_) | copy-start | bytes 1572868
  239.6 34.9 %copy-start.11 = (f32[8,16384]{1,0:T(8,128)}, f32[8,16384]{1,0:T(8,128)S(1)}, u32[]{:S(2)}) copy-start(f32[8,16384]{1,0:T(8,128)S(1)} %get-tuple-element.99.refs_9_) | copy-start | bytes 1572868
  239.6 34.9 %copy-start.12 = (f32[8,16384]{1,0:T(8,128)}, f32[8,16384]{1,0:T(8,128)S(1)}, u32[]{:S(2)}) copy-start(f32[8,16384]{1,0:T(8,128)S(1)} %get-tuple-element.100.refs_10_) | copy-start | bytes 1572868
  276.8 1.3 copy-start.7
  292.5 38.0 %all-to-all-start.7 = ((f32[32,32,512]{2,1,0:T(8,128)}), f32[32,32,512]{2,1,0:T(8,128)}, u32[]{:S(2)}, u32[]{:S(2)}) async-start(f32[32,32,512]{2,1,0:T(8,128)} %bitcast.11), calls=%async_computation.7 | async-start | bytes 4194304 | tf_op jit(solution)/shard_map/all_to_all | solution.py:401
  312.9 10.4 %collective-permute-start.9 = (f32[8,8192]{1,0:T(8,128)S(1)}, f32[8,8192]{1,0:T(8,128)S(1)}, u32[]{:S(2)}, u32[]{:S(2)}) collective-permute-start(f32[8,8192]{1,0:T(8,128)S(1)} %get-tuple-element.102.refs_0_), channel_id=1, source_target_pairs={{0,1},{1,2},{2,3},{3,0},{4,5},{5,6},{6,7},{7,4},{8,9},{9,10},{10,1... | collective-permute-start | bytes 786440 | tf_op jit(solution)/shard_map/ppermute | solution.py:404
  313.8 9.5 %collective-permute-start.12 = (f32[8,8192]{1,0:T(8,128)S(1)}, f32[8,8192]{1,0:T(8,128)S(1)}, u32[]{:S(2)}, u32[]{:S(2)}) collective-permute-start(f32[8,8192]{1,0:T(8,128)S(1)} %get-tuple-element.103.refs_1_), channel_id=1, source_target_pairs={{0,3},{1,0},{2,1},{3,2},{4,7},{5,4},{6,5},{7,6},{8,11},{9,8},{10,9... | collective-permute-start | bytes 786440 | tf_op jit(solution)/shard_map/ppermute | solution.py:404
  316.2 12.4 %collective-permute-start.11 = (f32[8,8192]{1,0:T(8,128)S(1)}, f32[8,8192]{1,0:T(8,128)S(1)}, u32[]{:S(2)}, u32[]{:S(2)}) collective-permute-start(f32[8,8192]{1,0:T(8,128)S(1)} %get-tuple-element.102.refs_0_), channel_id=1, source_target_pairs={{0,3},{1,0},{2,1},{3,2},{4,7},{5,4},{6,5},{7,6},{8,11},{9,8},{10,9... | collective-permute-start | bytes 786440 | tf_op jit(solution)/shard_map/ppermute | solution.py:404
  316.3 12.7 %collective-permute-start.10 = (f32[8,8192]{1,0:T(8,128)S(1)}, f32[8,8192]{1,0:T(8,128)S(1)}, u32[]{:S(2)}, u32[]{:S(2)}) collective-permute-start(f32[8,8192]{1,0:T(8,128)S(1)} %get-tuple-element.103.refs_1_), channel_id=1, source_target_pairs={{0,1},{1,2},{2,3},{3,0},{4,5},{5,6},{6,7},{7,4},{8,9},{9,10},{10,1... | collective-permute-start | bytes 786440 | tf_op jit(solution)/shard_map/ppermute | solution.py:404
  323.4 10.4 %collective-permute-start.13 = (f32[8,8192]{1,0:T(8,128)S(1)}, f32[8,8192]{1,0:T(8,128)S(1)}, u32[]{:S(2)}, u32[]{:S(2)}) collective-permute-start(f32[8,8192]{1,0:T(8,128)S(1)} %collective-permute-done.9.refs_2_), channel_id=1, source_target_pairs={{0,1},{1,2},{2,3},{3,0},{4,5},{5,6},{6,7},{7,4},{8,9},{9,10},{10,1... | collective-permute-start | bytes 786440 | tf_op jit(solution)/shard_map/ppermute | solution.py:404
  323.4 10.4 %collective-permute-start.14 = (f32[8,8192]{1,0:T(8,128)S(1)}, f32[8,8192]{1,0:T(8,128)S(1)}, u32[]{:S(2)}, u32[]{:S(2)}) collective-permute-start(f32[8,8192]{1,0:T(8,128)S(1)} %collective-permute-done.12.refs_5_), channel_id=1, source_target_pairs={{0,3},{1,0},{2,1},{3,2},{4,7},{5,4},{6,5},{7,6},{8,11},{9,8},{10,9... | collective-permute-start | bytes 786440 | tf_op jit(solution)/shard_map/ppermute | solution.py:404
  (4 other events, 3.1 us)

commit v8 on v7

--- a/solution.py
+++ b/solution.py
@@ -68,16 +68,20 @@
     lax.fori_loop(0, CHUNK // OWN // UNROLL, step, 0)
 
 
-def gather_kernel(part, blocks, *refs):
-    fill_trial(part, blocks, refs[:4], refs[4], flow_views(refs[5:10]), cost_views(refs[5:10]), refs[10])
-
-
 def flow_views(pairs):
     return [(pairs[0], 0), (pairs[1], 0), (pairs[2], 0), (pairs[4], 0)]
 
 
 def cost_views(pairs):
     return [(pairs[0], 8), (pairs[1], 8), (pairs[3], 0), (pairs[4], 8)]
+
+
+def trial_of(blocks, locals_, price, flow, cost, k, j, where):
+    head = jnp.broadcast_to(locals_[k][pl.ds(j, 1), :], (8, BLOCK))
+    tail = jnp.broadcast_to(locals_[k][pl.ds(BLOCK + j, 1), :], (8, BLOCK))
+    at_head = jnp.take_along_axis(price[:, node_slice(blocks[2 * k, j])], head, axis=1)
+    at_tail = jnp.take_along_axis(price[:, node_slice(blocks[2 * k + 1, j])], tail, axis=1)
+    return rows_at(flow[k], where) - step_primal * (rows_at(cost[k], where) - (at_head - at_tail))
 
 
 def fill_trial(part, blocks, locals_, price, flow, cost, trial):
@@ -87,17 +91,10 @@
         def step(o, carry):
             for u in range(UNROLL):
                 owner = o * UNROLL + u
-                start = owner * OWN
                 for q in range(QUADS):
-                    j = owner * QUADS + q
-                    head = jnp.broadcast_to(locals_[k][pl.ds(j, 1), :], (8, BLOCK))
-                    tail = jnp.broadcast_to(locals_[k][pl.ds(BLOCK + j, 1), :], (8, BLOCK))
-                    at_head = jnp.take_along_axis(price[:, node_slice(blocks[2 * k, j])], head, axis=1)
-                    at_tail = jnp.take_along_axis(price[:, node_slice(blocks[2 * k + 1, j])], tail, axis=1)
-                    where = arc_slice(start, q)
-                    trial[owner * SHARDS + shard, :, q * BLOCK : (q + 1) * BLOCK] = rows_at(
-                        flow[k], where
-                    ) - step_primal * (rows_at(cost[k], where) - (at_head - at_tail))
+                    trial[owner * SHARDS + shard, :, q * BLOCK : (q + 1) * BLOCK] = trial_of(
+                        blocks, locals_, price, flow, cost, k, owner * QUADS + q, arc_slice(owner * OWN, q)
+                    )
             return carry
 
         lax.fori_loop(0, OWNERS // UNROLL, step, 0)
@@ -149,12 +146,12 @@
 
 
 def step_kernel(part, blocks, *refs, first, last):
-    locals_, trial, theta, price, demand = refs[:4], refs[4], refs[5], refs[6], refs[7]
-    balance, rest = refs[-1], refs[8:-1]
+    locals_, theta, price, demand = refs[:4], refs[4], refs[5], refs[6]
+    balance, rest = refs[-1], refs[7:-1]
     if first:
         flow, cost, rest = flow_views(rest[:5]), cost_views(rest[:5]), rest[5:]
     else:
-        flow, rest = [(ref, 0) for ref in rest[:SHARDS]], rest[SHARDS:]
+        trial, flow, rest = rest[0], [(ref, 0) for ref in rest[1 : 1 + SHARDS]], rest[1 + SHARDS :]
         if not last:
             cost, rest = cost_views(rest[:5]), rest[5:]
     if last:
@@ -181,9 +178,11 @@
                     j = owner * QUADS + q
                     where = arc_slice(start, q)
                     limit = theta[owner * SHARDS + shard, q : q + 1, :]
-                    fresh = jnp.maximum(
-                        trial[owner * SHARDS + shard, :, q * BLOCK : (q + 1) * BLOCK] - limit, 0.0
-                    )
+                    if first:
+                        wanted = trial_of(blocks, locals_, price, flow, cost, k, j, where)
+                    else:
+                        wanted = trial[owner * SHARDS + shard, :, q * BLOCK : (q + 1) * BLOCK]
+                    fresh = jnp.maximum(wanted - limit, 0.0)
                     if not last:
                         fresh_out[k][:, where] = fresh
                     extra = 2.0 * fresh - rows_at(flow[k], where)
@@ -274,17 +273,6 @@
     )(*in_hbm([head_block, tail_block, head_local, tail_local, price, flow, cost]))
 
 
-def gather(part, blocks, locals_, price, flow_cost):
-    return pl.pallas_call(
-        gather_kernel,
-        in_specs=[smem, smem] + [vmem] * 10,
-        out_specs=vmem,
-        out_shape=jax.ShapeDtypeStruct((OWNERS * SHARDS, 8, OWN), f32),
-        compiler_params=params(52),
-        name="trial",
-    )(part, blocks, *locals_, price, *flow_cost)
-
-
 def project(levels, classes, values, last):
     shape = [jax.ShapeDtypeStruct((SHARDS * OWNERS, QUADS, BLOCK), f32)]
     if last:
@@ -304,12 +292,15 @@
 
 
 def advance(part, blocks, locals_, trial, theta, flow, price, demand, flow_cost, first, last):
-    if first or last:
-        trial, price, demand, *flow = in_hbm([trial, price, demand, *flow])
-    operands = [trial, theta, price, demand] + list(flow) + ([] if first or last else list(flow_cost))
+    if first:
+        operands = [theta, *in_hbm([price, demand]), *flow_cost]
+    elif last:
+        operands = [theta, *in_hbm([price, demand, trial, *flow])]
+    else:
+        operands = [theta, price, demand, trial, *flow, *flow_cost]
     shape = [jax.ShapeDtypeStruct((8, NODES // 2), f32)] * 2 if last else [jax.ShapeDtypeStruct((8, NODES), f32)]
     if not last:
-        shape = [jax.ShapeDtypeStruct(trial.shape, f32)] + shape
+        shape = [jax.ShapeDtypeStruct((OWNERS * SHARDS, 8, OWN), f32)] + shape
         shape = shape + [jax.ShapeDtypeStruct((8, OWNERS * OWN), f32)] * SHARDS
     out = pl.pallas_call(
         functools.partial(step_kernel, first=first, last=last),
@@ -408,13 +399,12 @@
 
     own = part.astype(jnp.int32).reshape(1)
     ids = [head_rows, tail_rows, head_block.reshape(1, BLOCK), tail_block.reshape(1, BLOCK)]
-    pieces = pack(own, flow_start, cost, ids)
-    pieces, flow_start, cost, price_start = lax.optimization_barrier((pieces, flow_start, cost, price_start))
-    here, near, far_flow, far_cost, behind, packed = pieces
+    first = own_trial(head_block, tail_block, head_rows, tail_rows, price_start, flow_start, cost)
+    first, flow_start, cost, ids = lax.optimization_barrier((first, flow_start, cost, ids))
+    values = exchange(first, "com").reshape(OWNERS * SHARDS, 8, OWN)
+    here, near, far_flow, far_cost, behind, packed = pack(own, flow_start, cost, ids)
     far_flow = around(far_flow, 1)
     far_cost = around(far_cost, 3)
-    first = own_trial(head_block, tail_block, head_rows, tail_rows, price_start, flow_start, cost)
-    values = exchange(first, "com").reshape(OWNERS * SHARDS, 8, OWN)
     far_flow, far_cost, packed, near, behind = lax.optimization_barrier((far_flow, far_cost, packed, near, behind))
     far_flow = around(far_flow, 1)
     far_cost = around(far_cost, 3)
@@ -428,8 +418,7 @@
     wanted = rows_of(demand, 0)
     classes = lax.dynamic_slice(cap_class.reshape(blocks, BLOCK), (place * QUADS, 0), (QUADS, BLOCK))
 
-    trial = gather(own, block_ids, locals_, price, flow_cost)
-    flow = flow_cost
+    trial = flow = None
     for step in range(ITERS):
         last = step == ITERS - 1
         if step > 0:

time: 336 us -> 339 us (level)
  waiting for transfers between devices: 29.9 us -> 44.2 us
  Pallas kernels: 97.9 us -> 89.8 us
  local copies, waits for them, and re-layouts: 12.7 us -> 7.77 us
    ppermute x15, waiting for transfers between devices: 26.7 us -> 42.9 us  [around(): lax.ppermute(values, 'arc', [(i, (i + k) % SHARDS) for i in range(SHARDS)])]
    pallas_call x1 -> x0, Pallas kernels: 7.6 us -> none  [gather(): pl.pallas_call(gather_kernel, in_specs=[smem, smem] + [vmem] * 10, out_sp...]
  transfers between devices with their start and end apart: 18 -> 18, of which waited for: 7 -> 9; matrix products, arithmetic and copies ran while one was open for 2% -> 1% of each run, Pallas kernels for 10% -> 7%
where the time goes in v8:
time: 339 us; the launch traced here: 338 us
  blocking collectives  150 us (44%)
  Pallas kernels  89.8 us (26%)
  starting transfers between devices  45.3 us (13%)
  waiting for transfers between devices  44.2 us (13%)
  local copies, waits for them, and re-layouts  7.77 us (2%)
    all_to_all x6, blocking collectives, exchange(): return lax.all_to_all(values, axes, split_axis=0, concat_axis=0, tiled=True)  150 us
    pallas_call x4, Pallas kernels, advance(): pl.pallas_call(functools.partial(step_kernel, first=first, last=last), in...  64.5 us
    ppermute x15, waiting for transfers between devices, around(): lax.ppermute(values, 'arc', [(i, (i + k) % SHARDS) for i in range(SHARDS)])  42.9 us
    ppermute x15, starting transfers between devices, around(): lax.ppermute(values, 'arc', [(i, (i + k) % SHARDS) for i in range(SHARDS)])  22.9 us
    all_to_all x3, starting transfers between devices, exchange(): return lax.all_to_all(values, axes, split_axis=0, concat_axis=0, tiled=True)  22.3 us
    pallas_call x4, Pallas kernels, project(): pl.pallas_call(project_kernel, in_specs=[smem, vmem, vmem], out_specs=[vm...  10.9 us
    pallas_call x1, Pallas kernels, own_trial(): pl.pallas_call(own_trial_kernel, grid=(SHARDS, OWNERS * OWN // CHUNK), in...  8.53 us
  transfers between devices with their start and end apart: 18, of which 9 were waited for; matrix products, arithmetic and copies ran while one was open for 1% of the time, Pallas kernels for 7%

profile of v8, /device:TPU:6, one launch (start us, length us, event | category | flops | bytes accessed | tf_op | source)
XLA Modules:
  0.0 338.0 jit_solution(6365124106002382141)
XLA Ops:
  0.6 8.5 %own_trial.1 = f32[32,32,512]{2,1,0:T(8,128)} custom-call(s32[128]{0:T(128)} %head_block.1, s32[128]{0:T(128)} %tail_block.1, s32[128,128]{1,0:T(8,128)} %bitcast.14, s32[128,128]{1,0:T(8,128)} %bitcast.16, f32[32,16384]{1,0:T(8,128)} %price.1, f32[32,16384]{1,0:T(8,128)} %refs_3_, f32[32,16384]{1,0:T(8,128)} %refs_7_), custom_call_target="tpu_custom_call" | custom-call | tf_op jit(solution)/shard_map/own_trial/pallas_call | solution.py:257
  9.2 7.7 %all-to-all-start = ((f32[32,32,512]{2,1,0:T(8,128)}), f32[32,32,512]{2,1,0:T(8,128)}, u32[]{:S(2)}, u32[]{:S(2)}) async-start(f32[32,32,512]{2,1,0:T(8,128)} %own_trial.1), calls=%async_computation | async-start | bytes 4194304 | tf_op jit(solution)/shard_map/all_to_all | solution.py:392
  16.9 3.6 %pack.1 = (f32[16,16384]{1,0:T(8,128)}, f32[16,16384]{1,0:T(8,128)}, f32[8,16384]{1,0:T(8,128)S(1)}, f32[8,16384]{1,0:T(8,128)S(1)}, f32[16,16384]{1,0:T(8,128)}, /*index=5*/s32[264,128]{1,0:T(8,128)S(1)}) custom-call(s32[1]{0:T(128)} %bitcast.1.part, f32[32,16384]{1,0:T(8,128)} %refs_3_, f32[32,16384]{1,0:T(8,128)} %refs_3_, f32[32,16384]{1,0:T(8,128)} %refs_3_, ...), custom_call_target="tpu_custom_call" | custom-call | tf_op jit(solution)/shard_map/pack/pallas_call | solution.py:241
  20.4 2.0 collective-permute-start
  22.4 2.2 collective-permute-start.1
  24.6 12.2 %collective-permute-done = f32[8,16384]{1,0:T(8,128)S(1)} collective-permute-done((f32[8,16384]{1,0:T(8,128)S(1)}, f32[8,16384]{1,0:T(8,128)S(1)}, u32[]{:S(2)}, u32[]{:S(2)}) %collective-permute-start) | collective-permute-done | bytes 524320 | tf_op jit(solution)/shard_map/ppermute | solution.py:395
  40.0 1.9 collective-permute-start.6
  43.3 13.6 %collective-permute-done.6.refs_3_ = s32[264,128]{1,0:T(8,128)S(1)} collective-permute-done((s32[264,128]{1,0:T(8,128)S(1)}, s32[264,128]{1,0:T(8,128)S(1)}, u32[]{:S(2)}, u32[]{:S(2)}) %collective-permute-start.6) | collective-permute-done | bytes 135200 | tf_op jit(solution)/shard_map/ppermute | solution.py:395
  57.0 3.7 %collective-permute-start.8 = (f32[16,16384]{1,0:T(8,128)}, f32[16,16384]{1,0:T(8,128)}, u32[]{:S(2)}, u32[]{:S(2)}) collective-permute-start(f32[16,16384]{1,0:T(8,128)} %get-tuple-element.77), channel_id=1, source_target_pairs={{0,3},{1,0},{2,1},{3,2},{4,7},{5,4},{6,5},{7,6},{8,11},{9,8},{10,9... | collective-permute-start | bytes 3145736 | tf_op jit(solution)/shard_map/ppermute | solution.py:395
  61.3 3.2 project.4
  65.2 8.6 %all-to-all-start.1 = ((f32[128,4,128]{2,1,0:T(4,128)}), f32[128,4,128]{2,1,0:T(4,128)}, u32[]{:S(2)}, u32[]{:S(2)}) async-start(f32[128,4,128]{2,1,0:T(4,128)} %copy-done.14), calls=%async_computation.1 | async-start | bytes 524288 | tf_op jit(solution)/shard_map/all_to_all | solution.py:392
  73.8 2.2 constant_dynamic-slice_fusion
  76.1 7.8 %collective-permute-done.7.refs_8_.refs_13_ = f32[16,16384]{1,0:T(8,128)S(1)} collective-permute-done((f32[16,16384]{1,0:T(8,128)}, f32[16,16384]{1,0:T(8,128)S(1)}, u32[]{:S(2)}, u32[]{:S(2)}) %collective-permute-start.7) | collective-permute-done | bytes 1048608 | tf_op jit(solution)/shard_map/ppermute | solution.py:395
  87.0 17.4 %step.4 = (f32[128,8,512]{2,1,0:T(8,128)S(1)}, f32[8,16384]{1,0:T(8,128)S(1)}, f32[8,16384]{1,0:T(8,128)S(1)}, f32[8,16384]{1,0:T(8,128)S(1)}, f32[8,16384]{1,0:T(8,128)S(1)}, /*index=5*/f32[8,16384]{1,0:T(8,128)S(1)}) custom-call(s32[1]{0:T(128)} %bitcast.1.part, s32[8,128]{1,0:T(8,128)S(1)} %pad_add_fusion.blocks, ...), custom_call_target="tpu_custom_call" | custom-call | flops 536870912 | bytes 40000000 | tf_op jit(solution)/shard_map/step/pallas_call | solution.py:305
  104.5 37.1 %all_to_all.45.values = f32[128,8,512]{2,1,0:T(8,128)S(1)} all-to-all(f32[128,8,512]{2,1,0:T(8,128)S(1)} %get-tuple-element.78.refs_7_), channel_id=1, replica_groups=mesh['com'=32,'arc'=4] {'com','arc'}, dimensions={0} | all-to-all | bytes 4194304 | tf_op jit(solution)/shard_map/all_to_all | solution.py:392
  141.6 2.1 project.5
  143.6 14.4 %all_to_all.46.refs_4_ = f32[128,4,128]{2,1,0:T(4,128)S(1)} all-to-all(f32[128,4,128]{2,1,0:T(4,128)S(1)} %project.5), channel_id=1, replica_groups=mesh['com'=32,'arc'=4] {'com','arc'}, dimensions={0} | all-to-all | bytes 524288 | tf_op jit(solution)/shard_map/all_to_all | solution.py:392
  158.1 16.6 %step.5 = (f32[128,8,512]{2,1,0:T(8,128)S(1)}, f32[8,16384]{1,0:T(8,128)S(1)}, f32[8,16384]{1,0:T(8,128)S(1)}, f32[8,16384]{1,0:T(8,128)S(1)}, f32[8,16384]{1,0:T(8,128)S(1)}, /*index=5*/f32[8,16384]{1,0:T(8,128)S(1)}) custom-call(s32[1]{0:T(128)} %bitcast.1.part, s32[8,128]{1,0:T(8,128)S(1)} %pad_add_fusion.blocks, ...), custom_call_target="tpu_custom_call" | custom-call | flops 536870912 | bytes 40000000 | tf_op jit(solution)/shard_map/step/pallas_call | solution.py:305
  174.7 34.9 %all_to_all.47.values = f32[128,8,512]{2,1,0:T(8,128)S(1)} all-to-all(f32[128,8,512]{2,1,0:T(8,128)S(1)} %get-tuple-element.84.refs_7_), channel_id=1, replica_groups=mesh['com'=32,'arc'=4] {'com','arc'}, dimensions={0} | all-to-all | bytes 4194304 | tf_op jit(solution)/shard_map/all_to_all | solution.py:392
  209.6 2.1 project.6
  211.6 14.4 %all_to_all.48.refs_4_ = f32[128,4,128]{2,1,0:T(4,128)S(1)} all-to-all(f32[128,4,128]{2,1,0:T(4,128)S(1)} %project.6), channel_id=1, replica_groups=mesh['com'=32,'arc'=4] {'com','arc'}, dimensions={0} | all-to-all | bytes 524288 | tf_op jit(solution)/shard_map/all_to_all | solution.py:392
  226.1 16.6 %step.6 = (f32[128,8,512]{2,1,0:T(8,128)S(1)}, f32[8,16384]{1,0:T(8,128)S(1)}, f32[8,16384]{1,0:T(8,128)S(1)}, f32[8,16384]{1,0:T(8,128)S(1)}, f32[8,16384]{1,0:T(8,128)S(1)}, /*index=5*/f32[8,16384]{1,0:T(8,128)S(1)}) custom-call(s32[1]{0:T(128)} %bitcast.1.part, s32[8,128]{1,0:T(8,128)S(1)} %pad_add_fusion.blocks, ...), custom_call_target="tpu_custom_call" | custom-call | flops 536870912 | bytes 40000000 | tf_op jit(solution)/shard_map/step/pallas_call | solution.py:305
  243.5 34.9 %all_to_all.49.values = f32[128,8,512]{2,1,0:T(8,128)S(1)} all-to-all(f32[128,8,512]{2,1,0:T(8,128)S(1)} %get-tuple-element.90.refs_7_), channel_id=1, replica_groups=mesh['com'=32,'arc'=4] {'com','arc'}, dimensions={0} | all-to-all | bytes 4194304 | tf_op jit(solution)/shard_map/all_to_all | solution.py:392
  278.4 3.6 %project.7 = (f32[128,4,128]{2,1,0:T(4,128)S(1)}, f32[128,8,512]{2,1,0:T(8,128)}) custom-call(f32[8]{0:T(128)S(1)} %copy-done.20, s32[4,128]{1,0:T(4,128)S(1)} %constant_dynamic-slice_fusion.2.classes, f32[128,8,512]{2,1,0:T(8,128)S(1)} %all_to_all.49.values), custom_call_target="tpu_custom_call" | custom-call | tf_op jit(solution)/shard_map/project/pallas_call | solution.py:280
  282.0 14.4 %all_to_all.50.refs_4_ = f32[128,4,128]{2,1,0:T(4,128)S(1)} all-to-all(f32[128,4,128]{2,1,0:T(4,128)S(1)} %get-tuple-element.92), channel_id=1, replica_groups=mesh['com'=32,'arc'=4] {'com','arc'}, dimensions={0} | all-to-all | bytes 524288 | tf_op jit(solution)/shard_map/all_to_all | solution.py:392
  296.4 6.0 %all-to-all-start.7 = ((f32[32,32,512]{2,1,0:T(8,128)}), f32[32,32,512]{2,1,0:T(8,128)S(1)}, u32[]{:S(2)}, u32[]{:S(2)}) async-start(f32[32,32,512]{2,1,0:T(8,128)} %bitcast.7), calls=%async_computation.7 | async-start | bytes 4194304 | tf_op jit(solution)/shard_map/all_to_all | solution.py:392
  302.5 13.8 %step.7 = (f32[8,8192]{1,0:T(8,128)S(1)}, f32[8,8192]{1,0:T(8,128)S(1)}) custom-call(s32[1]{0:T(128)} %bitcast.1.part, s32[8,128]{1,0:T(8,128)S(1)} %pad_add_fusion.blocks, s32[264,128]{1,0:T(8,128)S(1)} %get-tuple-element.68.refs_0_, s32[264,128]{1,0:T(8,128)S(1)} %copy-done.13, s32[264,128]{1,0:T(8,128)S(1)} %copy-done.9, ...), custom_call_target="tpu_custom_call" | custom-call | flops 536870912 | bytes 40000000 | tf_op jit(solution)/shard_map/step/pallas_call | solution.py:305
  317.2 2.4 collective-permute-start.12
  319.7 2.0 collective-permute-start.10
  321.6 5.1 %collective-permute-done.9.refs_2_ = f32[8,8192]{1,0:T(8,128)S(1)} collective-permute-done((f32[8,8192]{1,0:T(8,128)S(1)}, f32[8,8192]{1,0:T(8,128)S(1)}, u32[]{:S(2)}, u32[]{:S(2)}) %collective-permute-start.9) | collective-permute-done | bytes 262176 | tf_op jit(solution)/shard_map/ppermute | solution.py:395
  326.8 3.3 collective-permute-start.14
  330.0 2.0 collective-permute-done.11.refs_4_
  (74 shorter events, 16.9 us)
Async XLA Ops:
  0.6 42.6 %copy-start = (s32[16384]{0:T(1024)S(1)}, s32[16384]{0:T(1024)}, u32[]{:S(2)}) copy-start(s32[16384]{0:T(1024)} %param.18) | copy-start | bytes 196612
  9.2 51.5 %all-to-all-start = ((f32[32,32,512]{2,1,0:T(8,128)}), f32[32,32,512]{2,1,0:T(8,128)}, u32[]{:S(2)}, u32[]{:S(2)}) async-start(f32[32,32,512]{2,1,0:T(8,128)} %own_trial.1), calls=%async_computation | async-start | bytes 4194304 | tf_op jit(solution)/shard_map/all_to_all | solution.py:392
  16.9 44.4 %copy-start.20 = (f32[8]{0:T(128)S(1)}, f32[8]{0:T(128)}, u32[]{:S(2)}) copy-start(f32[8]{0:T(128)} %levels.7) | copy-start | bytes 100
  20.4 16.3 %collective-permute-start = (f32[8,16384]{1,0:T(8,128)S(1)}, f32[8,16384]{1,0:T(8,128)S(1)}, u32[]{:S(2)}, u32[]{:S(2)}) collective-permute-start(f32[8,16384]{1,0:T(8,128)S(1)} %get-tuple-element.60), channel_id=1, source_target_pairs={{0,1},{1,2},{2,3},{3,0},{4,5},{5,6},{6,7},{7,4},{8,9},{9,10},{10,1... | collective-permute-start | bytes 1572872 | tf_op jit(solution)/shard_map/ppermute | solution.py:395
  22.4 14.4 %collective-permute-start.1 = (f32[8,16384]{1,0:T(8,128)S(1)}, f32[8,16384]{1,0:T(8,128)}, u32[]{:S(2)}, u32[]{:S(2)}) collective-permute-start(f32[8,16384]{1,0:T(8,128)S(1)} %get-tuple-element.61), channel_id=1, source_target_pairs={{0,3},{1,0},{2,1},{3,2},{4,7},{5,4},{6,5},{7,6},{8,11},{9,8},{10,9... | collective-permute-start | bytes 1572872 | tf_op jit(solution)/shard_map/ppermute | solution.py:395
  36.8 23.8 %collective-permute-start.2 = (f32[8,16384]{1,0:T(8,128)S(1)}, f32[8,16384]{1,0:T(8,128)S(1)}, u32[]{:S(2)}, u32[]{:S(2)}) collective-permute-start(f32[8,16384]{1,0:T(8,128)S(1)} %collective-permute-done), channel_id=1, source_target_pairs={{0,1},{1,2},{2,3},{3,0},{4,5},{5,6},{6,7},{7,4},{8,9},{9,10},{10,1... | collective-permute-start | bytes 1572872 | tf_op jit(solution)/shard_map/ppermute | solution.py:395
  38.2 22.5 %collective-permute-start.3 = (f32[8,16384]{1,0:T(8,128)}, f32[8,16384]{1,0:T(8,128)S(1)}, u32[]{:S(2)}, u32[]{:S(2)}) collective-permute-start(f32[8,16384]{1,0:T(8,128)} %collective-permute-done.1), channel_id=1, source_target_pairs={{0,3},{1,0},{2,1},{3,2},{4,7},{5,4},{6,5},{7,6},{8,11},{9,8},{10,9... | collective-permute-start | bytes 1572872 | tf_op jit(solution)/shard_map/ppermute | solution.py:395
  40.0 16.8 %collective-permute-start.6 = (s32[264,128]{1,0:T(8,128)S(1)}, s32[264,128]{1,0:T(8,128)S(1)}, u32[]{:S(2)}, u32[]{:S(2)}) collective-permute-start(s32[264,128]{1,0:T(8,128)S(1)} %get-tuple-element.68.refs_0_), channel_id=1, source_target_pairs={{0,3},{1,0},{2,1},{3,2},{4,7},{5,4},{6,5},{7,6},{8,11},{9,8},{10,9... | collective-permute-start | bytes 405512 | tf_op jit(solution)/shard_map/ppermute | solution.py:395
  42.0 15.0 %collective-permute-start.5 = (s32[264,128]{1,0:T(8,128)S(1)}, s32[264,128]{1,0:T(8,128)S(1)}, u32[]{:S(2)}, u32[]{:S(2)}) collective-permute-start(s32[264,128]{1,0:T(8,128)S(1)} %get-tuple-element.68.refs_0_), channel_id=1, source_target_pairs={{0,2},{1,3},{2,0},{3,1},{4,6},{5,7},{6,4},{7,5},{8,10},{9,11},{10,... | collective-permute-start | bytes 405512 | tf_op jit(solution)/shard_map/ppermute | solution.py:395
  42.2 18.4 %collective-permute-start.4 = (s32[264,128]{1,0:T(8,128)S(1)}, s32[264,128]{1,0:T(8,128)S(1)}, u32[]{:S(2)}, u32[]{:S(2)}) collective-permute-start(s32[264,128]{1,0:T(8,128)S(1)} %get-tuple-element.68.refs_0_), channel_id=1, source_target_pairs={{0,1},{1,2},{2,3},{3,0},{4,5},{5,6},{6,7},{7,4},{8,9},{9,10},{10,1... | collective-permute-start | bytes 405512 | tf_op jit(solution)/shard_map/ppermute | solution.py:395
  56.9 27.0 %collective-permute-start.7 = (f32[16,16384]{1,0:T(8,128)}, f32[16,16384]{1,0:T(8,128)S(1)}, u32[]{:S(2)}, u32[]{:S(2)}) collective-permute-start(f32[16,16384]{1,0:T(8,128)} %get-tuple-element.74), channel_id=1, source_target_pairs={{0,1},{1,2},{2,3},{3,0},{4,5},{5,6},{6,7},{7,4},{8,9},{9,10},{10,1... | collective-permute-start | bytes 3145736 | tf_op jit(solution)/shard_map/ppermute | solution.py:395
  57.0 26.9 %collective-permute-start.8 = (f32[16,16384]{1,0:T(8,128)}, f32[16,16384]{1,0:T(8,128)}, u32[]{:S(2)}, u32[]{:S(2)}) collective-permute-start(f32[16,16384]{1,0:T(8,128)} %get-tuple-element.77), channel_id=1, source_target_pairs={{0,3},{1,0},{2,1},{3,2},{4,7},{5,4},{6,5},{7,6},{8,11},{9,8},{10,9... | collective-permute-start | bytes 3145736 | tf_op jit(solution)/shard_map/ppermute | solution.py:395
  60.6 24.6 %copy-start.4 = (f32[8,16384]{1,0:T(8,128)}, f32[8,16384]{1,0:T(8,128)S(1)}, u32[]{:S(2)}) copy-start(f32[8,16384]{1,0:T(8,128)S(1)} %collective-permute-done.3.refs_10_.refs_15_) | copy-start | bytes 1572868
  61.3 14.8 %slice-start.1 = ((s32[264,128]{1,0:T(8,128)}), s32[2,128]{1,0:T(2,128)S(1)}, s32[]{:S(2)}) async-start(s32[264,128]{1,0:T(8,128)} %copy-done.10), calls=%async_computation.10 | async-start | bytes 2048 | tf_op jit(solution)/shard_map/slice | solution.py:416
  61.3 23.9 %copy-start.2 = (f32[16,16384]{1,0:T(8,128)S(1)}, f32[16,16384]{1,0:T(8,128)}, u32[]{:S(2)}) copy-start(f32[16,16384]{1,0:T(8,128)} %get-tuple-element.73.refs_7_.refs_12_) | copy-start | bytes 3145732
  65.2 20.0 %all-to-all-start.1 = ((f32[128,4,128]{2,1,0:T(4,128)}), f32[128,4,128]{2,1,0:T(4,128)}, u32[]{:S(2)}, u32[]{:S(2)}) async-start(f32[128,4,128]{2,1,0:T(4,128)} %copy-done.14), calls=%async_computation.1 | async-start | bytes 524288 | tf_op jit(solution)/shard_map/all_to_all | solution.py:392
  141.5 16.5 %copy-start.1 = (f32[8,16384]{1,0:T(8,128)S(1)}, f32[8,16384]{1,0:T(8,128)}, u32[]{:S(2)}) copy-start(f32[8,16384]{1,0:T(8,128)} %get-tuple-element.104.refs_6_) | copy-start | bytes 1572868
  141.5 16.5 %copy-start.5 = (f32[8,16384]{1,0:T(8,128)S(1)}, f32[8,16384]{1,0:T(8,128)}, u32[]{:S(2)}) copy-start(f32[8,16384]{1,0:T(8,128)} %copy-done.4) | copy-start | bytes 1572868
  141.6 16.5 %copy-start.8 = (s32[264,128]{1,0:T(8,128)S(1)}, s32[264,128]{1,0:T(8,128)}, u32[]{:S(2)}) copy-start(s32[264,128]{1,0:T(8,128)} %copy-done.6) | copy-start | bytes 405508
  141.6 16.5 %copy-start.12 = (s32[264,128]{1,0:T(8,128)S(1)}, s32[264,128]{1,0:T(8,128)}, u32[]{:S(2)}) copy-start(s32[264,128]{1,0:T(8,128)} %copy-done.10) | copy-start | bytes 405508
  243.5 34.9 %copy-start.3 = (f32[128,8,512]{2,1,0:T(8,128)}, f32[128,8,512]{2,1,0:T(8,128)S(1)}, u32[]{:S(2)}) copy-start(f32[128,8,512]{2,1,0:T(8,128)S(1)} %get-tuple-element.90.refs_7_) | copy-start | bytes 6291460
  243.5 34.9 %copy-start.15 = (f32[8,16384]{1,0:T(8,128)}, f32[8,16384]{1,0:T(8,128)S(1)}, u32[]{:S(2)}) copy-start(f32[8,16384]{1,0:T(8,128)S(1)} %get-tuple-element.93.refs_5_) | copy-start | bytes 1572868
  243.5 34.9 %copy-start.16 = (f32[8,16384]{1,0:T(8,128)}, f32[8,16384]{1,0:T(8,128)S(1)}, u32[]{:S(2)}) copy-start(f32[8,16384]{1,0:T(8,128)S(1)} %get-tuple-element.94.refs_8_) | copy-start | bytes 1572868
  243.5 34.9 %copy-start.17 = (f32[8,16384]{1,0:T(8,128)}, f32[8,16384]{1,0:T(8,128)S(1)}, u32[]{:S(2)}) copy-start(f32[8,16384]{1,0:T(8,128)S(1)} %get-tuple-element.95.refs_9_) | copy-start | bytes 1572868
  243.5 34.9 %copy-start.18 = (f32[8,16384]{1,0:T(8,128)}, f32[8,16384]{1,0:T(8,128)S(1)}, u32[]{:S(2)}) copy-start(f32[8,16384]{1,0:T(8,128)S(1)} %get-tuple-element.96.refs_10_) | copy-start | bytes 1572868
  296.4 37.4 %all-to-all-start.7 = ((f32[32,32,512]{2,1,0:T(8,128)}), f32[32,32,512]{2,1,0:T(8,128)S(1)}, u32[]{:S(2)}, u32[]{:S(2)}) async-start(f32[32,32,512]{2,1,0:T(8,128)} %bitcast.7), calls=%async_computation.7 | async-start | bytes 4194304 | tf_op jit(solution)/shard_map/all_to_all | solution.py:392
  316.3 10.4 %collective-permute-start.9 = (f32[8,8192]{1,0:T(8,128)S(1)}, f32[8,8192]{1,0:T(8,128)S(1)}, u32[]{:S(2)}, u32[]{:S(2)}) collective-permute-start(f32[8,8192]{1,0:T(8,128)S(1)} %get-tuple-element.98.refs_0_), channel_id=1, source_target_pairs={{0,1},{1,2},{2,3},{3,0},{4,5},{5,6},{6,7},{7,4},{8,9},{9,10},{10,1... | collective-permute-start | bytes 786440 | tf_op jit(solution)/shard_map/ppermute | solution.py:395
  317.2 9.5 %collective-permute-start.12 = (f32[8,8192]{1,0:T(8,128)S(1)}, f32[8,8192]{1,0:T(8,128)S(1)}, u32[]{:S(2)}, u32[]{:S(2)}) collective-permute-start(f32[8,8192]{1,0:T(8,128)S(1)} %get-tuple-element.99.refs_1_), channel_id=1, source_target_pairs={{0,3},{1,0},{2,1},{3,2},{4,7},{5,4},{6,5},{7,6},{8,11},{9,8},{10,9... | collective-permute-start | bytes 786440 | tf_op jit(solution)/shard_map/ppermute | solution.py:395
  319.6 12.4 %collective-permute-start.11 = (f32[8,8192]{1,0:T(8,128)S(1)}, f32[8,8192]{1,0:T(8,128)S(1)}, u32[]{:S(2)}, u32[]{:S(2)}) collective-permute-start(f32[8,8192]{1,0:T(8,128)S(1)} %get-tuple-element.98.refs_0_), channel_id=1, source_target_pairs={{0,3},{1,0},{2,1},{3,2},{4,7},{5,4},{6,5},{7,6},{8,11},{9,8},{10,9... | collective-permute-start | bytes 786440 | tf_op jit(solution)/shard_map/ppermute | solution.py:395
  319.7 12.7 %collective-permute-start.10 = (f32[8,8192]{1,0:T(8,128)S(1)}, f32[8,8192]{1,0:T(8,128)S(1)}, u32[]{:S(2)}, u32[]{:S(2)}) collective-permute-start(f32[8,8192]{1,0:T(8,128)S(1)} %get-tuple-element.99.refs_1_), channel_id=1, source_target_pairs={{0,1},{1,2},{2,3},{3,0},{4,5},{5,6},{6,7},{7,4},{8,9},{9,10},{10,1... | collective-permute-start | bytes 786440 | tf_op jit(solution)/shard_map/ppermute | solution.py:395
  326.7 10.4 %collective-permute-start.13 = (f32[8,8192]{1,0:T(8,128)S(1)}, f32[8,8192]{1,0:T(8,128)S(1)}, u32[]{:S(2)}, u32[]{:S(2)}) collective-permute-start(f32[8,8192]{1,0:T(8,128)S(1)} %collective-permute-done.9.refs_2_), channel_id=1, source_target_pairs={{0,1},{1,2},{2,3},{3,0},{4,5},{5,6},{6,7},{7,4},{8,9},{9,10},{10,1... | collective-permute-start | bytes 786440 | tf_op jit(solution)/shard_map/ppermute | solution.py:395
  326.8 10.4 %collective-permute-start.14 = (f32[8,8192]{1,0:T(8,128)S(1)}, f32[8,8192]{1,0:T(8,128)S(1)}, u32[]{:S(2)}, u32[]{:S(2)}) collective-permute-start(f32[8,8192]{1,0:T(8,128)S(1)} %collective-permute-done.12.refs_5_), channel_id=1, source_target_pairs={{0,3},{1,0},{2,1},{3,2},{4,7},{5,4},{6,5},{7,6},{8,11},{9,8},{10,9... | collective-permute-start | bytes 786440 | tf_op jit(solution)/shard_map/ppermute | solution.py:395
  (9 other events, 34.6 us)

commit v9 on v8

--- a/solution.py
+++ b/solution.py
@@ -399,12 +399,13 @@
 
     own = part.astype(jnp.int32).reshape(1)
     ids = [head_rows, tail_rows, head_block.reshape(1, BLOCK), tail_block.reshape(1, BLOCK)]
-    first = own_trial(head_block, tail_block, head_rows, tail_rows, price_start, flow_start, cost)
-    first, flow_start, cost, ids = lax.optimization_barrier((first, flow_start, cost, ids))
-    values = exchange(first, "com").reshape(OWNERS * SHARDS, 8, OWN)
-    here, near, far_flow, far_cost, behind, packed = pack(own, flow_start, cost, ids)
+    pieces = pack(own, flow_start, cost, ids)
+    pieces, flow_start, cost, price_start = lax.optimization_barrier((pieces, flow_start, cost, price_start))
+    here, near, far_flow, far_cost, behind, packed = pieces
     far_flow = around(far_flow, 1)
     far_cost = around(far_cost, 3)
+    first = own_trial(head_block, tail_block, head_rows, tail_rows, price_start, flow_start, cost)
+    values = exchange(first, "com").reshape(OWNERS * SHARDS, 8, OWN)
     far_flow, far_cost, packed, near, behind = lax.optimization_barrier((far_flow, far_cost, packed, near, behind))
     far_flow = around(far_flow, 1)
     far_cost = around(far_cost, 3)

time: 339 us -> 326 us (0.962)
  waiting for transfers between devices: 44.2 us -> 30.2 us
    ppermute x15, waiting for transfers between devices: 42.9 us -> 26.7 us  [around(): lax.ppermute(values, 'arc', [(i, (i + k) % SHARDS) for i in range(SHARDS)])]
  transfers between devices with their start and end apart: 18 -> 18, of which waited for: 9 -> 8; matrix products, arithmetic and copies ran while one was open for 1% -> 2% of each run, Pallas kernels for 7% -> 8%
where the time goes in v9:
time: 326 us; the launch traced here: 325 us
  blocking collectives  149 us (46%)
  Pallas kernels  90.6 us (28%)
  starting transfers between devices  44.1 us (14%)
  waiting for transfers between devices  30.2 us (9%)
  local copies, waits for them, and re-layouts  10.9 us (3%)
    all_to_all x6, blocking collectives, exchange(): return lax.all_to_all(values, axes, split_axis=0, concat_axis=0, tiled=True)  149 us
    pallas_call x4, Pallas kernels, advance(): pl.pallas_call(functools.partial(step_kernel, first=first, last=last), in...  66.6 us
    ppermute x15, waiting for transfers between devices, around(): lax.ppermute(values, 'arc', [(i, (i + k) % SHARDS) for i in range(SHARDS)])  26.7 us
    ppermute x15, starting transfers between devices, around(): lax.ppermute(values, 'arc', [(i, (i + k) % SHARDS) for i in range(SHARDS)])  22.6 us
    all_to_all x3, starting transfers between devices, exchange(): return lax.all_to_all(values, axes, split_axis=0, concat_axis=0, tiled=True)  21.5 us
    pallas_call x4, Pallas kernels, project(): pl.pallas_call(project_kernel, in_specs=[smem, vmem, vmem], out_specs=[vm...  9.5 us
    pallas_call x1, Pallas kernels, own_trial(): pl.pallas_call(own_trial_kernel, grid=(SHARDS, OWNERS * OWN // CHUNK), in...  8.51 us
  transfers between devices with their start and end apart: 18, of which 8 were waited for; matrix products, arithmetic and copies ran while one was open for 2% of the time, Pallas kernels for 8%

profile of v9, /device:TPU:6, one launch (start us, length us, event | category | flops | bytes accessed | tf_op | source)
XLA Modules:
  0.0 325.4 jit_solution(1477961087648281814)
XLA Ops:
  0.6 3.7 %pack.1 = (f32[16,16384]{1,0:T(8,128)}, f32[16,16384]{1,0:T(8,128)}, f32[8,16384]{1,0:T(8,128)S(1)}, f32[8,16384]{1,0:T(8,128)S(1)}, f32[16,16384]{1,0:T(8,128)}, /*index=5*/s32[264,128]{1,0:T(8,128)S(1)}) custom-call(s32[1]{0:T(128)} %bitcast.1.part, f32[32,16384]{1,0:T(8,128)} %flow, f32[32,16384]{1,0:T(8,128)} %flow, f32[32,16384]{1,0:T(8,128)} %flow, ...), custom_call_target="tpu_custom_call" | custom-call | tf_op jit(solution)/shard_map/pack/pallas_call | solution.py:241
  6.3 2.2 collective-permute-start.1
  8.5 8.5 %own_trial.1 = f32[32,32,512]{2,1,0:T(8,128)} custom-call(s32[128]{0:T(128)} %head_block.1, s32[128]{0:T(128)} %tail_block.1, s32[128,128]{1,0:T(8,128)} %bitcast.14, s32[128,128]{1,0:T(8,128)} %bitcast.16, f32[32,16384]{1,0:T(8,128)} %price, f32[32,16384]{1,0:T(8,128)} %flow, f32[32,16384]{1,0:T(8,128)} %cost), custom_call_target="tpu_custom_call" | custom-call | tf_op jit(solution)/shard_map/own_trial/pallas_call | solution.py:257
  17.0 7.7 %all-to-all-start = ((f32[32,32,512]{2,1,0:T(8,128)}), f32[32,32,512]{2,1,0:T(8,128)}, u32[]{:S(2)}, u32[]{:S(2)}) async-start(f32[32,32,512]{2,1,0:T(8,128)} %own_trial.1), calls=%async_computation | async-start | bytes 4194304 | tf_op jit(solution)/shard_map/all_to_all | solution.py:392
  24.7 2.0 collective-permute-start.6
  28.0 2.2 collective-permute-start.2
  35.0 2.2 collective-permute-start.8
  37.3 10.7 %collective-permute-done.2.refs_9_.refs_14_ = f32[8,16384]{1,0:T(8,128)} collective-permute-done((f32[8,16384]{1,0:T(8,128)}, f32[8,16384]{1,0:T(8,128)}, u32[]{:S(2)}, u32[]{:S(2)}) %collective-permute-start.2) | collective-permute-done | bytes 524320 | tf_op jit(solution)/shard_map/ppermute | solution.py:395
  48.0 3.1 all-to-all-done
  51.8 3.1 project.4
  55.6 7.3 %all-to-all-start.1 = ((f32[128,4,128]{2,1,0:T(4,128)}), f32[128,4,128]{2,1,0:T(4,128)}, u32[]{:S(2)}, u32[]{:S(2)}) async-start(f32[128,4,128]{2,1,0:T(4,128)} %copy-done.6), calls=%async_computation.1 | async-start | bytes 524288 | tf_op jit(solution)/shard_map/all_to_all | solution.py:392
  64.4 8.3 %collective-permute-done.7.refs_8_.refs_13_ = f32[16,16384]{1,0:T(8,128)} collective-permute-done((f32[16,16384]{1,0:T(8,128)}, f32[16,16384]{1,0:T(8,128)}, u32[]{:S(2)}, u32[]{:S(2)}) %collective-permute-start.7) | collective-permute-done | bytes 1048608 | tf_op jit(solution)/shard_map/ppermute | solution.py:395
  73.1 18.1 %step.4 = (f32[128,8,512]{2,1,0:T(8,128)S(1)}, f32[8,16384]{1,0:T(8,128)S(1)}, f32[8,16384]{1,0:T(8,128)S(1)}, f32[8,16384]{1,0:T(8,128)S(1)}, f32[8,16384]{1,0:T(8,128)S(1)}, /*index=5*/f32[8,16384]{1,0:T(8,128)S(1)}) custom-call(s32[1]{0:T(128)} %bitcast.1.part, s32[8,128]{1,0:T(8,128)S(1)} %pad_add_fusion.blocks, ...), custom_call_target="tpu_custom_call" | custom-call | flops 536870912 | bytes 40000000 | tf_op jit(solution)/shard_map/step/pallas_call | solution.py:305
  91.3 35.8 %all_to_all.45.values = f32[128,8,512]{2,1,0:T(8,128)S(1)} all-to-all(f32[128,8,512]{2,1,0:T(8,128)S(1)} %get-tuple-element.82.refs_7_), channel_id=1, replica_groups=mesh['com'=32,'arc'=4] {'com','arc'}, dimensions={0} | all-to-all | bytes 4194304 | tf_op jit(solution)/shard_map/all_to_all | solution.py:392
  127.1 2.1 project.5
  129.1 14.4 %all_to_all.46.refs_4_ = f32[128,4,128]{2,1,0:T(4,128)S(1)} all-to-all(f32[128,4,128]{2,1,0:T(4,128)S(1)} %project.5), channel_id=1, replica_groups=mesh['com'=32,'arc'=4] {'com','arc'}, dimensions={0} | all-to-all | bytes 524288 | tf_op jit(solution)/shard_map/all_to_all | solution.py:392
  143.6 17.3 %step.5 = (f32[128,8,512]{2,1,0:T(8,128)S(1)}, f32[8,16384]{1,0:T(8,128)S(1)}, f32[8,16384]{1,0:T(8,128)S(1)}, f32[8,16384]{1,0:T(8,128)S(1)}, f32[8,16384]{1,0:T(8,128)S(1)}, /*index=5*/f32[8,16384]{1,0:T(8,128)S(1)}) custom-call(s32[1]{0:T(128)} %bitcast.1.part, s32[8,128]{1,0:T(8,128)S(1)} %pad_add_fusion.blocks, ...), custom_call_target="tpu_custom_call" | custom-call | flops 536870912 | bytes 40000000 | tf_op jit(solution)/shard_map/step/pallas_call | solution.py:305
  160.9 34.9 %all_to_all.47.values = f32[128,8,512]{2,1,0:T(8,128)S(1)} all-to-all(f32[128,8,512]{2,1,0:T(8,128)S(1)} %get-tuple-element.88.refs_7_), channel_id=1, replica_groups=mesh['com'=32,'arc'=4] {'com','arc'}, dimensions={0} | all-to-all | bytes 4194304 | tf_op jit(solution)/shard_map/all_to_all | solution.py:392
  195.7 2.1 project.6
  197.8 14.4 %all_to_all.48.refs_4_ = f32[128,4,128]{2,1,0:T(4,128)S(1)} all-to-all(f32[128,4,128]{2,1,0:T(4,128)S(1)} %project.6), channel_id=1, replica_groups=mesh['com'=32,'arc'=4] {'com','arc'}, dimensions={0} | all-to-all | bytes 524288 | tf_op jit(solution)/shard_map/all_to_all | solution.py:392
  212.3 17.3 %step.6 = (f32[128,8,512]{2,1,0:T(8,128)S(1)}, f32[8,16384]{1,0:T(8,128)S(1)}, f32[8,16384]{1,0:T(8,128)S(1)}, f32[8,16384]{1,0:T(8,128)S(1)}, f32[8,16384]{1,0:T(8,128)S(1)}, /*index=5*/f32[8,16384]{1,0:T(8,128)S(1)}) custom-call(s32[1]{0:T(128)} %bitcast.1.part, s32[8,128]{1,0:T(8,128)S(1)} %pad_add_fusion.blocks, ...), custom_call_target="tpu_custom_call" | custom-call | flops 536870912 | bytes 40000000 | tf_op jit(solution)/shard_map/step/pallas_call | solution.py:305
  230.4 34.9 %all_to_all.49.values = f32[128,8,512]{2,1,0:T(8,128)S(1)} all-to-all(f32[128,8,512]{2,1,0:T(8,128)S(1)} %get-tuple-element.94.refs_7_), channel_id=1, replica_groups=mesh['com'=32,'arc'=4] {'com','arc'}, dimensions={0} | all-to-all | bytes 4194304 | tf_op jit(solution)/shard_map/all_to_all | solution.py:392
  265.3 2.3 project.7
  268.9 14.4 %all_to_all.50.refs_4_ = f32[128,4,128]{2,1,0:T(4,128)S(1)} all-to-all(f32[128,4,128]{2,1,0:T(4,128)S(1)} %get-tuple-element.96), channel_id=1, replica_groups=mesh['com'=32,'arc'=4] {'com','arc'}, dimensions={0} | all-to-all | bytes 524288 | tf_op jit(solution)/shard_map/all_to_all | solution.py:392
  283.3 6.6 %all-to-all-start.7 = ((f32[32,32,512]{2,1,0:T(8,128)}), f32[32,32,512]{2,1,0:T(8,128)}, u32[]{:S(2)}, u32[]{:S(2)}) async-start(f32[32,32,512]{2,1,0:T(8,128)} %bitcast.11), calls=%async_computation.7 | async-start | bytes 4194304 | tf_op jit(solution)/shard_map/all_to_all | solution.py:392
  289.9 13.8 %step.7 = (f32[8,8192]{1,0:T(8,128)S(1)}, f32[8,8192]{1,0:T(8,128)S(1)}) custom-call(s32[1]{0:T(128)} %bitcast.1.part, s32[8,128]{1,0:T(8,128)S(1)} %pad_add_fusion.blocks, s32[264,128]{1,0:T(8,128)S(1)} %get-tuple-element.72.refs_0_, s32[264,128]{1,0:T(8,128)} %collective-permute-done.4.refs_1_, s32[264,128]{1,0:T(8,128)S(1)} %collective-permute-done.5.refs_2_, ...), custom_call_target="tpu_custom_call" | custom-call | flops 536870912 | bytes 40000000 | tf_op jit(solution)/shard_map/step/pallas_call | solution.py:305
  304.6 2.4 collective-permute-start.12
  307.1 2.0 collective-permute-start.10
  309.1 5.1 %collective-permute-done.9.refs_2_ = f32[8,8192]{1,0:T(8,128)S(1)} collective-permute-done((f32[8,8192]{1,0:T(8,128)S(1)}, f32[8,8192]{1,0:T(8,128)S(1)}, u32[]{:S(2)}, u32[]{:S(2)}) %collective-permute-start.9) | collective-permute-done | bytes 262176 | tf_op jit(solution)/shard_map/ppermute | solution.py:395
  314.2 3.3 %collective-permute-start.14 = (f32[8,8192]{1,0:T(8,128)S(1)}, f32[8,8192]{1,0:T(8,128)S(1)}, u32[]{:S(2)}, u32[]{:S(2)}) collective-permute-start(f32[8,8192]{1,0:T(8,128)S(1)} %collective-permute-done.12.refs_5_), channel_id=1, source_target_pairs={{0,3},{1,0},{2,1},{3,2},{4,7},{5,4},{6,5},{7,6},{8,11},{9,8},{10,9... | collective-permute-start | bytes 786440 | tf_op jit(solution)/shard_map/ppermute | solution.py:395
  317.4 2.0 collective-permute-done.11.refs_4_
  321.3 3.1 copy.14
  (63 shorter events, 17.3 us)
Async XLA Ops:
  0.6 62.2 %copy-start = (f32[32,16384]{1,0:T(8,128)S(1)}, f32[32,16384]{1,0:T(8,128)}, u32[]{:S(2)}) copy-start(f32[32,16384]{1,0:T(8,128)} %param.13) | copy-start | bytes 6291460
  4.3 20.4 %collective-permute-start = (f32[8,16384]{1,0:T(8,128)S(1)}, f32[8,16384]{1,0:T(8,128)}, u32[]{:S(2)}, u32[]{:S(2)}) collective-permute-start(f32[8,16384]{1,0:T(8,128)S(1)} %get-tuple-element.64), channel_id=1, source_target_pairs={{0,1},{1,2},{2,3},{3,0},{4,5},{5,6},{6,7},{7,4},{8,9},{9,10},{10,1... | collective-permute-start | bytes 1572872 | tf_op jit(solution)/shard_map/ppermute | solution.py:395
  6.3 18.4 %collective-permute-start.1 = (f32[8,16384]{1,0:T(8,128)S(1)}, f32[8,16384]{1,0:T(8,128)}, u32[]{:S(2)}, u32[]{:S(2)}) collective-permute-start(f32[8,16384]{1,0:T(8,128)S(1)} %get-tuple-element.65), channel_id=1, source_target_pairs={{0,3},{1,0},{2,1},{3,2},{4,7},{5,4},{6,5},{7,6},{8,11},{9,8},{10,9... | collective-permute-start | bytes 1572872 | tf_op jit(solution)/shard_map/ppermute | solution.py:395
  17.0 34.1 %all-to-all-start = ((f32[32,32,512]{2,1,0:T(8,128)}), f32[32,32,512]{2,1,0:T(8,128)}, u32[]{:S(2)}, u32[]{:S(2)}) async-start(f32[32,32,512]{2,1,0:T(8,128)} %own_trial.1), calls=%async_computation | async-start | bytes 4194304 | tf_op jit(solution)/shard_map/all_to_all | solution.py:392
  24.7 9.2 %collective-permute-start.6 = (s32[264,128]{1,0:T(8,128)S(1)}, s32[264,128]{1,0:T(8,128)S(1)}, u32[]{:S(2)}, u32[]{:S(2)}) collective-permute-start(s32[264,128]{1,0:T(8,128)S(1)} %get-tuple-element.72.refs_0_), channel_id=1, source_target_pairs={{0,3},{1,0},{2,1},{3,2},{4,7},{5,4},{6,5},{7,6},{8,11},{9,8},{10,9... | collective-permute-start | bytes 405512 | tf_op jit(solution)/shard_map/ppermute | solution.py:395
  26.7 8.3 %collective-permute-start.5 = (s32[264,128]{1,0:T(8,128)S(1)}, s32[264,128]{1,0:T(8,128)S(1)}, u32[]{:S(2)}, u32[]{:S(2)}) collective-permute-start(s32[264,128]{1,0:T(8,128)S(1)} %get-tuple-element.72.refs_0_), channel_id=1, source_target_pairs={{0,2},{1,3},{2,0},{3,1},{4,6},{5,7},{6,4},{7,5},{8,10},{9,11},{10,... | collective-permute-start | bytes 405512 | tf_op jit(solution)/shard_map/ppermute | solution.py:395
  26.7 10.5 %collective-permute-start.4 = (s32[264,128]{1,0:T(8,128)S(1)}, s32[264,128]{1,0:T(8,128)}, u32[]{:S(2)}, u32[]{:S(2)}) collective-permute-start(s32[264,128]{1,0:T(8,128)S(1)} %get-tuple-element.72.refs_0_), channel_id=1, source_target_pairs={{0,1},{1,2},{2,3},{3,0},{4,5},{5,6},{6,7},{7,4},{8,9},{9,10},{10,1... | collective-permute-start | bytes 405512 | tf_op jit(solution)/shard_map/ppermute | solution.py:395
  28.0 19.9 %collective-permute-start.2 = (f32[8,16384]{1,0:T(8,128)}, f32[8,16384]{1,0:T(8,128)}, u32[]{:S(2)}, u32[]{:S(2)}) collective-permute-start(f32[8,16384]{1,0:T(8,128)} %collective-permute-done), channel_id=1, source_target_pairs={{0,1},{1,2},{2,3},{3,0},{4,5},{5,6},{6,7},{7,4},{8,9},{9,10},{10,1... | collective-permute-start | bytes 1572872 | tf_op jit(solution)/shard_map/ppermute | solution.py:395
  30.2 17.7 %collective-permute-start.3 = (f32[8,16384]{1,0:T(8,128)}, f32[8,16384]{1,0:T(8,128)}, u32[]{:S(2)}, u32[]{:S(2)}) collective-permute-start(f32[8,16384]{1,0:T(8,128)} %collective-permute-done.1), channel_id=1, source_target_pairs={{0,3},{1,0},{2,1},{3,2},{4,7},{5,4},{6,5},{7,6},{8,11},{9,8},{10,9... | collective-permute-start | bytes 1572872 | tf_op jit(solution)/shard_map/ppermute | solution.py:395
  33.2 40.0 %copy-start.2 = (f32[16,16384]{1,0:T(8,128)S(1)}, f32[16,16384]{1,0:T(8,128)}, u32[]{:S(2)}) copy-start(f32[16,16384]{1,0:T(8,128)} %get-tuple-element.77.refs_7_.refs_12_) | copy-start | bytes 3145732
  34.0 30.4 %copy-start.12 = (s32[4,128]{1,0:T(4,128)}, s32[4,128]{1,0:T(4,128)S(1)}, u32[]{:S(2)}) copy-start(s32[4,128]{1,0:T(4,128)S(1)} %constant_dynamic-slice_fusion.2.classes) | copy-start | bytes 6148
  34.0 38.8 %collective-permute-start.7 = (f32[16,16384]{1,0:T(8,128)}, f32[16,16384]{1,0:T(8,128)}, u32[]{:S(2)}, u32[]{:S(2)}) collective-permute-start(f32[16,16384]{1,0:T(8,128)} %get-tuple-element.78), channel_id=1, source_target_pairs={{0,1},{1,2},{2,3},{3,0},{4,5},{5,6},{6,7},{7,4},{8,9},{9,10},{10,1... | collective-permute-start | bytes 3145736 | tf_op jit(solution)/shard_map/ppermute | solution.py:395
  35.0 37.7 %collective-permute-start.8 = (f32[16,16384]{1,0:T(8,128)}, f32[16,16384]{1,0:T(8,128)}, u32[]{:S(2)}, u32[]{:S(2)}) collective-permute-start(f32[16,16384]{1,0:T(8,128)} %get-tuple-element.81), channel_id=1, source_target_pairs={{0,3},{1,0},{2,1},{3,2},{4,7},{5,4},{6,5},{7,6},{8,11},{9,8},{10,9... | collective-permute-start | bytes 3145736 | tf_op jit(solution)/shard_map/ppermute | solution.py:395
  55.6 17.5 %all-to-all-start.1 = ((f32[128,4,128]{2,1,0:T(4,128)}), f32[128,4,128]{2,1,0:T(4,128)}, u32[]{:S(2)}, u32[]{:S(2)}) async-start(f32[128,4,128]{2,1,0:T(4,128)} %copy-done.6), calls=%async_computation.1 | async-start | bytes 524288 | tf_op jit(solution)/shard_map/all_to_all | solution.py:392
  91.2 35.8 %copy-start.13 = (s32[4,128]{1,0:T(4,128)S(1)}, s32[4,128]{1,0:T(4,128)}, u32[]{:S(2)}) copy-start(s32[4,128]{1,0:T(4,128)} %copy-done.12) | copy-start | bytes 6148
  91.3 35.8 %copy-start.15 = (f32[8]{0:T(128)S(1)}, f32[8]{0:T(128)}, u32[]{:S(2)}) copy-start(f32[8]{0:T(128)} %levels.7) | copy-start | bytes 100
  127.1 16.5 %copy-start.1 = (f32[8,16384]{1,0:T(8,128)S(1)}, f32[8,16384]{1,0:T(8,128)}, u32[]{:S(2)}) copy-start(f32[8,16384]{1,0:T(8,128)} %constant_dynamic-slice_fusion.refs_6_) | copy-start | bytes 1572868
  127.1 16.5 %copy-start.3 = (f32[16,16384]{1,0:T(8,128)S(1)}, f32[16,16384]{1,0:T(8,128)}, u32[]{:S(2)}) copy-start(f32[16,16384]{1,0:T(8,128)} %get-tuple-element.77.refs_7_.refs_12_) | copy-start | bytes 3145732
  229.6 0.8 copy-start.11
  230.4 34.9 %copy-start.4 = (f32[128,8,512]{2,1,0:T(8,128)}, f32[128,8,512]{2,1,0:T(8,128)S(1)}, u32[]{:S(2)}) copy-start(f32[128,8,512]{2,1,0:T(8,128)S(1)} %get-tuple-element.94.refs_7_) | copy-start | bytes 6291460
  230.4 34.9 %copy-start.7 = (f32[8,16384]{1,0:T(8,128)}, f32[8,16384]{1,0:T(8,128)S(1)}, u32[]{:S(2)}) copy-start(f32[8,16384]{1,0:T(8,128)S(1)} %get-tuple-element.97.refs_5_) | copy-start | bytes 1572868
  230.4 34.9 %copy-start.8 = (f32[8,16384]{1,0:T(8,128)}, f32[8,16384]{1,0:T(8,128)S(1)}, u32[]{:S(2)}) copy-start(f32[8,16384]{1,0:T(8,128)S(1)} %get-tuple-element.98.refs_8_) | copy-start | bytes 1572868
  230.4 34.9 %copy-start.9 = (f32[8,16384]{1,0:T(8,128)}, f32[8,16384]{1,0:T(8,128)S(1)}, u32[]{:S(2)}) copy-start(f32[8,16384]{1,0:T(8,128)S(1)} %get-tuple-element.99.refs_9_) | copy-start | bytes 1572868
  230.4 34.9 %copy-start.10 = (f32[8,16384]{1,0:T(8,128)}, f32[8,16384]{1,0:T(8,128)S(1)}, u32[]{:S(2)}) copy-start(f32[8,16384]{1,0:T(8,128)S(1)} %get-tuple-element.100.refs_10_) | copy-start | bytes 1572868
  267.6 1.3 copy-start.5
  283.3 38.0 %all-to-all-start.7 = ((f32[32,32,512]{2,1,0:T(8,128)}), f32[32,32,512]{2,1,0:T(8,128)}, u32[]{:S(2)}, u32[]{:S(2)}) async-start(f32[32,32,512]{2,1,0:T(8,128)} %bitcast.11), calls=%async_computation.7 | async-start | bytes 4194304 | tf_op jit(solution)/shard_map/all_to_all | solution.py:392
  303.7 10.4 %collective-permute-start.9 = (f32[8,8192]{1,0:T(8,128)S(1)}, f32[8,8192]{1,0:T(8,128)S(1)}, u32[]{:S(2)}, u32[]{:S(2)}) collective-permute-start(f32[8,8192]{1,0:T(8,128)S(1)} %get-tuple-element.102.refs_0_), channel_id=1, source_target_pairs={{0,1},{1,2},{2,3},{3,0},{4,5},{5,6},{6,7},{7,4},{8,9},{9,10},{10,1... | collective-permute-start | bytes 786440 | tf_op jit(solution)/shard_map/ppermute | solution.py:395
  304.6 9.5 %collective-permute-start.12 = (f32[8,8192]{1,0:T(8,128)S(1)}, f32[8,8192]{1,0:T(8,128)S(1)}, u32[]{:S(2)}, u32[]{:S(2)}) collective-permute-start(f32[8,8192]{1,0:T(8,128)S(1)} %get-tuple-element.103.refs_1_), channel_id=1, source_target_pairs={{0,3},{1,0},{2,1},{3,2},{4,7},{5,4},{6,5},{7,6},{8,11},{9,8},{10,9... | collective-permute-start | bytes 786440 | tf_op jit(solution)/shard_map/ppermute | solution.py:395
  307.0 12.4 %collective-permute-start.11 = (f32[8,8192]{1,0:T(8,128)S(1)}, f32[8,8192]{1,0:T(8,128)S(1)}, u32[]{:S(2)}, u32[]{:S(2)}) collective-permute-start(f32[8,8192]{1,0:T(8,128)S(1)} %get-tuple-element.102.refs_0_), channel_id=1, source_target_pairs={{0,3},{1,0},{2,1},{3,2},{4,7},{5,4},{6,5},{7,6},{8,11},{9,8},{10,9... | collective-permute-start | bytes 786440 | tf_op jit(solution)/shard_map/ppermute | solution.py:395
  307.1 12.7 %collective-permute-start.10 = (f32[8,8192]{1,0:T(8,128)S(1)}, f32[8,8192]{1,0:T(8,128)S(1)}, u32[]{:S(2)}, u32[]{:S(2)}) collective-permute-start(f32[8,8192]{1,0:T(8,128)S(1)} %get-tuple-element.103.refs_1_), channel_id=1, source_target_pairs={{0,1},{1,2},{2,3},{3,0},{4,5},{5,6},{6,7},{7,4},{8,9},{9,10},{10,1... | collective-permute-start | bytes 786440 | tf_op jit(solution)/shard_map/ppermute | solution.py:395
  314.2 10.4 %collective-permute-start.13 = (f32[8,8192]{1,0:T(8,128)S(1)}, f32[8,8192]{1,0:T(8,128)S(1)}, u32[]{:S(2)}, u32[]{:S(2)}) collective-permute-start(f32[8,8192]{1,0:T(8,128)S(1)} %collective-permute-done.9.refs_2_), channel_id=1, source_target_pairs={{0,1},{1,2},{2,3},{3,0},{4,5},{5,6},{6,7},{7,4},{8,9},{9,10},{10,1... | collective-permute-start | bytes 786440 | tf_op jit(solution)/shard_map/ppermute | solution.py:395
  314.2 10.4 %collective-permute-start.14 = (f32[8,8192]{1,0:T(8,128)S(1)}, f32[8,8192]{1,0:T(8,128)S(1)}, u32[]{:S(2)}, u32[]{:S(2)}) collective-permute-start(f32[8,8192]{1,0:T(8,128)S(1)} %collective-permute-done.12.refs_5_), channel_id=1, source_target_pairs={{0,3},{1,0},{2,1},{3,2},{4,7},{5,4},{6,5},{7,6},{8,11},{9,8},{10,9... | collective-permute-start | bytes 786440 | tf_op jit(solution)/shard_map/ppermute | solution.py:395
  (2 other events, 1.4 us)

commit v10 on v9

--- a/solution.py
+++ b/solution.py
@@ -26,6 +26,9 @@
 
 f32 = jnp.float32
 bf16 = jnp.bfloat16
+narrow = jnp.float8_e4m3fn
+PART = 32
+PARTS = 16
 vmem = pl.BlockSpec(memory_space=pltpu.VMEM)
 smem = pl.BlockSpec(memory_space=pltpu.SMEM)
 
@@ -145,9 +148,55 @@
         lax.fori_loop(0, groups // 8, keep, 0)
 
 
+def ends_table(local, j):
+    nodes = lax.broadcasted_iota(jnp.int32, (BLOCK, BLOCK), 0).astype(jnp.int16)
+    one = jnp.ones((), bf16)
+    zero = jnp.zeros((), bf16)
+
+    def table(row):
+        return jnp.where(nodes == jnp.broadcast_to(row.astype(jnp.int16), (BLOCK, BLOCK)), one, zero)
+
+    return jnp.concatenate([table(local[pl.ds(j, 1), :]), table(local[pl.ds(BLOCK + j, 1), :])], axis=0)
+
+
+def select_kernel(local, out):
+    first = pl.program_id(1) * PART
+    rows = lax.broadcasted_iota(jnp.int32, (BLOCK, BLOCK), 0)
+    cols = lax.broadcasted_iota(jnp.int32, (BLOCK, BLOCK), 1)
+    eye = jnp.where(rows == cols, 1.0, 0.0).astype(bf16)
+    for i in range(PART):
+        turned = lax.dot_general(
+            eye, ends_table(local.at[0], first + i), (((1,), (1,)), ((), ())), preferred_element_type=f32
+        )
+        out[0, i] = turned.astype(narrow)
+
+
+def select(local):
+    steps = BLOCK // PART
+    return pl.pallas_call(
+        select_kernel,
+        grid=(SHARDS, steps),
+        in_specs=[pl.BlockSpec((1, 2 * BLOCK + 8, BLOCK), lambda k, c: (k, 0, 0))],
+        out_specs=pl.BlockSpec((1, PART, BLOCK, 2 * BLOCK), lambda k, c: (k * steps + c, 0, 0, 0)),
+        out_shape=jax.ShapeDtypeStruct((PARTS, PART, BLOCK, 2 * BLOCK), narrow),
+        compiler_params=params(52),
+        cost_estimate=pl.CostEstimate(flops=2 * PARTS * PART * BLOCK * BLOCK * 2 * BLOCK, transcendentals=0, bytes_accessed=COVER),
+        name="select",
+    )(local)
+
+
 def step_kernel(part, blocks, *refs, first, last):
     locals_, theta, price, demand = refs[:4], refs[4], refs[5], refs[6]
-    balance, rest = refs[-1], refs[7:-1]
+    if first:
+        balance, rest = refs[-1], refs[7:-1]
+    else:
+        stored, tables, arrived, balance, rest = refs[7], refs[-2], refs[-1], refs[-3], refs[8:-3]
+
+        def piece(c):
+            return pltpu.make_async_copy(stored.at[c], tables.at[c], arrived.at[c])
+
+        for c in range(PARTS):
+            piece(c).start()
     if first:
         flow, cost, rest = flow_views(rest[:5]), cost_views(rest[:5]), rest[5:]
     else:
@@ -159,17 +208,12 @@
     else:
         following, price_out, fresh_out = rest[0], rest[1], rest[2:6]
     balance[...] = jnp.zeros_like(balance)
-    lanes = lax.broadcasted_iota(jnp.int32, (BLOCK, BLOCK), 0).astype(jnp.int16)
-    one = jnp.ones((), bf16)
-    zero = jnp.zeros((), bf16)
-
-    def table(local):
-        return jnp.where(lanes == jnp.broadcast_to(local.astype(jnp.int16), (BLOCK, BLOCK)), one, zero)
-
     for k in range(SHARDS):
         shard = (part[0] - k) & (SHARDS - 1)
 
         def step(o, carry):
+            if not first:
+                piece(k * (OWNERS // UNROLL) + o).wait()
             found = []
             for u in range(UNROLL):
                 owner = o * UNROLL + u
@@ -189,10 +233,13 @@
                     high = extra.astype(bf16)
                     low = (extra - high.astype(f32)).astype(bf16)
                     both = jnp.concatenate([high, low], axis=0)
-                    tables = jnp.concatenate(
-                        [table(locals_[k][pl.ds(j, 1), :]), table(locals_[k][pl.ds(BLOCK + j, 1), :])], axis=0
-                    )
-                    sums = lax.dot_general(both, tables, (((1,), (1,)), ((), ())), preferred_element_type=f32)
+                    if first:
+                        sums = lax.dot_general(
+                            both, ends_table(locals_[k], j), (((1,), (1,)), ((), ())), preferred_element_type=f32
+                        )
+                    else:
+                        chosen = tables[k * (OWNERS // UNROLL) + o, u * QUADS + q].astype(bf16)
+                        sums = lax.dot_general(both, chosen, (((1,), (0,)), ((), ())), preferred_element_type=f32)
                     found.append((j, sums[:8] + sums[8:]))
             for j, sums in found:
                 balance[:, node_slice(blocks[2 * k, j])] += sums[:, :BLOCK]
@@ -250,6 +297,26 @@
         compiler_params=params(52),
         name="pack",
     )(part, *in_hbm([flow] * SHARDS + [cost] * SHARDS + ids))
+
+
+def own_rows_kernel(part, price, demand, price_out, demand_out):
+    del part
+    price_out[...] = price[...]
+    demand_out[...] = demand[...]
+
+
+def own_rows(part, price, demand):
+    taken = pl.BlockSpec((8, CHUNK), lambda c, part: (part[0], c))
+    kept = pl.BlockSpec((8, CHUNK), lambda c, part: (0, c))
+    return pl.pallas_call(
+        own_rows_kernel,
+        grid_spec=pltpu.PrefetchScalarGridSpec(
+            num_scalar_prefetch=1, grid=(NODES // CHUNK,), in_specs=[taken] * 2, out_specs=[kept] * 2
+        ),
+        out_shape=[jax.ShapeDtypeStruct((8, NODES), f32)] * 2,
+        compiler_params=params(52),
+        name="own_rows",
+    )(part, *in_hbm([price, demand]))
 
 
 def own_trial(head_block, tail_block, head_local, tail_local, price, flow, cost):
@@ -291,24 +358,32 @@
     return [pltpu.with_memory_space_constraint(x, pltpu.HBM) for x in values]
 
 
-def advance(part, blocks, locals_, trial, theta, flow, price, demand, flow_cost, first, last):
+def advance(part, blocks, locals_, tables, trial, theta, flow, price, demand, flow_cost, step):
+    first, last = step == 0, step == ITERS - 1
     if first:
         operands = [theta, *in_hbm([price, demand]), *flow_cost]
     elif last:
-        operands = [theta, *in_hbm([price, demand, trial, *flow])]
+        operands = [theta, *in_hbm([price, demand, tables, trial, *flow])]
+    elif step == 1:
+        operands = [theta, *in_hbm([price, demand, tables, trial, *flow]), *flow_cost]
     else:
-        operands = [theta, price, demand, trial, *flow, *flow_cost]
+        operands = [theta, price, demand, *in_hbm([tables]), trial, *flow, *flow_cost]
     shape = [jax.ShapeDtypeStruct((8, NODES // 2), f32)] * 2 if last else [jax.ShapeDtypeStruct((8, NODES), f32)]
     if not last:
         shape = [jax.ShapeDtypeStruct((OWNERS * SHARDS, 8, OWN), f32)] + shape
         shape = shape + [jax.ShapeDtypeStruct((8, OWNERS * OWN), f32)] * SHARDS
+    specs = [smem, smem] + [vmem] * (SHARDS + len(operands))
+    scratch = [pltpu.VMEM((8, NODES), f32)]
+    if not first:
+        specs[2 + SHARDS + 3] = pl.BlockSpec(memory_space=pl.ANY)
+        scratch += [pltpu.VMEM(tables.shape, narrow), pltpu.SemaphoreType.DMA((PARTS,))]
     out = pl.pallas_call(
         functools.partial(step_kernel, first=first, last=last),
-        in_specs=[smem, smem] + [vmem] * (SHARDS + len(operands)),
+        in_specs=specs,
         out_specs=[vmem] * len(shape),
         out_shape=shape,
-        scratch_shapes=[pltpu.VMEM((8, NODES), f32)],
-        compiler_params=params(14),
+        scratch_shapes=scratch,
+        compiler_params=params(58 if first else 30),
         cost_estimate=pl.CostEstimate(flops=2 * 16 * 256 * OWNERS * OWN * SHARDS, transcendentals=0, bytes_accessed=COVER),
         name="step",
     )(part, blocks, *locals_, *operands)
@@ -394,9 +469,6 @@
     def around(values, k):
         return lax.ppermute(values, "arc", [(i, (i + k) % SHARDS) for i in range(SHARDS)])
 
-    def rows_of(values, k):
-        return lax.dynamic_slice(values, (((part + k) & (SHARDS - 1)) * 8, 0), (8, values.shape[1]))
-
     own = part.astype(jnp.int32).reshape(1)
     ids = [head_rows, tail_rows, head_block.reshape(1, BLOCK), tail_block.reshape(1, BLOCK)]
     pieces = pack(own, flow_start, cost, ids)
@@ -405,28 +477,36 @@
     far_flow = around(far_flow, 1)
     far_cost = around(far_cost, 3)
     first = own_trial(head_block, tail_block, head_rows, tail_rows, price_start, flow_start, cost)
+    first, far_flow, far_cost = lax.optimization_barrier((first, far_flow, far_cost))
     values = exchange(first, "com").reshape(OWNERS * SHARDS, 8, OWN)
     far_flow, far_cost, packed, near, behind = lax.optimization_barrier((far_flow, far_cost, packed, near, behind))
     far_flow = around(far_flow, 1)
     far_cost = around(far_cost, 3)
+    locals_ = [packed] + [around(packed, k) for k in range(1, SHARDS)]
+    locals_, far_flow, far_cost, near, behind = lax.optimization_barrier((locals_, far_flow, far_cost, near, behind))
     near = around(near, 1)
     behind = around(behind, 3)
-    locals_ = [packed] + [around(packed, k) for k in range(1, SHARDS)]
     values, far_flow, far_cost, locals_ = lax.optimization_barrier((values, far_flow, far_cost, locals_))
     flow_cost = [here, near, far_flow, far_cost, behind]
     block_ids = jnp.concatenate([x[2 * blocks : 2 * blocks + 2] for x in locals_], axis=0)
-    price = rows_of(price_start, 0)
-    wanted = rows_of(demand, 0)
+    price, wanted = own_rows(own, price_start, demand)
     classes = lax.dynamic_slice(cap_class.reshape(blocks, BLOCK), (place * QUADS, 0), (QUADS, BLOCK))
 
-    trial = flow = None
+    trial = flow = tables = None
     for step in range(ITERS):
         last = step == ITERS - 1
         if step > 0:
             values = exchange(trial, everyone)
+        if step == 1:
+            values, tables = lax.optimization_barrier((values, tables))
         theta, *kept = project(cap_levels, classes, values, last)
         theta = exchange(theta, everyone)
-        trial, price, flow = advance(own, block_ids, locals_, trial, theta, flow, price, wanted, flow_cost, step == 0, last)
+        trial, price, flow = advance(
+            own, block_ids, locals_, tables, trial, theta, flow, price, wanted, flow_cost, step
+        )
+        if step == 0:
+            trial, together = lax.optimization_barrier((trial, jnp.stack(locals_)))
+            tables = select(together)
     back = exchange(kept[0].reshape(OWNERS, com_rows, OWN), "com")
     out = back.transpose(1, 0, 2).reshape(com_rows, arc_cols)
     west, east = price

time: 326 us -> 334 us (1.025)
  blocking collectives: 149 us -> 113 us
  waiting for transfers between devices: 30.2 us -> 52.2 us
  Pallas kernels: 90.6 us -> 103 us
  starting transfers between devices: 44.1 us -> 53.6 us
    all_to_all x6 -> x5, blocking collectives: 149 us -> 113 us  [exchange(): return lax.all_to_all(values, axes, split_axis=0, concat_axis=0, tiled=True)]
    pallas_call x0 -> x2, Pallas kernels: none -> 15.8 us  [the longest x1 14.6 us: select(): pl.pallas_call(select_kernel, grid=(SHARDS, steps), in_specs=[pl.BlockSpe...]
    all_to_all x3 -> x4, waiting for transfers between devices: 3.52 us -> 15.4 us  [exchange(): return lax.all_to_all(values, axes, split_axis=0, concat_axis=0, tiled=True)]
    ppermute x15, waiting for transfers between devices: 26.7 us -> 36.8 us  [around(): lax.ppermute(values, 'arc', [(i, (i + k) % SHARDS) for i in range(SHARDS)])]
    all_to_all x3 -> x4, starting transfers between devices: 21.5 us -> 31.1 us  [exchange(): return lax.all_to_all(values, axes, split_axis=0, concat_axis=0, tiled=True)]
    pallas_call x4, Pallas kernels: 66.6 us -> 59.9 us  [advance(): pl.pallas_call(functools.partial(step_kernel, first=first, last=last), in...]
  transfers between devices with their start and end apart: 18 -> 19, of which waited for: 8 -> 11; matrix products, arithmetic and copies ran while one was open for 2% -> 1% of each run, Pallas kernels for 8% -> 12%
where the time goes in v10:
time: 334 us; the launch traced here: 333 us
  blocking collectives  113 us (34%)
  Pallas kernels  103 us (31%)
  starting transfers between devices  53.6 us (16%)
  waiting for transfers between devices  52.2 us (16%)
  local copies, waits for them, and re-layouts  9.22 us (3%)
    all_to_all x5, blocking collectives, exchange(): return lax.all_to_all(values, axes, split_axis=0, concat_axis=0, tiled=True)  113 us
    pallas_call x4, Pallas kernels, advance(): pl.pallas_call(functools.partial(step_kernel, first=first, last=last), in...  59.9 us
    ppermute x15, waiting for transfers between devices, around(): lax.ppermute(values, 'arc', [(i, (i + k) % SHARDS) for i in range(SHARDS)])  36.8 us
    all_to_all x4, starting transfers between devices, exchange(): return lax.all_to_all(values, axes, split_axis=0, concat_axis=0, tiled=True)  31.1 us
    ppermute x15, starting transfers between devices, around(): lax.ppermute(values, 'arc', [(i, (i + k) % SHARDS) for i in range(SHARDS)])  22.4 us
    all_to_all x4, waiting for transfers between devices, exchange(): return lax.all_to_all(values, axes, split_axis=0, concat_axis=0, tiled=True)  15.4 us
    pallas_call x1, Pallas kernels, select(): pl.pallas_call(select_kernel, grid=(SHARDS, steps), in_specs=[pl.BlockSpe...  14.6 us
    pallas_call x4, Pallas kernels, project(): pl.pallas_call(project_kernel, in_specs=[smem, vmem, vmem], out_specs=[vm...  12.7 us
  transfers between devices with their start and end apart: 19, of which 11 were waited for; matrix products, arithmetic and copies ran while one was open for 1% of the time, Pallas kernels for 12%

profile of v10, /device:TPU:6, one launch (start us, length us, event | category | flops | bytes accessed | tf_op | source)
XLA Modules:
  0.0 332.6 jit_solution(8681242319308782421)
XLA Ops:
  0.7 3.6 %pack.1 = (f32[16,16384]{1,0:T(8,128)}, f32[16,16384]{1,0:T(8,128)}, f32[8,16384]{1,0:T(8,128)S(1)}, f32[8,16384]{1,0:T(8,128)S(1)}, f32[16,16384]{1,0:T(8,128)}, /*index=5*/s32[264,128]{1,0:T(8,128)S(1)}) custom-call(s32[1]{0:T(128)} %bitcast.1.part, f32[32,16384]{1,0:T(8,128)} %flow, f32[32,16384]{1,0:T(8,128)} %flow, f32[32,16384]{1,0:T(8,128)} %flow, ...), custom_call_target="tpu_custom_call" | custom-call | tf_op jit(solution)/shard_map/pack/pallas_call | solution.py:288
  6.2 2.2 collective-permute-start.1
  8.4 8.5 %own_trial.1 = f32[32,32,512]{2,1,0:T(8,128)} custom-call(s32[128]{0:T(128)} %head_block.1, s32[128]{0:T(128)} %tail_block.1, s32[128,128]{1,0:T(8,128)} %bitcast.22, s32[128,128]{1,0:T(8,128)} %bitcast.24, f32[32,16384]{1,0:T(8,128)} %price.1, f32[32,16384]{1,0:T(8,128)} %flow, f32[32,16384]{1,0:T(8,128)} %cost), custom_call_target="tpu_custom_call" | custom-call | tf_op jit(solution)/shard_map/own_trial/pallas_call | solution.py:324
  17.0 3.3 %collective-permute-done = f32[8,16384]{1,0:T(8,128)S(1)} collective-permute-done((f32[8,16384]{1,0:T(8,128)S(1)}, f32[8,16384]{1,0:T(8,128)S(1)}, u32[]{:S(2)}, u32[]{:S(2)}) %collective-permute-start) | collective-permute-done | bytes 524320 | tf_op jit(solution)/shard_map/ppermute | solution.py:470
  20.3 7.7 %all-to-all-start = ((f32[32,32,512]{2,1,0:T(8,128)}), f32[32,32,512]{2,1,0:T(8,128)}, u32[]{:S(2)}, u32[]{:S(2)}) async-start(f32[32,32,512]{2,1,0:T(8,128)} %own_trial.1), calls=%async_computation | async-start | bytes 4194304 | tf_op jit(solution)/shard_map/all_to_all | solution.py:467
  34.4 14.1 %collective-permute-done.4.refs_3_ = s32[264,128]{1,0:T(8,128)S(1)} collective-permute-done((s32[264,128]{1,0:T(8,128)S(1)}, s32[264,128]{1,0:T(8,128)S(1)}, u32[]{:S(2)}, u32[]{:S(2)}) %collective-permute-start.4) | collective-permute-done | bytes 135200 | tf_op jit(solution)/shard_map/ppermute | solution.py:470
  49.9 2.4 collective-permute-start.7
  54.3 3.8 %project.4 = f32[128,4,128]{2,1,0:T(4,128)} custom-call(f32[8]{0:T(128)S(1)} %copy-done.33, s32[4,128]{1,0:T(4,128)S(1)} %constant_dynamic-slice_fusion.classes, f32[128,8,512]{2,1,0:T(8,128)} %bitcast.6.values), custom_call_target="tpu_custom_call" | custom-call | tf_op jit(solution)/shard_map/project/pallas_call | solution.py:347
  58.2 7.7 %all-to-all-start.1 = ((f32[128,4,128]{2,1,0:T(4,128)}), f32[128,4,128]{2,1,0:T(4,128)S(1)}, u32[]{:S(2)}, u32[]{:S(2)}) async-start(f32[128,4,128]{2,1,0:T(4,128)} %project.4), calls=%async_computation.1 | async-start | bytes 524288 | tf_op jit(solution)/shard_map/all_to_all | solution.py:467
  68.0 10.7 %collective-permute-done.7.refs_8_.refs_14_ = f32[16,16384]{1,0:T(8,128)S(1)} collective-permute-done((f32[16,16384]{1,0:T(8,128)}, f32[16,16384]{1,0:T(8,128)S(1)}, u32[]{:S(2)}, u32[]{:S(2)}) %collective-permute-start.7) | collective-permute-done | bytes 1048608 | tf_op jit(solution)/shard_map/ppermute | solution.py:470
  80.2 20.7 %step.4 = (f32[128,8,512]{2,1,0:T(8,128)}, f32[8,16384]{1,0:T(8,128)}, f32[8,16384]{1,0:T(8,128)}, f32[8,16384]{1,0:T(8,128)}, f32[8,16384]{1,0:T(8,128)}, /*index=5*/f32[8,16384]{1,0:T(8,128)}) custom-call(s32[1]{0:T(128)} %bitcast.1.part, s32[8,128]{1,0:T(8,128)} %pad_add_fusion.1.blocks, s32[264,128]{1,0:T(8,128)} %copy-done.14, s32[264,128]{1,0:T(8,128)} %copy-done.20, ...), custom_call_target="tpu_custom_call" | custom-call | flops 536870912 | bytes 40000000 | tf_op jit(solution)/shard_map/step/pallas_call | solution.py:380
  101.0 9.1 %all-to-all-start.2 = ((f32[128,8,512]{2,1,0:T(8,128)}), f32[128,8,512]{2,1,0:T(8,128)}, u32[]{:S(2)}, u32[]{:S(2)}) async-start(f32[128,8,512]{2,1,0:T(8,128)} %get-tuple-element.113.refs_8_), calls=%async_computation.2 | async-start | bytes 4194304 | tf_op jit(solution)/shard_map/all_to_all | solution.py:467
  110.1 14.6 %select.1.refs_7_ = f8e4m3fn[16,32,128,256]{3,2,1,0:T(32,128)(4,1)} custom-call(s32[4,264,128]{2,1,0:T(8,128)S(1)} %pad_add_fusion.local), custom_call_target="tpu_custom_call" | custom-call | flops 4294967296 | bytes 40000000 | tf_op jit(solution)/shard_map/select/pallas_call | solution.py:176
  124.6 14.2 %all-to-all-done.2.values = f32[128,8,512]{2,1,0:T(8,128)} async-done(((f32[128,8,512]{2,1,0:T(8,128)}), f32[128,8,512]{2,1,0:T(8,128)}, u32[]{:S(2)}, u32[]{:S(2)}) %all-to-all-start.2) | async-done | bytes 2097184 | tf_op jit(solution)/shard_map/all_to_all | solution.py:467
  140.2 3.2 project.5
  143.4 14.4 %all_to_all.45.refs_4_ = f32[128,4,128]{2,1,0:T(4,128)S(1)} all-to-all(f32[128,4,128]{2,1,0:T(4,128)S(1)} %project.5), channel_id=1, replica_groups=mesh['com'=32,'arc'=4] {'com','arc'}, dimensions={0} | all-to-all | bytes 524288 | tf_op jit(solution)/shard_map/all_to_all | solution.py:467
  159.8 15.0 %step.5 = (f32[128,8,512]{2,1,0:T(8,128)S(1)}, f32[8,16384]{1,0:T(8,128)S(1)}, f32[8,16384]{1,0:T(8,128)S(1)}, f32[8,16384]{1,0:T(8,128)S(1)}, f32[8,16384]{1,0:T(8,128)S(1)}, /*index=5*/f32[8,16384]{1,0:T(8,128)S(1)}) custom-call(s32[1]{0:T(128)} %bitcast.1.part, s32[8,128]{1,0:T(8,128)S(1)} %copy-done.29, s32[264,128]{1,0:T(8,128)S(1)} %copy-done.15, ...), custom_call_target="tpu_custom_call" | custom-call | flops 536870912 | bytes 40000000 | tf_op jit(solution)/shard_map/step/pallas_call | solution.py:380
  174.9 34.9 %all_to_all.46.values = f32[128,8,512]{2,1,0:T(8,128)S(1)} all-to-all(f32[128,8,512]{2,1,0:T(8,128)S(1)} %get-tuple-element.122.refs_8_), channel_id=1, replica_groups=mesh['com'=32,'arc'=4] {'com','arc'}, dimensions={0} | all-to-all | bytes 4194304 | tf_op jit(solution)/shard_map/all_to_all | solution.py:467
  209.7 2.1 project.6
  211.8 14.4 %all_to_all.47.refs_4_ = f32[128,4,128]{2,1,0:T(4,128)S(1)} all-to-all(f32[128,4,128]{2,1,0:T(4,128)S(1)} %project.6), channel_id=1, replica_groups=mesh['com'=32,'arc'=4] {'com','arc'}, dimensions={0} | all-to-all | bytes 524288 | tf_op jit(solution)/shard_map/all_to_all | solution.py:467
  226.2 13.2 %step.6 = (f32[128,8,512]{2,1,0:T(8,128)S(1)}, f32[8,16384]{1,0:T(8,128)S(1)}, f32[8,16384]{1,0:T(8,128)S(1)}, f32[8,16384]{1,0:T(8,128)S(1)}, f32[8,16384]{1,0:T(8,128)S(1)}, /*index=5*/f32[8,16384]{1,0:T(8,128)S(1)}) custom-call(s32[1]{0:T(128)} %bitcast.1.part, s32[8,128]{1,0:T(8,128)S(1)} %copy-done.29, s32[264,128]{1,0:T(8,128)S(1)} %copy-done.15, ...), custom_call_target="tpu_custom_call" | custom-call | flops 536870912 | bytes 40000000 | tf_op jit(solution)/shard_map/step/pallas_call | solution.py:380
  240.3 34.9 %all_to_all.48.values = f32[128,8,512]{2,1,0:T(8,128)S(1)} all-to-all(f32[128,8,512]{2,1,0:T(8,128)S(1)} %get-tuple-element.128.refs_8_), channel_id=1, replica_groups=mesh['com'=32,'arc'=4] {'com','arc'}, dimensions={0} | all-to-all | bytes 4194304 | tf_op jit(solution)/shard_map/all_to_all | solution.py:467
  275.2 3.6 %project.7 = (f32[128,4,128]{2,1,0:T(4,128)S(1)}, f32[128,8,512]{2,1,0:T(8,128)}) custom-call(f32[8]{0:T(128)S(1)} %copy-done.35, s32[4,128]{1,0:T(4,128)S(1)} %copy-done.32, f32[128,8,512]{2,1,0:T(8,128)S(1)} %all_to_all.48.values), custom_call_target="tpu_custom_call" | custom-call | tf_op jit(solution)/shard_map/project/pallas_call | solution.py:347
  278.8 14.4 %all_to_all.49.refs_4_ = f32[128,4,128]{2,1,0:T(4,128)S(1)} all-to-all(f32[128,4,128]{2,1,0:T(4,128)S(1)} %get-tuple-element.130), channel_id=1, replica_groups=mesh['com'=32,'arc'=4] {'com','arc'}, dimensions={0} | all-to-all | bytes 524288 | tf_op jit(solution)/shard_map/all_to_all | solution.py:467
  293.2 6.7 %all-to-all-start.7 = ((f32[32,32,512]{2,1,0:T(8,128)}), f32[32,32,512]{2,1,0:T(8,128)}, u32[]{:S(2)}, u32[]{:S(2)}) async-start(f32[32,32,512]{2,1,0:T(8,128)} %bitcast.11), calls=%async_computation.7 | async-start | bytes 4194304 | tf_op jit(solution)/shard_map/all_to_all | solution.py:467
  299.9 11.0 %step.7 = (f32[8,8192]{1,0:T(8,128)S(1)}, f32[8,8192]{1,0:T(8,128)S(1)}) custom-call(s32[1]{0:T(128)} %bitcast.1.part, s32[8,128]{1,0:T(8,128)S(1)} %copy-done.29, s32[264,128]{1,0:T(8,128)S(1)} %copy-done.15, s32[264,128]{1,0:T(8,128)S(1)} %copy-done.22, s32[264,128]{1,0:T(8,128)S(1)} %copy-done.19, s32[264,128]{1,0:T(8,128)S(1)} %copy-done.17, ...), custom_call_target="tpu_custom_call" | custom-call | flops 536870912 | bytes 40000000 | tf_op jit(solution)/shard_map/step/pallas_call | solution.py:380
  311.8 2.4 collective-permute-start.12
  314.2 2.0 collective-permute-start.10
  316.2 5.1 %collective-permute-done.9.refs_2_ = f32[8,8192]{1,0:T(8,128)S(1)} collective-permute-done((f32[8,8192]{1,0:T(8,128)S(1)}, f32[8,8192]{1,0:T(8,128)S(1)}, u32[]{:S(2)}, u32[]{:S(2)}) %collective-permute-start.9) | collective-permute-done | bytes 262176 | tf_op jit(solution)/shard_map/ppermute | solution.py:470
  321.3 3.3 collective-permute-start.14
  324.6 2.0 collective-permute-done.11.refs_4_
  328.4 3.1 copy.14
  (107 shorter events, 23.5 us)
Async XLA Ops:
  0.6 52.5 %copy-start = (s32[16384]{0:T(1024)S(1)}, s32[16384]{0:T(1024)}, u32[]{:S(2)}) copy-start(s32[16384]{0:T(1024)} %param.18) | copy-start | bytes 196612
  4.3 63.7 %copy-start.14 = (s32[264,128]{1,0:T(8,128)}, s32[264,128]{1,0:T(8,128)S(1)}, u32[]{:S(2)}) copy-start(s32[264,128]{1,0:T(8,128)S(1)} %get-tuple-element.100.refs_0_) | copy-start | bytes 405508
  4.3 16.0 %collective-permute-start = (f32[8,16384]{1,0:T(8,128)S(1)}, f32[8,16384]{1,0:T(8,128)S(1)}, u32[]{:S(2)}, u32[]{:S(2)}) collective-permute-start(f32[8,16384]{1,0:T(8,128)S(1)} %get-tuple-element.81), channel_id=1, source_target_pairs={{0,1},{1,2},{2,3},{3,0},{4,5},{5,6},{6,7},{7,4},{8,9},{9,10},{10,1... | collective-permute-start | bytes 1572872 | tf_op jit(solution)/shard_map/ppermute | solution.py:470
  6.2 14.0 %collective-permute-start.1 = (f32[8,16384]{1,0:T(8,128)S(1)}, f32[8,16384]{1,0:T(8,128)S(1)}, u32[]{:S(2)}, u32[]{:S(2)}) collective-permute-start(f32[8,16384]{1,0:T(8,128)S(1)} %get-tuple-element.82), channel_id=1, source_target_pairs={{0,3},{1,0},{2,1},{3,2},{4,7},{5,4},{6,5},{7,6},{8,11},{9,8},{10,9... | collective-permute-start | bytes 1572872 | tf_op jit(solution)/shard_map/ppermute | solution.py:470
  17.0 37.4 %copy-start.33 = (f32[8]{0:T(128)S(1)}, f32[8]{0:T(128)}, u32[]{:S(2)}) copy-start(f32[8]{0:T(128)} %levels.7) | copy-start | bytes 100
  20.3 34.0 %all-to-all-start = ((f32[32,32,512]{2,1,0:T(8,128)}), f32[32,32,512]{2,1,0:T(8,128)}, u32[]{:S(2)}, u32[]{:S(2)}) async-start(f32[32,32,512]{2,1,0:T(8,128)} %own_trial.1), calls=%async_computation | async-start | bytes 4194304 | tf_op jit(solution)/shard_map/all_to_all | solution.py:467
  28.0 21.1 %collective-permute-start.5 = (f32[8,16384]{1,0:T(8,128)S(1)}, f32[8,16384]{1,0:T(8,128)S(1)}, u32[]{:S(2)}, u32[]{:S(2)}) collective-permute-start(f32[8,16384]{1,0:T(8,128)S(1)} %collective-permute-done), channel_id=1, source_target_pairs={{0,1},{1,2},{2,3},{3,0},{4,5},{5,6},{6,7},{7,4},{8,9},{9,10},{10,1... | collective-permute-start | bytes 1572872 | tf_op jit(solution)/shard_map/ppermute | solution.py:470
  29.3 19.8 %collective-permute-start.6 = (f32[8,16384]{1,0:T(8,128)S(1)}, f32[8,16384]{1,0:T(8,128)S(1)}, u32[]{:S(2)}, u32[]{:S(2)}) collective-permute-start(f32[8,16384]{1,0:T(8,128)S(1)} %collective-permute-done.1), channel_id=1, source_target_pairs={{0,3},{1,0},{2,1},{3,2},{4,7},{5,4},{6,5},{7,6},{8,11},{9,8},{10,9... | collective-permute-start | bytes 1572872 | tf_op jit(solution)/shard_map/ppermute | solution.py:470
  31.3 17.2 %collective-permute-start.4 = (s32[264,128]{1,0:T(8,128)S(1)}, s32[264,128]{1,0:T(8,128)S(1)}, u32[]{:S(2)}, u32[]{:S(2)}) collective-permute-start(s32[264,128]{1,0:T(8,128)S(1)} %get-tuple-element.100.refs_0_), channel_id=1, source_target_pairs={{0,3},{1,0},{2,1},{3,2},{4,7},{5,4},{6,5},{7,6},{8,11},{9,8},{10,9... | collective-permute-start | bytes 405512 | tf_op jit(solution)/shard_map/ppermute | solution.py:470
  33.1 15.4 %collective-permute-start.3 = (s32[264,128]{1,0:T(8,128)S(1)}, s32[264,128]{1,0:T(8,128)S(1)}, u32[]{:S(2)}, u32[]{:S(2)}) collective-permute-start(s32[264,128]{1,0:T(8,128)S(1)} %get-tuple-element.100.refs_0_), channel_id=1, source_target_pairs={{0,2},{1,3},{2,0},{3,1},{4,6},{5,7},{6,4},{7,5},{8,10},{9,11},{10,... | collective-permute-start | bytes 405512 | tf_op jit(solution)/shard_map/ppermute | solution.py:470
  33.4 15.7 %collective-permute-start.2 = (s32[264,128]{1,0:T(8,128)S(1)}, s32[264,128]{1,0:T(8,128)S(1)}, u32[]{:S(2)}, u32[]{:S(2)}) collective-permute-start(s32[264,128]{1,0:T(8,128)S(1)} %get-tuple-element.100.refs_0_), channel_id=1, source_target_pairs={{0,1},{1,2},{2,3},{3,0},{4,5},{5,6},{6,7},{7,4},{8,9},{9,10},{10,1... | collective-permute-start | bytes 405512 | tf_op jit(solution)/shard_map/ppermute | solution.py:470
  49.9 28.7 %collective-permute-start.7 = (f32[16,16384]{1,0:T(8,128)}, f32[16,16384]{1,0:T(8,128)S(1)}, u32[]{:S(2)}, u32[]{:S(2)}) collective-permute-start(f32[16,16384]{1,0:T(8,128)} %get-tuple-element.108), channel_id=1, source_target_pairs={{0,1},{1,2},{2,3},{3,0},{4,5},{5,6},{6,7},{7,4},{8,9},{9,10},{10,1... | collective-permute-start | bytes 3145736 | tf_op jit(solution)/shard_map/ppermute | solution.py:470
  52.3 26.8 %collective-permute-start.8 = (f32[16,16384]{1,0:T(8,128)}, f32[16,16384]{1,0:T(8,128)S(1)}, u32[]{:S(2)}, u32[]{:S(2)}) collective-permute-start(f32[16,16384]{1,0:T(8,128)} %get-tuple-element.111), channel_id=1, source_target_pairs={{0,3},{1,0},{2,1},{3,2},{4,7},{5,4},{6,5},{7,6},{8,11},{9,8},{10,9... | collective-permute-start | bytes 3145736 | tf_op jit(solution)/shard_map/ppermute | solution.py:470
  58.2 21.0 %all-to-all-start.1 = ((f32[128,4,128]{2,1,0:T(4,128)}), f32[128,4,128]{2,1,0:T(4,128)S(1)}, u32[]{:S(2)}, u32[]{:S(2)}) async-start(f32[128,4,128]{2,1,0:T(4,128)} %project.4), calls=%async_computation.1 | async-start | bytes 524288 | tf_op jit(solution)/shard_map/all_to_all | solution.py:467
  101.0 37.9 %all-to-all-start.2 = ((f32[128,8,512]{2,1,0:T(8,128)}), f32[128,8,512]{2,1,0:T(8,128)}, u32[]{:S(2)}, u32[]{:S(2)}) async-start(f32[128,8,512]{2,1,0:T(8,128)} %get-tuple-element.113.refs_8_), calls=%async_computation.2 | async-start | bytes 4194304 | tf_op jit(solution)/shard_map/all_to_all | solution.py:467
  110.0 47.8 %copy-start.6 = (f32[16,16384]{1,0:T(8,128)S(1)}, f32[16,16384]{1,0:T(8,128)}, u32[]{:S(2)}) copy-start(f32[16,16384]{1,0:T(8,128)} %copy-done.5) | copy-start | bytes 3145732
  110.0 47.8 %copy-start.19 = (s32[264,128]{1,0:T(8,128)S(1)}, s32[264,128]{1,0:T(8,128)}, u32[]{:S(2)}) copy-start(s32[264,128]{1,0:T(8,128)} %copy-done.18) | copy-start | bytes 405508
  110.1 47.8 %copy-start.29 = (s32[8,128]{1,0:T(8,128)S(1)}, s32[8,128]{1,0:T(8,128)}, u32[]{:S(2)}) copy-start(s32[8,128]{1,0:T(8,128)} %pad_add_fusion.1.blocks) | copy-start | bytes 12292
  174.8 34.9 %copy-start.32 = (s32[4,128]{1,0:T(4,128)S(1)}, s32[4,128]{1,0:T(4,128)}, u32[]{:S(2)}) copy-start(s32[4,128]{1,0:T(4,128)} %copy-done.30) | copy-start | bytes 6148
  174.9 34.9 %copy-start.35 = (f32[8]{0:T(128)S(1)}, f32[8]{0:T(128)}, u32[]{:S(2)}) copy-start(f32[8]{0:T(128)} %levels.7) | copy-start | bytes 100
  240.3 34.9 %copy-start.7 = (f32[128,8,512]{2,1,0:T(8,128)}, f32[128,8,512]{2,1,0:T(8,128)S(1)}, u32[]{:S(2)}) copy-start(f32[128,8,512]{2,1,0:T(8,128)S(1)} %get-tuple-element.128.refs_8_) | copy-start | bytes 6291460
  240.3 34.9 %copy-start.23 = (f32[8,16384]{1,0:T(8,128)}, f32[8,16384]{1,0:T(8,128)S(1)}, u32[]{:S(2)}) copy-start(f32[8,16384]{1,0:T(8,128)S(1)} %get-tuple-element.131.refs_5_) | copy-start | bytes 1572868
  240.3 34.9 %copy-start.24 = (f32[8,16384]{1,0:T(8,128)}, f32[8,16384]{1,0:T(8,128)S(1)}, u32[]{:S(2)}) copy-start(f32[8,16384]{1,0:T(8,128)S(1)} %get-tuple-element.132.refs_9_) | copy-start | bytes 1572868
  240.3 34.9 %copy-start.25 = (f32[8,16384]{1,0:T(8,128)}, f32[8,16384]{1,0:T(8,128)S(1)}, u32[]{:S(2)}) copy-start(f32[8,16384]{1,0:T(8,128)S(1)} %get-tuple-element.133.refs_10_) | copy-start | bytes 1572868
  240.3 34.9 %copy-start.26 = (f32[8,16384]{1,0:T(8,128)}, f32[8,16384]{1,0:T(8,128)S(1)}, u32[]{:S(2)}) copy-start(f32[8,16384]{1,0:T(8,128)S(1)} %get-tuple-element.134.refs_11_) | copy-start | bytes 1572868
  293.2 35.2 %all-to-all-start.7 = ((f32[32,32,512]{2,1,0:T(8,128)}), f32[32,32,512]{2,1,0:T(8,128)}, u32[]{:S(2)}, u32[]{:S(2)}) async-start(f32[32,32,512]{2,1,0:T(8,128)} %bitcast.11), calls=%async_computation.7 | async-start | bytes 4194304 | tf_op jit(solution)/shard_map/all_to_all | solution.py:467
  310.9 10.4 %collective-permute-start.9 = (f32[8,8192]{1,0:T(8,128)S(1)}, f32[8,8192]{1,0:T(8,128)S(1)}, u32[]{:S(2)}, u32[]{:S(2)}) collective-permute-start(f32[8,8192]{1,0:T(8,128)S(1)} %get-tuple-element.136.refs_0_), channel_id=1, source_target_pairs={{0,1},{1,2},{2,3},{3,0},{4,5},{5,6},{6,7},{7,4},{8,9},{9,10},{10,1... | collective-permute-start | bytes 786440 | tf_op jit(solution)/shard_map/ppermute | solution.py:470
  311.8 9.5 %collective-permute-start.12 = (f32[8,8192]{1,0:T(8,128)S(1)}, f32[8,8192]{1,0:T(8,128)S(1)}, u32[]{:S(2)}, u32[]{:S(2)}) collective-permute-start(f32[8,8192]{1,0:T(8,128)S(1)} %get-tuple-element.137.refs_1_), channel_id=1, source_target_pairs={{0,3},{1,0},{2,1},{3,2},{4,7},{5,4},{6,5},{7,6},{8,11},{9,8},{10,9... | collective-permute-start | bytes 786440 | tf_op jit(solution)/shard_map/ppermute | solution.py:470
  314.2 12.4 %collective-permute-start.11 = (f32[8,8192]{1,0:T(8,128)S(1)}, f32[8,8192]{1,0:T(8,128)S(1)}, u32[]{:S(2)}, u32[]{:S(2)}) collective-permute-start(f32[8,8192]{1,0:T(8,128)S(1)} %get-tuple-element.136.refs_0_), channel_id=1, source_target_pairs={{0,3},{1,0},{2,1},{3,2},{4,7},{5,4},{6,5},{7,6},{8,11},{9,8},{10,9... | collective-permute-start | bytes 786440 | tf_op jit(solution)/shard_map/ppermute | solution.py:470
  314.2 12.7 %collective-permute-start.10 = (f32[8,8192]{1,0:T(8,128)S(1)}, f32[8,8192]{1,0:T(8,128)S(1)}, u32[]{:S(2)}, u32[]{:S(2)}) collective-permute-start(f32[8,8192]{1,0:T(8,128)S(1)} %get-tuple-element.137.refs_1_), channel_id=1, source_target_pairs={{0,1},{1,2},{2,3},{3,0},{4,5},{5,6},{6,7},{7,4},{8,9},{9,10},{10,1... | collective-permute-start | bytes 786440 | tf_op jit(solution)/shard_map/ppermute | solution.py:470
  321.3 10.4 %collective-permute-start.13 = (f32[8,8192]{1,0:T(8,128)S(1)}, f32[8,8192]{1,0:T(8,128)S(1)}, u32[]{:S(2)}, u32[]{:S(2)}) collective-permute-start(f32[8,8192]{1,0:T(8,128)S(1)} %collective-permute-done.9.refs_2_), channel_id=1, source_target_pairs={{0,1},{1,2},{2,3},{3,0},{4,5},{5,6},{6,7},{7,4},{8,9},{9,10},{10,1... | collective-permute-start | bytes 786440 | tf_op jit(solution)/shard_map/ppermute | solution.py:470
  321.3 10.4 %collective-permute-start.14 = (f32[8,8192]{1,0:T(8,128)S(1)}, f32[8,8192]{1,0:T(8,128)S(1)}, u32[]{:S(2)}, u32[]{:S(2)}) collective-permute-start(f32[8,8192]{1,0:T(8,128)S(1)} %collective-permute-done.12.refs_5_), channel_id=1, source_target_pairs={{0,3},{1,0},{2,1},{3,2},{4,7},{5,4},{6,5},{7,6},{8,11},{9,8},{10,9... | collective-permute-start | bytes 786440 | tf_op jit(solution)/shard_map/ppermute | solution.py:470
  (24 other events, 329.0 us)

commit v11 on v9

--- a/solution.py
+++ b/solution.py
@@ -26,6 +26,9 @@
 
 f32 = jnp.float32
 bf16 = jnp.bfloat16
+narrow = jnp.float8_e4m3fn
+PART = 32
+PARTS = 16
 vmem = pl.BlockSpec(memory_space=pltpu.VMEM)
 smem = pl.BlockSpec(memory_space=pltpu.SMEM)
 
@@ -145,9 +148,52 @@
         lax.fori_loop(0, groups // 8, keep, 0)
 
 
+def ends_table(local, j):
+    nodes = lax.broadcasted_iota(jnp.int32, (BLOCK, BLOCK), 0).astype(jnp.int16)
+    one = jnp.ones((), bf16)
+    zero = jnp.zeros((), bf16)
+
+    def table(row):
+        return jnp.where(nodes == jnp.broadcast_to(row.astype(jnp.int16), (BLOCK, BLOCK)), one, zero)
+
+    return jnp.concatenate([table(local[pl.ds(j, 1), :]), table(local[pl.ds(BLOCK + j, 1), :])], axis=0)
+
+
+def select_kernel(local, out):
+    first = pl.program_id(1) * PART
+    rows = lax.broadcasted_iota(jnp.int32, (BLOCK, BLOCK), 0)
+    cols = lax.broadcasted_iota(jnp.int32, (BLOCK, BLOCK), 1)
+    eye = jnp.where(rows == cols, 1.0, 0.0).astype(bf16)
+    for i in range(PART):
+        turned = lax.dot_general(
+            eye, ends_table(local.at[0], first + i), (((1,), (1,)), ((), ())), preferred_element_type=f32
+        )
+        out[0, i] = turned.astype(narrow)
+
+
+def select(local):
+    steps = BLOCK // PART
+    return pl.pallas_call(
+        select_kernel,
+        grid=(SHARDS, steps),
+        in_specs=[pl.BlockSpec((1, 2 * BLOCK + 8, BLOCK), lambda k, c: (k, 0, 0))],
+        out_specs=pl.BlockSpec((1, PART, BLOCK, 2 * BLOCK), lambda k, c: (k * steps + c, 0, 0, 0)),
+        out_shape=jax.ShapeDtypeStruct((PARTS, PART, BLOCK, 2 * BLOCK), narrow),
+        compiler_params=params(52),
+        cost_estimate=pl.CostEstimate(flops=2 * PARTS * PART * BLOCK * BLOCK * 2 * BLOCK, transcendentals=0, bytes_accessed=COVER),
+        name="select",
+    )(local)
+
+
 def step_kernel(part, blocks, *refs, first, last):
     locals_, theta, price, demand = refs[:4], refs[4], refs[5], refs[6]
-    balance, rest = refs[-1], refs[7:-1]
+    stored, tables, arrived, balance, rest = refs[7], refs[-2], refs[-1], refs[-3], refs[8:-3]
+
+    def piece(c):
+        return pltpu.make_async_copy(stored.at[c], tables.at[c], arrived.at[c])
+
+    for c in range(PARTS):
+        piece(c).start()
     if first:
         flow, cost, rest = flow_views(rest[:5]), cost_views(rest[:5]), rest[5:]
     else:
@@ -159,17 +205,11 @@
     else:
         following, price_out, fresh_out = rest[0], rest[1], rest[2:6]
     balance[...] = jnp.zeros_like(balance)
-    lanes = lax.broadcasted_iota(jnp.int32, (BLOCK, BLOCK), 0).astype(jnp.int16)
-    one = jnp.ones((), bf16)
-    zero = jnp.zeros((), bf16)
-
-    def table(local):
-        return jnp.where(lanes == jnp.broadcast_to(local.astype(jnp.int16), (BLOCK, BLOCK)), one, zero)
-
     for k in range(SHARDS):
         shard = (part[0] - k) & (SHARDS - 1)
 
         def step(o, carry):
+            piece(k * (OWNERS // UNROLL) + o).wait()
             found = []
             for u in range(UNROLL):
                 owner = o * UNROLL + u
@@ -189,10 +229,8 @@
                     high = extra.astype(bf16)
                     low = (extra - high.astype(f32)).astype(bf16)
                     both = jnp.concatenate([high, low], axis=0)
-                    tables = jnp.concatenate(
-                        [table(locals_[k][pl.ds(j, 1), :]), table(locals_[k][pl.ds(BLOCK + j, 1), :])], axis=0
-                    )
-                    sums = lax.dot_general(both, tables, (((1,), (1,)), ((), ())), preferred_element_type=f32)
+                    chosen = tables[k * (OWNERS // UNROLL) + o, u * QUADS + q].astype(bf16)
+                    sums = lax.dot_general(both, chosen, (((1,), (0,)), ((), ())), preferred_element_type=f32)
                     found.append((j, sums[:8] + sums[8:]))
             for j, sums in found:
                 balance[:, node_slice(blocks[2 * k, j])] += sums[:, :BLOCK]
@@ -291,24 +329,31 @@
     return [pltpu.with_memory_space_constraint(x, pltpu.HBM) for x in values]
 
 
-def advance(part, blocks, locals_, trial, theta, flow, price, demand, flow_cost, first, last):
+def advance(part, blocks, locals_, tables, trial, theta, flow, price, demand, flow_cost, first, last):
     if first:
-        operands = [theta, *in_hbm([price, demand]), *flow_cost]
+        operands = [theta, *in_hbm([price, demand, tables]), *flow_cost]
     elif last:
-        operands = [theta, *in_hbm([price, demand, trial, *flow])]
+        operands = [theta, *in_hbm([price, demand, tables, trial, *flow])]
     else:
-        operands = [theta, price, demand, trial, *flow, *flow_cost]
+        operands = [theta, price, demand, *in_hbm([tables]), trial, *flow, *flow_cost]
     shape = [jax.ShapeDtypeStruct((8, NODES // 2), f32)] * 2 if last else [jax.ShapeDtypeStruct((8, NODES), f32)]
     if not last:
         shape = [jax.ShapeDtypeStruct((OWNERS * SHARDS, 8, OWN), f32)] + shape
         shape = shape + [jax.ShapeDtypeStruct((8, OWNERS * OWN), f32)] * SHARDS
+    specs = [smem, smem] + [vmem] * (SHARDS + len(operands))
+    specs[2 + SHARDS + 3] = pl.BlockSpec(memory_space=pl.ANY)
+    scratch = [
+        pltpu.VMEM((8, NODES), f32),
+        pltpu.VMEM(tables.shape, narrow),
+        pltpu.SemaphoreType.DMA((PARTS,)),
+    ]
     out = pl.pallas_call(
         functools.partial(step_kernel, first=first, last=last),
-        in_specs=[smem, smem] + [vmem] * (SHARDS + len(operands)),
+        in_specs=specs,
         out_specs=[vmem] * len(shape),
         out_shape=shape,
-        scratch_shapes=[pltpu.VMEM((8, NODES), f32)],
-        compiler_params=params(14),
+        scratch_shapes=scratch,
+        compiler_params=params(30),
         cost_estimate=pl.CostEstimate(flops=2 * 16 * 256 * OWNERS * OWN * SHARDS, transcendentals=0, bytes_accessed=COVER),
         name="step",
     )(part, blocks, *locals_, *operands)
@@ -412,7 +457,8 @@
     near = around(near, 1)
     behind = around(behind, 3)
     locals_ = [packed] + [around(packed, k) for k in range(1, SHARDS)]
-    values, far_flow, far_cost, locals_ = lax.optimization_barrier((values, far_flow, far_cost, locals_))
+    tables = select(jnp.stack(locals_))
+    values, far_flow, far_cost, locals_, tables = lax.optimization_barrier((values, far_flow, far_cost, locals_, tables))
     flow_cost = [here, near, far_flow, far_cost, behind]
     block_ids = jnp.concatenate([x[2 * blocks : 2 * blocks + 2] for x in locals_], axis=0)
     price = rows_of(price_start, 0)
@@ -426,7 +472,9 @@
             values = exchange(trial, everyone)
         theta, *kept = project(cap_levels, classes, values, last)
         theta = exchange(theta, everyone)
-        trial, price, flow = advance(own, block_ids, locals_, trial, theta, flow, price, wanted, flow_cost, step == 0, last)
+        trial, price, flow = advance(
+            own, block_ids, locals_, tables, trial, theta, flow, price, wanted, flow_cost, step == 0, last
+        )
     back = exchange(kept[0].reshape(OWNERS, com_rows, OWN), "com")
     out = back.transpose(1, 0, 2).reshape(com_rows, arc_cols)
     west, east = price

time: 326 us -> 321 us (0.985)
  waiting for transfers between devices: 30.2 us -> 15.3 us
  local copies, waits for them, and re-layouts: 10.9 us -> 17 us
    ppermute x15, waiting for transfers between devices: 26.7 us -> 9.76 us  [around(): lax.ppermute(values, 'arc', [(i, (i + k) % SHARDS) for i in range(SHARDS)])]
    pallas_call x0 -> x1, Pallas kernels: none -> 14.4 us  [select(): pl.pallas_call(select_kernel, grid=(SHARDS, steps), in_specs=[pl.BlockSpe...]
    pallas_call x4, Pallas kernels: 66.6 us -> 55.1 us  [advance(): pl.pallas_call(functools.partial(step_kernel, first=first, last=last), in...]
    unnamed x32 -> x50, local copies, waits for them, and re-layouts: 3.51 us -> 9.78 us
  transfers between devices with their start and end apart: 18 -> 18, of which waited for: 8 -> 6; matrix products, arithmetic and copies ran while one was open for 2% -> 2% of each run, Pallas kernels for 8% -> 12%
where the time goes in v11:
time: 321 us; the launch traced here: 320 us
  blocking collectives  148 us (46%)
  Pallas kernels  93.5 us (29%)
  starting transfers between devices  45.1 us (14%)
  local copies, waits for them, and re-layouts  17 us (5%)
  waiting for transfers between devices  15.3 us (5%)
    all_to_all x6, blocking collectives, exchange(): return lax.all_to_all(values, axes, split_axis=0, concat_axis=0, tiled=True)  148 us
    pallas_call x4, Pallas kernels, advance(): pl.pallas_call(functools.partial(step_kernel, first=first, last=last), in...  55.1 us
    ppermute x15, starting transfers between devices, around(): lax.ppermute(values, 'arc', [(i, (i + k) % SHARDS) for i in range(SHARDS)])  22.5 us
    all_to_all x3, starting transfers between devices, exchange(): return lax.all_to_all(values, axes, split_axis=0, concat_axis=0, tiled=True)  22.5 us
    pallas_call x1, Pallas kernels, select(): pl.pallas_call(select_kernel, grid=(SHARDS, steps), in_specs=[pl.BlockSpe...  14.4 us
    unnamed x50, local copies, waits for them, and re-layouts  9.78 us
    ppermute x15, waiting for transfers between devices, around(): lax.ppermute(values, 'arc', [(i, (i + k) % SHARDS) for i in range(SHARDS)])  9.76 us
    pallas_call x4, Pallas kernels, project(): pl.pallas_call(project_kernel, in_specs=[smem, vmem, vmem], out_specs=[vm...  9.5 us
  transfers between devices with their start and end apart: 18, of which 6 were waited for; matrix products, arithmetic and copies ran while one was open for 2% of the time, Pallas kernels for 12%

profile of v11, /device:TPU:6, one launch (start us, length us, event | category | flops | bytes accessed | tf_op | source)
XLA Modules:
  0.0 319.6 jit_solution(4476721985504116497)
XLA Ops:
  0.7 3.7 %pack.1 = (f32[16,16384]{1,0:T(8,128)}, f32[16,16384]{1,0:T(8,128)}, f32[8,16384]{1,0:T(8,128)S(1)}, f32[8,16384]{1,0:T(8,128)S(1)}, f32[16,16384]{1,0:T(8,128)}, /*index=5*/s32[264,128]{1,0:T(8,128)S(1)}) custom-call(s32[1]{0:T(128)} %bitcast.1.part, f32[32,16384]{1,0:T(8,128)} %flow, f32[32,16384]{1,0:T(8,128)} %flow, f32[32,16384]{1,0:T(8,128)} %flow, ...), custom_call_target="tpu_custom_call" | custom-call | tf_op jit(solution)/shard_map/pack/pallas_call | solution.py:279
  6.3 2.2 collective-permute-start.1
  8.5 8.5 %own_trial.1 = f32[32,32,512]{2,1,0:T(8,128)} custom-call(s32[128]{0:T(128)} %head_block.1, s32[128]{0:T(128)} %tail_block.1, s32[128,128]{1,0:T(8,128)} %bitcast.22, s32[128,128]{1,0:T(8,128)} %bitcast.24, f32[32,16384]{1,0:T(8,128)} %price, f32[32,16384]{1,0:T(8,128)} %flow, f32[32,16384]{1,0:T(8,128)} %cost), custom_call_target="tpu_custom_call" | custom-call | tf_op jit(solution)/shard_map/own_trial/pallas_call | solution.py:295
  17.0 7.7 %all-to-all-start = ((f32[32,32,512]{2,1,0:T(8,128)}), f32[32,32,512]{2,1,0:T(8,128)}, u32[]{:S(2)}, u32[]{:S(2)}) async-start(f32[32,32,512]{2,1,0:T(8,128)} %own_trial.1), calls=%async_computation | async-start | bytes 4194304 | tf_op jit(solution)/shard_map/all_to_all | solution.py:437
  24.7 2.0 collective-permute-start.6
  30.6 2.2 collective-permute-start.2
  34.8 2.2 collective-permute-start.8
  37.7 14.4 %select.1.refs_7_ = f8e4m3fn[16,32,128,256]{3,2,1,0:T(32,128)(4,1)} custom-call(s32[4,264,128]{2,1,0:T(8,128)S(1)} %pad_add_fusion.local), custom_call_target="tpu_custom_call" | custom-call | flops 4294967296 | bytes 40000000 | tf_op jit(solution)/shard_map/select/pallas_call | solution.py:176
  54.5 3.1 project.4
  58.3 8.1 %all-to-all-start.1 = ((f32[128,4,128]{2,1,0:T(4,128)}), f32[128,4,128]{2,1,0:T(4,128)}, u32[]{:S(2)}, u32[]{:S(2)}) async-start(f32[128,4,128]{2,1,0:T(4,128)} %copy-done.15), calls=%async_computation.1 | async-start | bytes 524288 | tf_op jit(solution)/shard_map/all_to_all | solution.py:437
  68.0 2.1 collective-permute-done.7.refs_9_.refs_14_
  70.1 5.5 %all-to-all-done.1.refs_4_ = f32[128,4,128]{2,1,0:T(4,128)} async-done(((f32[128,4,128]{2,1,0:T(4,128)}), f32[128,4,128]{2,1,0:T(4,128)}, u32[]{:S(2)}, u32[]{:S(2)}) %all-to-all-start.1) | async-done | bytes 262176 | tf_op jit(solution)/shard_map/all_to_all | solution.py:437
  78.6 15.6 %step.4 = (f32[128,8,512]{2,1,0:T(8,128)S(1)}, f32[8,16384]{1,0:T(8,128)S(1)}, f32[8,16384]{1,0:T(8,128)S(1)}, f32[8,16384]{1,0:T(8,128)S(1)}, f32[8,16384]{1,0:T(8,128)S(1)}, /*index=5*/f32[8,16384]{1,0:T(8,128)S(1)}) custom-call(s32[1]{0:T(128)} %bitcast.1.part, s32[8,128]{1,0:T(8,128)S(1)} %pad_add_fusion.1.blocks, ...), custom_call_target="tpu_custom_call" | custom-call | flops 536870912 | bytes 40000000 | tf_op jit(solution)/shard_map/step/pallas_call | solution.py:350
  94.3 34.9 %all_to_all.45.values = f32[128,8,512]{2,1,0:T(8,128)S(1)} all-to-all(f32[128,8,512]{2,1,0:T(8,128)S(1)} %get-tuple-element.84.refs_8_), channel_id=1, replica_groups=mesh['com'=32,'arc'=4] {'com','arc'}, dimensions={0} | all-to-all | bytes 4194304 | tf_op jit(solution)/shard_map/all_to_all | solution.py:437
  129.2 2.1 project.5
  131.2 14.4 %all_to_all.46.refs_4_ = f32[128,4,128]{2,1,0:T(4,128)S(1)} all-to-all(f32[128,4,128]{2,1,0:T(4,128)S(1)} %project.5), channel_id=1, replica_groups=mesh['com'=32,'arc'=4] {'com','arc'}, dimensions={0} | all-to-all | bytes 524288 | tf_op jit(solution)/shard_map/all_to_all | solution.py:437
  145.7 14.2 %step.5 = (f32[128,8,512]{2,1,0:T(8,128)S(1)}, f32[8,16384]{1,0:T(8,128)S(1)}, f32[8,16384]{1,0:T(8,128)S(1)}, f32[8,16384]{1,0:T(8,128)S(1)}, f32[8,16384]{1,0:T(8,128)S(1)}, /*index=5*/f32[8,16384]{1,0:T(8,128)S(1)}) custom-call(s32[1]{0:T(128)} %bitcast.1.part, s32[8,128]{1,0:T(8,128)S(1)} %pad_add_fusion.1.blocks, ...), custom_call_target="tpu_custom_call" | custom-call | flops 536870912 | bytes 40000000 | tf_op jit(solution)/shard_map/step/pallas_call | solution.py:350
  159.9 34.9 %all_to_all.47.values = f32[128,8,512]{2,1,0:T(8,128)S(1)} all-to-all(f32[128,8,512]{2,1,0:T(8,128)S(1)} %get-tuple-element.90.refs_8_), channel_id=1, replica_groups=mesh['com'=32,'arc'=4] {'com','arc'}, dimensions={0} | all-to-all | bytes 4194304 | tf_op jit(solution)/shard_map/all_to_all | solution.py:437
  194.8 2.1 project.6
  196.9 14.4 %all_to_all.48.refs_4_ = f32[128,4,128]{2,1,0:T(4,128)S(1)} all-to-all(f32[128,4,128]{2,1,0:T(4,128)S(1)} %project.6), channel_id=1, replica_groups=mesh['com'=32,'arc'=4] {'com','arc'}, dimensions={0} | all-to-all | bytes 524288 | tf_op jit(solution)/shard_map/all_to_all | solution.py:437
  211.3 14.2 %step.6 = (f32[128,8,512]{2,1,0:T(8,128)S(1)}, f32[8,16384]{1,0:T(8,128)S(1)}, f32[8,16384]{1,0:T(8,128)S(1)}, f32[8,16384]{1,0:T(8,128)S(1)}, f32[8,16384]{1,0:T(8,128)S(1)}, /*index=5*/f32[8,16384]{1,0:T(8,128)S(1)}) custom-call(s32[1]{0:T(128)} %bitcast.1.part, s32[8,128]{1,0:T(8,128)S(1)} %pad_add_fusion.1.blocks, ...), custom_call_target="tpu_custom_call" | custom-call | flops 536870912 | bytes 40000000 | tf_op jit(solution)/shard_map/step/pallas_call | solution.py:350
  226.3 34.9 %all_to_all.49.values = f32[128,8,512]{2,1,0:T(8,128)S(1)} all-to-all(f32[128,8,512]{2,1,0:T(8,128)S(1)} %get-tuple-element.96.refs_8_), channel_id=1, replica_groups=mesh['com'=32,'arc'=4] {'com','arc'}, dimensions={0} | all-to-all | bytes 4194304 | tf_op jit(solution)/shard_map/all_to_all | solution.py:437
  261.2 2.3 project.7
  264.8 14.4 %all_to_all.50.refs_4_ = f32[128,4,128]{2,1,0:T(4,128)S(1)} all-to-all(f32[128,4,128]{2,1,0:T(4,128)S(1)} %get-tuple-element.98), channel_id=1, replica_groups=mesh['com'=32,'arc'=4] {'com','arc'}, dimensions={0} | all-to-all | bytes 524288 | tf_op jit(solution)/shard_map/all_to_all | solution.py:437
  279.3 6.7 %all-to-all-start.7 = ((f32[32,32,512]{2,1,0:T(8,128)}), f32[32,32,512]{2,1,0:T(8,128)}, u32[]{:S(2)}, u32[]{:S(2)}) async-start(f32[32,32,512]{2,1,0:T(8,128)} %bitcast.19), calls=%async_computation.7 | async-start | bytes 4194304 | tf_op jit(solution)/shard_map/all_to_all | solution.py:437
  286.0 11.0 %step.7 = (f32[8,8192]{1,0:T(8,128)S(1)}, f32[8,8192]{1,0:T(8,128)S(1)}) custom-call(s32[1]{0:T(128)} %bitcast.1.part, s32[8,128]{1,0:T(8,128)S(1)} %pad_add_fusion.1.blocks, s32[264,128]{1,0:T(8,128)S(1)} %get-tuple-element.73.refs_0_, s32[264,128]{1,0:T(8,128)S(1)} %copy-done.13, s32[264,128]{1,0:T(8,128)S(1)} %collective-permute-done.5.refs_2_, ...), custom_call_target="tpu_custom_call" | custom-call | flops 536870912 | bytes 40000000 | tf_op jit(solution)/shard_map/step/pallas_call | solution.py:350
  297.9 2.4 collective-permute-start.12
  300.3 2.0 collective-permute-start.10
  302.3 5.1 %collective-permute-done.9.refs_2_ = f32[8,8192]{1,0:T(8,128)S(1)} collective-permute-done((f32[8,8192]{1,0:T(8,128)S(1)}, f32[8,8192]{1,0:T(8,128)S(1)}, u32[]{:S(2)}, u32[]{:S(2)}) %collective-permute-start.9) | collective-permute-done | bytes 262176 | tf_op jit(solution)/shard_map/ppermute | solution.py:440
  307.4 3.3 %collective-permute-start.14 = (f32[8,8192]{1,0:T(8,128)S(1)}, f32[8,8192]{1,0:T(8,128)S(1)}, u32[]{:S(2)}, u32[]{:S(2)}) collective-permute-start(f32[8,8192]{1,0:T(8,128)S(1)} %collective-permute-done.12.refs_5_), channel_id=1, source_target_pairs={{0,3},{1,0},{2,1},{3,2},{4,7},{5,4},{6,5},{7,6},{8,11},{9,8},{10,9... | collective-permute-start | bytes 786440 | tf_op jit(solution)/shard_map/ppermute | solution.py:440
  310.7 2.0 collective-permute-done.11.refs_4_
  314.5 3.1 copy.14
  (83 shorter events, 23.0 us)
Async XLA Ops:
  0.6 65.8 %copy-start = (f32[32,16384]{1,0:T(8,128)S(1)}, f32[32,16384]{1,0:T(8,128)}, u32[]{:S(2)}) copy-start(f32[32,16384]{1,0:T(8,128)} %param.13) | copy-start | bytes 6291460
  4.3 20.4 %collective-permute-start = (f32[8,16384]{1,0:T(8,128)S(1)}, f32[8,16384]{1,0:T(8,128)}, u32[]{:S(2)}, u32[]{:S(2)}) collective-permute-start(f32[8,16384]{1,0:T(8,128)S(1)} %get-tuple-element.65), channel_id=1, source_target_pairs={{0,1},{1,2},{2,3},{3,0},{4,5},{5,6},{6,7},{7,4},{8,9},{9,10},{10,1... | collective-permute-start | bytes 1572872 | tf_op jit(solution)/shard_map/ppermute | solution.py:440
  6.3 18.4 %collective-permute-start.1 = (f32[8,16384]{1,0:T(8,128)S(1)}, f32[8,16384]{1,0:T(8,128)}, u32[]{:S(2)}, u32[]{:S(2)}) collective-permute-start(f32[8,16384]{1,0:T(8,128)S(1)} %get-tuple-element.66), channel_id=1, source_target_pairs={{0,3},{1,0},{2,1},{3,2},{4,7},{5,4},{6,5},{7,6},{8,11},{9,8},{10,9... | collective-permute-start | bytes 1572872 | tf_op jit(solution)/shard_map/ppermute | solution.py:440
  17.0 36.8 %all-to-all-start = ((f32[32,32,512]{2,1,0:T(8,128)}), f32[32,32,512]{2,1,0:T(8,128)}, u32[]{:S(2)}, u32[]{:S(2)}) async-start(f32[32,32,512]{2,1,0:T(8,128)} %own_trial.1), calls=%async_computation | async-start | bytes 4194304 | tf_op jit(solution)/shard_map/all_to_all | solution.py:437
  24.7 9.1 %collective-permute-start.6 = (s32[264,128]{1,0:T(8,128)S(1)}, s32[264,128]{1,0:T(8,128)S(1)}, u32[]{:S(2)}, u32[]{:S(2)}) collective-permute-start(s32[264,128]{1,0:T(8,128)S(1)} %get-tuple-element.73.refs_0_), channel_id=1, source_target_pairs={{0,3},{1,0},{2,1},{3,2},{4,7},{5,4},{6,5},{7,6},{8,11},{9,8},{10,9... | collective-permute-start | bytes 405512 | tf_op jit(solution)/shard_map/ppermute | solution.py:440
  26.7 8.1 %collective-permute-start.5 = (s32[264,128]{1,0:T(8,128)S(1)}, s32[264,128]{1,0:T(8,128)S(1)}, u32[]{:S(2)}, u32[]{:S(2)}) collective-permute-start(s32[264,128]{1,0:T(8,128)S(1)} %get-tuple-element.73.refs_0_), channel_id=1, source_target_pairs={{0,2},{1,3},{2,0},{3,1},{4,6},{5,7},{6,4},{7,5},{8,10},{9,11},{10,... | collective-permute-start | bytes 405512 | tf_op jit(solution)/shard_map/ppermute | solution.py:440
  26.8 10.3 %collective-permute-start.4 = (s32[264,128]{1,0:T(8,128)S(1)}, s32[264,128]{1,0:T(8,128)S(1)}, u32[]{:S(2)}, u32[]{:S(2)}) collective-permute-start(s32[264,128]{1,0:T(8,128)S(1)} %get-tuple-element.73.refs_0_), channel_id=1, source_target_pairs={{0,1},{1,2},{2,3},{3,0},{4,5},{5,6},{6,7},{7,4},{8,9},{9,10},{10,1... | collective-permute-start | bytes 405512 | tf_op jit(solution)/shard_map/ppermute | solution.py:440
  30.6 23.3 %copy-start.21 = (s32[4,128]{1,0:T(4,128)}, s32[4,128]{1,0:T(4,128)S(1)}, u32[]{:S(2)}) copy-start(s32[4,128]{1,0:T(4,128)S(1)} %constant_dynamic-slice_fusion.2.classes) | copy-start | bytes 6148
  30.6 21.6 %collective-permute-start.2 = (f32[8,16384]{1,0:T(8,128)}, f32[8,16384]{1,0:T(8,128)S(1)}, u32[]{:S(2)}, u32[]{:S(2)}) collective-permute-start(f32[8,16384]{1,0:T(8,128)} %collective-permute-done), channel_id=1, source_target_pairs={{0,1},{1,2},{2,3},{3,0},{4,5},{5,6},{6,7},{7,4},{8,9},{9,10},{10,1... | collective-permute-start | bytes 1572872 | tf_op jit(solution)/shard_map/ppermute | solution.py:440
  32.8 20.2 %collective-permute-start.3 = (f32[8,16384]{1,0:T(8,128)}, f32[8,16384]{1,0:T(8,128)S(1)}, u32[]{:S(2)}, u32[]{:S(2)}) collective-permute-start(f32[8,16384]{1,0:T(8,128)} %collective-permute-done.1), channel_id=1, source_target_pairs={{0,3},{1,0},{2,1},{3,2},{4,7},{5,4},{6,5},{7,6},{8,11},{9,8},{10,9... | collective-permute-start | bytes 1572872 | tf_op jit(solution)/shard_map/ppermute | solution.py:440
  33.8 36.3 %collective-permute-start.7 = (f32[16,16384]{1,0:T(8,128)}, f32[16,16384]{1,0:T(8,128)}, u32[]{:S(2)}, u32[]{:S(2)}) collective-permute-start(f32[16,16384]{1,0:T(8,128)} %get-tuple-element.80), channel_id=1, source_target_pairs={{0,1},{1,2},{2,3},{3,0},{4,5},{5,6},{6,7},{7,4},{8,9},{9,10},{10,1... | collective-permute-start | bytes 3145736 | tf_op jit(solution)/shard_map/ppermute | solution.py:440
  34.8 35.3 %collective-permute-start.8 = (f32[16,16384]{1,0:T(8,128)}, f32[16,16384]{1,0:T(8,128)}, u32[]{:S(2)}, u32[]{:S(2)}) collective-permute-start(f32[16,16384]{1,0:T(8,128)} %get-tuple-element.83), channel_id=1, source_target_pairs={{0,3},{1,0},{2,1},{3,2},{4,7},{5,4},{6,5},{7,6},{8,11},{9,8},{10,9... | collective-permute-start | bytes 3145736 | tf_op jit(solution)/shard_map/ppermute | solution.py:440
  52.1 23.5 %copy-start.3 = (f32[16,16384]{1,0:T(8,128)S(1)}, f32[16,16384]{1,0:T(8,128)}, u32[]{:S(2)}) copy-start(f32[16,16384]{1,0:T(8,128)} %get-tuple-element.79.refs_8_.refs_13_) | copy-start | bytes 3145732
  58.3 17.3 %all-to-all-start.1 = ((f32[128,4,128]{2,1,0:T(4,128)}), f32[128,4,128]{2,1,0:T(4,128)}, u32[]{:S(2)}, u32[]{:S(2)}) async-start(f32[128,4,128]{2,1,0:T(4,128)} %copy-done.15), calls=%async_computation.1 | async-start | bytes 524288 | tf_op jit(solution)/shard_map/all_to_all | solution.py:437
  94.2 34.9 %copy-start.22 = (s32[4,128]{1,0:T(4,128)S(1)}, s32[4,128]{1,0:T(4,128)}, u32[]{:S(2)}) copy-start(s32[4,128]{1,0:T(4,128)} %copy-done.21) | copy-start | bytes 6148
  94.2 34.9 %copy-start.24 = (f32[8]{0:T(128)S(1)}, f32[8]{0:T(128)}, u32[]{:S(2)}) copy-start(f32[8]{0:T(128)} %levels.7) | copy-start | bytes 100
  129.1 16.5 %copy-start.2 = (f32[8,16384]{1,0:T(8,128)S(1)}, f32[8,16384]{1,0:T(8,128)}, u32[]{:S(2)}) copy-start(f32[8,16384]{1,0:T(8,128)} %constant_dynamic-slice_fusion.refs_6_) | copy-start | bytes 1572868
  129.1 16.5 %copy-start.7 = (f32[8,16384]{1,0:T(8,128)S(1)}, f32[8,16384]{1,0:T(8,128)}, u32[]{:S(2)}) copy-start(f32[8,16384]{1,0:T(8,128)} %copy-done.5) | copy-start | bytes 1572868
  129.1 16.5 %copy-start.12 = (s32[264,128]{1,0:T(8,128)S(1)}, s32[264,128]{1,0:T(8,128)}, u32[]{:S(2)}) copy-start(s32[264,128]{1,0:T(8,128)} %copy-done.10) | copy-start | bytes 405508
  226.3 34.9 %copy-start.4 = (f32[128,8,512]{2,1,0:T(8,128)}, f32[128,8,512]{2,1,0:T(8,128)S(1)}, u32[]{:S(2)}) copy-start(f32[128,8,512]{2,1,0:T(8,128)S(1)} %get-tuple-element.96.refs_8_) | copy-start | bytes 6291460
  226.3 34.9 %copy-start.16 = (f32[8,16384]{1,0:T(8,128)}, f32[8,16384]{1,0:T(8,128)S(1)}, u32[]{:S(2)}) copy-start(f32[8,16384]{1,0:T(8,128)S(1)} %get-tuple-element.99.refs_5_) | copy-start | bytes 1572868
  226.3 34.9 %copy-start.17 = (f32[8,16384]{1,0:T(8,128)}, f32[8,16384]{1,0:T(8,128)S(1)}, u32[]{:S(2)}) copy-start(f32[8,16384]{1,0:T(8,128)S(1)} %get-tuple-element.100.refs_9_) | copy-start | bytes 1572868
  226.3 34.9 %copy-start.18 = (f32[8,16384]{1,0:T(8,128)}, f32[8,16384]{1,0:T(8,128)S(1)}, u32[]{:S(2)}) copy-start(f32[8,16384]{1,0:T(8,128)S(1)} %get-tuple-element.101.refs_10_) | copy-start | bytes 1572868
  226.3 34.9 %copy-start.19 = (f32[8,16384]{1,0:T(8,128)}, f32[8,16384]{1,0:T(8,128)S(1)}, u32[]{:S(2)}) copy-start(f32[8,16384]{1,0:T(8,128)S(1)} %get-tuple-element.102.refs_11_) | copy-start | bytes 1572868
  279.2 6.7 %copy-start.13 = (s32[264,128]{1,0:T(8,128)S(1)}, s32[264,128]{1,0:T(8,128)}, u32[]{:S(2)}) copy-start(s32[264,128]{1,0:T(8,128)} %copy-done.10) | copy-start | bytes 405508
  279.3 35.2 %all-to-all-start.7 = ((f32[32,32,512]{2,1,0:T(8,128)}), f32[32,32,512]{2,1,0:T(8,128)}, u32[]{:S(2)}, u32[]{:S(2)}) async-start(f32[32,32,512]{2,1,0:T(8,128)} %bitcast.19), calls=%async_computation.7 | async-start | bytes 4194304 | tf_op jit(solution)/shard_map/all_to_all | solution.py:437
  297.0 10.4 %collective-permute-start.9 = (f32[8,8192]{1,0:T(8,128)S(1)}, f32[8,8192]{1,0:T(8,128)S(1)}, u32[]{:S(2)}, u32[]{:S(2)}) collective-permute-start(f32[8,8192]{1,0:T(8,128)S(1)} %get-tuple-element.104.refs_0_), channel_id=1, source_target_pairs={{0,1},{1,2},{2,3},{3,0},{4,5},{5,6},{6,7},{7,4},{8,9},{9,10},{10,1... | collective-permute-start | bytes 786440 | tf_op jit(solution)/shard_map/ppermute | solution.py:440
  297.9 9.5 %collective-permute-start.12 = (f32[8,8192]{1,0:T(8,128)S(1)}, f32[8,8192]{1,0:T(8,128)S(1)}, u32[]{:S(2)}, u32[]{:S(2)}) collective-permute-start(f32[8,8192]{1,0:T(8,128)S(1)} %get-tuple-element.105.refs_1_), channel_id=1, source_target_pairs={{0,3},{1,0},{2,1},{3,2},{4,7},{5,4},{6,5},{7,6},{8,11},{9,8},{10,9... | collective-permute-start | bytes 786440 | tf_op jit(solution)/shard_map/ppermute | solution.py:440
  300.3 12.4 %collective-permute-start.11 = (f32[8,8192]{1,0:T(8,128)S(1)}, f32[8,8192]{1,0:T(8,128)S(1)}, u32[]{:S(2)}, u32[]{:S(2)}) collective-permute-start(f32[8,8192]{1,0:T(8,128)S(1)} %get-tuple-element.104.refs_0_), channel_id=1, source_target_pairs={{0,3},{1,0},{2,1},{3,2},{4,7},{5,4},{6,5},{7,6},{8,11},{9,8},{10,9... | collective-permute-start | bytes 786440 | tf_op jit(solution)/shard_map/ppermute | solution.py:440
  300.3 12.7 %collective-permute-start.10 = (f32[8,8192]{1,0:T(8,128)S(1)}, f32[8,8192]{1,0:T(8,128)S(1)}, u32[]{:S(2)}, u32[]{:S(2)}) collective-permute-start(f32[8,8192]{1,0:T(8,128)S(1)} %get-tuple-element.105.refs_1_), channel_id=1, source_target_pairs={{0,1},{1,2},{2,3},{3,0},{4,5},{5,6},{6,7},{7,4},{8,9},{9,10},{10,1... | collective-permute-start | bytes 786440 | tf_op jit(solution)/shard_map/ppermute | solution.py:440
  307.4 10.4 %collective-permute-start.13 = (f32[8,8192]{1,0:T(8,128)S(1)}, f32[8,8192]{1,0:T(8,128)S(1)}, u32[]{:S(2)}, u32[]{:S(2)}) collective-permute-start(f32[8,8192]{1,0:T(8,128)S(1)} %collective-permute-done.9.refs_2_), channel_id=1, source_target_pairs={{0,1},{1,2},{2,3},{3,0},{4,5},{5,6},{6,7},{7,4},{8,9},{9,10},{10,1... | collective-permute-start | bytes 786440 | tf_op jit(solution)/shard_map/ppermute | solution.py:440
  307.4 10.4 %collective-permute-start.14 = (f32[8,8192]{1,0:T(8,128)S(1)}, f32[8,8192]{1,0:T(8,128)S(1)}, u32[]{:S(2)}, u32[]{:S(2)}) collective-permute-start(f32[8,8192]{1,0:T(8,128)S(1)} %collective-permute-done.12.refs_5_), channel_id=1, source_target_pairs={{0,3},{1,0},{2,1},{3,2},{4,7},{5,4},{6,5},{7,6},{8,11},{9,8},{10,9... | collective-permute-start | bytes 786440 | tf_op jit(solution)/shard_map/ppermute | solution.py:440
  (11 other events, 10.6 us)

commit v12 on v11

--- a/solution.py
+++ b/solution.py
@@ -331,7 +331,7 @@
 
 def advance(part, blocks, locals_, tables, trial, theta, flow, price, demand, flow_cost, first, last):
     if first:
-        operands = [theta, *in_hbm([price, demand, tables]), *flow_cost]
+        operands = [theta, *in_hbm([price, demand, tables, *flow_cost])]
     elif last:
         operands = [theta, *in_hbm([price, demand, tables, trial, *flow])]
     else:

time: 321 us -> 318 us (level)
  local copies, waits for them, and re-layouts: 17 us -> 11.7 us
    unnamed x50 -> x36, local copies, waits for them, and re-layouts: 9.78 us -> 4.49 us
  transfers between devices with their start and end apart: 18 -> 18, of which waited for: 6 -> 6; matrix products, arithmetic and copies ran while one was open for 2% -> 3% of each run, Pallas kernels for 12% -> 12%
where the time goes in v12:
time: 318 us; the launch traced here: 316 us
  blocking collectives  148 us (47%)
  Pallas kernels  94.3 us (30%)
  starting transfers between devices  44.9 us (14%)
  waiting for transfers between devices  15.3 us (5%)
  local copies, waits for them, and re-layouts  11.7 us (4%)
    all_to_all x6, blocking collectives, exchange(): return lax.all_to_all(values, axes, split_axis=0, concat_axis=0, tiled=True)  148 us
    pallas_call x4, Pallas kernels, advance(): pl.pallas_call(functools.partial(step_kernel, first=first, last=last), in...  55.8 us
    ppermute x15, starting transfers between devices, around(): lax.ppermute(values, 'arc', [(i, (i + k) % SHARDS) for i in range(SHARDS)])  22.5 us
    all_to_all x3, starting transfers between devices, exchange(): return lax.all_to_all(values, axes, split_axis=0, concat_axis=0, tiled=True)  22.3 us
    pallas_call x1, Pallas kernels, select(): pl.pallas_call(select_kernel, grid=(SHARDS, steps), in_specs=[pl.BlockSpe...  14.5 us
    ppermute x15, waiting for transfers between devices, around(): lax.ppermute(values, 'arc', [(i, (i + k) % SHARDS) for i in range(SHARDS)])  11.7 us
    pallas_call x4, Pallas kernels, project(): pl.pallas_call(project_kernel, in_specs=[smem, vmem, vmem], out_specs=[vm...  9.5 us
    pallas_call x1, Pallas kernels, own_trial(): pl.pallas_call(own_trial_kernel, grid=(SHARDS, OWNERS * OWN // CHUNK), in...  8.52 us
  transfers between devices with their start and end apart: 18, of which 6 were waited for; matrix products, arithmetic and copies ran while one was open for 3% of the time, Pallas kernels for 12%

profile of v12, /device:TPU:6, one launch (start us, length us, event | category | flops | bytes accessed | tf_op | source)
XLA Modules:
  0.0 316.4 jit_solution(15737568377730454927)
XLA Ops:
  0.7 3.7 %pack.1 = (f32[16,16384]{1,0:T(8,128)}, f32[16,16384]{1,0:T(8,128)}, f32[8,16384]{1,0:T(8,128)S(1)}, f32[8,16384]{1,0:T(8,128)S(1)}, f32[16,16384]{1,0:T(8,128)}, /*index=5*/s32[264,128]{1,0:T(8,128)S(1)}) custom-call(s32[1]{0:T(128)} %bitcast.1.part, f32[32,16384]{1,0:T(8,128)} %flow, f32[32,16384]{1,0:T(8,128)} %flow, f32[32,16384]{1,0:T(8,128)} %flow, ...), custom_call_target="tpu_custom_call" | custom-call | tf_op jit(solution)/shard_map/pack/pallas_call | solution.py:279
  6.3 2.2 collective-permute-start.1
  8.5 8.5 %own_trial.1 = f32[32,32,512]{2,1,0:T(8,128)} custom-call(s32[128]{0:T(128)} %head_block.1, s32[128]{0:T(128)} %tail_block.1, s32[128,128]{1,0:T(8,128)} %bitcast.21, s32[128,128]{1,0:T(8,128)} %bitcast.23, f32[32,16384]{1,0:T(8,128)} %price, f32[32,16384]{1,0:T(8,128)} %flow, f32[32,16384]{1,0:T(8,128)} %cost), custom_call_target="tpu_custom_call" | custom-call | tf_op jit(solution)/shard_map/own_trial/pallas_call | solution.py:295
  17.0 7.7 %all-to-all-start = ((f32[32,32,512]{2,1,0:T(8,128)}), f32[32,32,512]{2,1,0:T(8,128)}, u32[]{:S(2)}, u32[]{:S(2)}) async-start(f32[32,32,512]{2,1,0:T(8,128)} %own_trial.1), calls=%async_computation | async-start | bytes 4194304 | tf_op jit(solution)/shard_map/all_to_all | solution.py:437
  24.7 2.0 collective-permute-start.6
  30.6 2.2 collective-permute-start.2
  34.8 2.2 collective-permute-start.8
  38.0 14.5 %select.1.refs_7_ = f8e4m3fn[16,32,128,256]{3,2,1,0:T(32,128)(4,1)} custom-call(s32[4,264,128]{2,1,0:T(8,128)S(1)} %pad_add_fusion.local), custom_call_target="tpu_custom_call" | custom-call | flops 4294967296 | bytes 40000000 | tf_op jit(solution)/shard_map/select/pallas_call | solution.py:176
  53.2 3.1 project.4
  57.1 8.1 %all-to-all-start.1 = ((f32[128,4,128]{2,1,0:T(4,128)}), f32[128,4,128]{2,1,0:T(4,128)}, u32[]{:S(2)}, u32[]{:S(2)}) async-start(f32[128,4,128]{2,1,0:T(4,128)} %copy-done.8), calls=%async_computation.1 | async-start | bytes 524288 | tf_op jit(solution)/shard_map/all_to_all | solution.py:437
  66.7 4.0 %collective-permute-done.7.refs_9_.refs_14_ = f32[16,16384]{1,0:T(8,128)S(1)} collective-permute-done((f32[16,16384]{1,0:T(8,128)}, f32[16,16384]{1,0:T(8,128)S(1)}, u32[]{:S(2)}, u32[]{:S(2)}) %collective-permute-start.7) | collective-permute-done | bytes 1048608 | tf_op jit(solution)/shard_map/ppermute | solution.py:440
  70.7 3.6 %all-to-all-done.1.refs_4_ = f32[128,4,128]{2,1,0:T(4,128)} async-done(((f32[128,4,128]{2,1,0:T(4,128)}), f32[128,4,128]{2,1,0:T(4,128)}, u32[]{:S(2)}, u32[]{:S(2)}) %all-to-all-start.1) | async-done | bytes 262176 | tf_op jit(solution)/shard_map/all_to_all | solution.py:437
  74.3 16.3 %step.4 = (f32[128,8,512]{2,1,0:T(8,128)S(1)}, f32[8,16384]{1,0:T(8,128)S(1)}, f32[8,16384]{1,0:T(8,128)S(1)}, f32[8,16384]{1,0:T(8,128)S(1)}, f32[8,16384]{1,0:T(8,128)S(1)}, /*index=5*/f32[8,16384]{1,0:T(8,128)S(1)}) custom-call(s32[1]{0:T(128)} %bitcast.1.part, s32[8,128]{1,0:T(8,128)S(1)} %pad_add_fusion.1.blocks, ...), custom_call_target="tpu_custom_call" | custom-call | flops 536870912 | bytes 40000000 | tf_op jit(solution)/shard_map/step/pallas_call | solution.py:350
  90.6 35.4 %all_to_all.45.values = f32[128,8,512]{2,1,0:T(8,128)S(1)} all-to-all(f32[128,8,512]{2,1,0:T(8,128)S(1)} %get-tuple-element.84.refs_8_), channel_id=1, replica_groups=mesh['com'=32,'arc'=4] {'com','arc'}, dimensions={0} | all-to-all | bytes 4194304 | tf_op jit(solution)/shard_map/all_to_all | solution.py:437
  126.1 2.1 project.5
  128.1 14.4 %all_to_all.46.refs_4_ = f32[128,4,128]{2,1,0:T(4,128)S(1)} all-to-all(f32[128,4,128]{2,1,0:T(4,128)S(1)} %project.5), channel_id=1, replica_groups=mesh['com'=32,'arc'=4] {'com','arc'}, dimensions={0} | all-to-all | bytes 524288 | tf_op jit(solution)/shard_map/all_to_all | solution.py:437
  142.6 14.3 %step.5 = (f32[128,8,512]{2,1,0:T(8,128)S(1)}, f32[8,16384]{1,0:T(8,128)S(1)}, f32[8,16384]{1,0:T(8,128)S(1)}, f32[8,16384]{1,0:T(8,128)S(1)}, f32[8,16384]{1,0:T(8,128)S(1)}, /*index=5*/f32[8,16384]{1,0:T(8,128)S(1)}) custom-call(s32[1]{0:T(128)} %bitcast.1.part, s32[8,128]{1,0:T(8,128)S(1)} %pad_add_fusion.1.blocks, ...), custom_call_target="tpu_custom_call" | custom-call | flops 536870912 | bytes 40000000 | tf_op jit(solution)/shard_map/step/pallas_call | solution.py:350
  156.8 34.9 %all_to_all.47.values = f32[128,8,512]{2,1,0:T(8,128)S(1)} all-to-all(f32[128,8,512]{2,1,0:T(8,128)S(1)} %get-tuple-element.90.refs_8_), channel_id=1, replica_groups=mesh['com'=32,'arc'=4] {'com','arc'}, dimensions={0} | all-to-all | bytes 4194304 | tf_op jit(solution)/shard_map/all_to_all | solution.py:437
  191.7 2.1 project.6
  193.8 14.4 %all_to_all.48.refs_4_ = f32[128,4,128]{2,1,0:T(4,128)S(1)} all-to-all(f32[128,4,128]{2,1,0:T(4,128)S(1)} %project.6), channel_id=1, replica_groups=mesh['com'=32,'arc'=4] {'com','arc'}, dimensions={0} | all-to-all | bytes 524288 | tf_op jit(solution)/shard_map/all_to_all | solution.py:437
  208.2 14.2 %step.6 = (f32[128,8,512]{2,1,0:T(8,128)S(1)}, f32[8,16384]{1,0:T(8,128)S(1)}, f32[8,16384]{1,0:T(8,128)S(1)}, f32[8,16384]{1,0:T(8,128)S(1)}, f32[8,16384]{1,0:T(8,128)S(1)}, /*index=5*/f32[8,16384]{1,0:T(8,128)S(1)}) custom-call(s32[1]{0:T(128)} %bitcast.1.part, s32[8,128]{1,0:T(8,128)S(1)} %pad_add_fusion.1.blocks, ...), custom_call_target="tpu_custom_call" | custom-call | flops 536870912 | bytes 40000000 | tf_op jit(solution)/shard_map/step/pallas_call | solution.py:350
  223.3 34.9 %all_to_all.49.values = f32[128,8,512]{2,1,0:T(8,128)S(1)} all-to-all(f32[128,8,512]{2,1,0:T(8,128)S(1)} %get-tuple-element.96.refs_8_), channel_id=1, replica_groups=mesh['com'=32,'arc'=4] {'com','arc'}, dimensions={0} | all-to-all | bytes 4194304 | tf_op jit(solution)/shard_map/all_to_all | solution.py:437
  258.2 2.3 project.7
  261.8 14.4 %all_to_all.50.refs_4_ = f32[128,4,128]{2,1,0:T(4,128)S(1)} all-to-all(f32[128,4,128]{2,1,0:T(4,128)S(1)} %get-tuple-element.98), channel_id=1, replica_groups=mesh['com'=32,'arc'=4] {'com','arc'}, dimensions={0} | all-to-all | bytes 524288 | tf_op jit(solution)/shard_map/all_to_all | solution.py:437
  276.2 6.6 %all-to-all-start.7 = ((f32[32,32,512]{2,1,0:T(8,128)}), f32[32,32,512]{2,1,0:T(8,128)}, u32[]{:S(2)}, u32[]{:S(2)}) async-start(f32[32,32,512]{2,1,0:T(8,128)} %bitcast.18), calls=%async_computation.7 | async-start | bytes 4194304 | tf_op jit(solution)/shard_map/all_to_all | solution.py:437
  282.8 11.0 %step.7 = (f32[8,8192]{1,0:T(8,128)S(1)}, f32[8,8192]{1,0:T(8,128)S(1)}) custom-call(s32[1]{0:T(128)} %bitcast.1.part, s32[8,128]{1,0:T(8,128)S(1)} %pad_add_fusion.1.blocks, s32[264,128]{1,0:T(8,128)S(1)} %get-tuple-element.73.refs_0_, s32[264,128]{1,0:T(8,128)} %collective-permute-done.4.refs_1_, s32[264,128]{1,0:T(8,128)S(1)} %collective-permute-done.5.refs_2_, ...), custom_call_target="tpu_custom_call" | custom-call | flops 536870912 | bytes 40000000 | tf_op jit(solution)/shard_map/step/pallas_call | solution.py:350
  294.7 2.4 collective-permute-start.12
  297.1 2.0 collective-permute-start.10
  299.1 5.1 %collective-permute-done.9.refs_2_ = f32[8,8192]{1,0:T(8,128)S(1)} collective-permute-done((f32[8,8192]{1,0:T(8,128)S(1)}, f32[8,8192]{1,0:T(8,128)S(1)}, u32[]{:S(2)}, u32[]{:S(2)}) %collective-permute-start.9) | collective-permute-done | bytes 262176 | tf_op jit(solution)/shard_map/ppermute | solution.py:440
  304.2 3.3 %collective-permute-start.14 = (f32[8,8192]{1,0:T(8,128)S(1)}, f32[8,8192]{1,0:T(8,128)S(1)}, u32[]{:S(2)}, u32[]{:S(2)}) collective-permute-start(f32[8,8192]{1,0:T(8,128)S(1)} %collective-permute-done.12.refs_5_), channel_id=1, source_target_pairs={{0,3},{1,0},{2,1},{3,2},{4,7},{5,4},{6,5},{7,6},{8,11},{9,8},{10,9... | collective-permute-start | bytes 786440 | tf_op jit(solution)/shard_map/ppermute | solution.py:440
  307.5 2.0 collective-permute-done.11.refs_4_
  311.3 3.1 copy.14
  (69 shorter events, 18.6 us)
Async XLA Ops:
  0.6 64.5 %copy-start = (f32[32,16384]{1,0:T(8,128)S(1)}, f32[32,16384]{1,0:T(8,128)}, u32[]{:S(2)}) copy-start(f32[32,16384]{1,0:T(8,128)} %param.13) | copy-start | bytes 6291460
  4.3 20.4 %collective-permute-start = (f32[8,16384]{1,0:T(8,128)S(1)}, f32[8,16384]{1,0:T(8,128)}, u32[]{:S(2)}, u32[]{:S(2)}) collective-permute-start(f32[8,16384]{1,0:T(8,128)S(1)} %get-tuple-element.65), channel_id=1, source_target_pairs={{0,1},{1,2},{2,3},{3,0},{4,5},{5,6},{6,7},{7,4},{8,9},{9,10},{10,1... | collective-permute-start | bytes 1572872 | tf_op jit(solution)/shard_map/ppermute | solution.py:440
  6.3 18.4 %collective-permute-start.1 = (f32[8,16384]{1,0:T(8,128)S(1)}, f32[8,16384]{1,0:T(8,128)}, u32[]{:S(2)}, u32[]{:S(2)}) collective-permute-start(f32[8,16384]{1,0:T(8,128)S(1)} %get-tuple-element.66), channel_id=1, source_target_pairs={{0,3},{1,0},{2,1},{3,2},{4,7},{5,4},{6,5},{7,6},{8,11},{9,8},{10,9... | collective-permute-start | bytes 1572872 | tf_op jit(solution)/shard_map/ppermute | solution.py:440
  17.0 35.5 %all-to-all-start = ((f32[32,32,512]{2,1,0:T(8,128)}), f32[32,32,512]{2,1,0:T(8,128)}, u32[]{:S(2)}, u32[]{:S(2)}) async-start(f32[32,32,512]{2,1,0:T(8,128)} %own_trial.1), calls=%async_computation | async-start | bytes 4194304 | tf_op jit(solution)/shard_map/all_to_all | solution.py:437
  24.7 9.1 %collective-permute-start.6 = (s32[264,128]{1,0:T(8,128)S(1)}, s32[264,128]{1,0:T(8,128)S(1)}, u32[]{:S(2)}, u32[]{:S(2)}) collective-permute-start(s32[264,128]{1,0:T(8,128)S(1)} %get-tuple-element.73.refs_0_), channel_id=1, source_target_pairs={{0,3},{1,0},{2,1},{3,2},{4,7},{5,4},{6,5},{7,6},{8,11},{9,8},{10,9... | collective-permute-start | bytes 405512 | tf_op jit(solution)/shard_map/ppermute | solution.py:440
  26.7 8.1 %collective-permute-start.5 = (s32[264,128]{1,0:T(8,128)S(1)}, s32[264,128]{1,0:T(8,128)S(1)}, u32[]{:S(2)}, u32[]{:S(2)}) collective-permute-start(s32[264,128]{1,0:T(8,128)S(1)} %get-tuple-element.73.refs_0_), channel_id=1, source_target_pairs={{0,2},{1,3},{2,0},{3,1},{4,6},{5,7},{6,4},{7,5},{8,10},{9,11},{10,... | collective-permute-start | bytes 405512 | tf_op jit(solution)/shard_map/ppermute | solution.py:440
  26.8 10.3 %collective-permute-start.4 = (s32[264,128]{1,0:T(8,128)S(1)}, s32[264,128]{1,0:T(8,128)}, u32[]{:S(2)}, u32[]{:S(2)}) collective-permute-start(s32[264,128]{1,0:T(8,128)S(1)} %get-tuple-element.73.refs_0_), channel_id=1, source_target_pairs={{0,1},{1,2},{2,3},{3,0},{4,5},{5,6},{6,7},{7,4},{8,9},{9,10},{10,1... | collective-permute-start | bytes 405512 | tf_op jit(solution)/shard_map/ppermute | solution.py:440
  30.6 22.0 %copy-start.14 = (s32[4,128]{1,0:T(4,128)}, s32[4,128]{1,0:T(4,128)S(1)}, u32[]{:S(2)}) copy-start(s32[4,128]{1,0:T(4,128)S(1)} %constant_dynamic-slice_fusion.2.classes) | copy-start | bytes 6148
  30.6 22.0 %collective-permute-start.2 = (f32[8,16384]{1,0:T(8,128)}, f32[8,16384]{1,0:T(8,128)}, u32[]{:S(2)}, u32[]{:S(2)}) collective-permute-start(f32[8,16384]{1,0:T(8,128)} %collective-permute-done), channel_id=1, source_target_pairs={{0,1},{1,2},{2,3},{3,0},{4,5},{5,6},{6,7},{7,4},{8,9},{9,10},{10,1... | collective-permute-start | bytes 1572872 | tf_op jit(solution)/shard_map/ppermute | solution.py:440
  32.8 19.7 %collective-permute-start.3 = (f32[8,16384]{1,0:T(8,128)}, f32[8,16384]{1,0:T(8,128)}, u32[]{:S(2)}, u32[]{:S(2)}) collective-permute-start(f32[8,16384]{1,0:T(8,128)} %collective-permute-done.1), channel_id=1, source_target_pairs={{0,3},{1,0},{2,1},{3,2},{4,7},{5,4},{6,5},{7,6},{8,11},{9,8},{10,9... | collective-permute-start | bytes 1572872 | tf_op jit(solution)/shard_map/ppermute | solution.py:440
  33.8 36.9 %collective-permute-start.7 = (f32[16,16384]{1,0:T(8,128)}, f32[16,16384]{1,0:T(8,128)S(1)}, u32[]{:S(2)}, u32[]{:S(2)}) collective-permute-start(f32[16,16384]{1,0:T(8,128)} %get-tuple-element.80), channel_id=1, source_target_pairs={{0,1},{1,2},{2,3},{3,0},{4,5},{5,6},{6,7},{7,4},{8,9},{9,10},{10,1... | collective-permute-start | bytes 3145736 | tf_op jit(solution)/shard_map/ppermute | solution.py:440
  34.8 35.9 %collective-permute-start.8 = (f32[16,16384]{1,0:T(8,128)}, f32[16,16384]{1,0:T(8,128)}, u32[]{:S(2)}, u32[]{:S(2)}) collective-permute-start(f32[16,16384]{1,0:T(8,128)} %get-tuple-element.83), channel_id=1, source_target_pairs={{0,3},{1,0},{2,1},{3,2},{4,7},{5,4},{6,5},{7,6},{8,11},{9,8},{10,9... | collective-permute-start | bytes 3145736 | tf_op jit(solution)/shard_map/ppermute | solution.py:440
  57.1 17.2 %all-to-all-start.1 = ((f32[128,4,128]{2,1,0:T(4,128)}), f32[128,4,128]{2,1,0:T(4,128)}, u32[]{:S(2)}, u32[]{:S(2)}) async-start(f32[128,4,128]{2,1,0:T(4,128)} %copy-done.8), calls=%async_computation.1 | async-start | bytes 524288 | tf_op jit(solution)/shard_map/all_to_all | solution.py:437
  70.7 3.6 %copy-start.4 = (f32[16,16384]{1,0:T(8,128)}, f32[16,16384]{1,0:T(8,128)S(1)}, u32[]{:S(2)}) copy-start(f32[16,16384]{1,0:T(8,128)S(1)} %collective-permute-done.7.refs_9_.refs_14_) | copy-start | bytes 3145732
  90.6 35.4 %copy-start.15 = (s32[4,128]{1,0:T(4,128)S(1)}, s32[4,128]{1,0:T(4,128)}, u32[]{:S(2)}) copy-start(s32[4,128]{1,0:T(4,128)} %copy-done.14) | copy-start | bytes 6148
  90.6 35.4 %copy-start.17 = (f32[8]{0:T(128)S(1)}, f32[8]{0:T(128)}, u32[]{:S(2)}) copy-start(f32[8]{0:T(128)} %levels.7) | copy-start | bytes 100
  126.0 16.5 %copy-start.2 = (f32[8,16384]{1,0:T(8,128)S(1)}, f32[8,16384]{1,0:T(8,128)}, u32[]{:S(2)}) copy-start(f32[8,16384]{1,0:T(8,128)} %constant_dynamic-slice_fusion.refs_6_) | copy-start | bytes 1572868
  126.0 16.5 %copy-start.3 = (f32[16,16384]{1,0:T(8,128)S(1)}, f32[16,16384]{1,0:T(8,128)}, u32[]{:S(2)}) copy-start(f32[16,16384]{1,0:T(8,128)} %get-tuple-element.79.refs_8_.refs_13_) | copy-start | bytes 3145732
  126.1 16.5 %copy-start.5 = (f32[16,16384]{1,0:T(8,128)S(1)}, f32[16,16384]{1,0:T(8,128)}, u32[]{:S(2)}) copy-start(f32[16,16384]{1,0:T(8,128)} %copy-done.4) | copy-start | bytes 3145732
  223.2 34.9 %copy-start.6 = (f32[128,8,512]{2,1,0:T(8,128)}, f32[128,8,512]{2,1,0:T(8,128)S(1)}, u32[]{:S(2)}) copy-start(f32[128,8,512]{2,1,0:T(8,128)S(1)} %get-tuple-element.96.refs_8_) | copy-start | bytes 6291460
  223.2 34.9 %copy-start.9 = (f32[8,16384]{1,0:T(8,128)}, f32[8,16384]{1,0:T(8,128)S(1)}, u32[]{:S(2)}) copy-start(f32[8,16384]{1,0:T(8,128)S(1)} %get-tuple-element.99.refs_5_) | copy-start | bytes 1572868
  223.2 34.9 %copy-start.10 = (f32[8,16384]{1,0:T(8,128)}, f32[8,16384]{1,0:T(8,128)S(1)}, u32[]{:S(2)}) copy-start(f32[8,16384]{1,0:T(8,128)S(1)} %get-tuple-element.100.refs_9_) | copy-start | bytes 1572868
  223.2 34.9 %copy-start.11 = (f32[8,16384]{1,0:T(8,128)}, f32[8,16384]{1,0:T(8,128)S(1)}, u32[]{:S(2)}) copy-start(f32[8,16384]{1,0:T(8,128)S(1)} %get-tuple-element.101.refs_10_) | copy-start | bytes 1572868
  223.3 34.9 %copy-start.12 = (f32[8,16384]{1,0:T(8,128)}, f32[8,16384]{1,0:T(8,128)S(1)}, u32[]{:S(2)}) copy-start(f32[8,16384]{1,0:T(8,128)S(1)} %get-tuple-element.102.refs_11_) | copy-start | bytes 1572868
  276.2 35.1 %all-to-all-start.7 = ((f32[32,32,512]{2,1,0:T(8,128)}), f32[32,32,512]{2,1,0:T(8,128)}, u32[]{:S(2)}, u32[]{:S(2)}) async-start(f32[32,32,512]{2,1,0:T(8,128)} %bitcast.18), calls=%async_computation.7 | async-start | bytes 4194304 | tf_op jit(solution)/shard_map/all_to_all | solution.py:437
  293.8 10.4 %collective-permute-start.9 = (f32[8,8192]{1,0:T(8,128)S(1)}, f32[8,8192]{1,0:T(8,128)S(1)}, u32[]{:S(2)}, u32[]{:S(2)}) collective-permute-start(f32[8,8192]{1,0:T(8,128)S(1)} %get-tuple-element.104.refs_0_), channel_id=1, source_target_pairs={{0,1},{1,2},{2,3},{3,0},{4,5},{5,6},{6,7},{7,4},{8,9},{9,10},{10,1... | collective-permute-start | bytes 786440 | tf_op jit(solution)/shard_map/ppermute | solution.py:440
  294.7 9.5 %collective-permute-start.12 = (f32[8,8192]{1,0:T(8,128)S(1)}, f32[8,8192]{1,0:T(8,128)S(1)}, u32[]{:S(2)}, u32[]{:S(2)}) collective-permute-start(f32[8,8192]{1,0:T(8,128)S(1)} %get-tuple-element.105.refs_1_), channel_id=1, source_target_pairs={{0,3},{1,0},{2,1},{3,2},{4,7},{5,4},{6,5},{7,6},{8,11},{9,8},{10,9... | collective-permute-start | bytes 786440 | tf_op jit(solution)/shard_map/ppermute | solution.py:440
  297.1 12.4 %collective-permute-start.11 = (f32[8,8192]{1,0:T(8,128)S(1)}, f32[8,8192]{1,0:T(8,128)S(1)}, u32[]{:S(2)}, u32[]{:S(2)}) collective-permute-start(f32[8,8192]{1,0:T(8,128)S(1)} %get-tuple-element.104.refs_0_), channel_id=1, source_target_pairs={{0,3},{1,0},{2,1},{3,2},{4,7},{5,4},{6,5},{7,6},{8,11},{9,8},{10,9... | collective-permute-start | bytes 786440 | tf_op jit(solution)/shard_map/ppermute | solution.py:440
  297.1 12.7 %collective-permute-start.10 = (f32[8,8192]{1,0:T(8,128)S(1)}, f32[8,8192]{1,0:T(8,128)S(1)}, u32[]{:S(2)}, u32[]{:S(2)}) collective-permute-start(f32[8,8192]{1,0:T(8,128)S(1)} %get-tuple-element.105.refs_1_), channel_id=1, source_target_pairs={{0,1},{1,2},{2,3},{3,0},{4,5},{5,6},{6,7},{7,4},{8,9},{9,10},{10,1... | collective-permute-start | bytes 786440 | tf_op jit(solution)/shard_map/ppermute | solution.py:440
  304.2 10.4 %collective-permute-start.13 = (f32[8,8192]{1,0:T(8,128)S(1)}, f32[8,8192]{1,0:T(8,128)S(1)}, u32[]{:S(2)}, u32[]{:S(2)}) collective-permute-start(f32[8,8192]{1,0:T(8,128)S(1)} %collective-permute-done.9.refs_2_), channel_id=1, source_target_pairs={{0,1},{1,2},{2,3},{3,0},{4,5},{5,6},{6,7},{7,4},{8,9},{9,10},{10,1... | collective-permute-start | bytes 786440 | tf_op jit(solution)/shard_map/ppermute | solution.py:440
  304.2 10.4 %collective-permute-start.14 = (f32[8,8192]{1,0:T(8,128)S(1)}, f32[8,8192]{1,0:T(8,128)S(1)}, u32[]{:S(2)}, u32[]{:S(2)}) collective-permute-start(f32[8,8192]{1,0:T(8,128)S(1)} %collective-permute-done.12.refs_5_), channel_id=1, source_target_pairs={{0,3},{1,0},{2,1},{3,2},{4,7},{5,4},{6,5},{7,6},{8,11},{9,8},{10,9... | collective-permute-start | bytes 786440 | tf_op jit(solution)/shard_map/ppermute | solution.py:440
  314.6 1.8 copy-start.1
  (4 other events, 3.5 us)
